TPU v7x, 32 devices: a whole 2x2x4 slice. The times are simulated.
32 devices in a mesh: dp: 8 (over z, y), seq: 4 (over x, core).
Axes of the slice: x: 2, y: 2, z: 4, core: 2. Of those that a mesh axis runs over, the one named last changes fastest.
Arguments:
- tokens: bfloat16 [8, 2048, 896], P('dp', 'seq'), may hold values from -30 to 30
- neighbours: bfloat16 [8, 32, 2, 128, 896], P('dp', 'seq'), may hold values from -6 to 6
- norm_gains: float32 [3, 896], replicated, may hold values from 0.25 to 1.75
- position_bias: float32 [16, 6], replicated, may hold values from -1.5 to 1.5
- query_self: bfloat16 [896, 1024], P('dp', 'seq'), may hold values from -0.1875 to 0.1875
- key_self: bfloat16 [896, 1024], P('dp', 'seq'), may hold values from -0.1875 to 0.1875
- value_self: bfloat16 [896, 1024], P('dp', 'seq'), may hold values from -0.1875 to 0.1875
- output_self: bfloat16 [1024, 896], P('dp', 'seq'), may hold values from -1 to 1
- query_cross: bfloat16 [896, 1024], P('dp', 'seq'), may hold values from -0.1875 to 0.1875
- key_cross: bfloat16 [896, 1024], P('dp', 'seq'), may hold values from -0.1875 to 0.1875
- value_cross: bfloat16 [896, 1024], P('dp', 'seq'), may hold values from -0.1875 to 0.1875
- output_cross: bfloat16 [1024, 896], P('dp', 'seq'), may hold values from -1.5 to 1.5
- inner_weight: bfloat16 [896, 3584], P('dp', 'seq'), may hold values from -0.1875 to 0.1875
- outer_weight: bfloat16 [3584, 896], P('dp', 'seq'), may hold values from -0.09375 to 0.09375
- cotangent: bfloat16 [8, 2048, 896], P('dp', 'seq'), may hold values from -6 to 6
Outputs:
- result: bfloat16 [8, 2048, 896], P('dp', 'seq')
- grad_tokens: bfloat16 [8, 2048, 896], P('dp', 'seq')
- grad_neighbours: bfloat16 [8, 32, 2, 128, 896], P('dp', 'seq')
- grad_gains: float32 [3, 896], replicated
- grad_bias: float32 [16, 6], replicated
- grad_query_self: float32 [896, 1024], P('dp', 'seq')
- grad_key_self: float32 [896, 1024], P('dp', 'seq')
- grad_value_self: float32 [896, 1024], P('dp', 'seq')
- grad_output_self: float32 [1024, 896], P('dp', 'seq')
- grad_query_cross: float32 [896, 1024], P('dp', 'seq')
- grad_key_cross: float32 [896, 1024], P('dp', 'seq')
- grad_value_cross: float32 [896, 1024], P('dp', 'seq')
- grad_output_cross: float32 [1024, 896], P('dp', 'seq')
- grad_inner: float32 [896, 3584], P('dp', 'seq')
- grad_outer: float32 [3584, 896], P('dp', 'seq')
All inputs are finite; a program needn't handle non-finite values.
Results may differ from a plain program's by a relative error of at most 0.025.
Values may be sent and summed in bfloat16 or wider, within the bound.
A program may use at most 384 MiB of HBM per device.

v0:
```python
import jax
import jax.numpy as jnp
from jax import lax
from jax.sharding import PartitionSpec as P

HD = 64
SEGMENT = 64
BLOCK = 256
NB = 6
SEQ_MIN = 2048


EPSILON = 1e-06
NEGATIVE = -1e30
HIGHEST = lax.Precision.HIGHEST


def passed_along(value, axis, by):
    peers = lax.axis_size(axis)
    pairs = [(i, i + by) for i in range(peers) if 0 <= i + by < peers]
    return lax.ppermute(value, axis, pairs)


def as_sent(value):
    return jax.tree.map(lambda a: a.astype(jnp.bfloat16) if a.dtype == jnp.float32 else a, value)


def linear(left_side, right_side):
    return jnp.dot(left_side, right_side, preferred_element_type=jnp.float32)


def weight_grad(left_side, right_side):
    return lax.dot_general(
        left_side, right_side, (((0,), (0,)), ((), ())), preferred_element_type=jnp.float32
    )


def input_grad(left_side, right_side):
    return lax.dot_general(
        left_side, right_side, (((1,), (1,)), ((), ())), preferred_element_type=jnp.float32
    )


def rounded(operand):
    return operand.astype(jnp.bfloat16)


def rms_apply(inputs, gain_row):
    factor = lax.rsqrt(jnp.mean(inputs * inputs, axis=-1, keepdims=True) + EPSILON)
    return inputs * factor * gain_row


def norm_back(inputs, gain_row, upstream):
    normed_value, pullback = jax.vjp(rms_apply, inputs, gain_row)
    return pullback(upstream)


def gelu_tanh(operand):
    return jax.nn.gelu(operand, approximate=True)


def split_heads(row_data, head_count):
    return row_data.reshape(row_data.shape[0], head_count, row_data.shape[1] // head_count)


def slot_pad(row_data, head_count):
    row_width = row_data.shape[1]
    front_rows = jnp.zeros((1, row_width), row_data.dtype)
    back_rows = jnp.zeros((SEGMENT - 1, row_width), row_data.dtype)
    padded = jnp.concatenate([front_rows, row_data, back_rows], axis=0)
    return padded.reshape(padded.shape[0] // SEGMENT, SEGMENT, head_count, row_width // head_count)


def slot_unpad(slotted, tok_rows):
    row_width = slotted.shape[2] * slotted.shape[3]
    return slotted.reshape(slotted.shape[0] * SEGMENT, row_width)[1 : tok_rows + 1]


def self_scores(query_heads, key_heads, offset, position, bias_table, block_dev):
    head_count = query_heads.shape[1]
    head_dim = query_heads.shape[2]
    tok_rows = query_heads.shape[0]
    logits = jnp.einsum(
        "qhd,khd->hqk", query_heads, key_heads, preferred_element_type=jnp.float32
    ) * head_dim ** (-0.5)
    blocks = jnp.arange(block_dev, dtype=jnp.int32)
    distance = offset * block_dev + blocks[:, None] - blocks[None, :]
    bucket = jnp.clip(distance, 0, NB - 1)
    onehot = (bucket[:, :, None] == jnp.arange(NB, dtype=jnp.int32)).astype(jnp.float32)
    bias_terms = jnp.einsum("hn,abn->hab", bias_table, onehot, precision=HIGHEST)
    allowed = (distance >= 0) & (offset <= position)
    shaped = (
        logits.reshape(head_count, block_dev, BLOCK, block_dev, BLOCK)
        + bias_terms[:, :, None, :, None]
    )
    shaped = jnp.where(allowed[None, :, None, :, None], shaped, NEGATIVE)
    return (shaped.reshape(head_count, tok_rows, tok_rows), onehot)


def bias_grad(grad_scores, onehot, block_dev):
    head_count = grad_scores.shape[0]
    block_sums = jnp.sum(
        grad_scores.astype(jnp.float32).reshape(head_count, block_dev, BLOCK, block_dev, BLOCK),
        axis=(2, 4),
    )
    return jnp.einsum("hab,abn->hn", block_sums, onehot, precision=HIGHEST)


def on_device(
    tokens,
    neighbours,
    norm_gains,
    position_bias,
    query_self,
    key_self,
    value_self,
    output_self,
    query_cross,
    key_cross,
    value_cross,
    output_cross,
    inner_weight,
    outer_weight,
    cotangent,
):
    tok_rows = tokens.shape[1]
    model_width = tokens.shape[2]
    head_count = position_bias.shape[0]
    head_dim = HD
    attn_width = head_count * head_dim
    factor = head_dim ** (-0.5)
    block_dev = tok_rows // BLOCK
    segment_count = tok_rows // SEGMENT
    neighbour_rows = neighbours.shape[2] * neighbours.shape[3]
    span_devs = min(lax.axis_size("seq"), max(2, SEQ_MIN // tok_rows))
    position = lax.axis_index("seq") % span_devs
    inputs = tokens.reshape(tok_rows, model_width).astype(jnp.float32)
    upstream = cotangent.reshape(tok_rows, model_width).astype(jnp.float32)
    shards = (
        query_self,
        key_self,
        value_self,
        output_self,
        query_cross,
        key_cross,
        value_cross,
        output_cross,
        inner_weight,
        outer_weight,
    )
    columns = (
        lax.all_gather(shards[0], "seq", axis=1, tiled=True),
        lax.all_gather(shards[1], "seq", axis=1, tiled=True),
        lax.all_gather(shards[2], "seq", axis=1, tiled=True),
        lax.all_gather(shards[3], "seq", axis=1, tiled=True),
        lax.all_gather(shards[4], "seq", axis=1, tiled=True),
        lax.all_gather(shards[5], "seq", axis=1, tiled=True),
        lax.all_gather(shards[6], "seq", axis=1, tiled=True),
        lax.all_gather(shards[7], "seq", axis=1, tiled=True),
        lax.all_gather(shards[8], "seq", axis=1, tiled=True),
        lax.all_gather(shards[9], "seq", axis=1, tiled=True),
    )
    gathered = (
        lax.all_gather(columns[0], "dp", axis=0, tiled=True),
        lax.all_gather(columns[1], "dp", axis=0, tiled=True),
        lax.all_gather(columns[2], "dp", axis=0, tiled=True),
        lax.all_gather(columns[3], "dp", axis=0, tiled=True),
        lax.all_gather(columns[4], "dp", axis=0, tiled=True),
        lax.all_gather(columns[5], "dp", axis=0, tiled=True),
        lax.all_gather(columns[6], "dp", axis=0, tiled=True),
        lax.all_gather(columns[7], "dp", axis=0, tiled=True),
        lax.all_gather(columns[8], "dp", axis=0, tiled=True),
        lax.all_gather(columns[9], "dp", axis=0, tiled=True),
    )
    (
        query_full,
        key_full,
        value_full,
        output_full,
        recall_query,
        recall_key,
        recall_value,
        recall_output,
        inner_full,
        outer_full,
    ) = gathered
    first_normed = rounded(rms_apply(inputs, norm_gains[0]))
    queries = rounded(linear(first_normed, query_full))
    own_pairs = rounded(linear(first_normed, jnp.concatenate([key_full, value_full], axis=1)))
    query_heads = split_heads(queries, head_count)
    received_list = [(0, own_pairs)]
    for offset in range(1, span_devs):
        received_list.append((offset, passed_along(own_pairs, "seq", offset)))
    running_max = jnp.full((head_count, tok_rows), NEGATIVE, jnp.float32)
    running_sum = jnp.zeros((head_count, tok_rows), jnp.float32)
    for offset, paired in received_list:
        scores, onehot = self_scores(
            query_heads,
            split_heads(paired[:, :attn_width], head_count),
            offset,
            position,
            position_bias,
            block_dev,
        )
        new_max = jnp.maximum(running_max, jnp.max(scores, axis=2))
        running_sum = running_sum * jnp.exp(running_max - new_max) + jnp.sum(
            jnp.exp(scores - new_max[:, :, None]), axis=2
        )
        running_max = new_max
    log_total = running_max + jnp.log(running_sum)
    attended = jnp.zeros((tok_rows, head_count, head_dim), jnp.float32)
    for offset, paired in received_list:
        scores, onehot = self_scores(
            query_heads,
            split_heads(paired[:, :attn_width], head_count),
            offset,
            position,
            position_bias,
            block_dev,
        )
        soft_round = rounded(jnp.exp(scores - log_total[:, :, None]))
        attended = attended + jnp.einsum(
            "hqk,khd->qhd",
            soft_round,
            split_heads(paired[:, attn_width:], head_count),
            preferred_element_type=jnp.float32,
        )
    attended = attended.reshape(tok_rows, attn_width)
    mixed_self = rounded(attended)
    after_self = inputs + linear(mixed_self, output_full)
    second_normed = rounded(rms_apply(after_self, norm_gains[1]))
    cross_queries = rounded(linear(second_normed, recall_query))
    flat_states = neighbours.reshape(segment_count * neighbour_rows, model_width)
    recall_pairs = rounded(
        linear(flat_states, jnp.concatenate([recall_key, recall_value], axis=1))
    ).reshape(segment_count, neighbour_rows, 2 * attn_width)
    edge_states = passed_along(recall_pairs[segment_count - 1], "seq", 1)
    edge_states = jnp.where(position > 0, edge_states, jnp.zeros_like(edge_states))
    slot_pairs = jnp.concatenate([edge_states[None], recall_pairs], axis=0)
    slot_keys = slot_pairs[:, :, :attn_width].reshape(
        segment_count + 1, neighbour_rows, head_count, head_dim
    )
    slot_values = slot_pairs[:, :, attn_width:].reshape(
        segment_count + 1, neighbour_rows, head_count, head_dim
    )
    padded_queries = slot_pad(cross_queries, head_count)
    cross_scores = (
        jnp.einsum("sqhd,skhd->shqk", padded_queries, slot_keys, preferred_element_type=jnp.float32)
        * factor
    )
    cross_soft = jax.nn.softmax(cross_scores, axis=-1)
    cross_round = rounded(cross_soft)
    cross_mixed = jnp.einsum(
        "shqk,skhd->sqhd", cross_round, slot_values, preferred_element_type=jnp.float32
    )
    mixed_cross = rounded(slot_unpad(cross_mixed, tok_rows))
    after_cross = after_self + linear(mixed_cross, recall_output)
    third_normed = rounded(rms_apply(after_cross, norm_gains[2]))
    gate_value = linear(third_normed, inner_full)
    activated, gelu_pull = jax.vjp(gelu_tanh, gate_value)
    hidden_act = rounded(activated)
    outcome = after_cross + linear(hidden_act, outer_full)
    columns_back = (
        lax.all_gather(shards[0], "seq", axis=1, tiled=True),
        lax.all_gather(shards[1], "seq", axis=1, tiled=True),
        lax.all_gather(shards[2], "seq", axis=1, tiled=True),
        lax.all_gather(shards[3], "seq", axis=1, tiled=True),
        lax.all_gather(shards[4], "seq", axis=1, tiled=True),
        lax.all_gather(shards[5], "seq", axis=1, tiled=True),
        lax.all_gather(shards[6], "seq", axis=1, tiled=True),
        lax.all_gather(shards[7], "seq", axis=1, tiled=True),
        lax.all_gather(shards[8], "seq", axis=1, tiled=True),
        lax.all_gather(shards[9], "seq", axis=1, tiled=True),
    )
    gathered_back = (
        lax.all_gather(columns_back[0], "dp", axis=0, tiled=True),
        lax.all_gather(columns_back[1], "dp", axis=0, tiled=True),
        lax.all_gather(columns_back[2], "dp", axis=0, tiled=True),
        lax.all_gather(columns_back[3], "dp", axis=0, tiled=True),
        lax.all_gather(columns_back[4], "dp", axis=0, tiled=True),
        lax.all_gather(columns_back[5], "dp", axis=0, tiled=True),
        lax.all_gather(columns_back[6], "dp", axis=0, tiled=True),
        lax.all_gather(columns_back[7], "dp", axis=0, tiled=True),
        lax.all_gather(columns_back[8], "dp", axis=0, tiled=True),
        lax.all_gather(columns_back[9], "dp", axis=0, tiled=True),
    )
    (
        query_full,
        key_full,
        value_full,
        output_full,
        recall_query,
        recall_key,
        recall_value,
        recall_output,
        inner_full,
        outer_full,
    ) = gathered_back
    grad_feed = rounded(upstream)
    grad_hidden = input_grad(grad_feed, outer_full)
    grad_gate = rounded(gelu_pull(grad_hidden)[0])
    feed_terms = (weight_grad(third_normed, grad_gate), weight_grad(hidden_act, grad_feed))
    norm_grad, gain_three = norm_back(after_cross, norm_gains[2], input_grad(grad_gate, inner_full))
    grad_late = upstream + norm_grad
    grad_cross = rounded(grad_late)
    grad_mixed = rounded(input_grad(grad_cross, recall_output))
    padded_grad = slot_pad(grad_mixed, head_count)
    values_grad = jnp.einsum(
        "shqk,sqhd->skhd", cross_round, padded_grad, preferred_element_type=jnp.float32
    )
    soft_grad = jnp.einsum(
        "sqhd,skhd->shqk", padded_grad, slot_values, preferred_element_type=jnp.float32
    )
    scores_grad = rounded(
        cross_soft * (soft_grad - jnp.sum(cross_soft * soft_grad, axis=-1, keepdims=True))
    )
    query_back = (
        jnp.einsum("shqk,skhd->sqhd", scores_grad, slot_keys, preferred_element_type=jnp.float32)
        * factor
    )
    probe_round = rounded(slot_unpad(query_back, tok_rows))
    keys_grad = (
        jnp.einsum(
            "shqk,sqhd->skhd", scores_grad, padded_queries, preferred_element_type=jnp.float32
        )
        * factor
    )
    pairs_grad = jnp.concatenate(
        [
            keys_grad.reshape(segment_count + 1, neighbour_rows, attn_width),
            values_grad.reshape(segment_count + 1, neighbour_rows, attn_width),
        ],
        axis=2,
    )
    sent_back = jnp.where(position > 0, pairs_grad[0], jnp.zeros_like(pairs_grad[0]))
    returned = passed_along(sent_back.astype(jnp.bfloat16), "seq", -1).astype(sent_back.dtype)
    local_pairs = pairs_grad[1:].at[segment_count - 1].add(returned)
    pair_round = rounded(local_pairs.reshape(segment_count * neighbour_rows, 2 * attn_width))
    grad_states = input_grad(pair_round, jnp.concatenate([recall_key, recall_value], axis=1))
    cross_terms = (
        weight_grad(second_normed, probe_round),
        weight_grad(flat_states, pair_round[:, :attn_width]),
        weight_grad(flat_states, pair_round[:, attn_width:]),
        weight_grad(mixed_cross, grad_cross),
    )
    norm_grad, gain_two = norm_back(
        after_self, norm_gains[1], input_grad(probe_round, recall_query)
    )
    grad_early = grad_late + norm_grad
    grad_self = rounded(grad_early)
    grad_attended = rounded(input_grad(grad_self, output_full))
    grad_heads = split_heads(grad_attended, head_count)
    row_dots = jnp.sum(
        grad_attended.astype(jnp.float32).reshape(tok_rows, head_count, head_dim)
        * attended.reshape(tok_rows, head_count, head_dim),
        axis=2,
    ).T
    grad_queries = jnp.zeros((tok_rows, head_count, head_dim), jnp.float32)
    bias_total = jnp.zeros((head_count, NB), jnp.float32)
    own_grad = jnp.zeros((tok_rows, 2 * attn_width), jnp.float32)
    for offset, paired in received_list:
        piece_keys = split_heads(paired[:, :attn_width], head_count)
        piece_values = split_heads(paired[:, attn_width:], head_count)
        scores, onehot = self_scores(
            query_heads, piece_keys, offset, position, position_bias, block_dev
        )
        soft_full = jnp.exp(scores - log_total[:, :, None])
        soft_round = rounded(soft_full)
        grad_values = jnp.einsum(
            "hqk,qhd->khd", soft_round, grad_heads, preferred_element_type=jnp.float32
        )
        grad_soft = jnp.einsum(
            "qhd,khd->hqk", grad_heads, piece_values, preferred_element_type=jnp.float32
        )
        grad_scores = rounded(soft_full * (grad_soft - row_dots[:, :, None]))
        grad_queries = (
            grad_queries
            + jnp.einsum(
                "hqk,khd->qhd", grad_scores, piece_keys, preferred_element_type=jnp.float32
            )
            * factor
        )
        grad_keys = (
            jnp.einsum("hqk,qhd->khd", grad_scores, query_heads, preferred_element_type=jnp.float32)
            * factor
        )
        bias_total = bias_total + bias_grad(grad_scores, onehot, block_dev)
        piece_grad = jnp.concatenate(
            [grad_keys.reshape(tok_rows, attn_width), grad_values.reshape(tok_rows, attn_width)],
            axis=1,
        )
        if offset == 0:
            own_grad = piece_grad
        else:
            own_grad = own_grad + passed_along(
                piece_grad.astype(jnp.bfloat16), "seq", -offset
            ).astype(piece_grad.dtype)
    own_round = rounded(own_grad)
    query_round = rounded(grad_queries.reshape(tok_rows, attn_width))
    self_terms = (
        weight_grad(first_normed, query_round),
        weight_grad(first_normed, own_round[:, :attn_width]),
        weight_grad(first_normed, own_round[:, attn_width:]),
        weight_grad(mixed_self, grad_self),
    )
    grad_first = input_grad(query_round, query_full) + input_grad(
        own_round, jnp.concatenate([key_full, value_full], axis=1)
    )
    norm_grad, gain_one = norm_back(inputs, norm_gains[0], grad_first)
    grad_inputs = grad_early + norm_grad
    grad_terms = self_terms + cross_terms + feed_terms
    partial_rows = jax.tree.map(
        lambda part: part.astype(jnp.float32),
        lax.psum_scatter(as_sent(grad_terms), "dp", scatter_dimension=0, tiled=True),
    )
    owned = jax.tree.map(
        lambda part: part.astype(jnp.float32),
        lax.psum_scatter(as_sent(partial_rows), "seq", scatter_dimension=1, tiled=True),
    )
    summed = lax.psum((jnp.stack([gain_one, gain_two, gain_three]), bias_total), ("dp", "seq"))
    return (
        outcome.astype(jnp.bfloat16).reshape(1, tok_rows, model_width),
        grad_inputs.astype(jnp.bfloat16).reshape(1, tok_rows, model_width),
        grad_states.astype(jnp.bfloat16).reshape(neighbours.shape),
        summed[0],
        summed[1],
        owned[0],
        owned[1],
        owned[2],
        owned[3],
        owned[4],
        owned[5],
        owned[6],
        owned[7],
        owned[8],
        owned[9],
    )


def solution(mesh):
    return jax.shard_map(
        on_device,
        mesh=mesh,
        in_specs=(
            P("dp", "seq", None),
            P("dp", "seq", None, None, None),
            P(),
            P(),
            P("dp", "seq"),
            P("dp", "seq"),
            P("dp", "seq"),
            P("dp", "seq"),
            P("dp", "seq"),
            P("dp", "seq"),
            P("dp", "seq"),
            P("dp", "seq"),
            P("dp", "seq"),
            P("dp", "seq"),
            P("dp", "seq", None),
        ),
        out_specs=(
            P("dp", "seq", None),
            P("dp", "seq", None),
            P("dp", "seq", None, None, None),
            P(),
            P(),
            P("dp", "seq"),
            P("dp", "seq"),
            P("dp", "seq"),
            P("dp", "seq"),
            P("dp", "seq"),
            P("dp", "seq"),
            P("dp", "seq"),
            P("dp", "seq"),
            P("dp", "seq"),
            P("dp", "seq"),
        ),
        check_vma=False,
    )
```

profile of v0, /device:TPU:0, one launch (start us, length us, event | category | flops | bytes accessed | tf_op | source)
XLA Modules:
  0.0 1656.5 jit_solution(2992293894193899908)
XLA Ops:
  74.7 9.4 all_gather.98
  101.7 21.7 %add.321 = f32[16,512,512]{1,2,0:T(8,128)} reshape(f32[16,2,256,2,256]{2,1,4,3,0:T(2,128)} %add.320) | data formatting | bytes 33554432 | tf_op jit(solution)/shard_map/add | solution.py:93
  130.0 21.7 %add.333 = f32[16,512,512]{1,2,0:T(8,128)} reshape(f32[16,2,256,2,256]{2,1,4,3,0:T(2,128)} %add.332) | data formatting | bytes 33554432 | tf_op jit(solution)/shard_map/add | solution.py:93
  158.2 21.7 %add.329 = f32[16,512,512]{1,2,0:T(8,128)} reshape(f32[16,2,256,2,256]{2,1,4,3,0:T(2,128)} %add.328) | data formatting | bytes 33554432 | tf_op jit(solution)/shard_map/add | solution.py:93
  186.5 21.6 %add.325 = f32[16,512,512]{1,2,0:T(8,128)} reshape(f32[16,2,256,2,256]{2,1,4,3,0:T(2,128)} %add.324) | data formatting | bytes 33554432 | tf_op jit(solution)/shard_map/add | solution.py:93
  255.1 10.9 convolution_convert_fusion
  272.8 11.2 fusion.147
  325.5 11.6 fusion.144
  337.1 11.3 fusion.145
  348.3 11.2 fusion.146
  359.6 12.9 exponential_reduce_fusion.2
  401.7 11.2 bitcast_convert_fusion
  428.3 9.6 fusion.148
  455.6 40.9 %all-gather.27.cloned.1.call-done = bf16[896,3584]{1,0:T(8,128)(2,1)} async-done(((bf16[112,3584]{1,0:T(8,128)(2,1)}), bf16[896,3584]{1,0:T(8,128)(2,1)}) %all-gather.27.cloned.1.call-update) | async-done | bytes 6422544 | tf_op jit(solution)/shard_map/all_gather | solution.py:172
  505.5 92.1 %all-gather.29.cloned.1.call-done = bf16[3584,896]{1,0:T(8,128)(2,1)} async-done(((bf16[448,896]{1,0:T(8,128)(2,1)}), bf16[3584,896]{1,0:T(8,128)(2,1)}) %all-gather.29.cloned.1.call-update) | async-done | bytes 6422544 | tf_op jit(solution)/shard_map/all_gather | solution.py:173
  597.6 11.2 fusion.13
  681.7 9.6 copy.251
  691.4 9.7 copy.250
  705.2 10.3 multiply_convert_fusion.1
  737.7 10.2 multiply_convert_fusion.3
  785.5 10.2 fusion.1
  827.9 9.7 fusion.75
  881.1 34.8 %collective-permute-done.5 = bf16[512,2048]{0,1:T(8,128)(2,1)S(1)} collective-permute-done((bf16[512,2048]{0,1:T(8,128)(2,1)S(1)}, bf16[512,2048]{0,1:T(8,128)(2,1)S(1)}, u32[]{:S(2)}, u32[]{:S(2)}) %collective-permute-start.5) | collective-permute-done | bytes 2097184 | tf_op jit(solution)/shard_map/ppermute | solution.py:21
  927.4 11.1 convolution_convert_fusion.1
  953.5 9.7 reduce-scatter.65.cloned.1.call-done
  965.1 67.0 %reduce-scatter.63.cloned.1.call-done = bf16[112,1024]{1,0:T(8,128)(2,1)} async-done(((bf16[896,1024]{1,0:T(8,128)(2,1)}), bf16[112,1024]{1,0:T(8,128)(2,1)}) %reduce-scatter.63.cloned.1.call-update) | async-done | bytes 229392
  1034.0 67.1 %reduce-scatter.41.cloned.1.call-done = bf16[112,1024]{1,0:T(8,128)(2,1)} async-done(((bf16[896,1024]{1,0:T(8,128)(2,1)}), bf16[112,1024]{1,0:T(8,128)(2,1)}) %reduce-scatter.41.cloned.1.call-update) | async-done | bytes 229392 | tf_op jit(solution)/shard_map/reduce_scatter | solution.py:414
  1101.1 18.2 %reshape.621 = f32[16,2,256,2,256]{2,1,4,3,0:T(2,128)} reshape(bf16[16,512,512]{1,2,0:T(8,128)(2,1)} %multiply_convert_fusion.3) | data formatting | bytes 25165824 | tf_op jit(solution)/shard_map/reshape | solution.py:103
  1119.3 18.1 %reshape.623 = f32[16,2,256,2,256]{2,1,4,3,0:T(2,128)} reshape(bf16[16,512,512]{1,2,0:T(8,128)(2,1)} %multiply_convert_fusion.2) | data formatting | bytes 25165824 | tf_op jit(solution)/shard_map/reshape | solution.py:103
  1137.4 11.2 reduce_sum.232
  1148.7 11.3 reduce_sum.233
  1160.3 9.6 reduce-scatter.37.cloned.1.call-done
  1170.3 18.3 %reshape.627 = f32[16,2,256,2,256]{2,1,4,3,0:T(2,128)} reshape(bf16[16,512,512]{1,2,0:T(8,128)(2,1)} %multiply_convert_fusion) | data formatting | bytes 25165824 | tf_op jit(solution)/shard_map/reshape | solution.py:103
  1188.5 18.1 %reshape.625 = f32[16,2,256,2,256]{2,1,4,3,0:T(2,128)} reshape(bf16[16,512,512]{1,2,0:T(8,128)(2,1)} %multiply_convert_fusion.1) | data formatting | bytes 25165824 | tf_op jit(solution)/shard_map/reshape | solution.py:103
  1206.7 11.2 reduce_sum.235
  1218.0 11.2 reduce_sum.234
  1229.9 62.6 %reduce-scatter.59.cloned.1.call-done = bf16[448,896]{1,0:T(8,128)(2,1)} async-done(((bf16[3584,896]{1,0:T(8,128)(2,1)}), bf16[448,896]{1,0:T(8,128)(2,1)}) %reduce-scatter.59.cloned.1.call-update) | async-done | bytes 802832 | tf_op jit(solution)/shard_map/reduce_scatter | solution.py:414
  1299.2 10.8 fusion.84
  1310.0 105.2 %reduce-scatter.57.cloned.1.call-done = bf16[112,3584]{1,0:T(8,128)(2,1)} async-done(((bf16[896,3584]{1,0:T(8,128)(2,1)}), bf16[112,3584]{1,0:T(8,128)(2,1)}) %reduce-scatter.57.cloned.1.call-update) | async-done | bytes 802832 | tf_op jit(solution)/shard_map/reduce_scatter | solution.py:414
  1417.6 13.8 convolution_convert_fusion.3
  1435.4 40.0 %all-reduce = (f32[3,896]{1,0:T(4,128)}, f32[16,6]{0,1:T(8,128)}) all-reduce(f32[3,896]{1,0:T(4,128)S(1)} %pad_maximum_fusion.5, f32[16,6]{0,1:T(8,128)S(1)} %fusion.85), channel_id=1, replica_groups=mesh['dp'=8,'seq'=4] {'dp','seq'}, use_global_device_ids=true, to_apply=%region_21.22 | all-reduce | flops 2784 | bytes 22272 | tf_op jit(solution)/shard_map/psum | solution.py:420
  1483.2 20.6 %reduce-scatter.35.cloned.1.call-done = bf16[112,256]{1,0:T(8,128)(2,1)} async-done(((bf16[112,1024]{1,0:T(8,128)(2,1)}), bf16[112,256]{1,0:T(8,128)(2,1)}) %reduce-scatter.35.cloned.1.call-update) | async-done | bytes 57360 | tf_op jit(solution)/shard_map/reduce_scatter | solution.py:418
  1505.3 21.6 %reduce-scatter.53.cloned.1.call-done = bf16[112,256]{0,1:T(8,128)(2,1)} async-done(((bf16[112,1024]{0,1:T(8,128)(2,1)}), bf16[112,256]{0,1:T(8,128)(2,1)}) %reduce-scatter.53.cloned.1.call-update) | async-done | bytes 57360 | tf_op jit(solution)/shard_map/reduce_scatter | solution.py:418
  1528.5 21.4 %reduce-scatter.51.cloned.1.call-done = bf16[112,256]{0,1:T(8,128)(2,1)} async-done(((bf16[112,1024]{0,1:T(8,128)(2,1)}), bf16[112,256]{0,1:T(8,128)(2,1)}) %reduce-scatter.51.cloned.1.call-update) | async-done | bytes 57360 | tf_op jit(solution)/shard_map/reduce_scatter | solution.py:418
  1551.5 20.7 %reduce-scatter.43.cloned.1.call-done = bf16[112,256]{1,0:T(8,128)(2,1)} async-done(((bf16[112,1024]{1,0:T(8,128)(2,1)}), bf16[112,256]{1,0:T(8,128)(2,1)}) %reduce-scatter.43.cloned.1.call-update) | async-done | bytes 57360 | tf_op jit(solution)/shard_map/reduce_scatter | solution.py:418
  1573.6 20.9 %reduce-scatter.39.cloned.1.call-done = bf16[112,256]{1,0:T(8,128)(2,1)} async-done(((bf16[112,1024]{1,0:T(8,128)(2,1)}), bf16[112,256]{1,0:T(8,128)(2,1)}) %reduce-scatter.39.cloned.1.call-update) | async-done | bytes 57360 | tf_op jit(solution)/shard_map/reduce_scatter | solution.py:418
  1596.0 25.2 %reduce-scatter.71.cloned.1.call-done = bf16[224,448]{1,0:T(8,128)(2,1)} async-done(((bf16[896,448]{1,0:T(8,128)(2,1)}), bf16[224,448]{1,0:T(8,128)(2,1)}) %reduce-scatter.71.cloned.1.call-update) | async-done | bytes 200720
  1623.0 24.6 %reduce-scatter.69.cloned.1.call-done = bf16[896,112]{1,0:T(8,128)(2,1)} async-done(((bf16[3584,112]{1,0:T(8,128)(2,1)}), bf16[896,112]{1,0:T(8,128)(2,1)}) %reduce-scatter.69.cloned.1.call-update) | async-done | bytes 200720
  (521 shorter events, 546.2 us)
Async XLA Ops:
  7.2 80.6 %copy-start = (f32[16,6]{0,1:T(8,128)S(1)}, f32[16,6]{0,1:T(8,128)}, u32[]{:S(2)}) copy-start(f32[16,6]{0,1:T(8,128)} %param.20) | copy-start | bytes 1156
  7.2 51.9 %copy-start.55 = (bf16[128,224]{0,1:T(8,128)(2,1)S(1)}, bf16[128,224]{0,1:T(8,128)(2,1)}, u32[]{:S(2)}) copy-start(bf16[128,224]{0,1:T(8,128)(2,1)} %param.28) | copy-start | bytes 172036
  7.2 58.1 %copy-start.54 = (bf16[112,896]{1,0:T(8,128)(2,1)S(1)}, bf16[112,896]{1,0:T(8,128)(2,1)}, u32[]{:S(2)}) copy-start(bf16[112,896]{1,0:T(8,128)(2,1)} %param.29) | copy-start | bytes 602116
  7.2 67.4 %copy-start.53 = (bf16[448,224]{1,0:T(8,128)(2,1)S(1)}, bf16[448,224]{1,0:T(8,128)(2,1)}, u32[]{:S(2)}) copy-start(bf16[448,224]{1,0:T(8,128)(2,1)} %param.30) | copy-start | bytes 602116
  7.2 200.9 %all-gather.11.cloned.1.call-start = ((), (), s32[]{:S(2)}) async-start(), calls=%async_computation.20 | async-start | bytes 2064384 | tf_op jit(solution)/shard_map/all_gather | solution.py:165
  16.2 194.9 %all-gather.13.cloned.1.call-start = ((), (), s32[]{:S(2)}) async-start(), calls=%async_computation.21 | async-start | bytes 2064384 | tf_op jit(solution)/shard_map/all_gather | solution.py:166
  22.9 209.9 %all-gather.15.cloned.1.call-start = ((), (), s32[]{:S(2)}) async-start(), calls=%async_computation.22 | async-start | bytes 2064384 | tf_op jit(solution)/shard_map/all_gather | solution.py:164
  30.4 209.6 %all-gather.19.cloned.1.call-start = ((), (), s32[]{:S(2)}) async-start(), calls=%async_computation.24 | async-start | bytes 2064384 | tf_op jit(solution)/shard_map/all_gather | solution.py:169
  37.1 214.9 %all-gather.21.cloned.1.call-start = ((), (), s32[]{:S(2)}) async-start(), calls=%async_computation.25 | async-start | bytes 2064384 | tf_op jit(solution)/shard_map/all_gather | solution.py:170
  44.6 368.2 %all-gather.17.cloned.1.call-start = ((), (), s32[]{:S(2)}) async-start(), calls=%async_computation.23 | async-start | bytes 2064384 | tf_op jit(solution)/shard_map/all_gather | solution.py:167
  51.4 365.9 %all-gather.23.cloned.1.call-start = ((), (), s32[]{:S(2)}) async-start(), calls=%async_computation.26 | async-start | bytes 2064384 | tf_op jit(solution)/shard_map/all_gather | solution.py:168
  59.0 393.1 %all-gather.25.cloned.1.call-start = ((), (), s32[]{:S(2)}) async-start(), calls=%async_computation.27 | async-start | bytes 2064384 | tf_op jit(solution)/shard_map/all_gather | solution.py:171
  65.2 431.3 %all-gather.27.cloned.1.call-start = ((), (), s32[]{:S(2)}) async-start(), calls=%async_computation.28 | async-start | bytes 7225344 | tf_op jit(solution)/shard_map/all_gather | solution.py:172
  74.5 523.1 %all-gather.29.cloned.1.call-start = ((), (), s32[]{:S(2)}) async-start(), calls=%async_computation.29 | async-start | bytes 7225344 | tf_op jit(solution)/shard_map/all_gather | solution.py:173
  85.4 863.0 %reduce-scatter.55.cloned.1.call-start = ((), (), s32[]{:S(2)}) async-start(), calls=%async_computation.41 | async-start | bytes 2064384 | tf_op jit(solution)/shard_map/reduce_scatter | solution.py:414
  86.5 146.3 %copy-start.65 = (f32[512]{0:T(512)}, f32[512]{0:T(512)S(1)}, u32[]{:S(2)}) copy-start(f32[512]{0:T(512)S(1)} %fusion.116) | copy-start | bytes 6148
  89.2 143.6 %copy-start.63 = (f32[896]{0:T(1024)}, f32[896]{0:T(1024)S(1)}, u32[]{:S(2)}) copy-start(f32[896]{0:T(1024)S(1)} %get-tuple-element.94) | copy-start | bytes 10756
  222.4 85.4 %collective-permute-start.1 = (bf16[512,2048]{1,0:T(8,128)(2,1)}, bf16[512,2048]{1,0:T(8,128)(2,1)}, u32[]{:S(2)}, u32[]{:S(2)}) collective-permute-start(bf16[512,2048]{1,0:T(8,128)(2,1)} %convolution_convert_fusion.4), channel_id=1, source_target_pairs={{0,2},{1,3},{4,6},{5,7},{8,10},{9,11},{12,14},{13,15},{16,18},{17,... | collective-permute-start | bytes 6291464 | tf_op jit(solution)/shard_map/ppermute | solution.py:21
  226.5 85.1 %collective-permute-start = (bf16[512,2048]{1,0:T(8,128)(2,1)}, bf16[512,2048]{1,0:T(8,128)(2,1)}, u32[]{:S(2)}, u32[]{:S(2)}) collective-permute-start(bf16[512,2048]{1,0:T(8,128)(2,1)} %convolution_convert_fusion.4), channel_id=1, source_target_pairs={{0,1},{1,2},{2,3},{4,5},{5,6},{6,7},{8,9},{9,10},{10,11},{12,13},{... | collective-permute-start | bytes 6291464 | tf_op jit(solution)/shard_map/ppermute | solution.py:21
  229.7 87.7 %collective-permute-start.2 = (bf16[512,2048]{1,0:T(8,128)(2,1)}, bf16[512,2048]{1,0:T(8,128)(2,1)}, u32[]{:S(2)}, u32[]{:S(2)}) collective-permute-start(bf16[512,2048]{1,0:T(8,128)(2,1)} %convolution_convert_fusion.4), channel_id=1, source_target_pairs={{0,3},{4,7},{8,11},{12,15},{16,19},{20,23},{24,27},{28,31}} | collective-permute-start | bytes 6291464 | tf_op jit(solution)/shard_map/ppermute | solution.py:21
  238.1 110.2 %copy-start.2 = (bf16[512,1024]{0,1:T(8,128)(2,1)}, bf16[512,1024]{0,1:T(8,128)(2,1)S(1)}, u32[]{:S(2)}) copy-start(bf16[512,1024]{0,1:T(8,128)(2,1)S(1)} %copy.204) | copy-start | bytes 3145732
  270.5 14.8 collective-permute-start.3
  455.6 153.3 %copy-start.35 = (f32[512,896]{1,0:T(8,128)}, f32[512,896]{1,0:T(8,128)S(1)}, u32[]{:S(2)}) copy-start(f32[512,896]{1,0:T(8,128)S(1)} %get-tuple-element.127) | copy-start | bytes 5505028
  455.6 158.0 %copy-start.67 = (f32[512]{0:T(512)}, f32[512]{0:T(512)S(1)}, u32[]{:S(2)}) copy-start(f32[512]{0:T(512)S(1)} %fusion.118) | copy-start | bytes 6148
  622.4 327.9 %reduce-scatter.45.cloned.1.call-start = ((), (), s32[]{:S(2)}) async-start(), calls=%async_computation.36 | async-start | bytes 2064384 | tf_op jit(solution)/shard_map/reduce_scatter | solution.py:414
  679.5 272.8 %reduce-scatter.47.cloned.1.call-start = ((), (), s32[]{:S(2)}) async-start(), calls=%async_computation.37 | async-start | bytes 2064384 | tf_op jit(solution)/shard_map/reduce_scatter | solution.py:414
  737.2 215.8 %reduce-scatter.33.cloned.1.call-start = ((), (), s32[]{:S(2)}) async-start(), calls=%async_computation.30 | async-start | bytes 2064384 | tf_op jit(solution)/shard_map/reduce_scatter | solution.py:414
  773.8 189.5 %reduce-scatter.65.cloned.1.call-start = ((), (), s32[]{:S(2)}) async-start(), calls=%async_computation.46 | async-start | bytes 2064384
  776.6 24.8 %collective-permute-start.7 = (bf16[256,2048]{1,0:T(8,128)(2,1)}, bf16[256,2048]{1,0:T(8,128)(2,1)}, u32[]{:S(2)}, u32[]{:S(2)}) collective-permute-start(bf16[256,2048]{1,0:T(8,128)(2,1)} %fusion.88), channel_id=1, source_target_pairs={{1,0},{2,1},{3,2},{5,4},{6,5},{7,6},{9,8},{10,9},{11,10},{13,12},{... | collective-permute-start | bytes 3145736 | tf_op jit(solution)/shard_map/ppermute | solution.py:21
  816.6 215.5 %reduce-scatter.63.cloned.1.call-start = ((), (), s32[]{:S(2)}) async-start(), calls=%async_computation.45 | async-start | bytes 2064384
  819.4 61.7 %collective-permute-start.6 = (bf16[512,2048]{0,1:T(8,128)(2,1)}, bf16[512,2048]{0,1:T(8,128)(2,1)}, u32[]{:S(2)}, u32[]{:S(2)}) collective-permute-start(bf16[512,2048]{0,1:T(8,128)(2,1)} %pad_maximum_fusion.4), channel_id=1, source_target_pairs={{3,0},{7,4},{11,8},{15,12},{19,16},{23,20},{27,24},{31,28}} | collective-permute-start | bytes 6291464 | tf_op jit(solution)/shard_map/ppermute | solution.py:21
  840.6 40.5 %collective-permute-start.4 = (bf16[512,2048]{0,1:T(8,128)(2,1)}, bf16[512,2048]{0,1:T(8,128)(2,1)}, u32[]{:S(2)}, u32[]{:S(2)}) collective-permute-start(bf16[512,2048]{0,1:T(8,128)(2,1)} %pad_maximum_fusion.2), channel_id=1, source_target_pairs={{1,0},{2,1},{3,2},{5,4},{6,5},{7,6},{9,8},{10,9},{11,10},{13,12},{... | collective-permute-start | bytes 6291464 | tf_op jit(solution)/shard_map/ppermute | solution.py:21
  859.7 241.3 %reduce-scatter.41.cloned.1.call-start = ((), (), s32[]{:S(2)}) async-start(), calls=%async_computation.34 | async-start | bytes 2064384 | tf_op jit(solution)/shard_map/reduce_scatter | solution.py:414
  866.1 49.9 %collective-permute-start.5 = (bf16[512,2048]{0,1:T(8,128)(2,1)S(1)}, bf16[512,2048]{0,1:T(8,128)(2,1)S(1)}, u32[]{:S(2)}, u32[]{:S(2)}) collective-permute-start(bf16[512,2048]{0,1:T(8,128)(2,1)S(1)} %pad_maximum_fusion.3), channel_id=1, source_target_pairs={{2,0},{3,1},{6,4},{7,5},{10,8},{11,9},{14,12},{15,13},{18,16},{19,... | collective-permute-start | bytes 6291464 | tf_op jit(solution)/shard_map/ppermute | solution.py:21
  923.4 246.5 %reduce-scatter.37.cloned.1.call-start = ((), (), s32[]{:S(2)}) async-start(), calls=%async_computation.32 | async-start | bytes 2064384 | tf_op jit(solution)/shard_map/reduce_scatter | solution.py:414
  927.4 365.1 %reduce-scatter.59.cloned.1.call-start = ((), (), s32[]{:S(2)}) async-start(), calls=%async_computation.43 | async-start | bytes 7225344 | tf_op jit(solution)/shard_map/reduce_scatter | solution.py:414
  938.6 476.6 %reduce-scatter.57.cloned.1.call-start = ((), (), s32[]{:S(2)}) async-start(), calls=%async_computation.42 | async-start | bytes 7225344 | tf_op jit(solution)/shard_map/reduce_scatter | solution.py:414
  948.4 530.0 %reduce-scatter.67.cloned.1.call-start = ((), (), s32[]{:S(2)}) async-start(), calls=%async_computation.47 | async-start | bytes 286720
  950.3 529.8 %reduce-scatter.61.cloned.1.call-start = ((), (), s32[]{:S(2)}) async-start(), calls=%async_computation.44 | async-start | bytes 286720
  952.2 529.6 %reduce-scatter.49.cloned.1.call-start = ((), (), s32[]{:S(2)}) async-start(), calls=%async_computation.38 | async-start | bytes 286720 | tf_op jit(solution)/shard_map/reduce_scatter | solution.py:418
  952.9 550.9 %reduce-scatter.35.cloned.1.call-start = ((), (), s32[]{:S(2)}) async-start(), calls=%async_computation.31 | async-start | bytes 286720 | tf_op jit(solution)/shard_map/reduce_scatter | solution.py:418
  953.5 573.5 %reduce-scatter.53.cloned.1.call-start = ((), (), s32[]{:S(2)}) async-start(), calls=%async_computation.40 | async-start | bytes 327680 | tf_op jit(solution)/shard_map/reduce_scatter | solution.py:418
  965.0 584.9 %reduce-scatter.51.cloned.1.call-start = ((), (), s32[]{:S(2)}) async-start(), calls=%async_computation.39 | async-start | bytes 327680 | tf_op jit(solution)/shard_map/reduce_scatter | solution.py:418
  1033.9 538.2 %reduce-scatter.43.cloned.1.call-start = ((), (), s32[]{:S(2)}) async-start(), calls=%async_computation.35 | async-start | bytes 286720 | tf_op jit(solution)/shard_map/reduce_scatter | solution.py:418
  1101.1 493.5 %reduce-scatter.39.cloned.1.call-start = ((), (), s32[]{:S(2)}) async-start(), calls=%async_computation.33 | async-start | bytes 286720 | tf_op jit(solution)/shard_map/reduce_scatter | solution.py:418
  1170.0 451.2 %reduce-scatter.71.cloned.1.call-start = ((), (), s32[]{:S(2)}) async-start(), calls=%async_computation.49 | async-start | bytes 1146880
  1294.8 352.8 %reduce-scatter.69.cloned.1.call-start = ((), (), s32[]{:S(2)}) async-start(), calls=%async_computation.48 | async-start | bytes 1146880
  1475.4 174.0 %copy-start.1 = (f32[16,6]{0,1:T(8,128)S(1)}, f32[16,6]{0,1:T(8,128)}, u32[]{:S(2)}) copy-start(f32[16,6]{0,1:T(8,128)} %param.20) | copy-start | bytes 1156
  (111 other events, 1224.5 us)
Sparse Core Ops, SparseCore 0:
  16.3 46.7 all-gather.10
  65.2 45.1 all-gather.12
  112.6 45.0 all-gather.14
  159.7 45.0 all-gather.18
  206.9 45.0 all-gather.20
  253.9 46.4 all-gather.16
  302.6 44.5 all-gather.22
  349.3 46.4 all-gather.24
  398.0 98.4 all-gather.26
  499.1 98.4 all-gather.28
  622.6 65.0 reduce-scatter.54
  691.0 65.4 reduce-scatter.44
  759.9 65.4 reduce-scatter.46
  828.8 65.4 reduce-scatter.32
  897.6 65.6 reduce-scatter.64
  966.6 65.5 reduce-scatter.62
  1035.4 65.5 reduce-scatter.40
  1104.4 65.5 reduce-scatter.36
  1173.5 118.9 reduce-scatter.58
  1295.9 119.2 reduce-scatter.56
  1417.6 19.1 reduce-scatter.66
  1439.3 19.8 reduce-scatter.60
  1461.7 19.8 reduce-scatter.48
  1483.9 19.8 reduce-scatter.34
  1506.9 20.0 reduce-scatter.52
  1529.8 20.0 reduce-scatter.50
  1552.2 19.8 reduce-scatter.42
  1574.6 19.8 reduce-scatter.38
  1597.1 24.0 reduce-scatter.70
  1623.6 23.9 reduce-scatter.68
where the time goes:
time: 1670 us; the launch traced here: 1660 us
  waiting for transfers between devices  654 us (39%)
  matrix products  388 us (23%)
  local copies, waits for them, and re-layouts  335 us (20%)
  other arithmetic  126 us (8%)
  blocking collectives  116 us (7%)
  starting transfers between devices  20.7 us (1%)
    reduce_scatter x8, waiting for transfers between devices, on_device(): lax.psum_scatter(as_sent(grad_terms), 'dp', scatter_dimension=0, tiled=True)  244 us
    unnamed x36, waiting for transfers between devices  128 us
    add x8, local copies, waits for them, and re-layouts, self_scores(): logits.reshape(head_count, block_dev, BLOCK, block_dev, BLOCK)  113 us
    reduce_scatter x6, waiting for transfers between devices, on_device(): lax.psum_scatter(as_sent(partial_rows), 'seq', scatter_dimension=1, tiled...  105 us
    all_gather x1, waiting for transfers between devices, on_device(): lax.all_gather(columns[9], 'dp', axis=0, tiled=True)  92.1 us
    reshape x4, local copies, waits for them, and re-layouts, bias_grad(): grad_scores.astype(jnp.float32)  72.6 us
    dot_general x10, matrix products, weight_grad(): lax.dot_general(left_side, right_side, (((0,), (0,)), ((), ())), preferre...  56.6 us
    unnamed x265, local copies, waits for them, and re-layouts  52 us
  transfers between devices with their start and end apart: 38, of which 17 were waited for; matrix products, arithmetic and copies ran while one was open for 49% of the time, Pallas kernels for 0%

commit v1 on v0

v1 whole, which is shorter than its diff:
```python
import functools

import jax
import jax.numpy as jnp
from jax import lax
from jax.experimental import pallas as pl
from jax.experimental.pallas import tpu as pltpu
from jax.sharding import PartitionSpec as P

HD = 64
SEGMENT = 64
BLOCK = 256
NB = 6
SEQ_MIN = 2048
EPSILON = 1e-06
NEGATIVE = -1e30
BF = jnp.bfloat16
F32 = jnp.float32
VMEM_LIMIT = 56 * 2**20
BOTH = ("dp", "seq")


def dot(a, b, ca=1, cb=0):
    return lax.dot_general(a, b, (((ca,), (cb,)), ((), ())), preferred_element_type=F32)


def linear(a, b):
    return dot(a, b)


def input_grad(a, b):
    return dot(a, b, 1, 1)


def weight_grad(a, b):
    return dot(a, b, 0, 0)


def rounded(v):
    return v.astype(BF)


def rms_apply(inputs, gain_row):
    factor = lax.rsqrt(jnp.mean(inputs * inputs, axis=-1, keepdims=True) + EPSILON)
    return inputs * factor * gain_row


def norm_back(inputs, gain_row, upstream):
    normed_value, pullback = jax.vjp(rms_apply, inputs, gain_row)
    return pullback(upstream)


def gelu_tanh(operand):
    return jax.nn.gelu(operand, approximate=True)


def swap(value, axis, by):
    peers = lax.axis_size(axis)
    return lax.ppermute(value, axis, [(i, i ^ by) for i in range(peers)])


def vmem_spec():
    return pl.BlockSpec(memory_space=pltpu.VMEM)


def smem_spec():
    return pl.BlockSpec(memory_space=pltpu.SMEM)


def copy_kernel(index_ref, in_ref, out_ref):
    out_ref[...] = in_ref[...].reshape(out_ref.shape)


def reorder_rows(stacked, mine):
    count, rows, cols = stacked.shape
    if rows % 16 or cols % 128:
        order = jnp.arange(count, dtype=jnp.int32) ^ mine
        return jnp.take(stacked, order, axis=0).reshape(count * rows, cols)
    spec = pltpu.PrefetchScalarGridSpec(
        num_scalar_prefetch=1,
        grid=(count,),
        in_specs=[pl.BlockSpec((1, rows, cols), lambda i, m: (m[0] ^ i, 0, 0))],
        out_specs=pl.BlockSpec((rows, cols), lambda i, m: (i, 0)),
    )
    return pl.pallas_call(
        copy_kernel,
        grid_spec=spec,
        out_shape=jax.ShapeDtypeStruct((count * rows, cols), stacked.dtype),
    )(mine.reshape(1), stacked)


def columns_from_blocks(stacked, mine):
    count, rows, cols = stacked.shape
    spec = pltpu.PrefetchScalarGridSpec(
        num_scalar_prefetch=1,
        grid=(count,),
        in_specs=[pl.BlockSpec((1, rows, cols), lambda i, m: (m[0] ^ i, 0, 0))],
        out_specs=pl.BlockSpec((rows, cols), lambda i, m: (0, i)),
    )
    return pl.pallas_call(
        copy_kernel,
        grid_spec=spec,
        out_shape=jax.ShapeDtypeStruct((rows, count * cols), stacked.dtype),
    )(mine.reshape(1), stacked)


def blocks_from_columns(flat, count, mine):
    rows, width = flat.shape
    cols = width // count
    spec = pltpu.PrefetchScalarGridSpec(
        num_scalar_prefetch=1,
        grid=(count,),
        in_specs=[pl.BlockSpec((rows, cols), lambda i, m: (0, m[0] ^ i))],
        out_specs=pl.BlockSpec((1, rows, cols), lambda i, m: (i, 0, 0)),
    )
    return pl.pallas_call(
        copy_kernel,
        grid_spec=spec,
        out_shape=jax.ShapeDtypeStruct((count, rows, cols), flat.dtype),
    )(mine.reshape(1), flat)


def assemble(blocks, dp, seq):
    _, rows, cols = blocks.shape
    return blocks.reshape(dp, seq, rows, cols).transpose(0, 2, 1, 3).reshape(dp * rows, seq * cols)


def block_sum(left, right):
    dp, seq = lax.axis_size("dp"), lax.axis_size("seq")
    rows, cols = left.shape[1] // dp, right.shape[1] // seq
    blocks = rounded(weight_grad(left, right)).reshape(dp, rows, seq, cols).transpose(0, 2, 1, 3)
    blocks = blocks.reshape(dp * seq, rows, cols)
    return lax.psum_scatter(blocks, BOTH, scatter_dimension=0, tiled=True)[0].astype(F32)


def device_pairs(target):
    dp, pairs = lax.axis_size("dp"), []
    for i in range(dp):
        for j in range(4):
            z, y, x, c = target(i // 2, i % 2, j // 2, j % 2)
            pairs.append((i * 4 + j, (z * 2 + y) * 4 + x * 2 + c))
    return pairs


def over_z(value, k):
    return lax.ppermute(value, BOTH, device_pairs(lambda z, y, x, c: (z ^ k, y, x, c)))


def over_a(value):
    return lax.ppermute(
        value, BOTH, device_pairs(lambda z, y, x, c: (z, y ^ c, x ^ (1 - c), c))
    )


def over_b(value):
    return lax.ppermute(
        value, BOTH, device_pairs(lambda z, y, x, c: (z, y ^ (1 - c), x ^ c, c))
    )


def over_core(value):
    return lax.ppermute(value, BOTH, device_pairs(lambda z, y, x, c: (z, y, x, 1 - c)))


def my_place():
    i, j = lax.axis_index("dp"), lax.axis_index("seq")
    return jnp.stack([i // 2, i % 2, j // 2, j % 2]).astype(jnp.int32)


def gather_group(shard):
    depth = lax.axis_size("dp") // 2
    near = jnp.stack([shard] + [over_z(shard, k) for k in range(1, depth)])
    both = jnp.concatenate([near, over_a(near)], axis=0)
    far = over_b(both)
    return [both, far, over_core(both), over_core(far)]


def piece_origin(place_ref, c, b, t, depth):
    z, y, x, core = (place_ref[i] for i in range(4))
    a, k = t // depth, t % depth
    core = core ^ c
    dx = jnp.where(core == 0, a, b)
    dy = jnp.where(core == 0, b, a)
    return (z ^ k) * 2 + (y ^ dy), (x ^ dx) * 2 + core


def assemble_attention_kernel(depth, place_ref, *refs):
    pieces, (recall, query, out_self, out_cross), sems = refs[:4], refs[4:8], refs[8]
    rows = query.shape[0] // (2 * depth)
    cols = query.shape[1] // 4
    half = cols // 2

    def step(t, carry):
        for i in range(4):
            i_dp, i_seq = piece_origin(place_ref, i // 2, i % 2, t, depth)
            down = pl.ds(pl.multiple_of(i_dp * rows, rows), rows)
            across = pl.multiple_of(i_seq * cols, cols)
            piece = pieces[i].at[t]

            def move(first, target, sem):
                pltpu.make_async_copy(piece.at[pl.ds(first, rows), :], target, sems.at[sem]).start()

            move(0, recall.at[down, pl.ds(across, cols)], 0)
            move(rows, recall.at[down, pl.ds(across + 4 * cols, cols)], 0)
            move(2 * rows, query.at[down, pl.ds(across, cols)], 1)
            lanes = pl.ds(pl.multiple_of(i_dp * half, half), half)
            for w, out in ((0, out_self), (1, out_cross)):
                for h in range(2):
                    top = pl.multiple_of((i_seq * 2 + h) * rows, rows)
                    pltpu.make_async_copy(
                        piece.at[pl.ds((3 + w) * rows, rows), pl.ds(h * half, half)],
                        out.at[pl.ds(top, rows), lanes],
                        sems.at[2 + w],
                    ).start()
        return carry

    lax.fori_loop(0, 2 * depth, step, 0)
    for sem, out in enumerate((recall, query, out_self, out_cross)):
        pltpu.make_async_copy(out, out, sems.at[sem]).wait()


def assemble_attention(pieces, place):
    count, packed, cols = pieces[0].shape
    rows = packed // 5
    model, width = rows * count, cols * 4
    shapes = [(model, 2 * width), (model, width), (8 * rows, width), (8 * rows, width)]
    return pl.pallas_call(
        functools.partial(assemble_attention_kernel, count // 2),
        in_specs=[smem_spec()] + [pl.BlockSpec(memory_space=pl.ANY)] * 4,
        out_specs=[vmem_spec()] * 4,
        out_shape=[jax.ShapeDtypeStruct(s, BF) for s in shapes],
        scratch_shapes=[pltpu.SemaphoreType.DMA((4,))],
        compiler_params=pltpu.CompilerParams(vmem_limit_bytes=VMEM_LIMIT),
    )(place, *pieces)


def assemble_feed_kernel(depth, place_ref, *refs):
    pieces, (inner, outer), stage, sems = refs[:4], refs[4:6], refs[6], refs[7]
    rows = inner.shape[0] // (2 * depth)
    cols = inner.shape[1] // 4
    part = cols // 4

    def step(t, carry):
        for i in range(4):
            i_dp, i_seq = piece_origin(place_ref, i // 2, i % 2, t, depth)
            piece = pieces[i].at[t]
            down = pl.ds(pl.multiple_of(i_dp * rows, rows), rows)
            across = pl.ds(pl.multiple_of(i_seq * cols, cols), cols)
            pltpu.make_async_copy(
                piece.at[pl.ds(rows, rows), :], stage.at[i_dp, i_seq], sems.at[1]
            ).start()
            pltpu.make_async_copy(
                piece.at[pl.ds(0, rows), :], inner.at[down, across], sems.at[0]
            ).start()
        return carry

    lax.fori_loop(0, 2 * depth, step, 0)
    pltpu.make_async_copy(stage, stage, sems.at[1]).wait()

    def spread(i, carry):
        for t in range(4):
            line = [stage[i, j, :, t * part : (t + 1) * part] for j in range(4)]
            where = pl.multiple_of((i * 4 + t) * rows, rows)
            outer[pl.ds(where, rows), :] = jnp.concatenate(line, axis=1)
        return carry

    lax.fori_loop(0, 2 * depth, spread, 0)
    pltpu.make_async_copy(inner, inner, sems.at[0]).wait()


def assemble_feed(pieces, place):
    count, packed, cols = pieces[0].shape
    rows = packed // 2
    return pl.pallas_call(
        functools.partial(assemble_feed_kernel, count // 2),
        in_specs=[smem_spec()] + [pl.BlockSpec(memory_space=pl.ANY)] * 4,
        out_specs=[vmem_spec()] * 2,
        out_shape=[
            jax.ShapeDtypeStruct((rows * count, cols * 4), BF),
            jax.ShapeDtypeStruct((4 * rows * count, cols), BF),
        ],
        scratch_shapes=[
            pltpu.VMEM((count, 4, rows, cols), BF),
            pltpu.SemaphoreType.DMA((2,)),
        ],
        compiler_params=pltpu.CompilerParams(vmem_limit_bytes=VMEM_LIMIT),
    )(place, *pieces)


def put_block(place_ref, out_ref, core, i_dp, flip, value):
    z, y = place_ref[0], place_ref[1]
    dy = (i_dp % 2) ^ y
    b = jnp.where(core == 0, dy, flip)
    a = jnp.where(core == 0, flip, dy)
    out_ref[b, a, (i_dp // 2) ^ z] = value


def wide_grad_kernel(*refs):
    place_ref, left, kept_right, sent_right = refs[:4]
    kept, sent = refs[-2:]
    flip = pl.program_id(1)
    rows = kept.shape[3]
    core = place_ref[3]
    for right, out, c in ((kept_right, kept, core), (sent_right, sent, 1 - core)):
        value = rounded(dot(left[...], right[...], 0, 0))
        for i_dp in range(value.shape[0] // rows):
            put_block(place_ref, out, c, i_dp, flip, value[i_dp * rows : (i_dp + 1) * rows])


def tall_grad_kernel(*refs):
    place_ref, left, right = refs[:3]
    kept, sent = refs[-2:]
    rows, cols = kept.shape[3], kept.shape[4]
    half = cols // 2
    x, core = place_ref[2], place_ref[3]
    for j in range(4):
        value = rounded(dot(right[:, 2 * j * rows : 2 * (j + 1) * rows], left[...], 0, 0))
        for out, mine in ((kept, core == j % 2), (sent, core != j % 2)):

            @pl.when(mine)
            def _():
                for i_dp in range(value.shape[1] // half):
                    lanes = slice(i_dp * half, (i_dp + 1) * half)
                    block = jnp.concatenate([value[:rows, lanes], value[rows:, lanes]], axis=1)
                    put_block(place_ref, out, j % 2, i_dp, (j // 2) ^ x, block)


def outer_grad_kernel(*refs):
    place_ref, left, right = refs[:3]
    kept, sent = refs[-2:]
    rows, cols = kept.shape[3], kept.shape[4]
    part = cols // 4
    i_z = pl.program_id(0)
    x, core = place_ref[2], place_ref[3]
    for j in range(4):
        value = rounded(dot(left[...], right[:, j * part : (j + 1) * part], 0, 0))
        for out, mine in ((kept, core == j % 2), (sent, core != j % 2)):

            @pl.when(mine)
            def _():
                for i_y in range(2):
                    base = i_y * 4 * rows
                    line = [value[base + t * rows : base + (t + 1) * rows] for t in range(4)]
                    block = jnp.concatenate(line, axis=1)
                    put_block(place_ref, out, j % 2, i_z * 2 + i_y, (j // 2) ^ x, block)


def group_grad(kind, place, left, right, first, total, before=None, parts=1):
    dp = lax.axis_size("dp")
    depth = dp // 2
    tokens, height = left.shape
    width = right.shape[1]
    if kind == "tall":
        rows, cols = width // 8, 2 * height // dp
    elif kind == "outer":
        rows, cols = height // dp // 4, width
    else:
        rows, cols = height // dp, width // 4 // parts
    whole = jax.ShapeDtypeStruct((2, 2, depth, total * rows, cols), BF)
    block = (2, 2, depth, rows, cols)
    if kind == "wide":
        kernel, grid, operands = wide_grad_kernel, (parts, 2), [left, right, right]
        specs = [
            pl.BlockSpec((tokens, height), lambda p, i, m: (0, 0)),
            pl.BlockSpec((tokens, cols), lambda p, i, m: (0, p * 4 + (m[2] ^ i) * 2 + m[3])),
            pl.BlockSpec((tokens, cols), lambda p, i, m: (0, p * 4 + (m[2] ^ i) * 2 + 1 - m[3])),
        ]
        out_spec = pl.BlockSpec(block, lambda p, i, m: (0, 0, 0, first + p, 0))
    elif kind == "outer":
        kernel, grid, operands = outer_grad_kernel, (depth,), [left, right]
        specs = [
            pl.BlockSpec((tokens, height // depth), lambda i, m: (0, i)),
            pl.BlockSpec((tokens, width), lambda i, m: (0, 0)),
        ]
        out_spec = pl.BlockSpec(block, lambda i, m: (0, 0, 0, first, 0))
    else:
        kernel, grid, operands = tall_grad_kernel, (1,), [left, right]
        specs = [
            pl.BlockSpec((tokens, height), lambda i, m: (0, 0)),
            pl.BlockSpec((tokens, width), lambda i, m: (0, 0)),
        ]
        out_spec = pl.BlockSpec(block, lambda i, m: (0, 0, 0, first, 0))
    aliases = {}
    if before is not None:
        aliases = {1 + len(operands): 0, 2 + len(operands): 1}
        operands = operands + list(before)
        specs = specs + [pl.BlockSpec(memory_space=pl.ANY)] * 2
    return pl.pallas_call(
        kernel,
        grid_spec=pltpu.PrefetchScalarGridSpec(
            num_scalar_prefetch=1, grid=grid, in_specs=specs, out_specs=[out_spec] * 2
        ),
        out_shape=[whole, whole],
        input_output_aliases=aliases,
        compiler_params=pltpu.CompilerParams(vmem_limit_bytes=VMEM_LIMIT),
        cost_estimate=pl.CostEstimate(
            flops=2 * tokens * height * width,
            bytes_accessed=2 * (left.size + right.size + height * width),
            transcendentals=0,
        ),
    )(place, *operands)


def sum_group(pieces):
    kept, sent = pieces
    got = over_core(sent).astype(F32)
    got_b = over_b(rounded(kept[1].astype(F32) + got[1])).astype(F32)
    near = kept[0].astype(F32) + got[0]
    got_a = over_a(rounded(near[1] + got_b[1])).astype(F32)
    line = rounded(near[0] + got_b[0] + got_a)
    total = line[0].astype(F32)
    for k in range(1, line.shape[0]):
        total = total + over_z(line[k], k).astype(F32)
    return total


def triple_grad_kernel(place_ref, left, right, kept, sent):
    value = rounded(dot(left[...], right[...], 0, 0))
    rows = kept.shape[1]
    z, y = place_ref[0], place_ref[1]
    for out, flip in ((kept, 0), (sent, 1)):
        for i_y in range(2):

            @pl.when((y ^ i_y) == flip)
            def _():
                for i_z in range(kept.shape[0]):
                    top = (i_z * 2 + i_y) * rows
                    out[i_z ^ z] = value[top : top + rows]


def triple_sum(place, left, right):
    dp = lax.axis_size("dp")
    rows, cols = left.shape[1] // dp, right.shape[1]
    shape = jax.ShapeDtypeStruct((dp // 2, rows, cols), BF)
    kept, sent = pl.pallas_call(
        triple_grad_kernel,
        in_specs=[smem_spec(), vmem_spec(), vmem_spec()],
        out_specs=[vmem_spec()] * 2,
        out_shape=[shape, shape],
        compiler_params=pltpu.CompilerParams(vmem_limit_bytes=VMEM_LIMIT),
        cost_estimate=pl.CostEstimate(
            flops=2 * left.size * cols, bytes_accessed=2 * (left.size + right.size), transcendentals=0
        ),
    )(place, left, right)
    line = rounded(kept.astype(F32) + swap(sent, "dp", 1).astype(F32))
    total = line[0].astype(F32)
    for k in range(1, dp // 2):
        total = total + swap(line[k], "dp", 2 * k).astype(F32)
    return total


def lane_mask(shape, head):
    lanes = lax.broadcasted_iota(jnp.int32, shape, len(shape) - 1)
    return (lanes >= head * HD) & (lanes < (head + 1) * HD)


def transposed(value):
    return value.astype(F32).T


def block_bias(bias_ref, head, query_block, key_block):
    distance = query_block - key_block
    kept = bias_ref[head, jnp.clip(distance, 0, NB - 1)]
    return jnp.where(distance >= 0, kept, NEGATIVE)


def self_fwd_kernel(pos_ref, bias_ref, qkv_ref, o_ref, lse_ref, kh_ref, vt_ref, s_ref, acc_ref):
    heads = kh_ref.shape[0]
    width = heads * HD
    devs, _, rows = vt_ref.shape
    per = rows // BLOCK
    a = pl.program_id(0)
    pos = pos_ref[0]

    @pl.when(a == 0)
    def _():
        for h in range(heads):
            kh_ref[h] = qkv_ref[:, width + h * HD : width + (h + 1) * HD]
        for d in range(devs):
            vt_ref[d] = rounded(transposed(qkv_ref[d * rows : (d + 1) * rows, 2 * width :]))

    first = pl.multiple_of(((a // per) ^ pos) * rows + (a % per) * BLOCK, BLOCK)
    qt = rounded(transposed(qkv_ref[pl.ds(first, BLOCK), :width]) * HD**-0.5)

    def scores(d, tops):
        where = pl.multiple_of((d ^ pos) * rows, rows)
        out = []
        for h in range(heads):
            raw = dot(kh_ref[h, pl.ds(where, rows), :], qt[h * HD : (h + 1) * HD])
            top = tops[h]
            for half in range(per):
                c = block_bias(bias_ref, h, a, d * per + half)
                piece = raw[half * BLOCK : (half + 1) * BLOCK] + c
                s_ref[h, pl.ds(pl.multiple_of(d * rows + half * BLOCK, BLOCK), BLOCK), :] = piece
                top = jnp.maximum(top, jnp.max(piece.reshape(BLOCK // 8, 8, BLOCK), axis=0))
            out.append(top)
        return tuple(out)

    count = a // per + 1
    tops = lax.fori_loop(
        0, count, scores, tuple(jnp.full((8, BLOCK), NEGATIVE, F32) for _ in range(heads))
    )
    tops = [jnp.max(t, axis=0, keepdims=True) for t in tops]
    acc_ref[...] = jnp.zeros_like(acc_ref)

    def mix(d, sums):
        out = []
        slot = d ^ pos
        for h in range(heads):
            e = jnp.exp(s_ref[h, pl.ds(pl.multiple_of(d * rows, rows), rows), :] - tops[h])
            out.append(sums[h] + jnp.sum(e.reshape(rows // 8, 8, BLOCK), axis=0))
            acc_ref[h * HD : (h + 1) * HD, :] += dot(
                vt_ref[slot, h * HD : (h + 1) * HD, :], rounded(e)
            )
        return tuple(out)

    sums = lax.fori_loop(
        0, count, mix, tuple(jnp.zeros((8, BLOCK), F32) for _ in range(heads))
    )
    for h in range(heads):
        total = jnp.sum(sums[h], axis=0, keepdims=True)
        lse_ref[a, h : h + 1, :] = tops[h] + jnp.log(total)
        acc_ref[h * HD : (h + 1) * HD, :] = acc_ref[h * HD : (h + 1) * HD, :] / total
    o_ref[pl.ds(first, BLOCK), :] = rounded(acc_ref[...].T)


def self_fwd(pos, bias, qkv, rows):
    tokens, triple = qkv.shape
    width = triple // 3
    heads = width // HD
    blocks = tokens // BLOCK
    return pl.pallas_call(
        self_fwd_kernel,
        grid=(blocks,),
        in_specs=[smem_spec(), smem_spec(), vmem_spec()],
        out_specs=[vmem_spec(), vmem_spec()],
        out_shape=[
            jax.ShapeDtypeStruct((tokens, width), BF),
            jax.ShapeDtypeStruct((blocks, 8, BLOCK), F32),
        ],
        scratch_shapes=[
            pltpu.VMEM((heads, tokens, HD), BF),
            pltpu.VMEM((tokens // rows, width, rows), BF),
            pltpu.VMEM((heads, tokens, BLOCK), F32),
            pltpu.VMEM((width, BLOCK), F32),
        ],
        compiler_params=pltpu.CompilerParams(vmem_limit_bytes=VMEM_LIMIT),
        cost_estimate=pl.CostEstimate(
            flops=2 * tokens * tokens * width * 2, bytes_accessed=8 * tokens * width,
            transcendentals=tokens * tokens * heads // 2,
        ),
    )(pos.reshape(1), bias, qkv)


def self_bwd_kernel(
    pos_ref, bias_ref, qkv_ref, o_ref, go_ref, lse_ref, dqkv_ref, bsum_ref,
    kh_ref, vh_ref, kt_ref, qm_ref, gm_ref, p_ref, ds_ref, dst_ref, dq_ref, dk_ref, dv_ref,
):
    heads = kh_ref.shape[0]
    width = heads * HD
    devs, _, rows = kt_ref.shape
    per = rows // BLOCK
    a = pl.program_id(0)
    pos = pos_ref[0]

    @pl.when(a == 0)
    def _():
        for h in range(heads):
            kh_ref[h] = qkv_ref[:, width + h * HD : width + (h + 1) * HD]
            vh_ref[h] = qkv_ref[:, 2 * width + h * HD : 2 * width + (h + 1) * HD]
        for d in range(devs):
            kt_ref[d] = rounded(transposed(qkv_ref[d * rows : (d + 1) * rows, width : 2 * width]))
        dk_ref[...] = jnp.zeros_like(dk_ref)
        dv_ref[...] = jnp.zeros_like(dv_ref)
        bsum_ref[...] = jnp.zeros_like(bsum_ref)

    first = pl.multiple_of(((a // per) ^ pos) * rows + (a % per) * BLOCK, BLOCK)
    q = qkv_ref[pl.ds(first, BLOCK), :width] * jnp.asarray(HD**-0.5, BF)
    go = go_ref[pl.ds(first, BLOCK), :]
    qt = rounded(transposed(q))
    got = transposed(go)
    prod = got * transposed(o_ref[pl.ds(first, BLOCK), :])
    got = rounded(got)
    zero = jnp.zeros((BLOCK, width), BF)
    dots, lses = [], []
    for h in range(heads):
        mask = lane_mask((BLOCK, width), h)
        qm_ref[h * BLOCK : (h + 1) * BLOCK, :] = jnp.where(mask, q, zero)
        gm_ref[h * BLOCK : (h + 1) * BLOCK, :] = jnp.where(mask, go, zero)
        dots.append(jnp.sum(prod[h * HD : (h + 1) * HD], axis=0, keepdims=True))
        lses.append(lse_ref[a, h : h + 1, :])
    dq_ref[...] = jnp.zeros_like(dq_ref)

    def step(d, carry):
        where = pl.multiple_of((d ^ pos) * rows, rows)
        slot = d ^ pos
        for h in range(heads):
            lanes = slice(h * HD, (h + 1) * HD)
            cols = slice(h * BLOCK, (h + 1) * BLOCK)
            raw = dot(kh_ref[h, pl.ds(where, rows), :], qt[lanes])
            gp = dot(vh_ref[h, pl.ds(where, rows), :], got[lanes])
            for half in range(per):
                part = slice(half * BLOCK, (half + 1) * BLOCK)
                key_block = d * per + half
                c = block_bias(bias_ref, h, a, key_block)
                pf = jnp.exp(raw[part] + (c - lses[h]))
                p_ref[part, cols] = rounded(pf)
                ds = rounded(pf * (gp[part] - dots[h]))
                ds_ref[part, cols] = ds
                dst_ref[h, part, :] = ds
                bucket = jnp.clip(a - key_block, 0, NB - 1)
                bsum_ref[h, bucket] += jnp.sum(
                    ds.astype(F32).reshape(BLOCK // 8, 8, BLOCK), axis=0
                )
            dq_ref[lanes, :] += dot(kt_ref[slot, lanes, :], dst_ref[h])
        dv_ref[pl.ds(where, rows), :] += dot(p_ref[...], gm_ref[...])
        dk_ref[pl.ds(where, rows), :] += dot(ds_ref[...], qm_ref[...])
        return carry

    lax.fori_loop(0, a // per + 1, step, 0)
    dqkv_ref[pl.ds(first, BLOCK), :width] = rounded(dq_ref[...].T * HD**-0.5)

    @pl.when(a == pl.num_programs(0) - 1)
    def _():
        dqkv_ref[:, width : 2 * width] = rounded(dk_ref[...])
        dqkv_ref[:, 2 * width :] = rounded(dv_ref[...])


def self_bwd(pos, bias, qkv, mixed, grad, lse, rows):
    tokens, triple = qkv.shape
    width = triple // 3
    heads = width // HD
    blocks = tokens // BLOCK
    return pl.pallas_call(
        self_bwd_kernel,
        grid=(blocks,),
        in_specs=[smem_spec(), smem_spec()] + [vmem_spec()] * 4,
        out_specs=[vmem_spec(), vmem_spec()],
        out_shape=[
            jax.ShapeDtypeStruct((tokens, triple), BF),
            jax.ShapeDtypeStruct((heads, NB, 8, BLOCK), F32),
        ],
        scratch_shapes=[
            pltpu.VMEM((heads, tokens, HD), BF),
            pltpu.VMEM((heads, tokens, HD), BF),
            pltpu.VMEM((tokens // rows, width, rows), BF),
            pltpu.VMEM((heads * BLOCK, width), BF),
            pltpu.VMEM((heads * BLOCK, width), BF),
            pltpu.VMEM((rows, heads * BLOCK), BF),
            pltpu.VMEM((rows, heads * BLOCK), BF),
            pltpu.VMEM((heads, rows, BLOCK), BF),
            pltpu.VMEM((width, BLOCK), F32),
            pltpu.VMEM((tokens, width), F32),
            pltpu.VMEM((tokens, width), F32),
        ],
        compiler_params=pltpu.CompilerParams(vmem_limit_bytes=VMEM_LIMIT),
        cost_estimate=pl.CostEstimate(
            flops=5 * tokens * tokens * width * 2, bytes_accessed=16 * tokens * width,
            transcendentals=tokens * tokens * heads // 2,
        ),
    )(pos.reshape(1), bias, qkv, mixed, grad, lse)


def slotted(value, pad_ref):
    rows = value.shape[0]
    rolled = pltpu.roll(value.astype(F32), 1, 0)
    first = lax.broadcasted_iota(jnp.int32, rolled.shape, 0) == 0
    pad_ref[:rows] = rounded(jnp.where(first, 0.0, rolled))
    pad_ref[rows:] = rounded(jnp.where(first, rolled, 0.0)[:SEGMENT])


def unslotted(pad_ref, rows):
    value = pad_ref[:rows]
    first = lax.broadcasted_iota(jnp.int32, value.shape, 0) == 0
    value = jnp.where(first, jnp.broadcast_to(pad_ref[rows : rows + 1], value.shape), value)
    return pltpu.roll(value, rows - 1, 0)


def masked_stack(value, group):
    return jnp.concatenate(
        [jnp.where(lane_mask(value.shape, h), value, jnp.zeros_like(value)) for h in range(group)], 0
    )


def cross_soft(keys, stacked):
    s = dot(keys, stacked, 1, 1)
    top = jnp.max(s, axis=0, keepdims=True)
    e = jnp.exp(s - top)
    return e / jnp.sum(e, axis=0, keepdims=True)


def merged(tall, group):
    rows, width = tall.shape[0] // group, tall.shape[1]
    out = jnp.zeros((rows, width), F32)
    for h in range(group):
        out = jnp.where(lane_mask((rows, width), h), tall[h * rows : (h + 1) * rows], out)
    return out


def cross_fwd_kernel(q_ref, k_ref, v_ref, out_ref, qp_ref, op_ref):
    slot = pl.program_id(0)
    rows = q_ref.shape[0]
    lanes = 4 * HD

    @pl.when(slot == 0)
    def _():
        slotted(q_ref[...], qp_ref)

    here = pl.ds(pl.multiple_of(slot * SEGMENT, SEGMENT), SEGMENT)
    scaled = qp_ref[here, :] * jnp.asarray(HD**-0.5, BF)
    for g in range(q_ref.shape[1] // lanes):
        part = slice(g * lanes, (g + 1) * lanes)
        soft = rounded(cross_soft(k_ref[:, part], masked_stack(scaled[:, part], 4)))
        op_ref[here, part] = merged(dot(soft, v_ref[:, part], 0, 0), 4)

    @pl.when(slot == pl.num_programs(0) - 1)
    def _():
        out_ref[...] = rounded(unslotted(op_ref, rows))


def cross_fwd(queries, pairs, neigh_rows):
    rows, width = queries.shape
    slots = rows // SEGMENT + 1
    return pl.pallas_call(
        cross_fwd_kernel,
        grid=(slots,),
        in_specs=[
            vmem_spec(),
            pl.BlockSpec((neigh_rows, width), lambda i: (i, 0)),
            pl.BlockSpec((neigh_rows, width), lambda i: (i, 1)),
        ],
        out_specs=vmem_spec(),
        out_shape=jax.ShapeDtypeStruct((rows, width), BF),
        scratch_shapes=[
            pltpu.VMEM((slots * SEGMENT, width), BF),
            pltpu.VMEM((slots * SEGMENT, width), F32),
        ],
        compiler_params=pltpu.CompilerParams(vmem_limit_bytes=VMEM_LIMIT),
        cost_estimate=pl.CostEstimate(
            flops=16 * slots * SEGMENT * neigh_rows * width, bytes_accessed=2 * pairs.size,
            transcendentals=slots * neigh_rows * width,
        ),
    )(queries, pairs, pairs)


def cross_bwd_kernel(q_ref, g_ref, k_ref, v_ref, dq_ref, dkv_ref, qp_ref, gp_ref, op_ref):
    slot = pl.program_id(0)
    rows, width = q_ref.shape
    lanes = 4 * HD

    @pl.when(slot == 0)
    def _():
        slotted(q_ref[...], qp_ref)
        slotted(g_ref[...], gp_ref)

    here = pl.ds(pl.multiple_of(slot * SEGMENT, SEGMENT), SEGMENT)
    scaled = qp_ref[here, :] * jnp.asarray(HD**-0.5, BF)
    grads = gp_ref[here, :]
    for g in range(width // lanes):
        part = slice(g * lanes, (g + 1) * lanes)
        queries = masked_stack(scaled[:, part], 4)
        grad = masked_stack(grads[:, part], 4)
        soft = cross_soft(k_ref[:, part], queries)
        gp = dot(v_ref[:, part], grad, 1, 1)
        ds = rounded(soft * (gp - jnp.sum(soft * gp, axis=0, keepdims=True)))
        op_ref[here, part] = merged(dot(ds, k_ref[:, part], 0, 0), 4) * HD**-0.5
        dkv_ref[:, part] = rounded(dot(ds, queries))
        dkv_ref[:, width + g * lanes : width + (g + 1) * lanes] = rounded(dot(rounded(soft), grad))

    @pl.when(slot == pl.num_programs(0) - 1)
    def _():
        dq_ref[...] = rounded(unslotted(op_ref, rows))


def cross_bwd(queries, grads, pairs, neigh_rows):
    rows, width = queries.shape
    slots = rows // SEGMENT + 1
    return pl.pallas_call(
        cross_bwd_kernel,
        grid=(slots,),
        in_specs=[
            vmem_spec(),
            vmem_spec(),
            pl.BlockSpec((neigh_rows, width), lambda i: (i, 0)),
            pl.BlockSpec((neigh_rows, width), lambda i: (i, 1)),
        ],
        out_specs=[vmem_spec(), pl.BlockSpec((neigh_rows, 2 * width), lambda i: (i, 0))],
        out_shape=[
            jax.ShapeDtypeStruct((rows, width), BF),
            jax.ShapeDtypeStruct(pairs.shape, BF),
        ],
        scratch_shapes=[
            pltpu.VMEM((slots * SEGMENT, width), BF),
            pltpu.VMEM((slots * SEGMENT, width), BF),
            pltpu.VMEM((slots * SEGMENT, width), F32),
        ],
        compiler_params=pltpu.CompilerParams(vmem_limit_bytes=VMEM_LIMIT),
        cost_estimate=pl.CostEstimate(
            flops=40 * slots * SEGMENT * neigh_rows * width, bytes_accessed=4 * pairs.size,
            transcendentals=slots * neigh_rows * width,
        ),
    )(queries, grads, pairs, pairs)


def on_device(
    tokens, neighbours, norm_gains, position_bias, query_self, key_self, value_self, output_self,
    query_cross, key_cross, value_cross, output_cross, inner_weight, outer_weight, cotangent,
):
    dp, seq = lax.axis_size("dp"), lax.axis_size("seq")
    rows, model = tokens.shape[1], tokens.shape[2]
    heads = position_bias.shape[0]
    width = heads * HD
    segments = rows // SEGMENT
    neigh_rows = neighbours.shape[2] * neighbours.shape[3]
    span = min(seq, max(2, SEQ_MIN // rows))
    group_width = width // span
    group_heads = heads // span
    my_dp = lax.axis_index("dp")
    pos = lax.axis_index("seq") % span

    fast = seq == 4 and span == 4 and rows % (2 * BLOCK) == 0 and model == 896
    place = my_place() if fast else None

    def whole(shard):
        return assemble(lax.all_gather(shard, BOTH, axis=0, tiled=False), dp, seq)

    triple = jnp.concatenate([query_self, key_self, value_self], axis=1)
    if fast:
        near = {0: triple}
        for k in range(2, dp, 2):
            near[k] = swap(triple, "dp", k)
        for k in list(near):
            near[k + 1] = swap(near[k], "dp", 1)
        triple_full = reorder_rows(jnp.stack([near[k] for k in range(dp)]), my_dp)

        def turned(shard):
            flat = shard.T
            half = flat.shape[0] // 2
            return jnp.concatenate([flat[:half], flat[half:]], axis=1)

        packed = jnp.concatenate(
            [key_cross, value_cross, query_cross, turned(output_self), turned(output_cross)], axis=0
        )
        recall_full, query_full, output_turned, cross_turned = assemble_attention(
            gather_group(packed), place
        )
        part = outer_weight.shape[0] // 4
        line = [outer_weight[t * part : (t + 1) * part] for t in range(4)]
        packed = jnp.concatenate([inner_weight, jnp.concatenate(line, axis=1)], axis=0)
        inner_full, outer_full = assemble_feed(gather_group(packed), place)
    else:
        pieces = []
        for shard in (query_self, key_self, value_self):
            pieces.append(lax.dynamic_slice_in_dim(whole(shard), pos * group_width, group_width, 1))
        triple_full = jnp.concatenate(pieces, axis=1)
        recall_full = jnp.concatenate([whole(key_cross), whole(value_cross)], axis=1)
        query_full = whole(query_cross)
        output_turned, cross_turned = whole(output_self).T, whole(output_cross).T
        inner_full, outer_full = whole(inner_weight), whole(outer_weight)

    own_tokens = tokens.reshape(rows, model)
    pieces = {0: own_tokens}
    bit = span // 2
    while bit:
        for k in list(pieces):
            pieces[k | bit] = swap(pieces[k], "seq", bit)
        bit //= 2
    states = neighbours.reshape(segments * neigh_rows, model)
    forward_pairs = [(i, i + 1) for i in range(seq - 1) if (i + 1) % span]
    back_pairs = [(i + 1, i) for i in range(seq - 1) if (i + 1) % span]
    edge = lax.ppermute(states[(segments - 1) * neigh_rows :], "seq", forward_pairs)
    states_all = jnp.concatenate([edge, states], axis=0)

    inputs = own_tokens.astype(F32)
    upstream = cotangent.reshape(rows, model).astype(F32)
    first_normed = jnp.concatenate(
        [rounded(rms_apply(pieces[k].astype(F32), norm_gains[0])) for k in range(span)], axis=0
    )
    qkv = rounded(linear(first_normed, triple_full))
    bias = lax.dynamic_slice_in_dim(position_bias, pos * group_heads, group_heads, 0)
    mixed_group, lse = self_fwd(pos, bias, qkv, rows)

    def exchanged(stack):
        return [stack[0]] + [swap(stack[k], "seq", k) for k in range(1, span)]

    mixed_blocks = mixed_group.reshape(span, rows, group_width)
    mixed_self = columns_from_blocks(jnp.stack(exchanged(mixed_blocks)), pos)

    recall_pairs = rounded(linear(states_all, recall_full))

    after_self = inputs + input_grad(mixed_self, output_turned)
    second_normed = rounded(rms_apply(after_self, norm_gains[1]))
    cross_queries = rounded(linear(second_normed, query_full))
    mixed_cross = cross_fwd(cross_queries, recall_pairs, neigh_rows)
    after_cross = after_self + input_grad(mixed_cross, cross_turned)
    third_normed = rounded(rms_apply(after_cross, norm_gains[2]))
    gate_value = linear(third_normed, inner_full)
    activated, gelu_pull = jax.vjp(gelu_tanh, gate_value)
    hidden_act = rounded(activated)
    outcome = after_cross + linear(hidden_act, outer_full)

    grad_feed = rounded(upstream)
    grad_hidden = input_grad(grad_feed, outer_full)
    grad_gate = rounded(gelu_pull(grad_hidden)[0])
    if fast:
        pieces = group_grad("outer", place, hidden_act, grad_feed, 1, 2)
        pieces = group_grad("wide", place, third_normed, grad_gate, 0, 2, pieces)
        own = sum_group(pieces)
        part = own.shape[0] // 2
        sum_inner = own[:part]
        sum_outer = own[part:].reshape(part, 4, model // 4).transpose(1, 0, 2).reshape(4 * part, -1)
    else:
        sum_outer = block_sum(hidden_act, grad_feed)
        sum_inner = block_sum(third_normed, grad_gate)
    norm_grad, gain_three = norm_back(after_cross, norm_gains[2], input_grad(grad_gate, inner_full))
    grad_late = upstream + norm_grad

    grad_cross = rounded(grad_late)
    grad_mixed = rounded(linear(grad_cross, cross_turned))
    probe, pair_round = cross_bwd(cross_queries, grad_mixed, recall_pairs, neigh_rows)

    def turned_back(own):
        half = own.shape[1] // 2
        return jnp.concatenate([own[:, :half].T, own[:, half:].T], axis=1)

    if fast:
        pieces = group_grad("tall", place, mixed_cross, grad_cross, 3, 4)
        pieces = group_grad("wide", place, second_normed, probe, 2, 4, pieces)
        pieces = group_grad("wide", place, states_all, pair_round, 0, 4, pieces, 2)
        own = sum_group(pieces)
        part = own.shape[0] // 4
        sum_key, sum_value, sum_query = (own[i * part : (i + 1) * part] for i in range(3))
        sum_cross = turned_back(own[3 * part :])
    else:
        sum_cross = block_sum(mixed_cross, grad_cross)
        sum_key = block_sum(states_all, pair_round[:, :width])
        sum_value = block_sum(states_all, pair_round[:, width:])
        sum_query = block_sum(second_normed, probe)
    norm_grad, gain_two = norm_back(after_self, norm_gains[1], input_grad(probe, query_full))
    grad_early = grad_late + norm_grad
    states_round = rounded(input_grad(pair_round, recall_full))
    returned = lax.ppermute(states_round[:neigh_rows], "seq", back_pairs)
    last = states_round[segments * neigh_rows :].astype(F32) + returned.astype(F32)
    grad_states = jnp.concatenate(
        [states_round[neigh_rows : segments * neigh_rows], rounded(last)], axis=0
    )

    grad_self = rounded(grad_early)
    if fast:
        sum_output = turned_back(sum_group(group_grad("tall", place, mixed_self, grad_self, 0, 1)))
    else:
        sum_output = block_sum(mixed_self, grad_self)
    grad_attended = rounded(linear(grad_self, output_turned))
    group_grads = exchanged(blocks_from_columns(grad_attended, span, pos))
    grad_group = jnp.concatenate(group_grads, axis=0)
    triple_grad, bias_sums = self_bwd(pos, bias, qkv, mixed_group, grad_group, lse, rows)
    partial = rounded(input_grad(triple_grad, triple_full)).reshape(span, rows, model)
    blocks = {k: partial[k] for k in range(span)}
    bit = 1
    while bit < span:
        for k in sorted(blocks):
            if not k & bit:
                got = swap(blocks[k | bit], "seq", bit)
                blocks[k] = blocks[k].astype(F32) + got.astype(F32)
                if bit * 2 < span and k:
                    blocks[k] = rounded(blocks[k])
        blocks = {k: v for k, v in blocks.items() if not k & bit}
        bit *= 2
    norm_grad, gain_one = norm_back(inputs, norm_gains[0], blocks[0])
    grad_inputs = grad_early + norm_grad

    if fast:
        own = triple_sum(place, first_normed, triple_grad)
        own_self = [own[:, i * group_width : (i + 1) * group_width] for i in range(3)]
    else:
        own_self = []
        for i in range(3):
            columns = triple_grad[:, i * group_width : (i + 1) * group_width]
            wide = jnp.zeros((span * rows, width), BF)
            wide = lax.dynamic_update_slice_in_dim(wide, columns, pos * group_width, 1)
            own_self.append(block_sum(first_normed, wide))

    bias_local = jnp.sum(bias_sums, axis=(2, 3))
    bias_all = lax.dynamic_update_slice_in_dim(
        jnp.zeros((heads, NB), F32), bias_local, pos * group_heads, 0
    )
    gains, bias_total = lax.psum((jnp.stack([gain_one, gain_two, gain_three]), bias_all), BOTH)
    return (
        rounded(outcome).reshape(1, rows, model),
        rounded(grad_inputs).reshape(1, rows, model),
        grad_states.reshape(neighbours.shape),
        gains,
        bias_total,
        own_self[0],
        own_self[1],
        own_self[2],
        sum_output,
        sum_query,
        sum_key,
        sum_value,
        sum_cross,
        sum_inner,
        sum_outer,
    )


def solution(mesh):
    weight = P("dp", "seq")
    lane = P("dp", "seq", None)
    wide = P("dp", "seq", None, None, None)
    return jax.shard_map(
        on_device,
        mesh=mesh,
        in_specs=(lane, wide, P(), P()) + (weight,) * 10 + (lane,),
        out_specs=(lane, lane, wide, P(), P()) + (weight,) * 10,
        check_vma=False,
    )
```

time: 1670 us -> 736 us (0.44)
  waiting for transfers between devices: 654 us -> 171 us
  matrix products: 388 us -> 85.5 us
  local copies, waits for them, and re-layouts: 335 us -> 48.9 us
  Pallas kernels: 0 us -> 205 us
  other arithmetic: 126 us -> 67.3 us
  starting transfers between devices: 20.7 us -> 76.8 us
  blocking collectives: 116 us -> 69.5 us
    reduce_scatter x14 -> x0, waiting for transfers between devices: 350 us -> none  [the longest x8 244 us: on_device(): lax.psum_scatter(as_sent(grad_terms), 'dp', scatter_dimension=0, tiled=True)]
    dot_general x63 -> x14, matrix products: 378 us -> 85.5 us  [dot(): lax.dot_general(a, b, (((ca,), (cb,)), ((), ())), preferred_element_type=...]
    pallas_call x0 -> x16, Pallas kernels: none -> 205 us  [the longest x6 58.5 us: group_grad(): pl.pallas_call(kernel, grid_spec=pltpu.PrefetchScalarGridSpec(num_scalar_...]
    all_gather x10 -> x0, waiting for transfers between devices: 142 us -> none  [the longest x1 92.1 us: on_device(): lax.all_gather(columns[9], 'dp', axis=0, tiled=True)]
    ppermute x8 -> x57, waiting for transfers between devices: 34.8 us -> 171 us  [the longest x15 79.3 us: over_z(): lax.ppermute(value, BOTH, device_pairs(lambda z, y, x, c: (z ^ k, y, x, c)))]
    unnamed x36 -> x0, waiting for transfers between devices: 128 us -> none
    add x8 -> x0, local copies, waits for them, and re-layouts: 113 us -> none  [self_scores(): logits.reshape(head_count, block_dev, BLOCK, block_dev, BLOCK)]
    reshape x12 -> x1, local copies, waits for them, and re-layouts: 108 us -> 0.36 us  [on_device(): own[part:].reshape(part, 4, model // 4).transpose(1, 0, 2)]
  transfers between devices with their start and end apart: 38 -> 57, of which waited for: 17 -> 17; matrix products, arithmetic and copies ran while one was open for 49% -> 19% of each run, Pallas kernels for 0% -> 20%
where the time goes in v1:
time: 736 us; the launch traced here: 726 us
  Pallas kernels  205 us (28%)
  waiting for transfers between devices  171 us (23%)
  matrix products  85.5 us (12%)
  starting transfers between devices  76.8 us (10%)
  blocking collectives  69.5 us (9%)
  other arithmetic  67.3 us (9%)
  local copies, waits for them, and re-layouts  48.9 us (7%)
    dot_general x14, matrix products, dot(): lax.dot_general(a, b, (((ca,), (cb,)), ((), ())), preferred_element_type=...  85.5 us
    ppermute x15, waiting for transfers between devices, over_z(): lax.ppermute(value, BOTH, device_pairs(lambda z, y, x, c: (z ^ k, y, x, c)))  79.3 us
    psum x1, blocking collectives, on_device(): lax.psum((jnp.stack([gain_one, gain_two, gain_three]), bias_all), BOTH)  69.5 us
    pallas_call x6, Pallas kernels, group_grad(): pl.pallas_call(kernel, grid_spec=pltpu.PrefetchScalarGridSpec(num_scalar_...  58.5 us
    pallas_call x1, Pallas kernels, self_bwd(): pl.pallas_call(self_bwd_kernel, grid=(blocks,), in_specs=[smem_spec(), sm...  46.6 us
    ppermute x5, waiting for transfers between devices, over_a(): lax.ppermute(value, BOTH, device_pairs(lambda z, y, x, c: (z, y ^ c, x ^...  38.1 us
    ppermute x23, starting transfers between devices, swap(): return lax.ppermute(value, axis, [(i, i ^ by) for i in range(peers)])  35.8 us
    ppermute x5, waiting for transfers between devices, over_b(): lax.ppermute(value, BOTH, device_pairs(lambda z, y, x, c: (z, y ^ 1 - c,...  31.7 us
  transfers between devices with their start and end apart: 57, of which 17 were waited for; matrix products, arithmetic and copies ran while one was open for 19% of the time, Pallas kernels for 20%

profile of v1, /device:TPU:0, one launch (start us, length us, event | category | flops | bytes accessed | tf_op | source)
XLA Modules:
  0.0 726.1 jit_solution(17576891945596495942)
XLA Ops:
  3.3 3.0 collective-permute-start.3
  22.7 3.5 collective-permute-start.14
  29.8 15.6 %collective-permute-done.14 = bf16[560,256]{1,0:T(8,128)(2,1)S(1)} collective-permute-done((bf16[560,256]{1,0:T(8,128)(2,1)S(1)}, bf16[560,256]{1,0:T(8,128)(2,1)S(1)}, u32[]{:S(2)}, u32[]{:S(2)}) %collective-permute-start.14) | collective-permute-done | bytes 286752 | tf_op jit(solution)/shard_map/ppermute | solution.py:146
  59.7 17.7 %collective-permute-done.22 = bf16[224,896]{1,0:T(8,128)(2,1)S(1)} collective-permute-done((bf16[224,896]{1,0:T(8,128)(2,1)S(1)}, bf16[224,896]{1,0:T(8,128)(2,1)S(1)}, u32[]{:S(2)}, u32[]{:S(2)}) %collective-permute-start.22) | collective-permute-done | bytes 401440 | tf_op jit(solution)/shard_map/ppermute | solution.py:146
  83.5 5.3 shard_map.262
  94.1 5.5 collective-permute-done.1
  100.2 34.0 %collective-permute-done.24 = bf16[4,224,896]{2,1,0:T(8,128)(2,1)} collective-permute-done((bf16[4,224,896]{2,1,0:T(8,128)(2,1)}, bf16[4,224,896]{2,1,0:T(8,128)(2,1)}, u32[]{:S(2)}, u32[]{:S(2)}) %collective-permute-start.24) | collective-permute-done | bytes 1605664 | tf_op jit(solution)/shard_map/ppermute | solution.py:150
  142.6 8.0 %convolution_convert_fusion.3.qkv_ref = bf16[2048,768]{1,0:T(8,128)(2,1)} fusion(bf16[896,768]{1,0:T(8,128)(2,1)S(1)} %copy-done.34, bf16[512,896]{1,0:T(8,128)(2,1)S(1)} %get-tuple-element.133, bf16[512,896]{1,0:T(8,128)(2,1)S(1)} %get-tuple-element.132, bf16[512,896]{1,0:T(8,128)(2,1)S(1)} %get-tuple-element.131, bf16[512,896]{1,0:T(8,128)(2,1)S(1)} %get-tuple-element.130), kind=kOutput, calls=%fused_computation.32 | convolution fusion | flops 2834825216 | bytes 8192000 | tf_op jit(solution)/shard_map/dot_general | solution.py:24
  150.6 25.5 %shard_map.263 = (bf16[2048,256]{1,0:T(8,128)(2,1)}, f32[8,8,256]{2,1,0:T(8,128)}) custom-call(s32[1]{0:T(128)} %bitcast.1.pos_ref.index_ref, f32[4,6]{1,0:T(4,128)} %copy.44.bias_ref, bf16[2048,768]{1,0:T(8,128)(2,1)} %convolution_convert_fusion.3.qkv_ref), custom_call_target="tpu_custom_call" | custom-call | flops 4294967296 | bytes 4194304 | tf_op jit(solution)/shard_map/pallas_call | solution.py:532
  179.6 3.3 pad_maximum_fusion.refs_1_
  183.3 2.9 collective-permute-done.12
  186.7 9.0 %pad_maximum_fusion.1.left = bf16[2048,896]{1,0:T(8,128)(2,1)} fusion(bf16[512,896]{1,0:T(8,128)(2,1)S(1)} %copy-done.23, bf16[512,896]{1,0:T(8,128)(2,1)S(1)} %get-tuple-element.132, bf16[512,896]{1,0:T(8,128)(2,1)S(1)} %get-tuple-element.131, bf16[512,896]{1,0:T(8,128)(2,1)S(1)} %get-tuple-element.130), kind=kLoop, calls=%fused_computation.24 | loop fusion | flops 14680064 | bytes 7340032 | tf_op jit(solution)/shard_map/concatenate | solution.py:876
  196.9 3.4 shard_map.264.refs_1_
  200.7 8.0 %shard_map.265 = (bf16[896,2048]{1,0:T(8,128)(2,1)}, bf16[896,1024]{1,0:T(8,128)(2,1)}, bf16[896,1024]{1,0:T(8,128)(2,1)}, bf16[896,1024]{1,0:T(8,128)(2,1)}) custom-call(s32[4]{0:T(128)} %pad_add_fusion.place_ref.refs_0_, bf16[8,560,256]{2,1,0:T(8,128)(2,1)} %constant_dynamic-update-slice_fusion.6.refs_0_, ...), custom_call_target="tpu_custom_call" | custom-call | tf_op jit(solution)/shard_map/pallas_call | solution.py:227
  208.8 2.9 multiply_reduce_fusion.5
  217.7 13.2 %convolution_convert_fusion.k_ref.v_ref = bf16[2304,2048]{1,0:T(8,128)(2,1)} fusion(bf16[896,2048]{1,0:T(8,128)(2,1)S(1)} %copy-done.52, bf16[2048,896]{1,0:T(8,128)(2,1)S(1)} %bitcast.235, bf16[256,896]{1,0:T(8,128)(2,1)} %collective-permute-done.20), kind=kOutput, calls=%fused_computation | convolution fusion | flops 8468692992 | bytes 17235968 | tf_op jit(solution)/shard_map/dot_general | solution.py:24
  230.9 13.3 %shard_map.266.refs_1_ = bf16[512,1024]{1,0:T(8,128)(2,1)} custom-call(bf16[512,1024]{1,0:T(8,128)(2,1)} %convolution_convert_fusion.6.q_ref, bf16[2304,2048]{1,0:T(8,128)(2,1)} %convolution_convert_fusion.k_ref.v_ref, bf16[2304,2048]{1,0:T(8,128)(2,1)} %convolution_convert_fusion.k_ref.v_ref), custom_call_target="tpu_custom_call" | custom-call | flops 2415919104 | bytes 9437184 | tf_op jit(solution)/shard_map/pallas_call | solution.py:724
  247.2 12.6 %shard_map.267 = (bf16[896,3584]{1,0:T(8,128)(2,1)}, bf16[3584,896]{1,0:T(8,128)(2,1)}) custom-call(s32[4]{0:T(128)} %pad_add_fusion.place_ref.refs_0_, bf16[8,224,896]{2,1,0:T(8,128)(2,1)} %constant_dynamic-update-slice_fusion.11.refs_0_, bf16[8,224,896]{2,1,0:T(8,128)(2,1)} %collective-permute-done.25.refs_1_, ...), custom_call_target="tpu_custom_call" | custom-call | tf_op jit(solution)/shard_map/pallas_call | solution.py:274
  259.8 9.8 %multiply_convert_fusion = (bf16[512,3584]{1,0:T(8,128)(2,1)}, f32[512,3584]{1,0:T(8,128)S(1)}) fusion(bf16[512,896]{1,0:T(8,128)(2,1)S(1)} %multiply_convert_fusion.1.refs_1_, bf16[896,3584]{1,0:T(8,128)(2,1)} %get-tuple-element.46), kind=kOutput, calls=%fused_computation.15 | convolution fusion | flops 3304849408 | bytes 18350080 | tf_op jit(solution)/shard_map/dot_general | solution.py:24
  269.7 7.9 %fusion.6.refs_2_.refs_3_ = bf16[512,3584]{1,0:T(8,128)(2,1)S(1)} fusion(f32[512,3584]{1,0:T(8,128)S(1)} %get-tuple-element.139, bf16[3584,896]{1,0:T(8,128)(2,1)S(1)} %copy-done.51, bf16[1,512,896]{2,1,0:T(8,128)(2,1)S(1)} %copy-done.28), kind=kOutput, calls=%fused_computation.9 | convolution fusion | flops 3325034496 | bytes 18350080 | tf_op jit(solution)/shard_map/dot_general | solution.py:24
  277.6 4.2 multiply_reduce_fusion
  286.3 21.2 %shard_map.268 = (bf16[512,1024]{1,0:T(8,128)(2,1)}, bf16[2304,2048]{1,0:T(8,128)(2,1)}) custom-call(bf16[512,1024]{1,0:T(8,128)(2,1)} %convolution_convert_fusion.6.q_ref, bf16[512,1024]{1,0:T(8,128)(2,1)} %convolution_convert_fusion.5.g_ref, bf16[2304,2048]{1,0:T(8,128)(2,1)} %convolution_convert_fusion.k_ref.v_ref, ...), custom_call_target="tpu_custom_call" | custom-call | flops 6039797760 | bytes 18874368 | tf_op jit(solution)/shard_map/pallas_call | solution.py:778
  307.4 13.0 %convolution_convert_fusion.1 = bf16[2304,896]{1,0:T(8,128)(2,1)S(1)} fusion(bf16[2304,2048]{1,0:T(8,128)(2,1)} %get-tuple-element.51.refs_2_.refs_3_, bf16[896,2048]{1,0:T(8,128)(2,1)S(1)} %copy-done.53), kind=kOutput, calls=%fused_computation.19 | convolution fusion | flops 8457781248 | bytes 17235968 | tf_op jit(solution)/shard_map/dot_general | solution.py:24
  327.1 18.3 %shard_map.276 = (bf16[2,2,4,224,896]{4,3,2,1,0:T(8,128)(2,1)}, bf16[2,2,4,224,896]{4,3,2,1,0:T(8,128)(2,1)}) custom-call(s32[4]{0:T(128)} %pad_add_fusion.place_ref.refs_0_, bf16[512,3584]{1,0:T(8,128)(2,1)} %get-tuple-element.138.refs_1_, bf16[512,896]{1,0:T(8,128)(2,1)} %bitcast.237), custom_call_target="tpu_custom_call" | custom-call | flops 3288334336 | bytes 11010048 | tf_op jit(solution)/shard_map/pallas_call | solution.py:388
  345.4 9.6 %shard_map.277 = (bf16[2,2,4,224,896]{4,3,2,1,0:T(8,128)(2,1)}, bf16[2,2,4,224,896]{4,3,2,1,0:T(8,128)(2,1)}) custom-call(s32[4]{0:T(128)} %pad_add_fusion.place_ref.refs_0_, bf16[512,896]{1,0:T(8,128)(2,1)} %copy-done.27, bf16[512,3584]{1,0:T(8,128)(2,1)} %copy-done.9, bf16[512,3584]{1,0:T(8,128)(2,1)} %copy-done.9, ...), custom_call_target="tpu_custom_call", output_to_operand_aliasing={{0}: (4, {}), {1}: (5, {})} | custom-call | flops 3288334336 | bytes 11010048 | tf_op jit(solution)/shard_map/pallas_call | solution.py:388
  355.1 3.8 fusion.65
  361.2 3.5 shard_map.269
  369.5 5.8 shard_map.273
  375.3 4.8 shard_map.274
  380.0 8.8 %fusion.42 = bf16[1,512,896]{2,1,0:T(8,128)(2,1)} fusion(f32[512,896]{1,0:T(8,128)S(1)} %get-tuple-element.137, bf16[512,3584]{1,0:T(8,128)(2,1)} %get-tuple-element.138.refs_1_, bf16[3584,896]{1,0:T(8,128)(2,1)} %get-tuple-element.47), kind=kOutput, calls=%fused_computation.97 | convolution fusion | flops 3289251840 | bytes 12845056 | tf_op jit(solution)/shard_map/dot_general | solution.py:24
  388.9 14.5 %shard_map.275 = (bf16[2,2,4,448,256]{4,3,2,1,0:T(8,128)(2,1)}, bf16[2,2,4,448,256]{4,3,2,1,0:T(8,128)(2,1)}) custom-call(s32[4]{0:T(128)} %pad_add_fusion.place_ref.refs_0_, bf16[2304,896]{1,0:T(8,128)(2,1)} %pad_maximum_fusion.refs_1_, bf16[2304,2048]{1,0:T(8,128)(2,1)} %get-tuple-element.51.refs_2_.refs_3_, ...), custom_call_target="tpu_custom_call", output_to_operand_aliasing={{0}: (4, {}), {1}: (5, {})} | custom-call | flops 8455716864 | bytes 17235968 | tf_op jit(solution)/shard_map/pallas_call | solution.py:388
  403.3 5.7 shard_map.272
  411.3 46.6 %shard_map.270 = (bf16[2048,768]{1,0:T(8,128)(2,1)}, f32[4,6,8,256]{3,2,1,0:T(8,128)}) custom-call(s32[1]{0:T(128)} %bitcast.1.pos_ref.index_ref, f32[4,6]{1,0:T(4,128)} %copy.44.bias_ref, bf16[2048,768]{1,0:T(8,128)(2,1)} %convolution_convert_fusion.3.qkv_ref, bf16[2048,256]{1,0:T(8,128)(2,1)} %get-tuple-element.41.o_ref, ...), custom_call_target="tpu_custom_call" | custom-call | flops 10737418240 | bytes 8388608 | tf_op jit(solution)/shard_map/pallas_call | solution.py:634
  458.0 5.6 convolution_convert_fusion.2
  467.4 7.4 %shard_map.271 = (bf16[4,112,768]{2,1,0:T(8,128)(2,1)}, bf16[4,112,768]{2,1,0:T(8,128)(2,1)}) custom-call(s32[4]{0:T(128)} %pad_add_fusion.place_ref.refs_0_, bf16[2048,896]{1,0:T(8,128)(2,1)} %pad_maximum_fusion.1.left, bf16[2048,768]{1,0:T(8,128)(2,1)} %get-tuple-element.50.right), custom_call_target="tpu_custom_call" | custom-call | flops 2818572288 | bytes 6815744 | tf_op jit(solution)/shard_map/pallas_call | solution.py:435
  481.9 10.6 %collective-permute-done.35 = bf16[4,112,768]{2,1,0:T(8,128)(2,1)S(1)} collective-permute-done((bf16[4,112,768]{2,1,0:T(8,128)(2,1)}, bf16[4,112,768]{2,1,0:T(8,128)(2,1)S(1)}, u32[]{:S(2)}, u32[]{:S(2)}) %collective-permute-start.35) | collective-permute-done | bytes 688160 | tf_op jit(solution)/shard_map/ppermute | solution.py:59
  497.4 13.0 %collective-permute-start.37 = (bf16[112,768]{1,0:T(8,128)(2,1)}, bf16[112,768]{1,0:T(8,128)(2,1)}, u32[]{:S(2)}, u32[]{:S(2)}) collective-permute-start(bf16[112,768]{1,0:T(8,128)(2,1)} %get-tuple-element.108), channel_id=1, source_target_pairs={{0,16},{4,20},{8,24},{12,28},{16,0},{20,4},{24,8},{28,12},{1,17},{... | collective-permute-start | bytes 516104 | tf_op jit(solution)/shard_map/ppermute | solution.py:59
  510.5 4.1 convert_element_type.338
  514.6 6.4 slice_add_fusion.1
  521.9 3.0 convert_element_type.323
  532.9 4.2 collective-permute-done.41
  550.8 30.6 %collective-permute-done.46 = bf16[2,4,448,256]{3,2,1,0:T(8,128)(2,1)S(1)} collective-permute-done((bf16[2,4,448,256]{3,2,1,0:T(8,128)(2,1)}, bf16[2,4,448,256]{3,2,1,0:T(8,128)(2,1)S(1)}, u32[]{:S(2)}, u32[]{:S(2)}) %collective-permute-start.46) | collective-permute-done | bytes 1835040 | tf_op jit(solution)/shard_map/ppermute | solution.py:156
  593.3 69.5 %all-reduce = (f32[3,896]{1,0:T(4,128)}, f32[16,6]{0,1:T(8,128)}) all-reduce(f32[3,896]{1,0:T(4,128)S(1)} %pad_maximum_fusion.9, f32[16,6]{0,1:T(8,128)S(1)} %dynamic_update_slice.3), channel_id=1, replica_groups=mesh['dp'=8,'seq'=4] {'dp','seq'}, use_global_device_ids=true, to_apply=%region_12.13 | all-reduce | flops 2784 | bytes 22272 | tf_op jit(solution)/shard_map/psum | solution.py:987
  670.1 3.1 fusion.44
  673.2 2.9 collective-permute-done.50
  676.1 10.7 %collective-permute-done.49 = bf16[448,256]{1,0:T(8,128)(2,1)S(1)} collective-permute-done((bf16[448,256]{1,0:T(8,128)(2,1)S(1)}, bf16[448,256]{1,0:T(8,128)(2,1)S(1)}, u32[]{:S(2)}, u32[]{:S(2)}) %collective-permute-start.49) | collective-permute-done | bytes 229408 | tf_op jit(solution)/shard_map/ppermute | solution.py:146
  694.9 8.3 %collective-permute-done.56 = bf16[224,896]{1,0:T(8,128)(2,1)S(1)} collective-permute-done((bf16[224,896]{1,0:T(8,128)(2,1)S(1)}, bf16[224,896]{1,0:T(8,128)(2,1)S(1)}, u32[]{:S(2)}, u32[]{:S(2)}) %collective-permute-start.56) | collective-permute-done | bytes 401440 | tf_op jit(solution)/shard_map/ppermute | solution.py:146
  703.2 20.2 %collective-permute-done.55 = bf16[224,896]{1,0:T(8,128)(2,1)S(1)} collective-permute-done((bf16[224,896]{1,0:T(8,128)(2,1)S(1)}, bf16[224,896]{1,0:T(8,128)(2,1)S(1)}, u32[]{:S(2)}, u32[]{:S(2)}) %collective-permute-start.55) | collective-permute-done | bytes 401440 | tf_op jit(solution)/shard_map/ppermute | solution.py:146
  (340 shorter events, 160.3 us)
Async XLA Ops:
  3.3 19.4 %collective-permute-start.3 = (bf16[112,768]{1,0:T(8,128)(2,1)S(1)}, bf16[112,768]{1,0:T(8,128)(2,1)S(1)}, u32[]{:S(2)}, u32[]{:S(2)}) collective-permute-start(bf16[112,768]{1,0:T(8,128)(2,1)S(1)} %constant_dynamic-update-slice_fusion), channel_id=1, source_target_pairs={{0,4},{4,0},{8,12},{12,8},{16,20},{20,16},{24,28},{28,24},{1,5},{5... | collective-permute-start | bytes 516104 | tf_op jit(solution)/shard_map/ppermute | solution.py:59
  6.3 20.5 %collective-permute-start.4 = (bf16[112,768]{1,0:T(8,128)(2,1)S(1)}, bf16[112,768]{1,0:T(8,128)(2,1)S(1)}, u32[]{:S(2)}, u32[]{:S(2)}) collective-permute-start(bf16[112,768]{1,0:T(8,128)(2,1)S(1)} %constant_dynamic-update-slice_fusion), channel_id=1, source_target_pairs={{0,8},{4,12},{8,0},{12,4},{16,24},{20,28},{24,16},{28,20},{1,9},{5... | collective-permute-start | bytes 516104 | tf_op jit(solution)/shard_map/ppermute | solution.py:59
  7.8 38.4 %collective-permute-start.6 = (bf16[112,768]{1,0:T(8,128)(2,1)S(1)}, bf16[112,768]{1,0:T(8,128)(2,1)S(1)}, u32[]{:S(2)}, u32[]{:S(2)}) collective-permute-start(bf16[112,768]{1,0:T(8,128)(2,1)S(1)} %constant_dynamic-update-slice_fusion), channel_id=1, source_target_pairs={{0,16},{4,20},{8,24},{12,28},{16,0},{20,4},{24,8},{28,12},{1,17},{... | collective-permute-start | bytes 516104 | tf_op jit(solution)/shard_map/ppermute | solution.py:59
  10.4 45.1 %collective-permute-start.8 = (bf16[112,768]{1,0:T(8,128)(2,1)S(1)}, bf16[112,768]{1,0:T(8,128)(2,1)S(1)}, u32[]{:S(2)}, u32[]{:S(2)}) collective-permute-start(bf16[112,768]{1,0:T(8,128)(2,1)S(1)} %constant_dynamic-update-slice_fusion), channel_id=1, source_target_pairs={{0,24},{4,28},{8,16},{12,20},{16,8},{20,12},{24,0},{28,4},{1,25},{... | collective-permute-start | bytes 516104 | tf_op jit(solution)/shard_map/ppermute | solution.py:59
  14.7 14.4 %collective-permute-start.13 = (bf16[560,256]{1,0:T(8,128)(2,1)S(1)}, bf16[560,256]{1,0:T(8,128)(2,1)S(1)}, u32[]{:S(2)}, u32[]{:S(2)}) collective-permute-start(bf16[560,256]{1,0:T(8,128)(2,1)S(1)} %maximum_dynamic-update-slice_fusion), channel_id=1, source_target_pairs={{0,8},{1,9},{2,10},{3,11},{4,12},{5,13},{6,14},{7,15},{8,0},{9,1},... | collective-permute-start | bytes 860168 | tf_op jit(solution)/shard_map/ppermute | solution.py:146
  22.7 22.8 %collective-permute-start.14 = (bf16[560,256]{1,0:T(8,128)(2,1)S(1)}, bf16[560,256]{1,0:T(8,128)(2,1)S(1)}, u32[]{:S(2)}, u32[]{:S(2)}) collective-permute-start(bf16[560,256]{1,0:T(8,128)(2,1)S(1)} %maximum_dynamic-update-slice_fusion), channel_id=1, source_target_pairs={{0,16},{1,17},{2,18},{3,19},{4,20},{5,21},{6,22},{7,23},{8,24},{9,... | collective-permute-start | bytes 860168 | tf_op jit(solution)/shard_map/ppermute | solution.py:146
  26.8 19.9 %collective-permute-start.15 = (bf16[560,256]{1,0:T(8,128)(2,1)S(1)}, bf16[560,256]{1,0:T(8,128)(2,1)S(1)}, u32[]{:S(2)}, u32[]{:S(2)}) collective-permute-start(bf16[560,256]{1,0:T(8,128)(2,1)S(1)} %maximum_dynamic-update-slice_fusion), channel_id=1, source_target_pairs={{0,24},{1,25},{2,26},{3,27},{4,28},{5,29},{6,30},{7,31},{8,16},{9,... | collective-permute-start | bytes 860168 | tf_op jit(solution)/shard_map/ppermute | solution.py:146
  29.1 30.6 %collective-permute-start.21 = (bf16[224,896]{1,0:T(8,128)(2,1)S(1)}, bf16[224,896]{1,0:T(8,128)(2,1)S(1)}, u32[]{:S(2)}, u32[]{:S(2)}) collective-permute-start(bf16[224,896]{1,0:T(8,128)(2,1)S(1)} %get-tuple-element.81), channel_id=1, source_target_pairs={{0,8},{1,9},{2,10},{3,11},{4,12},{5,13},{6,14},{7,15},{8,0},{9,1},... | collective-permute-start | bytes 1204232 | tf_op jit(solution)/shard_map/ppermute | solution.py:146
  45.5 31.9 %collective-permute-start.22 = (bf16[224,896]{1,0:T(8,128)(2,1)S(1)}, bf16[224,896]{1,0:T(8,128)(2,1)S(1)}, u32[]{:S(2)}, u32[]{:S(2)}) collective-permute-start(bf16[224,896]{1,0:T(8,128)(2,1)S(1)} %get-tuple-element.81), channel_id=1, source_target_pairs={{0,16},{1,17},{2,18},{3,19},{4,20},{5,21},{6,22},{7,23},{8,24},{9,... | collective-permute-start | bytes 1204232 | tf_op jit(solution)/shard_map/ppermute | solution.py:146
  46.7 11.1 %collective-permute-start.7 = (bf16[112,768]{1,0:T(8,128)(2,1)S(1)}, bf16[112,768]{1,0:T(8,128)(2,1)S(1)}, u32[]{:S(2)}, u32[]{:S(2)}) collective-permute-start(bf16[112,768]{1,0:T(8,128)(2,1)S(1)} %collective-permute-done.6), channel_id=1, source_target_pairs={{0,4},{4,0},{8,12},{12,8},{16,20},{20,16},{24,28},{28,24},{1,5},{5... | collective-permute-start | bytes 516104 | tf_op jit(solution)/shard_map/ppermute | solution.py:59
  52.6 36.2 %collective-permute-start.16 = (bf16[4,560,256]{2,1,0:T(8,128)(2,1)}, bf16[4,560,256]{2,1,0:T(8,128)(2,1)}, u32[]{:S(2)}, u32[]{:S(2)}) collective-permute-start(bf16[4,560,256]{2,1,0:T(8,128)(2,1)} %pad_maximum_fusion.4), channel_id=1, source_target_pairs={{0,2},{1,5},{2,0},{3,7},{4,6},{5,1},{6,4},{7,3},{8,10},{9,13},{10,... | collective-permute-start | bytes 3440648 | tf_op jit(solution)/shard_map/ppermute | solution.py:150
  55.5 23.4 %collective-permute-start.23 = (bf16[224,896]{1,0:T(8,128)(2,1)S(1)}, bf16[224,896]{1,0:T(8,128)(2,1)S(1)}, u32[]{:S(2)}, u32[]{:S(2)}) collective-permute-start(bf16[224,896]{1,0:T(8,128)(2,1)S(1)} %get-tuple-element.81), channel_id=1, source_target_pairs={{0,24},{1,25},{2,26},{3,27},{4,28},{5,29},{6,30},{7,31},{8,16},{9,... | collective-permute-start | bytes 1204232 | tf_op jit(solution)/shard_map/ppermute | solution.py:146
  57.9 24.5 %collective-permute-start.9 = (bf16[112,768]{1,0:T(8,128)(2,1)S(1)}, bf16[112,768]{1,0:T(8,128)(2,1)S(1)}, u32[]{:S(2)}, u32[]{:S(2)}) collective-permute-start(bf16[112,768]{1,0:T(8,128)(2,1)S(1)} %collective-permute-done.8), channel_id=1, source_target_pairs={{0,4},{4,0},{8,12},{12,8},{16,20},{20,16},{24,28},{28,24},{1,5},{5... | collective-permute-start | bytes 516104 | tf_op jit(solution)/shard_map/ppermute | solution.py:59
  59.7 40.2 %collective-permute-start = (bf16[512,896]{1,0:T(8,128)(2,1)S(1)}, bf16[512,896]{1,0:T(8,128)(2,1)S(1)}, u32[]{:S(2)}, u32[]{:S(2)}) collective-permute-start(bf16[512,896]{1,0:T(8,128)(2,1)S(1)} %bitcast.232), channel_id=1, source_target_pairs={{0,1},{1,0},{2,3},{3,2},{4,5},{5,4},{6,7},{7,6},{8,9},{9,8},{10,11... | collective-permute-start | bytes 2752520 | tf_op jit(solution)/shard_map/ppermute | solution.py:59
  77.4 22.2 %collective-permute-start.1 = (bf16[512,896]{1,0:T(8,128)(2,1)S(1)}, bf16[512,896]{1,0:T(8,128)(2,1)S(1)}, u32[]{:S(2)}, u32[]{:S(2)}) collective-permute-start(bf16[512,896]{1,0:T(8,128)(2,1)S(1)} %bitcast.233), channel_id=1, source_target_pairs={{0,2},{1,3},{2,0},{3,1},{4,6},{5,7},{6,4},{7,5},{8,10},{9,11},{10,... | collective-permute-start | bytes 2752520 | tf_op jit(solution)/shard_map/ppermute | solution.py:59
  78.9 100.7 %collective-permute-start.20 = (bf16[256,896]{1,0:T(8,128)(2,1)}, bf16[256,896]{1,0:T(8,128)(2,1)}, u32[]{:S(2)}, u32[]{:S(2)}) collective-permute-start(bf16[256,896]{1,0:T(8,128)(2,1)} %bitcast.25), channel_id=1, source_target_pairs={{0,1},{1,2},{2,3},{4,5},{5,6},{6,7},{8,9},{9,10},{10,11},{12,13},{... | collective-permute-start | bytes 1376264 | tf_op jit(solution)/shard_map/ppermute | solution.py:871
  82.4 51.8 %collective-permute-start.24 = (bf16[4,224,896]{2,1,0:T(8,128)(2,1)}, bf16[4,224,896]{2,1,0:T(8,128)(2,1)}, u32[]{:S(2)}, u32[]{:S(2)}) collective-permute-start(bf16[4,224,896]{2,1,0:T(8,128)(2,1)} %pad_maximum_fusion.3), channel_id=1, source_target_pairs={{0,2},{1,5},{2,0},{3,7},{4,6},{5,1},{6,4},{7,3},{8,10},{9,13},{10,... | collective-permute-start | bytes 4816904 | tf_op jit(solution)/shard_map/ppermute | solution.py:150
  91.3 48.9 %collective-permute-start.17 = (bf16[8,560,256]{2,1,0:T(8,128)(2,1)}, bf16[8,560,256]{2,1,0:T(8,128)(2,1)}, u32[]{:S(2)}, u32[]{:S(2)}) collective-permute-start(bf16[8,560,256]{2,1,0:T(8,128)(2,1)} %constant_dynamic-update-slice_fusion.6.refs_0_), channel_id=1, source_target_pairs={{0,4},{1,3},{2,6},{3,1},{4,0},{5,7},{6,2},{7,5},{8,12},{9,11},{10,... | collective-permute-start | bytes 6881288 | tf_op jit(solution)/shard_map/ppermute | solution.py:156
  99.6 37.7 %collective-permute-start.2 = (bf16[512,896]{1,0:T(8,128)(2,1)S(1)}, bf16[512,896]{1,0:T(8,128)(2,1)S(1)}, u32[]{:S(2)}, u32[]{:S(2)}) collective-permute-start(bf16[512,896]{1,0:T(8,128)(2,1)S(1)} %collective-permute-done.1), channel_id=1, source_target_pairs={{0,1},{1,0},{2,3},{3,2},{4,5},{5,4},{6,7},{7,6},{8,9},{9,8},{10,11... | collective-permute-start | bytes 2752520 | tf_op jit(solution)/shard_map/ppermute | solution.py:59
  136.9 63.5 %collective-permute-start.25 = (bf16[8,224,896]{2,1,0:T(8,128)(2,1)}, bf16[8,224,896]{2,1,0:T(8,128)(2,1)}, u32[]{:S(2)}, u32[]{:S(2)}) collective-permute-start(bf16[8,224,896]{2,1,0:T(8,128)(2,1)} %constant_dynamic-update-slice_fusion.11.refs_0_), channel_id=1, source_target_pairs={{0,4},{1,3},{2,6},{3,1},{4,0},{5,7},{6,2},{7,5},{8,12},{9,11},{10,... | collective-permute-start | bytes 9633800 | tf_op jit(solution)/shard_map/ppermute | solution.py:156
  137.4 63.3 %collective-permute-start.18 = (bf16[8,560,256]{2,1,0:T(8,128)(2,1)}, bf16[8,560,256]{2,1,0:T(8,128)(2,1)}, u32[]{:S(2)}, u32[]{:S(2)}) collective-permute-start(bf16[8,560,256]{2,1,0:T(8,128)(2,1)} %constant_dynamic-update-slice_fusion.6.refs_0_), channel_id=1, source_target_pairs={{0,1},{1,0},{2,3},{3,2},{4,5},{5,4},{6,7},{7,6},{8,9},{9,8},{10,11... | collective-permute-start | bytes 6881288 | tf_op jit(solution)/shard_map/ppermute | solution.py:162
  140.2 60.5 %collective-permute-start.19 = (bf16[8,560,256]{2,1,0:T(8,128)(2,1)}, bf16[8,560,256]{2,1,0:T(8,128)(2,1)}, u32[]{:S(2)}, u32[]{:S(2)}) collective-permute-start(bf16[8,560,256]{2,1,0:T(8,128)(2,1)} %collective-permute-done.17.refs_1_), channel_id=1, source_target_pairs={{0,1},{1,0},{2,3},{3,2},{4,5},{5,4},{6,7},{7,6},{8,9},{9,8},{10,11... | collective-permute-start | bytes 6881288 | tf_op jit(solution)/shard_map/ppermute | solution.py:162
  182.9 12.8 %collective-permute-start.11 = (bf16[512,256]{1,0:T(8,128)(2,1)S(1)}, bf16[512,256]{1,0:T(8,128)(2,1)S(1)}, u32[]{:S(2)}, u32[]{:S(2)}) collective-permute-start(bf16[512,256]{1,0:T(8,128)(2,1)S(1)} %get-tuple-element.99), channel_id=1, source_target_pairs={{0,2},{1,3},{2,0},{3,1},{4,6},{5,7},{6,4},{7,5},{8,10},{9,11},{10,... | collective-permute-start | bytes 786440 | tf_op jit(solution)/shard_map/ppermute | solution.py:59
  195.7 51.5 %collective-permute-start.26 = (bf16[8,224,896]{2,1,0:T(8,128)(2,1)}, bf16[8,224,896]{2,1,0:T(8,128)(2,1)}, u32[]{:S(2)}, u32[]{:S(2)}) collective-permute-start(bf16[8,224,896]{2,1,0:T(8,128)(2,1)} %constant_dynamic-update-slice_fusion.11.refs_0_), channel_id=1, source_target_pairs={{0,1},{1,0},{2,3},{3,2},{4,5},{5,4},{6,7},{7,6},{8,9},{9,8},{10,11... | collective-permute-start | bytes 9633800 | tf_op jit(solution)/shard_map/ppermute | solution.py:162
  200.3 46.9 %collective-permute-start.27 = (bf16[8,224,896]{2,1,0:T(8,128)(2,1)}, bf16[8,224,896]{2,1,0:T(8,128)(2,1)}, u32[]{:S(2)}, u32[]{:S(2)}) collective-permute-start(bf16[8,224,896]{2,1,0:T(8,128)(2,1)} %collective-permute-done.25.refs_1_), channel_id=1, source_target_pairs={{0,1},{1,0},{2,3},{3,2},{4,5},{5,4},{6,7},{7,6},{8,9},{9,8},{10,11... | collective-permute-start | bytes 9633800 | tf_op jit(solution)/shard_map/ppermute | solution.py:162
  354.9 155.5 %collective-permute-start.51 = (bf16[2,2,4,224,896]{4,3,2,1,0:T(8,128)(2,1)}, bf16[2,2,4,224,896]{4,3,2,1,0:T(8,128)(2,1)}, u32[]{:S(2)}, u32[]{:S(2)}) collective-permute-start(bf16[2,2,4,224,896]{4,3,2,1,0:T(8,128)(2,1)} %get-tuple-element.66), channel_id=1, source_target_pairs={{0,1},{1,0},{2,3},{3,2},{4,5},{5,4},{6,7},{7,6},{8,9},{9,8},{10,11... | collective-permute-start | bytes 19267592 | tf_op jit(solution)/shard_map/ppermute | solution.py:162
  366.0 43.1 %collective-permute-start.30 = (bf16[512,256]{1,0:T(8,128)(2,1)S(1)}, bf16[512,256]{1,0:T(8,128)(2,1)S(1)}, u32[]{:S(2)}, u32[]{:S(2)}) collective-permute-start(bf16[512,256]{1,0:T(8,128)(2,1)S(1)} %get-tuple-element.94), channel_id=1, source_target_pairs={{0,3},{1,2},{2,1},{3,0},{4,7},{5,6},{6,5},{7,4},{8,11},{9,10},{10,... | collective-permute-start | bytes 786440 | tf_op jit(solution)/shard_map/ppermute | solution.py:59
  368.0 42.2 %collective-permute-start.29 = (bf16[512,256]{1,0:T(8,128)(2,1)S(1)}, bf16[512,256]{1,0:T(8,128)(2,1)S(1)}, u32[]{:S(2)}, u32[]{:S(2)}) collective-permute-start(bf16[512,256]{1,0:T(8,128)(2,1)S(1)} %get-tuple-element.95), channel_id=1, source_target_pairs={{0,2},{1,3},{2,0},{3,1},{4,6},{5,7},{6,4},{7,5},{8,10},{9,11},{10,... | collective-permute-start | bytes 786440 | tf_op jit(solution)/shard_map/ppermute | solution.py:59
  368.1 42.2 %collective-permute-start.28 = (bf16[512,256]{1,0:T(8,128)(2,1)S(1)}, bf16[512,256]{1,0:T(8,128)(2,1)S(1)}, u32[]{:S(2)}, u32[]{:S(2)}) collective-permute-start(bf16[512,256]{1,0:T(8,128)(2,1)S(1)} %get-tuple-element.96), channel_id=1, source_target_pairs={{0,1},{1,0},{2,3},{3,2},{4,5},{5,4},{6,7},{7,6},{8,9},{9,8},{10,11... | collective-permute-start | bytes 786440 | tf_op jit(solution)/shard_map/ppermute | solution.py:59
  368.2 106.6 %collective-permute-start.34 = (bf16[256,896]{1,0:T(8,128)(2,1)}, bf16[256,896]{1,0:T(8,128)(2,1)}, u32[]{:S(2)}, u32[]{:S(2)}) collective-permute-start(bf16[256,896]{1,0:T(8,128)(2,1)} %slice.378), channel_id=1, source_target_pairs={{1,0},{2,1},{3,2},{5,4},{6,5},{7,6},{9,8},{10,9},{11,10},{13,12},{... | collective-permute-start | bytes 1376264 | tf_op jit(solution)/shard_map/ppermute | solution.py:942
  409.1 69.5 %collective-permute-start.39 = (bf16[2,2,4,112,256]{4,3,2,1,0:T(8,128)(2,1)}, bf16[2,2,4,112,256]{4,3,2,1,0:T(8,128)(2,1)}, u32[]{:S(2)}, u32[]{:S(2)}) collective-permute-start(bf16[2,2,4,112,256]{4,3,2,1,0:T(8,128)(2,1)} %get-tuple-element.56), channel_id=1, source_target_pairs={{0,1},{1,0},{2,3},{3,2},{4,5},{5,4},{6,7},{7,6},{8,9},{9,8},{10,11... | collective-permute-start | bytes 2752520 | tf_op jit(solution)/shard_map/ppermute | solution.py:162
  410.2 111.7 %collective-permute-start.45 = (bf16[2,2,4,448,256]{4,3,2,1,0:T(8,128)(2,1)}, bf16[2,2,4,448,256]{4,3,2,1,0:T(8,128)(2,1)}, u32[]{:S(2)}, u32[]{:S(2)}) collective-permute-start(bf16[2,2,4,448,256]{4,3,2,1,0:T(8,128)(2,1)} %get-tuple-element.62), channel_id=1, source_target_pairs={{0,1},{1,0},{2,3},{3,2},{4,5},{5,4},{6,7},{7,6},{8,9},{9,8},{10,11... | collective-permute-start | bytes 11010056 | tf_op jit(solution)/shard_map/ppermute | solution.py:162
  466.5 72.2 %collective-permute-start.32 = (bf16[512,896]{1,0:T(8,128)(2,1)S(1)}, bf16[512,896]{1,0:T(8,128)(2,1)}, u32[]{:S(2)}, u32[]{:S(2)}) collective-permute-start(bf16[512,896]{1,0:T(8,128)(2,1)S(1)} %get-tuple-element.87), channel_id=1, source_target_pairs={{0,1},{1,0},{2,3},{3,2},{4,5},{5,4},{6,7},{7,6},{8,9},{9,8},{10,11... | collective-permute-start | bytes 2752520 | tf_op jit(solution)/shard_map/ppermute | solution.py:59
  474.8 17.7 %collective-permute-start.35 = (bf16[4,112,768]{2,1,0:T(8,128)(2,1)}, bf16[4,112,768]{2,1,0:T(8,128)(2,1)S(1)}, u32[]{:S(2)}, u32[]{:S(2)}) collective-permute-start(bf16[4,112,768]{2,1,0:T(8,128)(2,1)} %get-tuple-element.54), channel_id=1, source_target_pairs={{0,4},{4,0},{8,12},{12,8},{16,20},{20,16},{24,28},{28,24},{1,5},{5... | collective-permute-start | bytes 2064392 | tf_op jit(solution)/shard_map/ppermute | solution.py:59
  480.3 17.1 %collective-permute-start.40 = (bf16[2,4,112,256]{3,2,1,0:T(8,128)(2,1)S(1)}, bf16[2,4,112,256]{3,2,1,0:T(8,128)(2,1)S(1)}, u32[]{:S(2)}, u32[]{:S(2)}) collective-permute-start(bf16[2,4,112,256]{3,2,1,0:T(8,128)(2,1)S(1)} %get-tuple-element.89), channel_id=1, source_target_pairs={{0,4},{1,3},{2,6},{3,1},{4,0},{5,7},{6,2},{7,5},{8,12},{9,11},{10,... | collective-permute-start | bytes 1376264 | tf_op jit(solution)/shard_map/ppermute | solution.py:156
  493.4 33.8 %collective-permute-start.38 = (bf16[112,768]{1,0:T(8,128)(2,1)S(1)}, bf16[112,768]{1,0:T(8,128)(2,1)S(1)}, u32[]{:S(2)}, u32[]{:S(2)}) collective-permute-start(bf16[112,768]{1,0:T(8,128)(2,1)S(1)} %get-tuple-element.107), channel_id=1, source_target_pairs={{0,24},{4,28},{8,16},{12,20},{16,8},{20,12},{24,0},{28,4},{1,25},{... | collective-permute-start | bytes 516104 | tf_op jit(solution)/shard_map/ppermute | solution.py:59
  497.4 30.6 %collective-permute-start.37 = (bf16[112,768]{1,0:T(8,128)(2,1)}, bf16[112,768]{1,0:T(8,128)(2,1)}, u32[]{:S(2)}, u32[]{:S(2)}) collective-permute-start(bf16[112,768]{1,0:T(8,128)(2,1)} %get-tuple-element.108), channel_id=1, source_target_pairs={{0,16},{4,20},{8,24},{12,28},{16,0},{20,4},{24,8},{28,12},{1,17},{... | collective-permute-start | bytes 516104 | tf_op jit(solution)/shard_map/ppermute | solution.py:59
  521.0 66.3 %collective-permute-start.52 = (bf16[2,4,224,896]{3,2,1,0:T(8,128)(2,1)}, bf16[2,4,224,896]{3,2,1,0:T(8,128)(2,1)}, u32[]{:S(2)}, u32[]{:S(2)}) collective-permute-start(bf16[2,4,224,896]{3,2,1,0:T(8,128)(2,1)} %get-tuple-element.83), channel_id=1, source_target_pairs={{0,4},{1,3},{2,6},{3,1},{4,0},{5,7},{6,2},{7,5},{8,12},{9,11},{10,... | collective-permute-start | bytes 9633800 | tf_op jit(solution)/shard_map/ppermute | solution.py:156
  528.0 58.3 %collective-permute-start.31 = (bf16[512,896]{1,0:T(8,128)(2,1)}, bf16[512,896]{1,0:T(8,128)(2,1)S(1)}, u32[]{:S(2)}, u32[]{:S(2)}) collective-permute-start(bf16[512,896]{1,0:T(8,128)(2,1)} %get-tuple-element.86), channel_id=1, source_target_pairs={{0,1},{1,0},{2,3},{3,2},{4,5},{5,4},{6,7},{7,6},{8,9},{9,8},{10,11... | collective-permute-start | bytes 2752520 | tf_op jit(solution)/shard_map/ppermute | solution.py:59
  530.6 50.7 %collective-permute-start.46 = (bf16[2,4,448,256]{3,2,1,0:T(8,128)(2,1)}, bf16[2,4,448,256]{3,2,1,0:T(8,128)(2,1)S(1)}, u32[]{:S(2)}, u32[]{:S(2)}) collective-permute-start(bf16[2,4,448,256]{3,2,1,0:T(8,128)(2,1)} %get-tuple-element.85), channel_id=1, source_target_pairs={{0,4},{1,3},{2,6},{3,1},{4,0},{5,7},{6,2},{7,5},{8,12},{9,11},{10,... | collective-permute-start | bytes 5505032 | tf_op jit(solution)/shard_map/ppermute | solution.py:156
  543.2 43.1 %collective-permute-start.33 = (bf16[512,896]{1,0:T(8,128)(2,1)S(1)}, bf16[512,896]{1,0:T(8,128)(2,1)S(1)}, u32[]{:S(2)}, u32[]{:S(2)}) collective-permute-start(bf16[512,896]{1,0:T(8,128)(2,1)S(1)} %add_convert_fusion), channel_id=1, source_target_pairs={{0,2},{1,3},{2,0},{3,1},{4,6},{5,7},{6,4},{7,5},{8,10},{9,11},{10,... | collective-permute-start | bytes 2752520 | tf_op jit(solution)/shard_map/ppermute | solution.py:59
  583.7 79.0 %collective-permute-start.47 = (bf16[4,448,256]{2,1,0:T(8,128)(2,1)}, bf16[4,448,256]{2,1,0:T(8,128)(2,1)}, u32[]{:S(2)}, u32[]{:S(2)}) collective-permute-start(bf16[4,448,256]{2,1,0:T(8,128)(2,1)} %fusion.43), channel_id=1, source_target_pairs={{0,2},{1,5},{2,0},{3,7},{4,6},{5,1},{6,4},{7,3},{8,10},{9,13},{10,... | collective-permute-start | bytes 2752520 | tf_op jit(solution)/shard_map/ppermute | solution.py:150
  593.2 93.7 %collective-permute-start.53 = (bf16[4,224,896]{2,1,0:T(8,128)(2,1)}, bf16[4,224,896]{2,1,0:T(8,128)(2,1)}, u32[]{:S(2)}, u32[]{:S(2)}) collective-permute-start(bf16[4,224,896]{2,1,0:T(8,128)(2,1)} %fusion.41), channel_id=1, source_target_pairs={{0,2},{1,5},{2,0},{3,7},{4,6},{5,1},{6,4},{7,3},{8,10},{9,13},{10,... | collective-permute-start | bytes 4816904 | tf_op jit(solution)/shard_map/ppermute | solution.py:150
  667.4 19.4 %collective-permute-start.49 = (bf16[448,256]{1,0:T(8,128)(2,1)S(1)}, bf16[448,256]{1,0:T(8,128)(2,1)S(1)}, u32[]{:S(2)}, u32[]{:S(2)}) collective-permute-start(bf16[448,256]{1,0:T(8,128)(2,1)S(1)} %get-tuple-element.103), channel_id=1, source_target_pairs={{0,16},{1,17},{2,18},{3,19},{4,20},{5,21},{6,22},{7,23},{8,24},{9,... | collective-permute-start | bytes 688136 | tf_op jit(solution)/shard_map/ppermute | solution.py:146
  667.4 19.4 %collective-permute-start.48 = (bf16[448,256]{1,0:T(8,128)(2,1)S(1)}, bf16[448,256]{1,0:T(8,128)(2,1)S(1)}, u32[]{:S(2)}, u32[]{:S(2)}) collective-permute-start(bf16[448,256]{1,0:T(8,128)(2,1)S(1)} %get-tuple-element.101), channel_id=1, source_target_pairs={{0,8},{1,9},{2,10},{3,11},{4,12},{5,13},{6,14},{7,15},{8,0},{9,1},... | collective-permute-start | bytes 688136 | tf_op jit(solution)/shard_map/ppermute | solution.py:146
  689.1 14.1 %collective-permute-start.56 = (bf16[224,896]{1,0:T(8,128)(2,1)S(1)}, bf16[224,896]{1,0:T(8,128)(2,1)S(1)}, u32[]{:S(2)}, u32[]{:S(2)}) collective-permute-start(bf16[224,896]{1,0:T(8,128)(2,1)S(1)} %get-tuple-element.91), channel_id=1, source_target_pairs={{0,24},{1,25},{2,26},{3,27},{4,28},{5,29},{6,30},{7,31},{8,16},{9,... | collective-permute-start | bytes 1204232 | tf_op jit(solution)/shard_map/ppermute | solution.py:146
  691.2 32.2 %collective-permute-start.55 = (bf16[224,896]{1,0:T(8,128)(2,1)S(1)}, bf16[224,896]{1,0:T(8,128)(2,1)S(1)}, u32[]{:S(2)}, u32[]{:S(2)}) collective-permute-start(bf16[224,896]{1,0:T(8,128)(2,1)S(1)} %get-tuple-element.92), channel_id=1, source_target_pairs={{0,16},{1,17},{2,18},{3,19},{4,20},{5,21},{6,22},{7,23},{8,24},{9,... | collective-permute-start | bytes 1204232 | tf_op jit(solution)/shard_map/ppermute | solution.py:146
  691.2 32.2 %collective-permute-start.54 = (bf16[224,896]{1,0:T(8,128)(2,1)S(1)}, bf16[224,896]{1,0:T(8,128)(2,1)S(1)}, u32[]{:S(2)}, u32[]{:S(2)}) collective-permute-start(bf16[224,896]{1,0:T(8,128)(2,1)S(1)} %get-tuple-element.90), channel_id=1, source_target_pairs={{0,8},{1,9},{2,10},{3,11},{4,12},{5,13},{6,14},{7,15},{8,0},{9,1},... | collective-permute-start | bytes 1204232 | tf_op jit(solution)/shard_map/ppermute | solution.py:146
  (75 other events, 1043.0 us)

commit v2 on v1

--- a/solution.py
+++ b/solution.py
@@ -59,6 +59,10 @@
     return lax.ppermute(value, axis, [(i, i ^ by) for i in range(peers)])
 
 
+def after(value, *others):
+    return lax.optimization_barrier((value,) + others)[0]
+
+
 def vmem_spec():
     return pl.BlockSpec(memory_space=pltpu.VMEM)
 
@@ -71,22 +75,23 @@
     out_ref[...] = in_ref[...].reshape(out_ref.shape)
 
 
-def reorder_rows(stacked, mine):
-    count, rows, cols = stacked.shape
-    if rows % 16 or cols % 128:
-        order = jnp.arange(count, dtype=jnp.int32) ^ mine
-        return jnp.take(stacked, order, axis=0).reshape(count * rows, cols)
-    spec = pltpu.PrefetchScalarGridSpec(
-        num_scalar_prefetch=1,
-        grid=(count,),
-        in_specs=[pl.BlockSpec((1, rows, cols), lambda i, m: (m[0] ^ i, 0, 0))],
-        out_specs=pl.BlockSpec((rows, cols), lambda i, m: (i, 0)),
-    )
+def reorder_triple_kernel(place_ref, near_ref, far_ref, out_ref):
+    count, rows, _ = near_ref.shape
+    z, y = place_ref[0], place_ref[1]
+    for ref, flip in ((near_ref, 0), (far_ref, 1)):
+        for k in range(count):
+            where = ((z ^ k) * 2 + (y ^ flip)) * rows
+            out_ref[pl.ds(pl.multiple_of(where, rows), rows), :] = ref[k]
+
+
+def reorder_triple(near, far, place):
+    count, rows, cols = near.shape
     return pl.pallas_call(
-        copy_kernel,
-        grid_spec=spec,
-        out_shape=jax.ShapeDtypeStruct((count * rows, cols), stacked.dtype),
-    )(mine.reshape(1), stacked)
+        reorder_triple_kernel,
+        in_specs=[smem_spec(), vmem_spec(), vmem_spec()],
+        out_specs=vmem_spec(),
+        out_shape=jax.ShapeDtypeStruct((2 * count * rows, cols), near.dtype),
+    )(place, near, far)
 
 
 def columns_from_blocks(stacked, mine):
@@ -234,27 +239,25 @@
     )(place, *pieces)
 
 
-def assemble_feed_kernel(depth, place_ref, *refs):
-    pieces, (inner, outer), stage, sems = refs[:4], refs[4:6], refs[6], refs[7]
-    rows = inner.shape[0] // (2 * depth)
+def assemble_feed_kernel(blocks, inner, outer, stage, sems):
+    count = blocks.shape[0]
+    rows = inner.shape[0] // (count // 4)
     cols = inner.shape[1] // 4
     part = cols // 4
 
-    def step(t, carry):
-        for i in range(4):
-            i_dp, i_seq = piece_origin(place_ref, i // 2, i % 2, t, depth)
-            piece = pieces[i].at[t]
-            down = pl.ds(pl.multiple_of(i_dp * rows, rows), rows)
-            across = pl.ds(pl.multiple_of(i_seq * cols, cols), cols)
+    def step(i, carry):
+        for j in range(4):
+            piece = blocks.at[i * 4 + j]
+            down = pl.ds(pl.multiple_of(i * rows, rows), rows)
             pltpu.make_async_copy(
-                piece.at[pl.ds(rows, rows), :], stage.at[i_dp, i_seq], sems.at[1]
+                piece.at[pl.ds(rows, rows), :], stage.at[i, j], sems.at[1]
             ).start()
             pltpu.make_async_copy(
-                piece.at[pl.ds(0, rows), :], inner.at[down, across], sems.at[0]
+                piece.at[pl.ds(0, rows), :], inner.at[down, pl.ds(j * cols, cols)], sems.at[0]
             ).start()
         return carry
 
-    lax.fori_loop(0, 2 * depth, step, 0)
+    lax.fori_loop(0, count // 4, step, 0)
     pltpu.make_async_copy(stage, stage, sems.at[1]).wait()
 
     def spread(i, carry):
@@ -264,27 +267,27 @@
             outer[pl.ds(where, rows), :] = jnp.concatenate(line, axis=1)
         return carry
 
-    lax.fori_loop(0, 2 * depth, spread, 0)
+    lax.fori_loop(0, count // 4, spread, 0)
     pltpu.make_async_copy(inner, inner, sems.at[0]).wait()
 
 
-def assemble_feed(pieces, place):
-    count, packed, cols = pieces[0].shape
-    rows = packed // 2
+def assemble_feed(blocks):
+    count, packed, cols = blocks.shape
+    rows, deep = packed // 2, count // 4
     return pl.pallas_call(
-        functools.partial(assemble_feed_kernel, count // 2),
-        in_specs=[smem_spec()] + [pl.BlockSpec(memory_space=pl.ANY)] * 4,
+        assemble_feed_kernel,
+        in_specs=[pl.BlockSpec(memory_space=pl.ANY)],
         out_specs=[vmem_spec()] * 2,
         out_shape=[
-            jax.ShapeDtypeStruct((rows * count, cols * 4), BF),
-            jax.ShapeDtypeStruct((4 * rows * count, cols), BF),
+            jax.ShapeDtypeStruct((rows * deep, cols * 4), BF),
+            jax.ShapeDtypeStruct((4 * rows * deep, cols), BF),
         ],
         scratch_shapes=[
-            pltpu.VMEM((count, 4, rows, cols), BF),
+            pltpu.VMEM((deep, 4, rows, cols), BF),
             pltpu.SemaphoreType.DMA((2,)),
         ],
         compiler_params=pltpu.CompilerParams(vmem_limit_bytes=VMEM_LIMIT),
-    )(place, *pieces)
+    )(blocks)
 
 
 def put_block(place_ref, out_ref, core, i_dp, flip, value):
@@ -325,24 +328,61 @@
                     put_block(place_ref, out, j % 2, i_dp, (j // 2) ^ x, block)
 
 
-def outer_grad_kernel(*refs):
-    place_ref, left, right = refs[:3]
-    kept, sent = refs[-2:]
-    rows, cols = kept.shape[3], kept.shape[4]
+def outer_grad_kernel(left, right, out_ref):
+    rows, cols = out_ref.shape[2], out_ref.shape[3]
     part = cols // 4
-    i_z = pl.program_id(0)
-    x, core = place_ref[2], place_ref[3]
-    for j in range(4):
-        value = rounded(dot(left[...], right[:, j * part : (j + 1) * part], 0, 0))
-        for out, mine in ((kept, core == j % 2), (sent, core != j % 2)):
-
-            @pl.when(mine)
-            def _():
-                for i_y in range(2):
-                    base = i_y * 4 * rows
-                    line = [value[base + t * rows : base + (t + 1) * rows] for t in range(4)]
-                    block = jnp.concatenate(line, axis=1)
-                    put_block(place_ref, out, j % 2, i_z * 2 + i_y, (j // 2) ^ x, block)
+    value = rounded(dot(left[...], right[...], 0, 0))
+    for i_y in range(2):
+        for j in range(4):
+            base = i_y * 4 * rows
+            lanes = slice(j * part, (j + 1) * part)
+            line = [value[base + t * rows : base + (t + 1) * rows, lanes] for t in range(4)]
+            out_ref[i_y, j] = jnp.concatenate(line, axis=1)
+
+
+def inner_grad_kernel(left, right, before, out_ref):
+    value = rounded(dot(left[...], right[...], 0, 0))
+    out_ref[...] = value.reshape(out_ref.shape)
+
+
+def feed_grad(normed, grad_gate, hidden, grad_feed):
+    dp = lax.axis_size("dp")
+    tokens, model = normed.shape
+    inner = grad_gate.shape[1]
+    rows, cols = model // dp, inner // 4
+    shape = jax.ShapeDtypeStruct((dp, 4, 2 * rows, cols), BF)
+    params = pltpu.CompilerParams(vmem_limit_bytes=VMEM_LIMIT)
+    cost = pl.CostEstimate(
+        flops=2 * tokens * model * inner,
+        bytes_accessed=2 * (tokens * (model + inner) + model * inner),
+        transcendentals=0,
+    )
+    outer = pl.pallas_call(
+        outer_grad_kernel,
+        grid=(dp // 2,),
+        in_specs=[
+            pl.BlockSpec((tokens, 2 * inner // dp), lambda i: (0, i)),
+            pl.BlockSpec((tokens, model), lambda i: (0, 0)),
+        ],
+        out_specs=pl.BlockSpec((2, 4, rows, cols), lambda i: (i, 0, 1, 0)),
+        out_shape=shape,
+        compiler_params=params,
+        cost_estimate=cost,
+    )(hidden, grad_feed)
+    return pl.pallas_call(
+        inner_grad_kernel,
+        grid=(4,),
+        in_specs=[
+            pl.BlockSpec((tokens, model), lambda i: (0, 0)),
+            pl.BlockSpec((tokens, cols), lambda i: (0, i)),
+            pl.BlockSpec(memory_space=pl.ANY),
+        ],
+        out_specs=pl.BlockSpec((dp, 1, rows, cols), lambda i: (0, i, 0, 0)),
+        out_shape=shape,
+        input_output_aliases={2: 0},
+        compiler_params=params,
+        cost_estimate=cost,
+    )(normed, grad_gate, outer)
 
 
 def group_grad(kind, place, left, right, first, total, before=None, parts=1):
@@ -352,8 +392,6 @@
     width = right.shape[1]
     if kind == "tall":
         rows, cols = width // 8, 2 * height // dp
-    elif kind == "outer":
-        rows, cols = height // dp // 4, width
     else:
         rows, cols = height // dp, width // 4 // parts
     whole = jax.ShapeDtypeStruct((2, 2, depth, total * rows, cols), BF)
@@ -366,13 +404,6 @@
             pl.BlockSpec((tokens, cols), lambda p, i, m: (0, p * 4 + (m[2] ^ i) * 2 + 1 - m[3])),
         ]
         out_spec = pl.BlockSpec(block, lambda p, i, m: (0, 0, 0, first + p, 0))
-    elif kind == "outer":
-        kernel, grid, operands = outer_grad_kernel, (depth,), [left, right]
-        specs = [
-            pl.BlockSpec((tokens, height // depth), lambda i, m: (0, i)),
-            pl.BlockSpec((tokens, width), lambda i, m: (0, 0)),
-        ]
-        out_spec = pl.BlockSpec(block, lambda i, m: (0, 0, 0, first, 0))
     else:
         kernel, grid, operands = tall_grad_kernel, (1,), [left, right]
         specs = [
@@ -401,17 +432,35 @@
     )(place, *operands)
 
 
+def wide_sum(*values):
+    total = values[0].astype(F32)
+    for value in values[1:]:
+        total = total + value.astype(F32)
+    return total
+
+
 def sum_group(pieces):
     kept, sent = pieces
-    got = over_core(sent).astype(F32)
-    got_b = over_b(rounded(kept[1].astype(F32) + got[1])).astype(F32)
-    near = kept[0].astype(F32) + got[0]
-    got_a = over_a(rounded(near[1] + got_b[1])).astype(F32)
-    line = rounded(near[0] + got_b[0] + got_a)
-    total = line[0].astype(F32)
-    for k in range(1, line.shape[0]):
-        total = total + over_z(line[k], k).astype(F32)
-    return total
+    got = over_core(sent)
+    out_b = rounded(wide_sum(kept[1], got[1]))
+    yield out_b
+    got_b = over_b(out_b)
+    out_a = rounded(wide_sum(kept[0, 1], got[0, 1], got_b[1]))
+    yield out_a
+    got_a = over_a(out_a)
+    line = rounded(wide_sum(kept[0, 0], got[0, 0], got_b[0], got_a))
+    yield line
+    yield wide_sum(line[0], *[over_z(line[k], k) for k in range(1, line.shape[0])])
+
+
+def butterfly(value):
+    k = 1
+    while k < lax.axis_size("dp") // 2:
+        value = value + over_z(value, k)
+        k *= 2
+    for step in (over_a, over_b, over_core):
+        value = value + step(value)
+    return value
 
 
 def triple_grad_kernel(place_ref, left, right, kept, sent):
@@ -442,11 +491,8 @@
             flops=2 * left.size * cols, bytes_accessed=2 * (left.size + right.size), transcendentals=0
         ),
     )(place, left, right)
-    line = rounded(kept.astype(F32) + swap(sent, "dp", 1).astype(F32))
-    total = line[0].astype(F32)
-    for k in range(1, dp // 2):
-        total = total + swap(line[k], "dp", 2 * k).astype(F32)
-    return total
+    line = rounded(wide_sum(kept, swap(sent, "dp", 1)))
+    return wide_sum(line[0], *[swap(line[k], "dp", 2 * k) for k in range(1, dp // 2)])
 
 
 def lane_mask(shape, head):
@@ -826,12 +872,8 @@
 
     triple = jnp.concatenate([query_self, key_self, value_self], axis=1)
     if fast:
-        near = {0: triple}
-        for k in range(2, dp, 2):
-            near[k] = swap(triple, "dp", k)
-        for k in list(near):
-            near[k + 1] = swap(near[k], "dp", 1)
-        triple_full = reorder_rows(jnp.stack([near[k] for k in range(dp)]), my_dp)
+        line = jnp.stack([triple] + [swap(triple, "dp", 2 * k) for k in range(1, dp // 2)])
+        triple_full = reorder_triple(line, swap(line, "dp", 1), place)
 
         def turned(shard):
             flat = shard.T
@@ -842,12 +884,13 @@
             [key_cross, value_cross, query_cross, turned(output_self), turned(output_cross)], axis=0
         )
         recall_full, query_full, output_turned, cross_turned = assemble_attention(
-            gather_group(packed), place
+            gather_group(after(packed, line)), place
         )
         part = outer_weight.shape[0] // 4
         line = [outer_weight[t * part : (t + 1) * part] for t in range(4)]
         packed = jnp.concatenate([inner_weight, jnp.concatenate(line, axis=1)], axis=0)
-        inner_full, outer_full = assemble_feed(gather_group(packed), place)
+        feed_blocks = lax.all_gather(packed, BOTH, axis=0, tiled=False)
+        inner_full, outer_full = assemble_feed(feed_blocks)
     else:
         pieces = []
         for shard in (query_self, key_self, value_self):
@@ -859,22 +902,22 @@
         inner_full, outer_full = whole(inner_weight), whole(outer_weight)
 
     own_tokens = tokens.reshape(rows, model)
-    pieces = {0: own_tokens}
+    pieces_tok = {0: own_tokens}
     bit = span // 2
     while bit:
-        for k in list(pieces):
-            pieces[k | bit] = swap(pieces[k], "seq", bit)
+        for k in list(pieces_tok):
+            pieces_tok[k | bit] = swap(pieces_tok[k], "seq", bit)
         bit //= 2
     states = neighbours.reshape(segments * neigh_rows, model)
     forward_pairs = [(i, i + 1) for i in range(seq - 1) if (i + 1) % span]
     back_pairs = [(i + 1, i) for i in range(seq - 1) if (i + 1) % span]
     edge = lax.ppermute(states[(segments - 1) * neigh_rows :], "seq", forward_pairs)
-    states_all = jnp.concatenate([edge, states], axis=0)
+    states_all = lax.optimization_barrier(jnp.concatenate([edge, states], axis=0))
 
     inputs = own_tokens.astype(F32)
     upstream = cotangent.reshape(rows, model).astype(F32)
     first_normed = jnp.concatenate(
-        [rounded(rms_apply(pieces[k].astype(F32), norm_gains[0])) for k in range(span)], axis=0
+        [rounded(rms_apply(pieces_tok[k].astype(F32), norm_gains[0])) for k in range(span)], axis=0
     )
     qkv = rounded(linear(first_normed, triple_full))
     bias = lax.dynamic_slice_in_dim(position_bias, pos * group_heads, group_heads, 0)
@@ -903,9 +946,9 @@
     grad_hidden = input_grad(grad_feed, outer_full)
     grad_gate = rounded(gelu_pull(grad_hidden)[0])
     if fast:
-        pieces = group_grad("outer", place, hidden_act, grad_feed, 1, 2)
-        pieces = group_grad("wide", place, third_normed, grad_gate, 0, 2, pieces)
-        own = sum_group(pieces)
+        blocks = feed_grad(third_normed, grad_gate, hidden_act, grad_feed)
+        blocks = blocks.reshape((dp * seq,) + blocks.shape[2:])
+        own = lax.psum_scatter(blocks, BOTH, scatter_dimension=0, tiled=True)[0].astype(F32)
         part = own.shape[0] // 2
         sum_inner = own[:part]
         sum_outer = own[part:].reshape(part, 4, model // 4).transpose(1, 0, 2).reshape(4 * part, -1)
@@ -924,13 +967,9 @@
         return jnp.concatenate([own[:, :half].T, own[:, half:].T], axis=1)
 
     if fast:
-        pieces = group_grad("tall", place, mixed_cross, grad_cross, 3, 4)
-        pieces = group_grad("wide", place, second_normed, probe, 2, 4, pieces)
-        pieces = group_grad("wide", place, states_all, pair_round, 0, 4, pieces, 2)
-        own = sum_group(pieces)
-        part = own.shape[0] // 4
-        sum_key, sum_value, sum_query = (own[i * part : (i + 1) * part] for i in range(3))
-        sum_cross = turned_back(own[3 * part :])
+        pieces = group_grad("tall", place, mixed_cross, grad_cross, 3, 5)
+        pieces = group_grad("wide", place, second_normed, probe, 2, 5, pieces)
+        pieces = group_grad("wide", place, states_all, pair_round, 0, 5, pieces, 2)
     else:
         sum_cross = block_sum(mixed_cross, grad_cross)
         sum_key = block_sum(states_all, pair_round[:, :width])
@@ -947,14 +986,28 @@
 
     grad_self = rounded(grad_early)
     if fast:
-        sum_output = turned_back(sum_group(group_grad("tall", place, mixed_self, grad_self, 0, 1)))
+        steps = sum_group(group_grad("tall", place, mixed_self, grad_self, 4, 5, pieces))
+        sent_b = next(steps)
+        sent_a = next(steps)
+        sent_z = next(steps)
+        own = next(steps)
+        part = own.shape[0] // 5
+        sum_key, sum_value, sum_query = (own[i * part : (i + 1) * part] for i in range(3))
+        sum_cross = turned_back(own[3 * part : 4 * part])
+        sum_output = turned_back(own[4 * part :])
     else:
         sum_output = block_sum(mixed_self, grad_self)
     grad_attended = rounded(linear(grad_self, output_turned))
     group_grads = exchanged(blocks_from_columns(grad_attended, span, pos))
     grad_group = jnp.concatenate(group_grads, axis=0)
+    if fast:
+        grad_group = after(grad_group, sent_b)
     triple_grad, bias_sums = self_bwd(pos, bias, qkv, mixed_group, grad_group, lse, rows)
-    partial = rounded(input_grad(triple_grad, triple_full)).reshape(span, rows, model)
+    partial = input_grad(triple_grad, triple_full)
+    all_tokens = jnp.concatenate([pieces_tok[k] for k in range(span)], axis=0).astype(F32)
+    factor = lax.rsqrt(jnp.mean(all_tokens * all_tokens, axis=-1, keepdims=True) + EPSILON)
+    gain_one = jnp.sum(partial * all_tokens * factor, axis=0)
+    partial = rounded(partial).reshape(span, rows, model)
     blocks = {k: partial[k] for k in range(span)}
     bit = 1
     while bit < span:
@@ -966,7 +1019,7 @@
                     blocks[k] = rounded(blocks[k])
         blocks = {k: v for k, v in blocks.items() if not k & bit}
         bit *= 2
-    norm_grad, gain_one = norm_back(inputs, norm_gains[0], blocks[0])
+    norm_grad, _ = norm_back(inputs, norm_gains[0], blocks[0])
     grad_inputs = grad_early + norm_grad
 
     if fast:
@@ -984,7 +1037,15 @@
     bias_all = lax.dynamic_update_slice_in_dim(
         jnp.zeros((heads, NB), F32), bias_local, pos * group_heads, 0
     )
-    gains, bias_total = lax.psum((jnp.stack([gain_one, gain_two, gain_three]), bias_all), BOTH)
+    small = jnp.concatenate([gain_one, gain_two, gain_three, bias_all.reshape(-1)])
+    if fast:
+        size = small.shape[0]
+        small = jnp.pad(small, (0, -size % 1024)).reshape(-1, 128)
+        small = butterfly(small).reshape(-1)[:size]
+    else:
+        small = lax.psum(small, BOTH)
+    gains = small[: 3 * model].reshape(3, model)
+    bias_total = small[3 * model :].reshape(heads, NB)
     return (
         rounded(outcome).reshape(1, rows, model),
         rounded(grad_inputs).reshape(1, rows, model),

time: 736 us -> 623 us (0.85)
  blocking collectives: 69.5 us -> 0 us
  starting transfers between devices: 76.8 us -> 48 us
  local copies, waits for them, and re-layouts: 48.9 us -> 27.7 us
  other arithmetic: 67.3 us -> 52.2 us
  waiting for transfers between devices: 171 us -> 186 us
  between operations: 2.06 us -> 15.1 us
  Pallas kernels: 205 us -> 192 us
  matrix products: 85.5 us -> 96.4 us
    psum x1 -> x0, blocking collectives: 69.5 us -> none  [on_device(): lax.psum((jnp.stack([gain_one, gain_two, gain_three]), bias_all), BOTH)]
    ppermute x23 -> x20, waiting for transfers between devices: 21.5 us -> 78.8 us  [swap(): return lax.ppermute(value, axis, [(i, i ^ by) for i in range(peers)])]
    ppermute x5 -> x3, waiting for transfers between devices: 31.7 us -> 0.01 us  [over_b(): lax.ppermute(value, BOTH, device_pairs(lambda z, y, x, c: (z, y ^ 1 - c,...]
    ppermute x15 -> x8, waiting for transfers between devices: 79.3 us -> 52.1 us  [over_z(): lax.ppermute(value, BOTH, device_pairs(lambda z, y, x, c: (z ^ k, y, x, c)))]
    pallas_call x6 -> x4, Pallas kernels: 58.5 us -> 31.7 us  [group_grad(): pl.pallas_call(kernel, grid_spec=pltpu.PrefetchScalarGridSpec(num_scalar_...]
    unnamed x150 -> x117, local copies, waits for them, and re-layouts: 28.8 us -> 11.6 us
    ppermute x5 -> x3, waiting for transfers between devices: 38.1 us -> 55.1 us  [over_a(): lax.ppermute(value, BOTH, device_pairs(lambda z, y, x, c: (z, y ^ c, x ^...]
    ppermute x23 -> x20, starting transfers between devices: 35.8 us -> 21.7 us  [swap(): return lax.ppermute(value, axis, [(i, i ^ by) for i in range(peers)])]
  transfers between devices with their start and end apart: 57 -> 42, of which waited for: 17 -> 18; matrix products, arithmetic and copies ran while one was open for 19% -> 24% of each run, Pallas kernels for 20% -> 27%
where the time goes in v2:
time: 623 us; the launch traced here: 618 us
  Pallas kernels  192 us (31%)
  waiting for transfers between devices  186 us (30%)
  matrix products  96.4 us (15%)
  other arithmetic  52.2 us (8%)
  starting transfers between devices  48 us (8%)
  local copies, waits for them, and re-layouts  27.7 us (4%)
  between operations  15.1 us (2%)
    dot_general x14, matrix products, dot(): lax.dot_general(a, b, (((ca,), (cb,)), ((), ())), preferred_element_type=...  96.4 us
    ppermute x20, waiting for transfers between devices, swap(): return lax.ppermute(value, axis, [(i, i ^ by) for i in range(peers)])  78.8 us
    ppermute x3, waiting for transfers between devices, over_a(): lax.ppermute(value, BOTH, device_pairs(lambda z, y, x, c: (z, y ^ c, x ^...  55.1 us
    ppermute x8, waiting for transfers between devices, over_z(): lax.ppermute(value, BOTH, device_pairs(lambda z, y, x, c: (z ^ k, y, x, c)))  52.1 us
    pallas_call x1, Pallas kernels, self_bwd(): pl.pallas_call(self_bwd_kernel, grid=(blocks,), in_specs=[smem_spec(), sm...  46.3 us
    pallas_call x4, Pallas kernels, group_grad(): pl.pallas_call(kernel, grid_spec=pltpu.PrefetchScalarGridSpec(num_scalar_...  31.7 us
    pallas_call x1, Pallas kernels, self_fwd(): pl.pallas_call(self_fwd_kernel, grid=(blocks,), in_specs=[smem_spec(), sm...  25.6 us
    ppermute x20, starting transfers between devices, swap(): return lax.ppermute(value, axis, [(i, i ^ by) for i in range(peers)])  21.7 us
  transfers between devices with their start and end apart: 42, of which 18 were waited for; matrix products, arithmetic and copies ran while one was open for 24% of the time, Pallas kernels for 27%

profile of v2, /device:TPU:0, one launch (start us, length us, event | category | flops | bytes accessed | tf_op | source)
XLA Modules:
  0.0 617.7 jit_solution(1824312344772396556)
XLA Ops:
  12.6 5.1 collective-permute-start.5
  20.0 3.0 collective-permute-done.5
  23.1 17.8 %collective-permute-done.4 = bf16[112,768]{1,0:T(8,128)(2,1)S(1)} collective-permute-done((bf16[112,768]{1,0:T(8,128)(2,1)S(1)}, bf16[112,768]{1,0:T(8,128)(2,1)S(1)}, u32[]{:S(2)}, u32[]{:S(2)}) %collective-permute-start.4) | collective-permute-done | bytes 172064 | tf_op jit(solution)/shard_map/ppermute | solution.py:59
  41.0 3.4 collective-permute-start.12
  45.4 12.2 %collective-permute-done.12 = bf16[560,256]{1,0:T(8,128)(2,1)S(1)} collective-permute-done((bf16[560,256]{1,0:T(8,128)(2,1)S(1)}, bf16[560,256]{1,0:T(8,128)(2,1)S(1)}, u32[]{:S(2)}, u32[]{:S(2)}) %collective-permute-start.12) | collective-permute-done | bytes 286752 | tf_op jit(solution)/shard_map/ppermute | solution.py:151
  57.6 25.7 %collective-permute-done.11 = bf16[560,256]{1,0:T(8,128)(2,1)S(1)} collective-permute-done((bf16[560,256]{1,0:T(8,128)(2,1)S(1)}, bf16[560,256]{1,0:T(8,128)(2,1)S(1)}, u32[]{:S(2)}, u32[]{:S(2)}) %collective-permute-start.11) | collective-permute-done | bytes 286752 | tf_op jit(solution)/shard_map/ppermute | solution.py:151
  88.5 44.6 %collective-permute-done.13 = bf16[4,560,256]{2,1,0:T(8,128)(2,1)S(1)} collective-permute-done((bf16[4,560,256]{2,1,0:T(8,128)(2,1)S(1)}, bf16[4,560,256]{2,1,0:T(8,128)(2,1)S(1)}, u32[]{:S(2)}, u32[]{:S(2)}) %collective-permute-start.13) | collective-permute-done | bytes 1146912 | tf_op jit(solution)/shard_map/ppermute | solution.py:155
  136.0 3.2 collective-permute-start.17
  141.6 11.9 %collective-permute-done.1 = bf16[512,896]{1,0:T(8,128)(2,1)S(1)} collective-permute-done((bf16[512,896]{1,0:T(8,128)(2,1)S(1)}, bf16[512,896]{1,0:T(8,128)(2,1)S(1)}, u32[]{:S(2)}, u32[]{:S(2)}) %collective-permute-start.1) | collective-permute-done | bytes 917536 | tf_op jit(solution)/shard_map/ppermute | solution.py:59
  154.8 22.5 %collective-permute-done.6.far_ref = bf16[4,112,768]{2,1,0:T(8,128)(2,1)} collective-permute-done((bf16[4,112,768]{2,1,0:T(8,128)(2,1)S(1)}, bf16[4,112,768]{2,1,0:T(8,128)(2,1)}, u32[]{:S(2)}, u32[]{:S(2)}) %collective-permute-start.6) | collective-permute-done | bytes 688160 | tf_op jit(solution)/shard_map/ppermute | solution.py:59
  184.8 8.6 %convolution_convert_fusion.2.qkv_ref = bf16[2048,768]{1,0:T(8,128)(2,1)} fusion(bf16[896,768]{1,0:T(8,128)(2,1)S(1)} %copy-done.32, bf16[512,896]{1,0:T(8,128)(2,1)S(1)} %get-tuple-element.126, bf16[512,896]{1,0:T(8,128)(2,1)S(1)} %get-tuple-element.125, bf16[512,896]{1,0:T(8,128)(2,1)S(1)} %get-tuple-element.124, bf16[512,896]{1,0:T(8,128)(2,1)S(1)} %get-tuple-element.123), kind=kOutput, calls=%fused_computation.32 | convolution fusion | flops 2834825216 | bytes 8192000 | tf_op jit(solution)/shard_map/dot_general | solution.py:24
  193.4 25.6 %shard_map.263 = (bf16[2048,256]{1,0:T(8,128)(2,1)}, f32[8,8,256]{2,1,0:T(8,128)}) custom-call(s32[1]{0:T(128)} %bitcast.1.pos_ref.index_ref, f32[4,6]{1,0:T(4,128)} %copy.45.bias_ref, bf16[2048,768]{1,0:T(8,128)(2,1)} %convolution_convert_fusion.2.qkv_ref), custom_call_target="tpu_custom_call" | custom-call | flops 4294967296 | bytes 4194304 | tf_op jit(solution)/shard_map/pallas_call | solution.py:578
  222.9 3.3 pad_maximum_fusion.refs_1_
  229.1 5.8 collective-permute-done.8
  236.0 3.4 shard_map.264.refs_1_
  239.4 8.2 %shard_map.265 = (bf16[896,2048]{1,0:T(8,128)(2,1)}, bf16[896,1024]{1,0:T(8,128)(2,1)}, bf16[896,1024]{1,0:T(8,128)(2,1)}, bf16[896,1024]{1,0:T(8,128)(2,1)}) custom-call(s32[4]{0:T(128)} %pad_add_fusion.place_ref.refs_0_, bf16[8,560,256]{2,1,0:T(8,128)(2,1)} %constant_dynamic-update-slice_fusion.6.refs_0_, ...), custom_call_target="tpu_custom_call" | custom-call | tf_op jit(solution)/shard_map/pallas_call | solution.py:232
  256.7 12.0 %convolution_convert_fusion.k_ref.v_ref = bf16[2304,2048]{1,0:T(8,128)(2,1)} fusion(bf16[2304,896]{1,0:T(8,128)(2,1)S(1)} %copy-done.3, bf16[896,2048]{1,0:T(8,128)(2,1)S(1)} %copy-done.47), kind=kOutput, calls=%fused_computation | convolution fusion | flops 8460435456 | bytes 17235968 | tf_op jit(solution)/shard_map/dot_general | solution.py:24
  268.7 13.5 %shard_map.266.refs_1_ = bf16[512,1024]{1,0:T(8,128)(2,1)} custom-call(bf16[512,1024]{1,0:T(8,128)(2,1)} %convolution_convert_fusion.5.q_ref, bf16[2304,2048]{1,0:T(8,128)(2,1)} %convolution_convert_fusion.k_ref.v_ref, bf16[2304,2048]{1,0:T(8,128)(2,1)} %convolution_convert_fusion.k_ref.v_ref), custom_call_target="tpu_custom_call" | custom-call | flops 2415919104 | bytes 9437184 | tf_op jit(solution)/shard_map/pallas_call | solution.py:770
  286.0 11.7 %shard_map.267 = (bf16[896,3584]{1,0:T(8,128)(2,1)}, bf16[3584,896]{1,0:T(8,128)(2,1)}) custom-call(bf16[32,224,896]{2,1,0:T(8,128)(2,1)} %bitcast.160), custom_call_target="tpu_custom_call" | custom-call | tf_op jit(solution)/shard_map/pallas_call | solution.py:277
  297.8 9.9 %multiply_convert_fusion = (bf16[512,3584]{1,0:T(8,128)(2,1)}, f32[512,3584]{1,0:T(8,128)S(1)}) fusion(bf16[512,896]{1,0:T(8,128)(2,1)S(1)} %copy-done.29, bf16[896,3584]{1,0:T(8,128)(2,1)} %get-tuple-element.45), kind=kOutput, calls=%fused_computation.20 | convolution fusion | flops 3304849408 | bytes 18350080 | tf_op jit(solution)/shard_map/dot_general | solution.py:24
  307.7 10.2 %fusion.9.right = bf16[512,3584]{1,0:T(8,128)(2,1)} fusion(f32[512,3584]{1,0:T(8,128)S(1)} %get-tuple-element.134, bf16[3584,896]{1,0:T(8,128)(2,1)S(1)} %copy-done.46, bf16[1,512,896]{2,1,0:T(8,128)(2,1)S(1)} %copy-done.10), kind=kOutput, calls=%fused_computation.14 | convolution fusion | flops 3325034496 | bytes 18350080 | tf_op jit(solution)/shard_map/dot_general | solution.py:24
  317.8 8.1 %shard_map.276.before = bf16[8,4,224,896]{3,2,1,0:T(8,128)(2,1)} custom-call(bf16[512,3584]{1,0:T(8,128)(2,1)} %get-tuple-element.133.left, bf16[512,896]{1,0:T(8,128)(2,1)} %bitcast.161), custom_call_target="tpu_custom_call" | custom-call | flops 3288334336 | bytes 11010048 | tf_op jit(solution)/shard_map/pallas_call | solution.py:360
  326.0 8.0 %shard_map.277 = bf16[8,4,224,896]{3,2,1,0:T(8,128)(2,1)} custom-call(bf16[512,896]{1,0:T(8,128)(2,1)} %multiply_convert_fusion.1.left, bf16[512,3584]{1,0:T(8,128)(2,1)} %fusion.9.right, bf16[8,4,224,896]{3,2,1,0:T(8,128)(2,1)} %shard_map.276.before), custom_call_target="tpu_custom_call", output_to_operand_aliasing={{}: (2, {})} | custom-call | flops 3288334336 | bytes 11010048 | tf_op jit(solution)/shard_map/pallas_call | solution.py:372
  334.0 9.6 %multiply_reduce_fusion = (f32[896]{0:T(1024)S(1)}, f32[512]{0:T(512)S(1)}, f32[512,896]{1,0:T(8,128)S(1)}) fusion(f32[512,896]{1,0:T(8,128)S(1)} %get-tuple-element.130, f32[512]{0:T(512)S(1)} %fusion.43, f32[896]{0:T(1024)S(1)} %get-tuple-element.82, bf16[512,3584]{1,0:T(8,128)(2,1)} %fusion.9.right, bf16[896,3584]{1,0:T(8,128)(2,1)} %get-tuple-element.45), kind=kOutput, calls=%fused_computation.65 | convolution fusion | flops 3291085312 | bytes 13773824 | tf_op jit(solution)/shard_map/dot_general | solution.py:24
  345.1 5.9 shard_map.270
  351.1 3.8 convolution_convert_fusion.4.g_ref
  354.8 21.1 %shard_map.268 = (bf16[512,1024]{1,0:T(8,128)(2,1)}, bf16[2304,2048]{1,0:T(8,128)(2,1)}) custom-call(bf16[512,1024]{1,0:T(8,128)(2,1)} %convolution_convert_fusion.5.q_ref, bf16[512,1024]{1,0:T(8,128)(2,1)} %convolution_convert_fusion.4.g_ref, bf16[2304,2048]{1,0:T(8,128)(2,1)} %convolution_convert_fusion.k_ref.v_ref, ...), custom_call_target="tpu_custom_call" | custom-call | flops 6039797760 | bytes 18874368 | tf_op jit(solution)/shard_map/pallas_call | solution.py:824
  375.9 4.9 shard_map.271
  380.8 3.4 multiply_reduce_fusion.1
  386.6 14.5 %shard_map.272 = (bf16[2,2,4,560,256]{4,3,2,1,0:T(8,128)(2,1)}, bf16[2,2,4,560,256]{4,3,2,1,0:T(8,128)(2,1)}) custom-call(s32[4]{0:T(128)} %pad_add_fusion.place_ref.refs_0_, bf16[2304,896]{1,0:T(8,128)(2,1)} %pad_maximum_fusion.refs_1_, bf16[2304,2048]{1,0:T(8,128)(2,1)} %get-tuple-element.48.refs_2_.refs_3_, ...), custom_call_target="tpu_custom_call", output_to_operand_aliasing={{0}: (4, {}), {1}: (5, {})} | custom-call | flops 8455716864 | bytes 17235968 | tf_op jit(solution)/shard_map/pallas_call | solution.py:419
  401.1 6.4 %shard_map.273 = (bf16[2,2,4,560,256]{4,3,2,1,0:T(8,128)(2,1)}, bf16[2,2,4,560,256]{4,3,2,1,0:T(8,128)(2,1)}) custom-call(s32[4]{0:T(128)} %pad_add_fusion.place_ref.refs_0_, bf16[512,1024]{1,0:T(8,128)(2,1)} %shard_map.264.refs_1_, bf16[512,896]{1,0:T(8,128)(2,1)} %get-tuple-element.85.refs_2_, ...), custom_call_target="tpu_custom_call", output_to_operand_aliasing={{0}: (3, {}), {1}: (4, {})} | custom-call | flops 939524096 | bytes 3801088 | tf_op jit(solution)/shard_map/pallas_call | solution.py:419
  410.5 8.8 %pad_maximum_fusion.1.left = bf16[2048,896]{1,0:T(8,128)(2,1)} fusion(bf16[512,896]{1,0:T(8,128)(2,1)S(1)} %copy-done.27, bf16[512,896]{1,0:T(8,128)(2,1)S(1)} %copy-done.25, bf16[512,896]{1,0:T(8,128)(2,1)S(1)} %copy-done.23, bf16[512,896]{1,0:T(8,128)(2,1)S(1)} %copy-done.21), kind=kLoop, calls=%fused_computation.24 | loop fusion | flops 14680064 | bytes 7340032 | tf_op jit(solution)/shard_map/concatenate | solution.py:919
  421.5 3.4 shard_map.269
  428.7 13.9 %convolution_convert_fusion.1 = bf16[2304,896]{1,0:T(8,128)(2,1)S(1)} fusion(bf16[2304,2048]{1,0:T(8,128)(2,1)} %get-tuple-element.48.refs_2_.refs_3_, bf16[896,2048]{1,0:T(8,128)(2,1)} %get-tuple-element.43), kind=kOutput, calls=%fused_computation.21 | convolution fusion | flops 8457781248 | bytes 17235968 | tf_op jit(solution)/shard_map/dot_general | solution.py:24
  444.2 8.3 %collective-permute-done.19 = bf16[512,256]{1,0:T(8,128)(2,1)S(1)} collective-permute-done((bf16[512,256]{1,0:T(8,128)(2,1)S(1)}, bf16[512,256]{1,0:T(8,128)(2,1)S(1)}, u32[]{:S(2)}, u32[]{:S(2)}) %collective-permute-start.19) | collective-permute-done | bytes 262176 | tf_op jit(solution)/shard_map/ppermute | solution.py:59
  453.5 3.8 fusion.13
  457.3 7.2 %collective-permute-start.35 = (bf16[2,4,560,256]{3,2,1,0:T(8,128)(2,1)}, bf16[2,4,560,256]{3,2,1,0:T(8,128)(2,1)}, u32[]{:S(2)}, u32[]{:S(2)}) collective-permute-start(bf16[2,4,560,256]{3,2,1,0:T(8,128)(2,1)} %fusion.13), channel_id=1, source_target_pairs={{0,4},{1,3},{2,6},{3,1},{4,0},{5,7},{6,2},{7,5},{8,12},{9,11},{10,... | collective-permute-start | bytes 6881288 | tf_op jit(solution)/shard_map/ppermute | solution.py:161
  464.5 46.3 %shard_map.274 = (bf16[2048,768]{1,0:T(8,128)(2,1)}, f32[4,6,8,256]{3,2,1,0:T(8,128)}) custom-call(s32[1]{0:T(128)} %bitcast.1.pos_ref.index_ref, f32[4,6]{1,0:T(4,128)} %copy.45.bias_ref, bf16[2048,768]{1,0:T(8,128)(2,1)} %convolution_convert_fusion.2.qkv_ref, bf16[2048,256]{1,0:T(8,128)(2,1)} %get-tuple-element.39.o_ref, ...), custom_call_target="tpu_custom_call" | custom-call | flops 10737418240 | bytes 8388608 | tf_op jit(solution)/shard_map/pallas_call | solution.py:680
  512.0 7.4 %fusion.1 = (f32[896]{0:T(1024)S(1)}, bf16[2048,896]{1,0:T(8,128)(2,1)S(1)}) fusion(f32[2048]{0:T(1024)S(1)} %add_rsqrt_fusion, bf16[512,896]{1,0:T(8,128)(2,1)} %collective-permute-done.2, bf16[512,896]{1,0:T(8,128)(2,1)} %copy-done.6, bf16[512,896]{1,0:T(8,128)(2,1)} %copy-done.8, bf16[512,896]{1,0:T(8,128)(2,1)S(1)} %bitcast.159, ...), kind=kOutput, calls=%fused_computation.6 | convolution fusion | flops 2840591360 | bytes 11873792 | tf_op jit(solution)/shard_map/dot_general | solution.py:24
  519.5 8.7 %shard_map.275 = (bf16[4,112,768]{2,1,0:T(8,128)(2,1)}, bf16[4,112,768]{2,1,0:T(8,128)(2,1)}) custom-call(s32[4]{0:T(128)} %pad_add_fusion.place_ref.refs_0_, bf16[2048,896]{1,0:T(8,128)(2,1)} %pad_maximum_fusion.1.left, bf16[2048,768]{1,0:T(8,128)(2,1)} %get-tuple-element.59.right), custom_call_target="tpu_custom_call" | custom-call | flops 2818572288 | bytes 6815744 | tf_op jit(solution)/shard_map/pallas_call | solution.py:484
  529.5 3.5 collective-permute-done.27
  533.1 7.8 %fusion.34 = bf16[1,512,896]{2,1,0:T(8,128)(2,1)} fusion(f32[512,896]{1,0:T(8,128)S(1)} %get-tuple-element.130, bf16[512,3584]{1,0:T(8,128)(2,1)S(1)} %copy-done.19, bf16[3584,896]{1,0:T(8,128)(2,1)} %get-tuple-element.46), kind=kOutput, calls=%fused_computation.81 | convolution fusion | flops 3289251840 | bytes 12845056 | tf_op jit(solution)/shard_map/dot_general | solution.py:24
  544.2 3.0 collective-permute-start.22
  551.2 3.4 fusion.14
  554.6 3.2 collective-permute-start.33
  574.2 10.6 %collective-permute-done.36 = bf16[4,560,256]{2,1,0:T(8,128)(2,1)} collective-permute-done((bf16[4,560,256]{2,1,0:T(8,128)(2,1)}, bf16[4,560,256]{2,1,0:T(8,128)(2,1)}, u32[]{:S(2)}, u32[]{:S(2)}) %collective-permute-start.36) | collective-permute-done | bytes 1146912 | tf_op jit(solution)/shard_map/ppermute | solution.py:155
  596.4 3.6 collective-permute-done.39
  600.0 5.9 collective-permute-done.38
  (265 shorter events, 106.8 us)
Async XLA Ops:
  7.2 134.0 %copy-start = (f32[16,6]{0,1:T(8,128)S(1)}, f32[16,6]{0,1:T(8,128)}, u32[]{:S(2)}) copy-start(f32[16,6]{0,1:T(8,128)} %param.18) | copy-start | bytes 1156
  7.2 278.8 %all-gather.3.cloned.1.call-start = ((), (), s32[]{:S(2)}) async-start(), calls=%async_computation.2 | async-start | bytes 13246464 | tf_op jit(solution)/shard_map/all_gather | solution.py:892
  10.0 597.4 %reduce-scatter.2.cloned.1.call-start = ((), (), s32[]{:S(2)}) async-start(), calls=%async_computation.1 | async-start | bytes 13246464 | tf_op jit(solution)/shard_map/reduce_scatter | solution.py:951
  11.7 73.1 %copy-start.2 = (bf16[1,512,896]{2,1,0:T(8,128)(2,1)S(1)}, bf16[1,512,896]{2,1,0:T(8,128)(2,1)}, u32[]{:S(2)}) copy-start(bf16[1,512,896]{2,1,0:T(8,128)(2,1)} %param.15) | copy-start | bytes 2752516
  12.6 10.4 %collective-permute-start.5 = (bf16[112,768]{1,0:T(8,128)(2,1)S(1)}, bf16[112,768]{1,0:T(8,128)(2,1)S(1)}, u32[]{:S(2)}, u32[]{:S(2)}) collective-permute-start(bf16[112,768]{1,0:T(8,128)(2,1)S(1)} %constant_dynamic-update-slice_fusion), channel_id=1, source_target_pairs={{0,24},{4,28},{8,16},{12,20},{16,8},{20,12},{24,0},{28,4},{1,25},{... | collective-permute-start | bytes 516104 | tf_op jit(solution)/shard_map/ppermute | solution.py:59
  17.7 23.1 %collective-permute-start.4 = (bf16[112,768]{1,0:T(8,128)(2,1)S(1)}, bf16[112,768]{1,0:T(8,128)(2,1)S(1)}, u32[]{:S(2)}, u32[]{:S(2)}) collective-permute-start(bf16[112,768]{1,0:T(8,128)(2,1)S(1)} %constant_dynamic-update-slice_fusion), channel_id=1, source_target_pairs={{0,16},{4,20},{8,24},{12,28},{16,0},{20,4},{24,8},{28,12},{1,17},{... | collective-permute-start | bytes 516104 | tf_op jit(solution)/shard_map/ppermute | solution.py:59
  17.7 23.1 %collective-permute-start.3 = (bf16[112,768]{1,0:T(8,128)(2,1)S(1)}, bf16[112,768]{1,0:T(8,128)(2,1)S(1)}, u32[]{:S(2)}, u32[]{:S(2)}) collective-permute-start(bf16[112,768]{1,0:T(8,128)(2,1)S(1)} %constant_dynamic-update-slice_fusion), channel_id=1, source_target_pairs={{0,8},{4,12},{8,0},{12,4},{16,24},{20,28},{24,16},{28,20},{1,9},{5... | collective-permute-start | bytes 516104 | tf_op jit(solution)/shard_map/ppermute | solution.py:59
  41.0 98.2 %copy-start.30 = (bf16[4,112,768]{2,1,0:T(8,128)(2,1)}, bf16[4,112,768]{2,1,0:T(8,128)(2,1)S(1)}, u32[]{:S(2)}) copy-start(bf16[4,112,768]{2,1,0:T(8,128)(2,1)S(1)} %pad_maximum_fusion.7.near_ref) | copy-start | bytes 2064388
  41.0 16.7 %collective-permute-start.12 = (bf16[560,256]{1,0:T(8,128)(2,1)S(1)}, bf16[560,256]{1,0:T(8,128)(2,1)S(1)}, u32[]{:S(2)}, u32[]{:S(2)}) collective-permute-start(bf16[560,256]{1,0:T(8,128)(2,1)S(1)} %maximum_dynamic-update-slice_fusion), channel_id=1, source_target_pairs={{0,24},{1,25},{2,26},{3,27},{4,28},{5,29},{6,30},{7,31},{8,16},{9,... | collective-permute-start | bytes 860168 | tf_op jit(solution)/shard_map/ppermute | solution.py:151
  44.4 38.9 %collective-permute-start.11 = (bf16[560,256]{1,0:T(8,128)(2,1)S(1)}, bf16[560,256]{1,0:T(8,128)(2,1)S(1)}, u32[]{:S(2)}, u32[]{:S(2)}) collective-permute-start(bf16[560,256]{1,0:T(8,128)(2,1)S(1)} %maximum_dynamic-update-slice_fusion), channel_id=1, source_target_pairs={{0,16},{1,17},{2,18},{3,19},{4,20},{5,21},{6,22},{7,23},{8,24},{9,... | collective-permute-start | bytes 860168 | tf_op jit(solution)/shard_map/ppermute | solution.py:151
  44.4 38.9 %collective-permute-start.10 = (bf16[560,256]{1,0:T(8,128)(2,1)S(1)}, bf16[560,256]{1,0:T(8,128)(2,1)S(1)}, u32[]{:S(2)}, u32[]{:S(2)}) collective-permute-start(bf16[560,256]{1,0:T(8,128)(2,1)S(1)} %maximum_dynamic-update-slice_fusion), channel_id=1, source_target_pairs={{0,8},{1,9},{2,10},{3,11},{4,12},{5,13},{6,14},{7,15},{8,0},{9,1},... | collective-permute-start | bytes 860168 | tf_op jit(solution)/shard_map/ppermute | solution.py:151
  83.5 49.6 %collective-permute-start.13 = (bf16[4,560,256]{2,1,0:T(8,128)(2,1)S(1)}, bf16[4,560,256]{2,1,0:T(8,128)(2,1)S(1)}, u32[]{:S(2)}, u32[]{:S(2)}) collective-permute-start(bf16[4,560,256]{2,1,0:T(8,128)(2,1)S(1)} %pad_maximum_fusion.4), channel_id=1, source_target_pairs={{0,2},{1,5},{2,0},{3,7},{4,6},{5,1},{6,4},{7,3},{8,10},{9,13},{10,... | collective-permute-start | bytes 3440648 | tf_op jit(solution)/shard_map/ppermute | solution.py:155
  84.8 68.6 %collective-permute-start.1 = (bf16[512,896]{1,0:T(8,128)(2,1)S(1)}, bf16[512,896]{1,0:T(8,128)(2,1)S(1)}, u32[]{:S(2)}, u32[]{:S(2)}) collective-permute-start(bf16[512,896]{1,0:T(8,128)(2,1)S(1)} %bitcast.156), channel_id=1, source_target_pairs={{0,2},{1,3},{2,0},{3,1},{4,6},{5,7},{6,4},{7,5},{8,10},{9,11},{10,... | collective-permute-start | bytes 2752520 | tf_op jit(solution)/shard_map/ppermute | solution.py:59
  87.8 67.0 %copy-start.45 = (f32[3,896]{1,0:T(4,128)S(1)}, f32[3,896]{1,0:T(4,128)}, u32[]{:S(2)}) copy-start(f32[3,896]{1,0:T(4,128)} %param.17) | copy-start | bytes 32260
  134.2 47.8 %collective-permute-start.14 = (bf16[8,560,256]{2,1,0:T(8,128)(2,1)}, bf16[8,560,256]{2,1,0:T(8,128)(2,1)}, u32[]{:S(2)}, u32[]{:S(2)}) collective-permute-start(bf16[8,560,256]{2,1,0:T(8,128)(2,1)} %constant_dynamic-update-slice_fusion.6.refs_0_), channel_id=1, source_target_pairs={{0,4},{1,3},{2,6},{3,1},{4,0},{5,7},{6,2},{7,5},{8,12},{9,11},{10,... | collective-permute-start | bytes 6881288 | tf_op jit(solution)/shard_map/ppermute | solution.py:161
  134.2 46.0 %collective-permute-start = (bf16[512,896]{1,0:T(8,128)(2,1)S(1)}, bf16[512,896]{1,0:T(8,128)(2,1)S(1)}, u32[]{:S(2)}, u32[]{:S(2)}) collective-permute-start(bf16[512,896]{1,0:T(8,128)(2,1)S(1)} %bitcast.157), channel_id=1, source_target_pairs={{0,1},{1,0},{2,3},{3,2},{4,5},{5,4},{6,7},{7,6},{8,9},{9,8},{10,11... | collective-permute-start | bytes 2752520 | tf_op jit(solution)/shard_map/ppermute | solution.py:59
  136.0 86.9 %collective-permute-start.17 = (bf16[256,896]{1,0:T(8,128)(2,1)}, bf16[256,896]{1,0:T(8,128)(2,1)}, u32[]{:S(2)}, u32[]{:S(2)}) collective-permute-start(bf16[256,896]{1,0:T(8,128)(2,1)} %bitcast.20), channel_id=1, source_target_pairs={{0,1},{1,2},{2,3},{4,5},{5,6},{6,7},{8,9},{9,10},{10,11},{12,13},{... | collective-permute-start | bytes 1376264 | tf_op jit(solution)/shard_map/ppermute | solution.py:914
  139.2 38.2 %collective-permute-start.6 = (bf16[4,112,768]{2,1,0:T(8,128)(2,1)S(1)}, bf16[4,112,768]{2,1,0:T(8,128)(2,1)}, u32[]{:S(2)}, u32[]{:S(2)}) collective-permute-start(bf16[4,112,768]{2,1,0:T(8,128)(2,1)S(1)} %pad_maximum_fusion.7.near_ref), channel_id=1, source_target_pairs={{0,4},{4,0},{8,12},{12,8},{16,20},{20,16},{24,28},{28,24},{1,5},{5... | collective-permute-start | bytes 2064392 | tf_op jit(solution)/shard_map/ppermute | solution.py:59
  141.6 41.0 %copy-start.43 = (f32[512]{0:T(512)}, f32[512]{0:T(512)S(1)}, u32[]{:S(2)}) copy-start(f32[512]{0:T(512)S(1)} %fusion.41) | copy-start | bytes 6148
  153.4 27.1 %collective-permute-start.2 = (bf16[512,896]{1,0:T(8,128)(2,1)S(1)}, bf16[512,896]{1,0:T(8,128)(2,1)}, u32[]{:S(2)}, u32[]{:S(2)}) collective-permute-start(bf16[512,896]{1,0:T(8,128)(2,1)S(1)} %collective-permute-done.1), channel_id=1, source_target_pairs={{0,1},{1,0},{2,3},{3,2},{4,5},{5,4},{6,7},{7,6},{8,9},{9,8},{10,11... | collective-permute-start | bytes 2752520 | tf_op jit(solution)/shard_map/ppermute | solution.py:59
  180.4 59.0 %collective-permute-start.15 = (bf16[8,560,256]{2,1,0:T(8,128)(2,1)}, bf16[8,560,256]{2,1,0:T(8,128)(2,1)}, u32[]{:S(2)}, u32[]{:S(2)}) collective-permute-start(bf16[8,560,256]{2,1,0:T(8,128)(2,1)} %constant_dynamic-update-slice_fusion.6.refs_0_), channel_id=1, source_target_pairs={{0,1},{1,0},{2,3},{3,2},{4,5},{5,4},{6,7},{7,6},{8,9},{9,8},{10,11... | collective-permute-start | bytes 6881288 | tf_op jit(solution)/shard_map/ppermute | solution.py:167
  182.0 57.5 %collective-permute-start.16 = (bf16[8,560,256]{2,1,0:T(8,128)(2,1)}, bf16[8,560,256]{2,1,0:T(8,128)(2,1)}, u32[]{:S(2)}, u32[]{:S(2)}) collective-permute-start(bf16[8,560,256]{2,1,0:T(8,128)(2,1)} %collective-permute-done.14.refs_1_), channel_id=1, source_target_pairs={{0,1},{1,0},{2,3},{3,2},{4,5},{5,4},{6,7},{7,6},{8,9},{9,8},{10,11... | collective-permute-start | bytes 6881288 | tf_op jit(solution)/shard_map/ppermute | solution.py:167
  220.2 8.9 %collective-permute-start.9 = (bf16[512,256]{1,0:T(8,128)(2,1)S(1)}, bf16[512,256]{1,0:T(8,128)(2,1)S(1)}, u32[]{:S(2)}, u32[]{:S(2)}) collective-permute-start(bf16[512,256]{1,0:T(8,128)(2,1)S(1)} %get-tuple-element.99), channel_id=1, source_target_pairs={{0,3},{1,2},{2,1},{3,0},{4,7},{5,6},{6,5},{7,4},{8,11},{9,10},{10,... | collective-permute-start | bytes 786440 | tf_op jit(solution)/shard_map/ppermute | solution.py:59
  222.4 12.5 %collective-permute-start.8 = (bf16[512,256]{1,0:T(8,128)(2,1)S(1)}, bf16[512,256]{1,0:T(8,128)(2,1)S(1)}, u32[]{:S(2)}, u32[]{:S(2)}) collective-permute-start(bf16[512,256]{1,0:T(8,128)(2,1)S(1)} %get-tuple-element.100), channel_id=1, source_target_pairs={{0,2},{1,3},{2,0},{3,1},{4,6},{5,7},{6,4},{7,5},{8,10},{9,11},{10,... | collective-permute-start | bytes 786440 | tf_op jit(solution)/shard_map/ppermute | solution.py:59
  222.9 12.0 %collective-permute-start.7 = (bf16[512,256]{1,0:T(8,128)(2,1)S(1)}, bf16[512,256]{1,0:T(8,128)(2,1)S(1)}, u32[]{:S(2)}, u32[]{:S(2)}) collective-permute-start(bf16[512,256]{1,0:T(8,128)(2,1)S(1)} %get-tuple-element.101), channel_id=1, source_target_pairs={{0,1},{1,0},{2,3},{3,2},{4,5},{5,4},{6,7},{7,6},{8,9},{9,8},{10,11... | collective-permute-start | bytes 786440 | tf_op jit(solution)/shard_map/ppermute | solution.py:59
  250.5 31.7 %copy-start.13 = (f32[512,896]{1,0:T(8,128)}, f32[512,896]{1,0:T(8,128)S(1)}, u32[]{:S(2)}) copy-start(f32[512,896]{1,0:T(8,128)S(1)} %get-tuple-element.128) | copy-start | bytes 5505028
  407.5 46.0 %collective-permute-start.21 = (bf16[2,2,4,560,256]{4,3,2,1,0:T(8,128)(2,1)}, bf16[2,2,4,560,256]{4,3,2,1,0:T(8,128)(2,1)}, u32[]{:S(2)}, u32[]{:S(2)}) collective-permute-start(bf16[2,2,4,560,256]{4,3,2,1,0:T(8,128)(2,1)} %get-tuple-element.56), channel_id=1, source_target_pairs={{0,1},{1,0},{2,3},{3,2},{4,5},{5,4},{6,7},{7,6},{8,9},{9,8},{10,11... | collective-permute-start | bytes 13762568 | tf_op jit(solution)/shard_map/ppermute | solution.py:167
  426.1 18.0 %collective-permute-start.20 = (bf16[512,256]{1,0:T(8,128)(2,1)S(1)}, bf16[512,256]{1,0:T(8,128)(2,1)S(1)}, u32[]{:S(2)}, u32[]{:S(2)}) collective-permute-start(bf16[512,256]{1,0:T(8,128)(2,1)S(1)} %get-tuple-element.95), channel_id=1, source_target_pairs={{0,3},{1,2},{2,1},{3,0},{4,7},{5,6},{6,5},{7,4},{8,11},{9,10},{10,... | collective-permute-start | bytes 786440 | tf_op jit(solution)/shard_map/ppermute | solution.py:59
  428.5 24.0 %collective-permute-start.19 = (bf16[512,256]{1,0:T(8,128)(2,1)S(1)}, bf16[512,256]{1,0:T(8,128)(2,1)S(1)}, u32[]{:S(2)}, u32[]{:S(2)}) collective-permute-start(bf16[512,256]{1,0:T(8,128)(2,1)S(1)} %get-tuple-element.96), channel_id=1, source_target_pairs={{0,2},{1,3},{2,0},{3,1},{4,6},{5,7},{6,4},{7,5},{8,10},{9,11},{10,... | collective-permute-start | bytes 786440 | tf_op jit(solution)/shard_map/ppermute | solution.py:59
  428.5 24.0 %collective-permute-start.18 = (bf16[512,256]{1,0:T(8,128)(2,1)S(1)}, bf16[512,256]{1,0:T(8,128)(2,1)S(1)}, u32[]{:S(2)}, u32[]{:S(2)}) collective-permute-start(bf16[512,256]{1,0:T(8,128)(2,1)S(1)} %get-tuple-element.97), channel_id=1, source_target_pairs={{0,1},{1,0},{2,3},{3,2},{4,5},{5,4},{6,7},{7,6},{8,9},{9,8},{10,11... | collective-permute-start | bytes 786440 | tf_op jit(solution)/shard_map/ppermute | solution.py:59
  442.7 100.2 %collective-permute-start.25 = (bf16[256,896]{1,0:T(8,128)(2,1)S(1)}, bf16[256,896]{1,0:T(8,128)(2,1)}, u32[]{:S(2)}, u32[]{:S(2)}) collective-permute-start(bf16[256,896]{1,0:T(8,128)(2,1)S(1)} %slice.283), channel_id=1, source_target_pairs={{1,0},{2,1},{3,2},{5,4},{6,5},{7,6},{9,8},{10,9},{11,10},{13,12},{... | collective-permute-start | bytes 1376264 | tf_op jit(solution)/shard_map/ppermute | solution.py:981
  457.3 92.9 %collective-permute-start.35 = (bf16[2,4,560,256]{3,2,1,0:T(8,128)(2,1)}, bf16[2,4,560,256]{3,2,1,0:T(8,128)(2,1)}, u32[]{:S(2)}, u32[]{:S(2)}) collective-permute-start(bf16[2,4,560,256]{3,2,1,0:T(8,128)(2,1)} %fusion.13), channel_id=1, source_target_pairs={{0,4},{1,3},{2,6},{3,1},{4,0},{5,7},{6,2},{7,5},{8,12},{9,11},{10,... | collective-permute-start | bytes 6881288 | tf_op jit(solution)/shard_map/ppermute | solution.py:161
  519.4 8.9 %collective-permute-start.26 = (f32[24,128]{1,0:T(8,128)S(1)}, f32[24,128]{1,0:T(8,128)S(1)}, u32[]{:S(2)}, u32[]{:S(2)}) collective-permute-start(f32[24,128]{1,0:T(8,128)S(1)} %fusion.40), channel_id=1, source_target_pairs={{0,8},{1,9},{2,10},{3,11},{4,12},{5,13},{6,14},{7,15},{8,0},{9,1},... | collective-permute-start | bytes 36872 | tf_op jit(solution)/shard_map/ppermute | solution.py:151
  528.2 19.0 %collective-permute-start.31 = (bf16[4,112,768]{2,1,0:T(8,128)(2,1)}, bf16[4,112,768]{2,1,0:T(8,128)(2,1)S(1)}, u32[]{:S(2)}, u32[]{:S(2)}) collective-permute-start(bf16[4,112,768]{2,1,0:T(8,128)(2,1)} %get-tuple-element.62), channel_id=1, source_target_pairs={{0,4},{4,0},{8,12},{12,8},{16,20},{20,16},{24,28},{28,24},{1,5},{5... | collective-permute-start | bytes 2064392 | tf_op jit(solution)/shard_map/ppermute | solution.py:59
  528.3 4.7 collective-permute-start.27
  529.5 19.0 %collective-permute-start.23 = (bf16[512,896]{1,0:T(8,128)(2,1)S(1)}, bf16[512,896]{1,0:T(8,128)(2,1)S(1)}, u32[]{:S(2)}, u32[]{:S(2)}) collective-permute-start(bf16[512,896]{1,0:T(8,128)(2,1)S(1)} %get-tuple-element.90), channel_id=1, source_target_pairs={{0,1},{1,0},{2,3},{3,2},{4,5},{5,4},{6,7},{7,6},{8,9},{9,8},{10,11... | collective-permute-start | bytes 2752520 | tf_op jit(solution)/shard_map/ppermute | solution.py:59
  533.0 7.9 %collective-permute-start.28 = (f32[24,128]{1,0:T(8,128)S(1)}, f32[24,128]{1,0:T(8,128)S(1)}, u32[]{:S(2)}, u32[]{:S(2)}) collective-permute-start(f32[24,128]{1,0:T(8,128)S(1)} %fusion.81), channel_id=1, source_target_pairs={{0,2},{1,5},{2,0},{3,7},{4,6},{5,1},{6,4},{7,3},{8,10},{9,13},{10,... | collective-permute-start | bytes 36872 | tf_op jit(solution)/shard_map/ppermute | solution.py:155
  540.9 6.3 %collective-permute-start.29 = (f32[24,128]{1,0:T(8,128)S(1)}, f32[24,128]{1,0:T(8,128)S(1)}, u32[]{:S(2)}, u32[]{:S(2)}) collective-permute-start(f32[24,128]{1,0:T(8,128)S(1)} %add.213), channel_id=1, source_target_pairs={{0,4},{1,3},{2,6},{3,1},{4,0},{5,7},{6,2},{7,5},{8,12},{9,11},{10,... | collective-permute-start | bytes 36872 | tf_op jit(solution)/shard_map/ppermute | solution.py:161
  544.2 25.2 %collective-permute-start.22 = (bf16[512,896]{1,0:T(8,128)(2,1)}, bf16[512,896]{1,0:T(8,128)(2,1)S(1)}, u32[]{:S(2)}, u32[]{:S(2)}) collective-permute-start(bf16[512,896]{1,0:T(8,128)(2,1)} %get-tuple-element.89), channel_id=1, source_target_pairs={{0,1},{1,0},{2,3},{3,2},{4,5},{5,4},{6,7},{7,6},{8,9},{9,8},{10,11... | collective-permute-start | bytes 2752520 | tf_op jit(solution)/shard_map/ppermute | solution.py:59
  547.2 7.4 %collective-permute-start.30 = (f32[24,128]{1,0:T(8,128)S(1)}, f32[24,128]{1,0:T(8,128)S(1)}, u32[]{:S(2)}, u32[]{:S(2)}) collective-permute-start(f32[24,128]{1,0:T(8,128)S(1)} %add.214), channel_id=1, source_target_pairs={{0,1},{1,0},{2,3},{3,2},{4,5},{5,4},{6,7},{7,6},{8,9},{9,8},{10,11... | collective-permute-start | bytes 36872 | tf_op jit(solution)/shard_map/ppermute | solution.py:167
  548.2 10.4 %collective-permute-start.32 = (bf16[112,768]{1,0:T(8,128)(2,1)S(1)}, bf16[112,768]{1,0:T(8,128)(2,1)S(1)}, u32[]{:S(2)}, u32[]{:S(2)}) collective-permute-start(bf16[112,768]{1,0:T(8,128)(2,1)S(1)} %get-tuple-element.102), channel_id=1, source_target_pairs={{0,8},{4,12},{8,0},{12,4},{16,24},{20,28},{24,16},{28,20},{1,9},{5... | collective-permute-start | bytes 516104 | tf_op jit(solution)/shard_map/ppermute | solution.py:59
  548.5 16.3 %collective-permute-start.34 = (bf16[112,768]{1,0:T(8,128)(2,1)}, bf16[112,768]{1,0:T(8,128)(2,1)}, u32[]{:S(2)}, u32[]{:S(2)}) collective-permute-start(bf16[112,768]{1,0:T(8,128)(2,1)} %get-tuple-element.103), channel_id=1, source_target_pairs={{0,24},{4,28},{8,16},{12,20},{16,8},{20,12},{24,0},{28,4},{1,25},{... | collective-permute-start | bytes 516104 | tf_op jit(solution)/shard_map/ppermute | solution.py:59
  550.2 22.2 %collective-permute-start.24 = (bf16[512,896]{1,0:T(8,128)(2,1)}, bf16[512,896]{1,0:T(8,128)(2,1)S(1)}, u32[]{:S(2)}, u32[]{:S(2)}) collective-permute-start(bf16[512,896]{1,0:T(8,128)(2,1)} %add_convert_fusion.1), channel_id=1, source_target_pairs={{0,2},{1,3},{2,0},{3,1},{4,6},{5,7},{6,4},{7,5},{8,10},{9,11},{10,... | collective-permute-start | bytes 2752520 | tf_op jit(solution)/shard_map/ppermute | solution.py:59
  554.6 12.9 %collective-permute-start.33 = (bf16[112,768]{1,0:T(8,128)(2,1)}, bf16[112,768]{1,0:T(8,128)(2,1)}, u32[]{:S(2)}, u32[]{:S(2)}) collective-permute-start(bf16[112,768]{1,0:T(8,128)(2,1)} %get-tuple-element.104), channel_id=1, source_target_pairs={{0,16},{4,20},{8,24},{12,28},{16,0},{20,4},{24,8},{28,12},{1,17},{... | collective-permute-start | bytes 516104 | tf_op jit(solution)/shard_map/ppermute | solution.py:59
  558.6 26.1 %collective-permute-start.36 = (bf16[4,560,256]{2,1,0:T(8,128)(2,1)}, bf16[4,560,256]{2,1,0:T(8,128)(2,1)}, u32[]{:S(2)}, u32[]{:S(2)}) collective-permute-start(bf16[4,560,256]{2,1,0:T(8,128)(2,1)} %fusion.14), channel_id=1, source_target_pairs={{0,2},{1,5},{2,0},{3,7},{4,6},{5,1},{6,4},{7,3},{8,10},{9,13},{10,... | collective-permute-start | bytes 3440648 | tf_op jit(solution)/shard_map/ppermute | solution.py:155
  587.8 8.6 %collective-permute-start.37 = (bf16[560,256]{1,0:T(8,128)(2,1)S(1)}, bf16[560,256]{1,0:T(8,128)(2,1)S(1)}, u32[]{:S(2)}, u32[]{:S(2)}) collective-permute-start(bf16[560,256]{1,0:T(8,128)(2,1)S(1)} %get-tuple-element.91), channel_id=1, source_target_pairs={{0,8},{1,9},{2,10},{3,11},{4,12},{5,13},{6,14},{7,15},{8,0},{9,1},... | collective-permute-start | bytes 860168 | tf_op jit(solution)/shard_map/ppermute | solution.py:151
  589.6 10.4 %collective-permute-start.39 = (bf16[560,256]{1,0:T(8,128)(2,1)S(1)}, bf16[560,256]{1,0:T(8,128)(2,1)S(1)}, u32[]{:S(2)}, u32[]{:S(2)}) collective-permute-start(bf16[560,256]{1,0:T(8,128)(2,1)S(1)} %get-tuple-element.92), channel_id=1, source_target_pairs={{0,24},{1,25},{2,26},{3,27},{4,28},{5,29},{6,30},{7,31},{8,16},{9,... | collective-permute-start | bytes 860168 | tf_op jit(solution)/shard_map/ppermute | solution.py:151
  592.2 13.7 %collective-permute-start.38 = (bf16[560,256]{1,0:T(8,128)(2,1)S(1)}, bf16[560,256]{1,0:T(8,128)(2,1)S(1)}, u32[]{:S(2)}, u32[]{:S(2)}) collective-permute-start(bf16[560,256]{1,0:T(8,128)(2,1)S(1)} %get-tuple-element.93), channel_id=1, source_target_pairs={{0,16},{1,17},{2,18},{3,19},{4,20},{5,21},{6,22},{7,23},{8,24},{9,... | collective-permute-start | bytes 860168 | tf_op jit(solution)/shard_map/ppermute | solution.py:151
  (48 other events, 483.0 us)
Sparse Core Ops, SparseCore 0:
  11.4 141.0 all-gather.2
  334.1 172.2 reduce-scatter.1

commit v3 on v2

--- a/solution.py
+++ b/solution.py
@@ -63,16 +63,18 @@
     return lax.optimization_barrier((value,) + others)[0]
 
 
+def estimate(flops, bytes_accessed, transcendentals):
+    return pl.CostEstimate(
+        flops=flops // 50, bytes_accessed=bytes_accessed // 50, transcendentals=transcendentals // 50
+    )
+
+
 def vmem_spec():
     return pl.BlockSpec(memory_space=pltpu.VMEM)
 
 
 def smem_spec():
     return pl.BlockSpec(memory_space=pltpu.SMEM)
-
-
-def copy_kernel(index_ref, in_ref, out_ref):
-    out_ref[...] = in_ref[...].reshape(out_ref.shape)
 
 
 def reorder_triple_kernel(place_ref, near_ref, far_ref, out_ref):
@@ -84,44 +86,74 @@
             out_ref[pl.ds(pl.multiple_of(where, rows), rows), :] = ref[k]
 
 
-def reorder_triple(near, far, place):
-    count, rows, cols = near.shape
+def project_kernel(place_ref, near_ref, far_ref, gain_ref, *refs):
+    tokens, (normed_ref, qkv_ref, full_ref) = refs[:-3], refs[-3:]
+    reorder_triple_kernel(place_ref, near_ref, far_ref, full_ref)
+    rows = tokens[0].shape[0]
+    part = rows // 2
+    for k, ref in enumerate(tokens):
+
+        def step(i, carry):
+            here = pl.ds(pl.multiple_of(i * part, part), part)
+            there = pl.ds(pl.multiple_of(k * rows + i * part, part), part)
+            normed = rounded(rms_apply(ref[here, :].astype(F32), gain_ref[...]))
+            normed_ref[there, :] = normed
+            qkv_ref[there, :] = rounded(dot(normed, full_ref[...]))
+            return carry
+
+        lax.fori_loop(0, 2, step, 0)
+
+
+def project(near, far, gain, tokens, place):
+    count, height, cols = near.shape
+    rows, model = tokens[0].shape
+    total = rows * len(tokens)
     return pl.pallas_call(
-        reorder_triple_kernel,
-        in_specs=[smem_spec(), vmem_spec(), vmem_spec()],
+        project_kernel,
+        in_specs=[smem_spec()] + [vmem_spec()] * (3 + len(tokens)),
+        out_specs=[vmem_spec()] * 3,
+        out_shape=[
+            jax.ShapeDtypeStruct((total, model), BF),
+            jax.ShapeDtypeStruct((total, cols), BF),
+            jax.ShapeDtypeStruct((2 * count * height, cols), BF),
+        ],
+        compiler_params=pltpu.CompilerParams(vmem_limit_bytes=VMEM_LIMIT),
+        cost_estimate=estimate(
+            flops=2 * total * model * cols, bytes_accessed=8 * total * model, transcendentals=0
+        ),
+    )(place, near, far, gain, *tokens)
+
+
+def join_kernel(mine_ref, *refs):
+    out_ref = refs[-1]
+    cols = refs[0].shape[1]
+    for k, ref in enumerate(refs[:-1]):
+        out_ref[:, pl.ds(pl.multiple_of((mine_ref[0] ^ k) * cols, cols), cols)] = ref[...]
+
+
+def join_columns(pieces, mine):
+    rows, cols = pieces[0].shape
+    return pl.pallas_call(
+        join_kernel,
+        in_specs=[smem_spec()] + [vmem_spec()] * len(pieces),
         out_specs=vmem_spec(),
-        out_shape=jax.ShapeDtypeStruct((2 * count * rows, cols), near.dtype),
-    )(place, near, far)
-
-
-def columns_from_blocks(stacked, mine):
-    count, rows, cols = stacked.shape
-    spec = pltpu.PrefetchScalarGridSpec(
-        num_scalar_prefetch=1,
-        grid=(count,),
-        in_specs=[pl.BlockSpec((1, rows, cols), lambda i, m: (m[0] ^ i, 0, 0))],
-        out_specs=pl.BlockSpec((rows, cols), lambda i, m: (0, i)),
-    )
+        out_shape=jax.ShapeDtypeStruct((rows, cols * len(pieces)), pieces[0].dtype),
+    )(mine.reshape(1), *pieces)
+
+
+def split_kernel(mine_ref, in_ref, *outs):
+    cols = outs[0].shape[1]
+    for k, ref in enumerate(outs):
+        ref[...] = in_ref[:, pl.ds(pl.multiple_of((mine_ref[0] ^ k) * cols, cols), cols)]
+
+
+def split_columns(flat, count, mine):
+    rows, width = flat.shape
     return pl.pallas_call(
-        copy_kernel,
-        grid_spec=spec,
-        out_shape=jax.ShapeDtypeStruct((rows, count * cols), stacked.dtype),
-    )(mine.reshape(1), stacked)
-
-
-def blocks_from_columns(flat, count, mine):
-    rows, width = flat.shape
-    cols = width // count
-    spec = pltpu.PrefetchScalarGridSpec(
-        num_scalar_prefetch=1,
-        grid=(count,),
-        in_specs=[pl.BlockSpec((rows, cols), lambda i, m: (0, m[0] ^ i))],
-        out_specs=pl.BlockSpec((1, rows, cols), lambda i, m: (i, 0, 0)),
-    )
-    return pl.pallas_call(
-        copy_kernel,
-        grid_spec=spec,
-        out_shape=jax.ShapeDtypeStruct((count, rows, cols), flat.dtype),
+        split_kernel,
+        in_specs=[smem_spec(), vmem_spec()],
+        out_specs=[vmem_spec()] * count,
+        out_shape=[jax.ShapeDtypeStruct((rows, width // count), flat.dtype)] * count,
     )(mine.reshape(1), flat)
 
 
@@ -172,12 +204,9 @@
     return jnp.stack([i // 2, i % 2, j // 2, j % 2]).astype(jnp.int32)
 
 
-def gather_group(shard):
+def gather_near(shard):
     depth = lax.axis_size("dp") // 2
-    near = jnp.stack([shard] + [over_z(shard, k) for k in range(1, depth)])
-    both = jnp.concatenate([near, over_a(near)], axis=0)
-    far = over_b(both)
-    return [both, far, over_core(both), over_core(far)]
+    return [shard] + [over_z(shard, k) for k in range(1, depth)]
 
 
 def piece_origin(place_ref, c, b, t, depth):
@@ -239,25 +268,26 @@
     )(place, *pieces)
 
 
-def assemble_feed_kernel(blocks, inner, outer, stage, sems):
-    count = blocks.shape[0]
-    rows = inner.shape[0] // (count // 4)
-    cols = inner.shape[1] // 4
+def assemble_feed_kernel(depth, place_ref, *refs):
+    pieces, (inner, outer, stage, sems) = refs[:4], refs[4:]
+    rows, cols = stage.shape[2:]
     part = cols // 4
 
-    def step(i, carry):
-        for j in range(4):
-            piece = blocks.at[i * 4 + j]
-            down = pl.ds(pl.multiple_of(i * rows, rows), rows)
+    def step(t, carry):
+        for i in range(4):
+            i_dp, i_seq = piece_origin(place_ref, i // 2, i % 2, t, depth)
+            piece = pieces[i].at[t]
+            down = pl.ds(pl.multiple_of(i_dp * rows, rows), rows)
+            across = pl.ds(pl.multiple_of(i_seq * cols, cols), cols)
             pltpu.make_async_copy(
-                piece.at[pl.ds(rows, rows), :], stage.at[i, j], sems.at[1]
+                piece.at[pl.ds(rows, rows), :], stage.at[i_dp, i_seq], sems.at[1]
             ).start()
             pltpu.make_async_copy(
-                piece.at[pl.ds(0, rows), :], inner.at[down, pl.ds(j * cols, cols)], sems.at[0]
+                piece.at[pl.ds(0, rows), :], inner.at[down, across], sems.at[0]
             ).start()
         return carry
 
-    lax.fori_loop(0, count // 4, step, 0)
+    lax.fori_loop(0, 2 * depth, step, 0)
     pltpu.make_async_copy(stage, stage, sems.at[1]).wait()
 
     def spread(i, carry):
@@ -267,16 +297,16 @@
             outer[pl.ds(where, rows), :] = jnp.concatenate(line, axis=1)
         return carry
 
-    lax.fori_loop(0, count // 4, spread, 0)
+    lax.fori_loop(0, 2 * depth, spread, 0)
     pltpu.make_async_copy(inner, inner, sems.at[0]).wait()
 
 
-def assemble_feed(blocks):
-    count, packed, cols = blocks.shape
-    rows, deep = packed // 2, count // 4
+def assemble_feed(pieces, place):
+    deep, packed, cols = pieces[0].shape
+    rows = packed // 2
     return pl.pallas_call(
-        assemble_feed_kernel,
-        in_specs=[pl.BlockSpec(memory_space=pl.ANY)],
+        functools.partial(assemble_feed_kernel, deep // 2),
+        in_specs=[smem_spec()] + [pl.BlockSpec(memory_space=pl.ANY)] * 4,
         out_specs=[vmem_spec()] * 2,
         out_shape=[
             jax.ShapeDtypeStruct((rows * deep, cols * 4), BF),
@@ -287,7 +317,7 @@
             pltpu.SemaphoreType.DMA((2,)),
         ],
         compiler_params=pltpu.CompilerParams(vmem_limit_bytes=VMEM_LIMIT),
-    )(blocks)
+    )(place, *pieces)
 
 
 def put_block(place_ref, out_ref, core, i_dp, flip, value):
@@ -328,61 +358,53 @@
                     put_block(place_ref, out, j % 2, i_dp, (j // 2) ^ x, block)
 
 
-def outer_grad_kernel(left, right, out_ref):
-    rows, cols = out_ref.shape[2], out_ref.shape[3]
+def feed_outer_kernel(place_ref, left, right, kept, sent):
+    rows, cols = kept.shape[3:]
     part = cols // 4
+    y, x, core = place_ref[1], place_ref[2], place_ref[3]
     value = rounded(dot(left[...], right[...], 0, 0))
-    for i_y in range(2):
-        for j in range(4):
-            base = i_y * 4 * rows
-            lanes = slice(j * part, (j + 1) * part)
-            line = [value[base + t * rows : base + (t + 1) * rows, lanes] for t in range(4)]
-            out_ref[i_y, j] = jnp.concatenate(line, axis=1)
-
-
-def inner_grad_kernel(left, right, before, out_ref):
-    value = rounded(dot(left[...], right[...], 0, 0))
-    out_ref[...] = value.reshape(out_ref.shape)
-
-
-def feed_grad(normed, grad_gate, hidden, grad_feed):
+    for j in range(4):
+        for out, mine in ((kept, core == j % 2), (sent, core != j % 2)):
+
+            @pl.when(mine)
+            def _():
+                for i_y in range(2):
+                    base = i_y * 4 * rows
+                    lanes = slice(j * part, (j + 1) * part)
+                    line = [value[base + t * rows : base + (t + 1) * rows, lanes] for t in range(4)]
+                    dy, flip = i_y ^ y, (j // 2) ^ x
+                    b, a = (dy, flip) if j % 2 == 0 else (flip, dy)
+                    out[b, a, 0] = jnp.concatenate(line, axis=1)
+
+
+def feed_grad(place, normed, grad_gate, hidden, grad_feed):
     dp = lax.axis_size("dp")
+    depth = dp // 2
     tokens, model = normed.shape
     inner = grad_gate.shape[1]
     rows, cols = model // dp, inner // 4
-    shape = jax.ShapeDtypeStruct((dp, 4, 2 * rows, cols), BF)
-    params = pltpu.CompilerParams(vmem_limit_bytes=VMEM_LIMIT)
-    cost = pl.CostEstimate(
-        flops=2 * tokens * model * inner,
-        bytes_accessed=2 * (tokens * (model + inner) + model * inner),
-        transcendentals=0,
-    )
-    outer = pl.pallas_call(
-        outer_grad_kernel,
-        grid=(dp // 2,),
-        in_specs=[
-            pl.BlockSpec((tokens, 2 * inner // dp), lambda i: (0, i)),
-            pl.BlockSpec((tokens, model), lambda i: (0, 0)),
-        ],
-        out_specs=pl.BlockSpec((2, 4, rows, cols), lambda i: (i, 0, 1, 0)),
-        out_shape=shape,
-        compiler_params=params,
-        cost_estimate=cost,
-    )(hidden, grad_feed)
-    return pl.pallas_call(
-        inner_grad_kernel,
-        grid=(4,),
-        in_specs=[
-            pl.BlockSpec((tokens, model), lambda i: (0, 0)),
-            pl.BlockSpec((tokens, cols), lambda i: (0, i)),
-            pl.BlockSpec(memory_space=pl.ANY),
-        ],
-        out_specs=pl.BlockSpec((dp, 1, rows, cols), lambda i: (0, i, 0, 0)),
-        out_shape=shape,
-        input_output_aliases={2: 0},
-        compiler_params=params,
-        cost_estimate=cost,
-    )(normed, grad_gate, outer)
+    shape = jax.ShapeDtypeStruct((2, 2, depth, 2 * rows, cols), BF)
+    out_spec = pl.BlockSpec((2, 2, 1, rows, cols), lambda i, m: (0, 0, m[0] ^ i, 1, 0))
+    pieces = pl.pallas_call(
+        feed_outer_kernel,
+        grid_spec=pltpu.PrefetchScalarGridSpec(
+            num_scalar_prefetch=1,
+            grid=(depth,),
+            in_specs=[
+                pl.BlockSpec((tokens, inner // depth), lambda i, m: (0, i)),
+                pl.BlockSpec((tokens, model), lambda i, m: (0, 0)),
+            ],
+            out_specs=[out_spec] * 2,
+        ),
+        out_shape=[shape, shape],
+        compiler_params=pltpu.CompilerParams(vmem_limit_bytes=VMEM_LIMIT),
+        cost_estimate=estimate(
+            flops=2 * tokens * model * inner,
+            bytes_accessed=2 * (tokens * (model + inner) + model * inner),
+            transcendentals=0,
+        ),
+    )(place, hidden, grad_feed)
+    return group_grad("wide", place, normed, grad_gate, 0, 2, pieces)
 
 
 def group_grad(kind, place, left, right, first, total, before=None, parts=1):
@@ -424,7 +446,7 @@
         out_shape=[whole, whole],
         input_output_aliases=aliases,
         compiler_params=pltpu.CompilerParams(vmem_limit_bytes=VMEM_LIMIT),
-        cost_estimate=pl.CostEstimate(
+        cost_estimate=estimate(
             flops=2 * tokens * height * width,
             bytes_accessed=2 * (left.size + right.size + height * width),
             transcendentals=0,
@@ -439,18 +461,16 @@
     return total
 
 
-def sum_group(pieces):
-    kept, sent = pieces
-    got = over_core(sent)
-    out_b = rounded(wide_sum(kept[1], got[1]))
-    yield out_b
-    got_b = over_b(out_b)
-    out_a = rounded(wide_sum(kept[0, 1], got[0, 1], got_b[1]))
-    yield out_a
-    got_a = over_a(out_a)
-    line = rounded(wide_sum(kept[0, 0], got[0, 0], got_b[0], got_a))
-    yield line
-    yield wide_sum(line[0], *[over_z(line[k], k) for k in range(1, line.shape[0])])
+def sum_second(kept, got, got_b):
+    return rounded(wide_sum(kept[0, 1], got[0, 1], got_b[1]))
+
+
+def sum_third(kept, got, got_b, got_a):
+    return rounded(wide_sum(kept[0, 0], got[0, 0], got_b[0], got_a))
+
+
+def sum_over_z(line):
+    return wide_sum(line[0], *[over_z(line[k], k) for k in range(1, line.shape[0])])
 
 
 def butterfly(value):
@@ -477,22 +497,20 @@
                     out[i_z ^ z] = value[top : top + rows]
 
 
-def triple_sum(place, left, right):
+def triple_pieces(place, left, right):
     dp = lax.axis_size("dp")
     rows, cols = left.shape[1] // dp, right.shape[1]
     shape = jax.ShapeDtypeStruct((dp // 2, rows, cols), BF)
-    kept, sent = pl.pallas_call(
+    return pl.pallas_call(
         triple_grad_kernel,
         in_specs=[smem_spec(), vmem_spec(), vmem_spec()],
         out_specs=[vmem_spec()] * 2,
         out_shape=[shape, shape],
         compiler_params=pltpu.CompilerParams(vmem_limit_bytes=VMEM_LIMIT),
-        cost_estimate=pl.CostEstimate(
+        cost_estimate=estimate(
             flops=2 * left.size * cols, bytes_accessed=2 * (left.size + right.size), transcendentals=0
         ),
     )(place, left, right)
-    line = rounded(wide_sum(kept, swap(sent, "dp", 1)))
-    return wide_sum(line[0], *[swap(line[k], "dp", 2 * k) for k in range(1, dp // 2)])
 
 
 def lane_mask(shape, head):
@@ -591,7 +609,7 @@
             pltpu.VMEM((width, BLOCK), F32),
         ],
         compiler_params=pltpu.CompilerParams(vmem_limit_bytes=VMEM_LIMIT),
-        cost_estimate=pl.CostEstimate(
+        cost_estimate=estimate(
             flops=2 * tokens * tokens * width * 2, bytes_accessed=8 * tokens * width,
             transcendentals=tokens * tokens * heads // 2,
         ),
@@ -700,7 +718,7 @@
             pltpu.VMEM((tokens, width), F32),
         ],
         compiler_params=pltpu.CompilerParams(vmem_limit_bytes=VMEM_LIMIT),
-        cost_estimate=pl.CostEstimate(
+        cost_estimate=estimate(
             flops=5 * tokens * tokens * width * 2, bytes_accessed=16 * tokens * width,
             transcendentals=tokens * tokens * heads // 2,
         ),
@@ -782,7 +800,7 @@
             pltpu.VMEM((slots * SEGMENT, width), F32),
         ],
         compiler_params=pltpu.CompilerParams(vmem_limit_bytes=VMEM_LIMIT),
-        cost_estimate=pl.CostEstimate(
+        cost_estimate=estimate(
             flops=16 * slots * SEGMENT * neigh_rows * width, bytes_accessed=2 * pairs.size,
             transcendentals=slots * neigh_rows * width,
         ),
@@ -841,7 +859,7 @@
             pltpu.VMEM((slots * SEGMENT, width), F32),
         ],
         compiler_params=pltpu.CompilerParams(vmem_limit_bytes=VMEM_LIMIT),
-        cost_estimate=pl.CostEstimate(
+        cost_estimate=estimate(
             flops=40 * slots * SEGMENT * neigh_rows * width, bytes_accessed=4 * pairs.size,
             transcendentals=slots * neigh_rows * width,
         ),
@@ -870,10 +888,28 @@
     def whole(shard):
         return assemble(lax.all_gather(shard, BOTH, axis=0, tiled=False), dp, seq)
 
+    own_tokens = tokens.reshape(rows, model)
+    states = neighbours.reshape(segments * neigh_rows, model)
+    forward_pairs = [(i, i + 1) for i in range(seq - 1) if (i + 1) % span]
+    back_pairs = [(i + 1, i) for i in range(seq - 1) if (i + 1) % span]
+    inputs = own_tokens.astype(F32)
+    upstream = cotangent.reshape(rows, model).astype(F32)
+    bias = lax.dynamic_slice_in_dim(position_bias, pos * group_heads, group_heads, 0)
     triple = jnp.concatenate([query_self, key_self, value_self], axis=1)
-    if fast:
-        line = jnp.stack([triple] + [swap(triple, "dp", 2 * k) for k in range(1, dp // 2)])
-        triple_full = reorder_triple(line, swap(line, "dp", 1), place)
+
+    pieces_tok = {0: own_tokens}
+    bit = span // 2
+    while bit:
+        for k in list(pieces_tok):
+            pieces_tok[k | bit] = swap(pieces_tok[k], "seq", bit)
+        bit //= 2
+    lane_tokens = [pieces_tok[k] for k in range(span)]
+
+    if fast:
+        near = jnp.stack([triple] + [swap(triple, "dp", 2 * k) for k in range(1, dp // 2)])
+        far = swap(near, "dp", 1)
+        lane_tokens = list(lax.optimization_barrier(tuple(lane_tokens) + (far,)))
+        far = lane_tokens.pop()
 
         def turned(shard):
             flat = shard.T
@@ -883,15 +919,19 @@
         packed = jnp.concatenate(
             [key_cross, value_cross, query_cross, turned(output_self), turned(output_cross)], axis=0
         )
-        recall_full, query_full, output_turned, cross_turned = assemble_attention(
-            gather_group(after(packed, line)), place
-        )
         part = outer_weight.shape[0] // 4
         line = [outer_weight[t * part : (t + 1) * part] for t in range(4)]
-        packed = jnp.concatenate([inner_weight, jnp.concatenate(line, axis=1)], axis=0)
-        feed_blocks = lax.all_gather(packed, BOTH, axis=0, tiled=False)
-        inner_full, outer_full = assemble_feed(feed_blocks)
+        feed = jnp.concatenate([inner_weight, jnp.concatenate(line, axis=1)], axis=0)
+        group_near = jnp.stack(gather_near(packed))
+        feed_line = gather_near(after(feed, group_near))
+        edge_source = after(states[(segments - 1) * neigh_rows :], far)
+        group_near = after(group_near, far)
+        group_both = jnp.concatenate([group_near, over_a(group_near)], axis=0)
+        first_normed, qkv, triple_full = project(near, far, norm_gains[:1], lane_tokens, place)
+        group_both = after(group_both, qkv)
+        group_far = over_b(group_both)
     else:
+        edge_source = states[(segments - 1) * neigh_rows :]
         pieces = []
         for shard in (query_self, key_self, value_self):
             pieces.append(lax.dynamic_slice_in_dim(whole(shard), pos * group_width, group_width, 1))
@@ -900,43 +940,48 @@
         query_full = whole(query_cross)
         output_turned, cross_turned = whole(output_self).T, whole(output_cross).T
         inner_full, outer_full = whole(inner_weight), whole(outer_weight)
-
-    own_tokens = tokens.reshape(rows, model)
-    pieces_tok = {0: own_tokens}
-    bit = span // 2
-    while bit:
-        for k in list(pieces_tok):
-            pieces_tok[k | bit] = swap(pieces_tok[k], "seq", bit)
-        bit //= 2
-    states = neighbours.reshape(segments * neigh_rows, model)
-    forward_pairs = [(i, i + 1) for i in range(seq - 1) if (i + 1) % span]
-    back_pairs = [(i + 1, i) for i in range(seq - 1) if (i + 1) % span]
-    edge = lax.ppermute(states[(segments - 1) * neigh_rows :], "seq", forward_pairs)
+        first_normed = jnp.concatenate(
+            [rounded(rms_apply(v.astype(F32), norm_gains[0])) for v in lane_tokens], axis=0
+        )
+        qkv = rounded(linear(first_normed, triple_full))
+
+    edge = lax.ppermute(edge_source, "seq", forward_pairs)
+    mixed_group, lse = self_fwd(pos, bias, qkv, rows)
+    if fast:
+        feed_line = list(lax.optimization_barrier(tuple(feed_line) + (edge, mixed_group, group_far)))
+        group_far, mixed_group, edge = feed_line.pop(), feed_line.pop(), feed_line.pop()
+
     states_all = lax.optimization_barrier(jnp.concatenate([edge, states], axis=0))
 
-    inputs = own_tokens.astype(F32)
-    upstream = cotangent.reshape(rows, model).astype(F32)
-    first_normed = jnp.concatenate(
-        [rounded(rms_apply(pieces_tok[k].astype(F32), norm_gains[0])) for k in range(span)], axis=0
-    )
-    qkv = rounded(linear(first_normed, triple_full))
-    bias = lax.dynamic_slice_in_dim(position_bias, pos * group_heads, group_heads, 0)
-    mixed_group, lse = self_fwd(pos, bias, qkv, rows)
-
-    def exchanged(stack):
-        return [stack[0]] + [swap(stack[k], "seq", k) for k in range(1, span)]
-
-    mixed_blocks = mixed_group.reshape(span, rows, group_width)
-    mixed_self = columns_from_blocks(jnp.stack(exchanged(mixed_blocks)), pos)
+    def exchanged(blocks):
+        return [blocks[0]] + [swap(blocks[k], "seq", k) for k in range(1, span)]
+
+    mixed_blocks = [mixed_group[k * rows : (k + 1) * rows] for k in range(span)]
+    mixed_self = join_columns(exchanged(mixed_blocks), pos)
+    if fast:
+        feed_near = after(jnp.stack(feed_line), mixed_self)
+        feed_next = over_a(feed_near)
+        recall_full, query_full, output_turned, cross_turned = assemble_attention(
+            [group_both, group_far, over_core(group_both), over_core(group_far)], place
+        )
 
     recall_pairs = rounded(linear(states_all, recall_full))
 
     after_self = inputs + input_grad(mixed_self, output_turned)
     second_normed = rounded(rms_apply(after_self, norm_gains[1]))
+    if fast:
+        feed_both = jnp.concatenate([feed_near, after(feed_next, second_normed)], axis=0)
+        feed_far = over_b(feed_both)
     cross_queries = rounded(linear(second_normed, query_full))
     mixed_cross = cross_fwd(cross_queries, recall_pairs, neigh_rows)
+    if fast:
+        mixed_cross, feed_far = lax.optimization_barrier((mixed_cross, feed_far))
     after_cross = after_self + input_grad(mixed_cross, cross_turned)
     third_normed = rounded(rms_apply(after_cross, norm_gains[2]))
+    if fast:
+        inner_full, outer_full = assemble_feed(
+            [feed_both, feed_far, over_core(feed_both), over_core(feed_far)], place
+        )
     gate_value = linear(third_normed, inner_full)
     activated, gelu_pull = jax.vjp(gelu_tanh, gate_value)
     hidden_act = rounded(activated)
@@ -946,12 +991,8 @@
     grad_hidden = input_grad(grad_feed, outer_full)
     grad_gate = rounded(gelu_pull(grad_hidden)[0])
     if fast:
-        blocks = feed_grad(third_normed, grad_gate, hidden_act, grad_feed)
-        blocks = blocks.reshape((dp * seq,) + blocks.shape[2:])
-        own = lax.psum_scatter(blocks, BOTH, scatter_dimension=0, tiled=True)[0].astype(F32)
-        part = own.shape[0] // 2
-        sum_inner = own[:part]
-        sum_outer = own[part:].reshape(part, 4, model // 4).transpose(1, 0, 2).reshape(4 * part, -1)
+        kept, sent = feed_grad(place, third_normed, grad_gate, hidden_act, grad_feed)
+        got = over_core(sent)
     else:
         sum_outer = block_sum(hidden_act, grad_feed)
         sum_inner = block_sum(third_normed, grad_gate)
@@ -960,6 +1001,11 @@
 
     grad_cross = rounded(grad_late)
     grad_mixed = rounded(linear(grad_cross, cross_turned))
+    if fast:
+        got = after(got, grad_mixed)
+        sent_b = rounded(wide_sum(kept[1], got[1]))
+        grad_mixed = after(grad_mixed, sent_b)
+        got_b = over_b(sent_b)
     probe, pair_round = cross_bwd(cross_queries, grad_mixed, recall_pairs, neigh_rows)
 
     def turned_back(own):
@@ -970,6 +1016,9 @@
         pieces = group_grad("tall", place, mixed_cross, grad_cross, 3, 5)
         pieces = group_grad("wide", place, second_normed, probe, 2, 5, pieces)
         pieces = group_grad("wide", place, states_all, pair_round, 0, 5, pieces, 2)
+        probe, got_b = lax.optimization_barrier((probe, got_b, pieces[0]))[:2]
+        sent_a = sum_second(kept, got, got_b)
+        got_a = over_a(sent_a)
     else:
         sum_cross = block_sum(mixed_cross, grad_cross)
         sum_key = block_sum(states_all, pair_round[:, :width])
@@ -978,54 +1027,76 @@
     norm_grad, gain_two = norm_back(after_self, norm_gains[1], input_grad(probe, query_full))
     grad_early = grad_late + norm_grad
     states_round = rounded(input_grad(pair_round, recall_full))
+
+    grad_self = rounded(grad_early)
+    if fast:
+        last_kept, last_sent = group_grad("tall", place, mixed_self, grad_self, 4, 5, pieces)
+        last_got = over_core(last_sent)
+    else:
+        sum_output = block_sum(mixed_self, grad_self)
+    grad_attended = rounded(linear(grad_self, output_turned))
+    if fast:
+        grad_attended = after(grad_attended, sent_a)
+    grad_parts = exchanged(split_columns(grad_attended, span, pos))
+    if fast:
+        grad_parts = list(lax.optimization_barrier(tuple(grad_parts) + (states_round, last_got)))
+        last_got, states_round = grad_parts.pop(), grad_parts.pop()
+        line = sum_third(kept, got, got_b, after(got_a, grad_parts[-1]))
+        last_b = rounded(wide_sum(last_kept[1], last_got[1]))
+        grad_parts[0] = after(grad_parts[0], line, last_b)
+        last_far = over_b(last_b)
+        feed_own = sum_over_z(line)
+        part = feed_own.shape[0] // 2
+        sum_inner = feed_own[:part]
+        sum_outer = feed_own[part:].reshape(part, 4, model // 4)
+        sum_outer = sum_outer.transpose(1, 0, 2).reshape(4 * part, -1)
+    grad_group = jnp.concatenate(grad_parts, axis=0)
     returned = lax.ppermute(states_round[:neigh_rows], "seq", back_pairs)
     last = states_round[segments * neigh_rows :].astype(F32) + returned.astype(F32)
     grad_states = jnp.concatenate(
         [states_round[neigh_rows : segments * neigh_rows], rounded(last)], axis=0
     )
-
-    grad_self = rounded(grad_early)
-    if fast:
-        steps = sum_group(group_grad("tall", place, mixed_self, grad_self, 4, 5, pieces))
-        sent_b = next(steps)
-        sent_a = next(steps)
-        sent_z = next(steps)
-        own = next(steps)
+    triple_grad, bias_sums = self_bwd(pos, bias, qkv, mixed_group, grad_group, lse, rows)
+    if fast:
+        triple_grad, last_far = lax.optimization_barrier((triple_grad, last_far, feed_own))[:2]
+        last_a = sum_second(last_kept, last_got, last_far)
+        last_near = over_a(last_a)
+        own_y, other_y = triple_pieces(place, first_normed, after(triple_grad, last_a))
+        got_y = swap(other_y, "dp", 1)
+        triple_grad = after(triple_grad, other_y)
+    partial = input_grad(triple_grad, triple_full)
+    gain_one = jnp.sum(partial * first_normed.astype(F32), axis=0) / norm_gains[0]
+    partial = rounded(partial)
+    if fast:
+        partial, last_near = lax.optimization_barrier((partial, last_near))
+        line = sum_third(last_kept, last_got, last_far, last_near)
+        own = sum_over_z(line)
         part = own.shape[0] // 5
         sum_key, sum_value, sum_query = (own[i * part : (i + 1) * part] for i in range(3))
         sum_cross = turned_back(own[3 * part : 4 * part])
         sum_output = turned_back(own[4 * part :])
-    else:
-        sum_output = block_sum(mixed_self, grad_self)
-    grad_attended = rounded(linear(grad_self, output_turned))
-    group_grads = exchanged(blocks_from_columns(grad_attended, span, pos))
-    grad_group = jnp.concatenate(group_grads, axis=0)
-    if fast:
-        grad_group = after(grad_group, sent_b)
-    triple_grad, bias_sums = self_bwd(pos, bias, qkv, mixed_group, grad_group, lse, rows)
-    partial = input_grad(triple_grad, triple_full)
-    all_tokens = jnp.concatenate([pieces_tok[k] for k in range(span)], axis=0).astype(F32)
-    factor = lax.rsqrt(jnp.mean(all_tokens * all_tokens, axis=-1, keepdims=True) + EPSILON)
-    gain_one = jnp.sum(partial * all_tokens * factor, axis=0)
-    partial = rounded(partial).reshape(span, rows, model)
+    partial = partial.reshape(span, rows, model)
     blocks = {k: partial[k] for k in range(span)}
     bit = 1
     while bit < span:
         for k in sorted(blocks):
             if not k & bit:
-                got = swap(blocks[k | bit], "seq", bit)
+                leaves = blocks[k | bit]
+                if fast and bit == 2:
+                    leaves, got_y = lax.optimization_barrier((leaves, got_y))
+                got = swap(leaves, "seq", bit)
                 blocks[k] = blocks[k].astype(F32) + got.astype(F32)
                 if bit * 2 < span and k:
                     blocks[k] = rounded(blocks[k])
         blocks = {k: v for k, v in blocks.items() if not k & bit}
         bit *= 2
+    if fast:
+        own = sum_over_z(rounded(wide_sum(own_y, got_y)))
+        own_self = [own[:, i * group_width : (i + 1) * group_width] for i in range(3)]
     norm_grad, _ = norm_back(inputs, norm_gains[0], blocks[0])
     grad_inputs = grad_early + norm_grad
 
-    if fast:
-        own = triple_sum(place, first_normed, triple_grad)
-        own_self = [own[:, i * group_width : (i + 1) * group_width] for i in range(3)]
-    else:
+    if not fast:
         own_self = []
         for i in range(3):
             columns = triple_grad[:, i * group_width : (i + 1) * group_width]

time: 623 us -> 547 us (0.88)
  waiting for transfers between devices: 186 us -> 99.5 us
  starting transfers between devices: 48 us -> 75.4 us
  between operations: 15.1 us -> 1.6 us
  Pallas kernels: 192 us -> 202 us
  matrix products: 96.4 us -> 88.5 us
  other arithmetic: 52.2 us -> 44.9 us
    ppermute x20 -> x17, waiting for transfers between devices: 78.8 us -> 31.4 us  [swap(): return lax.ppermute(value, axis, [(i, i ^ by) for i in range(peers)])]
    ppermute x3 -> x5, waiting for transfers between devices: 55.1 us -> 11.4 us  [over_a(): lax.ppermute(value, BOTH, device_pairs(lambda z, y, x, c: (z, y ^ c, x ^...]
    ppermute x8 -> x17, starting transfers between devices: 9 us -> 43.3 us  [over_z(): lax.ppermute(value, BOTH, device_pairs(lambda z, y, x, c: (z ^ k, y, x, c)))]
    pallas_call x4 -> x5, Pallas kernels: 31.7 us -> 40.6 us  [group_grad(): pl.pallas_call(kernel, grid_spec=pltpu.PrefetchScalarGridSpec(num_scalar_...]
    ppermute x3 -> x5, waiting for transfers between devices: 0.01 us -> 8.21 us  [over_b(): lax.ppermute(value, BOTH, device_pairs(lambda z, y, x, c: (z, y ^ 1 - c,...]
    convert_element_type x11 -> x13, other arithmetic: 20.2 us -> 28.1 us  [rounded(): return v.astype(BF)]
    dot_general x14 -> x13, matrix products: 96.4 us -> 88.5 us  [dot(): lax.dot_general(a, b, (((ca,), (cb,)), ((), ())), preferred_element_type=...]
    ppermute x20 -> x17, starting transfers between devices: 21.7 us -> 14.3 us  [swap(): return lax.ppermute(value, axis, [(i, i ^ by) for i in range(peers)])]
  transfers between devices with their start and end apart: 42 -> 53, of which waited for: 18 -> 21; matrix products, arithmetic and copies ran while one was open for 24% -> 21% of each run, Pallas kernels for 27% -> 29%
where the time goes in v3:
time: 547 us; the launch traced here: 542 us
  Pallas kernels  202 us (37%)
  waiting for transfers between devices  99.5 us (18%)
  matrix products  88.5 us (16%)
  starting transfers between devices  75.4 us (14%)
  other arithmetic  44.9 us (8%)
  local copies, waits for them, and re-layouts  29.5 us (5%)
    dot_general x13, matrix products, dot(): lax.dot_general(a, b, (((ca,), (cb,)), ((), ())), preferred_element_type=...  88.5 us
    pallas_call x1, Pallas kernels, self_bwd(): pl.pallas_call(self_bwd_kernel, grid=(blocks,), in_specs=[smem_spec(), sm...  46.7 us
    ppermute x17, waiting for transfers between devices, over_z(): lax.ppermute(value, BOTH, device_pairs(lambda z, y, x, c: (z ^ k, y, x, c)))  45.8 us
    ppermute x17, starting transfers between devices, over_z(): lax.ppermute(value, BOTH, device_pairs(lambda z, y, x, c: (z ^ k, y, x, c)))  43.3 us
    pallas_call x5, Pallas kernels, group_grad(): pl.pallas_call(kernel, grid_spec=pltpu.PrefetchScalarGridSpec(num_scalar_...  40.6 us
    ppermute x17, waiting for transfers between devices, swap(): return lax.ppermute(value, axis, [(i, i ^ by) for i in range(peers)])  31.4 us
    convert_element_type x13, other arithmetic, rounded(): return v.astype(BF)  28.1 us
    pallas_call x1, Pallas kernels, self_fwd(): pl.pallas_call(self_fwd_kernel, grid=(blocks,), in_specs=[smem_spec(), sm...  25.7 us
  transfers between devices with their start and end apart: 53, of which 21 were waited for; matrix products, arithmetic and copies ran while one was open for 21% of the time, Pallas kernels for 29%

profile of v3, /device:TPU:0, one launch (start us, length us, event | category | flops | bytes accessed | tf_op | source)
XLA Modules:
  0.0 541.9 jit_solution(3577278536270432501)
XLA Ops:
  6.2 3.6 collective-permute-start.11
  14.7 10.3 %collective-permute-done.7.refs_2_ = bf16[512,896]{1,0:T(8,128)(2,1)S(1)} collective-permute-done((bf16[512,896]{1,0:T(8,128)(2,1)}, bf16[512,896]{1,0:T(8,128)(2,1)S(1)}, u32[]{:S(2)}, u32[]{:S(2)}) %collective-permute-start.7) | collective-permute-done | bytes 917536 | tf_op jit(solution)/shard_map/ppermute | solution.py:59
  25.0 3.9 collective-permute-start.2
  30.6 6.1 %collective-permute-done.2 = bf16[560,256]{1,0:T(8,128)(2,1)S(1)} collective-permute-done((bf16[560,256]{1,0:T(8,128)(2,1)S(1)}, bf16[560,256]{1,0:T(8,128)(2,1)S(1)}, u32[]{:S(2)}, u32[]{:S(2)}) %collective-permute-start.2) | collective-permute-done | bytes 286752 | tf_op jit(solution)/shard_map/ppermute | solution.py:183
  36.7 12.2 %collective-permute-start = (bf16[560,256]{1,0:T(8,128)(2,1)S(1)}, bf16[560,256]{1,0:T(8,128)(2,1)S(1)}, u32[]{:S(2)}, u32[]{:S(2)}) collective-permute-start(bf16[560,256]{1,0:T(8,128)(2,1)S(1)} %maximum_dynamic-update-slice_fusion), channel_id=1, source_target_pairs={{0,8},{1,9},{2,10},{3,11},{4,12},{5,13},{6,14},{7,15},{8,0},{9,1},... | collective-permute-start | bytes 860168 | tf_op jit(solution)/shard_map/ppermute | solution.py:183
  48.8 5.2 collective-permute-done.1
  54.1 6.0 %collective-permute-done = bf16[560,256]{1,0:T(8,128)(2,1)S(1)} collective-permute-done((bf16[560,256]{1,0:T(8,128)(2,1)S(1)}, bf16[560,256]{1,0:T(8,128)(2,1)S(1)}, u32[]{:S(2)}, u32[]{:S(2)}) %collective-permute-start) | collective-permute-done | bytes 286752 | tf_op jit(solution)/shard_map/ppermute | solution.py:183
  64.6 10.9 %shard_map.262 = (bf16[2048,896]{1,0:T(8,128)(2,1)}, bf16[2048,768]{1,0:T(8,128)(2,1)}, bf16[896,768]{1,0:T(8,128)(2,1)}) custom-call(s32[4]{0:T(128)} %pad_add_fusion.place_ref.refs_0_, bf16[4,112,768]{2,1,0:T(8,128)(2,1)} %copy-done.28, bf16[4,112,768]{2,1,0:T(8,128)(2,1)} %copy-done.33, f32[1,896]{1,0:T(1,128)} %get-tuple-element.226.gain_ref, ...), custom_call_target="tpu_custom_call" | custom-call | flops 56371444 | bytes 293601 | tf_op jit(solution)/shard_map/pallas_call | solution.py:111
  83.7 3.0 collective-permute-start.4
  88.8 25.7 %shard_map.263 = (bf16[2048,256]{1,0:T(8,128)(2,1)}, f32[8,8,256]{2,1,0:T(8,128)}) custom-call(s32[1]{0:T(128)} %bitcast.1.pos_ref.mine_ref, f32[4,6]{1,0:T(4,128)} %copy.46.bias_ref, bf16[2048,768]{1,0:T(8,128)(2,1)} %get-tuple-element.96.qkv_ref), custom_call_target="tpu_custom_call" | custom-call | flops 85899344 | bytes 83886 | tf_op jit(solution)/shard_map/pallas_call | solution.py:596
  123.0 4.0 collective-permute-done.17.refs_2_
  127.0 3.7 collective-permute-done.18.refs_3_
  138.2 8.2 %shard_map.265 = (bf16[896,2048]{1,0:T(8,128)(2,1)}, bf16[896,1024]{1,0:T(8,128)(2,1)}, bf16[896,1024]{1,0:T(8,128)(2,1)}, bf16[896,1024]{1,0:T(8,128)(2,1)}) custom-call(s32[4]{0:T(128)} %pad_add_fusion.place_ref.refs_0_, bf16[8,560,256]{2,1,0:T(8,128)(2,1)} %copy-done.5, bf16[8,560,256]{2,1,0:T(8,128)(2,1)} %collective-permute-done.15.refs_1_, ...), custom_call_target="tpu_custom_call" | custom-call | tf_op jit(solution)/shard_map/pallas_call | solution.py:261
  146.4 3.0 multiply_reduce_fusion.6
  149.8 5.2 collective-permute-done.21
  163.1 12.0 %convolution_convert_fusion.k_ref.v_ref = bf16[2304,2048]{1,0:T(8,128)(2,1)} fusion(bf16[2304,896]{1,0:T(8,128)(2,1)S(1)} %pad_maximum_fusion.refs_1_, bf16[896,2048]{1,0:T(8,128)(2,1)S(1)} %copy-done.43), kind=kOutput, calls=%fused_computation | convolution fusion | flops 8460435456 | bytes 17235968 | tf_op jit(solution)/shard_map/dot_general | solution.py:24
  175.1 13.2 %shard_map.266.refs_1_ = bf16[512,1024]{1,0:T(8,128)(2,1)} custom-call(bf16[512,1024]{1,0:T(8,128)(2,1)} %convolution_convert_fusion.4.q_ref, bf16[2304,2048]{1,0:T(8,128)(2,1)} %convolution_convert_fusion.k_ref.v_ref, bf16[2304,2048]{1,0:T(8,128)(2,1)} %convolution_convert_fusion.k_ref.v_ref), custom_call_target="tpu_custom_call" | custom-call | flops 48318384 | bytes 188743 | tf_op jit(solution)/shard_map/pallas_call | solution.py:788
  188.3 6.5 %collective-permute-done.22.refs_1_ = bf16[8,224,896]{2,1,0:T(8,128)(2,1)} collective-permute-done((bf16[8,224,896]{2,1,0:T(8,128)(2,1)S(1)}, bf16[8,224,896]{2,1,0:T(8,128)(2,1)}, u32[]{:S(2)}, u32[]{:S(2)}) %collective-permute-start.22) | collective-permute-done | bytes 3211296 | tf_op jit(solution)/shard_map/ppermute | solution.py:193
  194.8 3.2 multiply_reduce_fusion.5
  200.9 13.0 %shard_map.267 = (bf16[896,3584]{1,0:T(8,128)(2,1)}, bf16[3584,896]{1,0:T(8,128)(2,1)}) custom-call(s32[4]{0:T(128)} %pad_add_fusion.place_ref.refs_0_, bf16[8,224,896]{2,1,0:T(8,128)(2,1)} %copy-done.17, bf16[8,224,896]{2,1,0:T(8,128)(2,1)} %collective-permute-done.22.refs_1_, bf16[8,224,896]{2,1,0:T(8,128)(2,1)} %collective-permute-done.23.refs_2_, ...), custom_call_target="tpu_custom_call" | custom-call | tf_op jit(solution)/shard_map/pallas_call | solution.py:307
  213.9 9.9 %multiply_convert_fusion = (bf16[512,3584]{1,0:T(8,128)(2,1)}, f32[512,3584]{1,0:T(8,128)S(1)}) fusion(bf16[512,896]{1,0:T(8,128)(2,1)S(1)} %multiply_convert_fusion.1.refs_1_, bf16[896,3584]{1,0:T(8,128)(2,1)} %get-tuple-element.115), kind=kOutput, calls=%fused_computation.16 | convolution fusion | flops 3304849408 | bytes 18350080 | tf_op jit(solution)/shard_map/dot_general | solution.py:24
  223.8 10.2 %fusion.6.refs_2_.refs_3_ = bf16[512,3584]{1,0:T(8,128)(2,1)} fusion(f32[512,3584]{1,0:T(8,128)S(1)} %get-tuple-element.235, bf16[3584,896]{1,0:T(8,128)(2,1)S(1)} %copy-done.42, bf16[1,512,896]{2,1,0:T(8,128)(2,1)S(1)} %copy-done.8), kind=kOutput, calls=%fused_computation.9 | convolution fusion | flops 3325034496 | bytes 18350080 | tf_op jit(solution)/shard_map/dot_general | solution.py:24
  233.9 11.0 %shard_map.268 = (bf16[2,2,4,224,896]{4,3,2,1,0:T(8,128)(2,1)}, bf16[2,2,4,224,896]{4,3,2,1,0:T(8,128)(2,1)}) custom-call(s32[4]{0:T(128)} %pad_add_fusion.place_ref.refs_0_, bf16[512,3584]{1,0:T(8,128)(2,1)} %get-tuple-element.234.left, bf16[512,896]{1,0:T(8,128)(2,1)} %bitcast.159), custom_call_target="tpu_custom_call" | custom-call | flops 65766688 | bytes 220200 | tf_op jit(solution)/shard_map/pallas_call | solution.py:388
  244.9 9.8 %shard_map.269 = (bf16[2,2,4,224,896]{4,3,2,1,0:T(8,128)(2,1)}, bf16[2,2,4,224,896]{4,3,2,1,0:T(8,128)(2,1)}) custom-call(s32[4]{0:T(128)} %pad_add_fusion.place_ref.refs_0_, bf16[512,896]{1,0:T(8,128)(2,1)} %copy-done.26, bf16[512,3584]{1,0:T(8,128)(2,1)} %fusion.6.refs_2_.refs_3_, ...), custom_call_target="tpu_custom_call", output_to_operand_aliasing={{0}: (4, {}), {1}: (5, {})} | custom-call | flops 65766688 | bytes 220200 | tf_op jit(solution)/shard_map/pallas_call | solution.py:441
  254.8 8.6 %multiply_reduce_fusion.1 = (f32[896]{0:T(1024)S(1)}, f32[512]{0:T(512)S(1)}, f32[512,896]{1,0:T(8,128)S(1)}) fusion(f32[512,896]{1,0:T(8,128)S(1)} %get-tuple-element.232, f32[512]{0:T(512)S(1)} %fusion.34, f32[896]{0:T(1024)S(1)} %get-tuple-element.185, bf16[512,3584]{1,0:T(8,128)(2,1)S(1)} %copy-done.3, bf16[896,3584]{1,0:T(8,128)(2,1)} %get-tuple-element.115), kind=kOutput, calls=%fused_computation.48 | convolution fusion | flops 3291085312 | bytes 13773824 | tf_op jit(solution)/shard_map/dot_general | solution.py:24
  271.5 5.8 %shard_map.271 = (bf16[2,2,4,560,256]{4,3,2,1,0:T(8,128)(2,1)}, bf16[2,2,4,560,256]{4,3,2,1,0:T(8,128)(2,1)}) custom-call(s32[4]{0:T(128)} %pad_add_fusion.place_ref.refs_0_, bf16[512,1024]{1,0:T(8,128)(2,1)} %shard_map.266.refs_1_, bf16[512,896]{1,0:T(8,128)(2,1)} %copy-done.25), custom_call_target="tpu_custom_call" | custom-call | flops 18790480 | bytes 76021 | tf_op jit(solution)/shard_map/pallas_call | solution.py:441
  277.3 21.0 %shard_map.270 = (bf16[512,1024]{1,0:T(8,128)(2,1)}, bf16[2304,2048]{1,0:T(8,128)(2,1)}) custom-call(bf16[512,1024]{1,0:T(8,128)(2,1)} %convolution_convert_fusion.4.q_ref, bf16[512,1024]{1,0:T(8,128)(2,1)} %convolution_convert_fusion.3.g_ref, bf16[2304,2048]{1,0:T(8,128)(2,1)} %convolution_convert_fusion.k_ref.v_ref, ...), custom_call_target="tpu_custom_call" | custom-call | flops 120795952 | bytes 377487 | tf_op jit(solution)/shard_map/pallas_call | solution.py:842
  298.4 4.7 shard_map.272
  303.1 14.5 %shard_map.273 = (bf16[2,2,4,560,256]{4,3,2,1,0:T(8,128)(2,1)}, bf16[2,2,4,560,256]{4,3,2,1,0:T(8,128)(2,1)}) custom-call(s32[4]{0:T(128)} %pad_add_fusion.place_ref.refs_0_, bf16[2304,896]{1,0:T(8,128)(2,1)} %copy-done.2, bf16[2304,2048]{1,0:T(8,128)(2,1)} %get-tuple-element.124.refs_2_.refs_3_, ...), custom_call_target="tpu_custom_call", output_to_operand_aliasing={{0}: (4, {}), {1}: (5, {})} | custom-call | flops 169114336 | bytes 344719 | tf_op jit(solution)/shard_map/pallas_call | solution.py:441
  317.6 4.0 multiply_reduce_fusion.2
  324.2 5.8 %shard_map.275 = (bf16[2,2,4,560,256]{4,3,2,1,0:T(8,128)(2,1)}, bf16[2,2,4,560,256]{4,3,2,1,0:T(8,128)(2,1)}) custom-call(s32[4]{0:T(128)} %pad_add_fusion.place_ref.refs_0_, bf16[512,1024]{1,0:T(8,128)(2,1)} %shard_map.264.refs_1_, bf16[512,896]{1,0:T(8,128)(2,1)} %get-tuple-element.187.refs_2_, ...), custom_call_target="tpu_custom_call", output_to_operand_aliasing={{0}: (3, {}), {1}: (4, {})} | custom-call | flops 18790480 | bytes 76021 | tf_op jit(solution)/shard_map/pallas_call | solution.py:441
  330.8 3.8 fusion.13
  341.8 15.6 %convolution_convert_fusion.1 = bf16[2304,896]{1,0:T(8,128)(2,1)} fusion(bf16[2304,2048]{1,0:T(8,128)(2,1)} %get-tuple-element.124.refs_2_.refs_3_, bf16[896,2048]{1,0:T(8,128)(2,1)} %get-tuple-element.105), kind=kOutput, calls=%fused_computation.18 | convolution fusion | flops 8457781248 | bytes 17235968 | tf_op jit(solution)/shard_map/dot_general | solution.py:24
  357.4 6.7 %collective-permute-done.28 = bf16[512,256]{1,0:T(8,128)(2,1)S(1)} collective-permute-done((bf16[512,256]{1,0:T(8,128)(2,1)}, bf16[512,256]{1,0:T(8,128)(2,1)S(1)}, u32[]{:S(2)}, u32[]{:S(2)}) %collective-permute-start.28) | collective-permute-done | bytes 262176 | tf_op jit(solution)/shard_map/ppermute | solution.py:59
  365.2 3.8 fusion.14
  370.3 3.7 fusion.12
  377.5 6.4 %collective-permute-start.34 = (bf16[224,896]{1,0:T(8,128)(2,1)}, bf16[224,896]{1,0:T(8,128)(2,1)}, u32[]{:S(2)}, u32[]{:S(2)}) collective-permute-start(bf16[224,896]{1,0:T(8,128)(2,1)} %get-tuple-element.195), channel_id=1, source_target_pairs={{0,16},{1,17},{2,18},{3,19},{4,20},{5,21},{6,22},{7,23},{8,24},{9,... | collective-permute-start | bytes 1204232 | tf_op jit(solution)/shard_map/ppermute | solution.py:183
  385.1 46.7 %shard_map.276 = (bf16[2048,768]{1,0:T(8,128)(2,1)}, f32[4,6,8,256]{3,2,1,0:T(8,128)}) custom-call(s32[1]{0:T(128)} %bitcast.1.pos_ref.mine_ref, f32[4,6]{1,0:T(4,128)} %copy.46.bias_ref, bf16[2048,768]{1,0:T(8,128)(2,1)} %get-tuple-element.96.qkv_ref, bf16[2048,256]{1,0:T(8,128)(2,1)} %get-tuple-element.100.o_ref, ...), custom_call_target="tpu_custom_call" | custom-call | flops 214748368 | bytes 167772 | tf_op jit(solution)/shard_map/pallas_call | solution.py:698
  434.5 3.4 fusion.17
  437.8 7.4 %shard_map.277 = (bf16[4,112,768]{2,1,0:T(8,128)(2,1)}, bf16[4,112,768]{2,1,0:T(8,128)(2,1)}) custom-call(s32[4]{0:T(128)} %pad_add_fusion.place_ref.refs_0_, bf16[2048,896]{1,0:T(8,128)(2,1)} %get-tuple-element.150.left, bf16[2048,768]{1,0:T(8,128)(2,1)} %get-tuple-element.154.right), custom_call_target="tpu_custom_call" | custom-call | flops 56371444 | bytes 136314 | tf_op jit(solution)/shard_map/pallas_call | solution.py:504
  445.3 7.6 %multiply_reduce_fusion = (f32[896]{0:T(1024)S(1)}, bf16[2048,896]{1,0:T(8,128)(2,1)}) fusion(bf16[2048,896]{1,0:T(8,128)(2,1)S(1)} %copy-done.24, bf16[2048,768]{1,0:T(8,128)(2,1)} %get-tuple-element.154.right, bf16[896,768]{1,0:T(8,128)(2,1)S(1)} %copy-done.47), kind=kOutput, calls=%fused_computation.15 | convolution fusion | flops 2825911296 | bytes 11865600 | tf_op jit(solution)/shard_map/dot_general | solution.py:24
  459.7 7.7 %fusion.24 = bf16[1,512,896]{2,1,0:T(8,128)(2,1)} fusion(f32[512,896]{1,0:T(8,128)S(1)} %get-tuple-element.232, bf16[512,3584]{1,0:T(8,128)(2,1)S(1)} %copy-done.23, bf16[3584,896]{1,0:T(8,128)(2,1)} %get-tuple-element.116), kind=kOutput, calls=%fused_computation.65 | convolution fusion | flops 3289251840 | bytes 12845056 | tf_op jit(solution)/shard_map/dot_general | solution.py:24
  472.7 4.4 collective-permute-done.44
  483.0 3.0 fusion.16
  498.8 15.3 %collective-permute-done.51 = bf16[560,256]{1,0:T(8,128)(2,1)} collective-permute-done((bf16[560,256]{1,0:T(8,128)(2,1)}, bf16[560,256]{1,0:T(8,128)(2,1)}, u32[]{:S(2)}, u32[]{:S(2)}) %collective-permute-start.51) | collective-permute-done | bytes 286752 | tf_op jit(solution)/shard_map/ppermute | solution.py:183
  524.5 4.1 collective-permute-done.49
  528.5 5.5 %collective-permute-done.48 = bf16[112,768]{1,0:T(8,128)(2,1)S(1)} collective-permute-done((bf16[112,768]{1,0:T(8,128)(2,1)S(1)}, bf16[112,768]{1,0:T(8,128)(2,1)S(1)}, u32[]{:S(2)}, u32[]{:S(2)}) %collective-permute-start.48) | collective-permute-done | bytes 172064 | tf_op jit(solution)/shard_map/ppermute | solution.py:183
  534.8 4.4 collective-permute-done.40
  (272 shorter events, 126.7 us)
Async XLA Ops:
  0.7 59.6 %collective-permute-start.6 = (bf16[512,896]{1,0:T(8,128)(2,1)}, bf16[512,896]{1,0:T(8,128)(2,1)S(1)}, u32[]{:S(2)}, u32[]{:S(2)}) collective-permute-start(bf16[512,896]{1,0:T(8,128)(2,1)} %bitcast.156), channel_id=1, source_target_pairs={{0,1},{1,0},{2,3},{3,2},{4,5},{5,4},{6,7},{7,6},{8,9},{9,8},{10,11... | collective-permute-start | bytes 2752520 | tf_op jit(solution)/shard_map/ppermute | solution.py:59
  1.2 23.7 %collective-permute-start.7 = (bf16[512,896]{1,0:T(8,128)(2,1)}, bf16[512,896]{1,0:T(8,128)(2,1)S(1)}, u32[]{:S(2)}, u32[]{:S(2)}) collective-permute-start(bf16[512,896]{1,0:T(8,128)(2,1)} %bitcast.157), channel_id=1, source_target_pairs={{0,2},{1,3},{2,0},{3,1},{4,6},{5,7},{6,4},{7,5},{8,10},{9,11},{10,... | collective-permute-start | bytes 2752520 | tf_op jit(solution)/shard_map/ppermute | solution.py:59
  6.2 18.7 %collective-permute-start.11 = (bf16[112,768]{1,0:T(8,128)(2,1)S(1)}, bf16[112,768]{1,0:T(8,128)(2,1)S(1)}, u32[]{:S(2)}, u32[]{:S(2)}) collective-permute-start(bf16[112,768]{1,0:T(8,128)(2,1)S(1)} %constant_dynamic-update-slice_fusion.3), channel_id=1, source_target_pairs={{0,24},{4,28},{8,16},{12,20},{16,8},{20,12},{24,0},{28,4},{1,25},{... | collective-permute-start | bytes 516104 | tf_op jit(solution)/shard_map/ppermute | solution.py:59
  9.8 19.0 %collective-permute-start.10 = (bf16[112,768]{1,0:T(8,128)(2,1)S(1)}, bf16[112,768]{1,0:T(8,128)(2,1)S(1)}, u32[]{:S(2)}, u32[]{:S(2)}) collective-permute-start(bf16[112,768]{1,0:T(8,128)(2,1)S(1)} %constant_dynamic-update-slice_fusion.3), channel_id=1, source_target_pairs={{0,16},{4,20},{8,24},{12,28},{16,0},{20,4},{24,8},{28,12},{1,17},{... | collective-permute-start | bytes 516104 | tf_op jit(solution)/shard_map/ppermute | solution.py:59
  9.9 19.0 %collective-permute-start.9 = (bf16[112,768]{1,0:T(8,128)(2,1)S(1)}, bf16[112,768]{1,0:T(8,128)(2,1)S(1)}, u32[]{:S(2)}, u32[]{:S(2)}) collective-permute-start(bf16[112,768]{1,0:T(8,128)(2,1)S(1)} %constant_dynamic-update-slice_fusion.3), channel_id=1, source_target_pairs={{0,8},{4,12},{8,0},{12,4},{16,24},{20,28},{24,16},{28,20},{1,9},{5... | collective-permute-start | bytes 516104 | tf_op jit(solution)/shard_map/ppermute | solution.py:59
  24.9 35.4 %collective-permute-start.8 = (bf16[512,896]{1,0:T(8,128)(2,1)S(1)}, bf16[512,896]{1,0:T(8,128)(2,1)S(1)}, u32[]{:S(2)}, u32[]{:S(2)}) collective-permute-start(bf16[512,896]{1,0:T(8,128)(2,1)S(1)} %collective-permute-done.7.refs_2_), channel_id=1, source_target_pairs={{0,1},{1,0},{2,3},{3,2},{4,5},{5,4},{6,7},{7,6},{8,9},{9,8},{10,11... | collective-permute-start | bytes 2752520 | tf_op jit(solution)/shard_map/ppermute | solution.py:59
  25.0 11.7 %collective-permute-start.2 = (bf16[560,256]{1,0:T(8,128)(2,1)S(1)}, bf16[560,256]{1,0:T(8,128)(2,1)S(1)}, u32[]{:S(2)}, u32[]{:S(2)}) collective-permute-start(bf16[560,256]{1,0:T(8,128)(2,1)S(1)} %maximum_dynamic-update-slice_fusion), channel_id=1, source_target_pairs={{0,24},{1,25},{2,26},{3,27},{4,28},{5,29},{6,30},{7,31},{8,16},{9,... | collective-permute-start | bytes 860168 | tf_op jit(solution)/shard_map/ppermute | solution.py:183
  29.0 31.3 %collective-permute-start.12 = (bf16[4,112,768]{2,1,0:T(8,128)(2,1)S(1)}, bf16[4,112,768]{2,1,0:T(8,128)(2,1)S(1)}, u32[]{:S(2)}, u32[]{:S(2)}) collective-permute-start(bf16[4,112,768]{2,1,0:T(8,128)(2,1)S(1)} %pad_maximum_fusion.6.near_ref), channel_id=1, source_target_pairs={{0,4},{4,0},{8,12},{12,8},{16,20},{20,16},{24,28},{28,24},{1,5},{5... | collective-permute-start | bytes 2064392 | tf_op jit(solution)/shard_map/ppermute | solution.py:59
  30.6 23.5 %collective-permute-start.1 = (bf16[560,256]{1,0:T(8,128)(2,1)S(1)}, bf16[560,256]{1,0:T(8,128)(2,1)S(1)}, u32[]{:S(2)}, u32[]{:S(2)}) collective-permute-start(bf16[560,256]{1,0:T(8,128)(2,1)S(1)} %maximum_dynamic-update-slice_fusion), channel_id=1, source_target_pairs={{0,16},{1,17},{2,18},{3,19},{4,20},{5,21},{6,22},{7,23},{8,24},{9,... | collective-permute-start | bytes 860168 | tf_op jit(solution)/shard_map/ppermute | solution.py:183
  36.7 23.4 %collective-permute-start = (bf16[560,256]{1,0:T(8,128)(2,1)S(1)}, bf16[560,256]{1,0:T(8,128)(2,1)S(1)}, u32[]{:S(2)}, u32[]{:S(2)}) collective-permute-start(bf16[560,256]{1,0:T(8,128)(2,1)S(1)} %maximum_dynamic-update-slice_fusion), channel_id=1, source_target_pairs={{0,8},{1,9},{2,10},{3,11},{4,12},{5,13},{6,14},{7,15},{8,0},{9,1},... | collective-permute-start | bytes 860168 | tf_op jit(solution)/shard_map/ppermute | solution.py:183
  61.3 16.0 %collective-permute-start.14 = (bf16[4,560,256]{2,1,0:T(8,128)(2,1)S(1)}, bf16[4,560,256]{2,1,0:T(8,128)(2,1)}, u32[]{:S(2)}, u32[]{:S(2)}) collective-permute-start(bf16[4,560,256]{2,1,0:T(8,128)(2,1)S(1)} %pad_maximum_fusion.4), channel_id=1, source_target_pairs={{0,2},{1,5},{2,0},{3,7},{4,6},{5,1},{6,4},{7,3},{8,10},{9,13},{10,... | collective-permute-start | bytes 3440648 | tf_op jit(solution)/shard_map/ppermute | solution.py:187
  78.7 36.5 %collective-permute-start.15 = (bf16[8,560,256]{2,1,0:T(8,128)(2,1)S(1)}, bf16[8,560,256]{2,1,0:T(8,128)(2,1)}, u32[]{:S(2)}, u32[]{:S(2)}) collective-permute-start(bf16[8,560,256]{2,1,0:T(8,128)(2,1)S(1)} %pad_maximum_fusion.2.refs_0_), channel_id=1, source_target_pairs={{0,4},{1,3},{2,6},{3,1},{4,0},{5,7},{6,2},{7,5},{8,12},{9,11},{10,... | collective-permute-start | bytes 6881288 | tf_op jit(solution)/shard_map/ppermute | solution.py:193
  81.4 33.9 %collective-permute-start.13 = (bf16[256,896]{1,0:T(8,128)(2,1)S(1)}, bf16[256,896]{1,0:T(8,128)(2,1)}, u32[]{:S(2)}, u32[]{:S(2)}) collective-permute-start(bf16[256,896]{1,0:T(8,128)(2,1)S(1)} %bitcast.165), channel_id=1, source_target_pairs={{0,1},{1,2},{2,3},{4,5},{5,6},{6,7},{8,9},{9,10},{10,11},{12,13},{... | collective-permute-start | bytes 1376264 | tf_op jit(solution)/shard_map/ppermute | solution.py:948
  83.6 30.9 %collective-permute-start.3 = (bf16[224,896]{1,0:T(8,128)(2,1)S(1)}, bf16[224,896]{1,0:T(8,128)(2,1)}, u32[]{:S(2)}, u32[]{:S(2)}) collective-permute-start(bf16[224,896]{1,0:T(8,128)(2,1)S(1)} %maximum_maximum_fusion), channel_id=1, source_target_pairs={{0,8},{1,9},{2,10},{3,11},{4,12},{5,13},{6,14},{7,15},{8,0},{9,1},... | collective-permute-start | bytes 1204232 | tf_op jit(solution)/shard_map/ppermute | solution.py:183
  83.7 31.6 %collective-permute-start.4 = (bf16[224,896]{1,0:T(8,128)(2,1)S(1)}, bf16[224,896]{1,0:T(8,128)(2,1)}, u32[]{:S(2)}, u32[]{:S(2)}) collective-permute-start(bf16[224,896]{1,0:T(8,128)(2,1)S(1)} %maximum_maximum_fusion), channel_id=1, source_target_pairs={{0,16},{1,17},{2,18},{3,19},{4,20},{5,21},{6,22},{7,23},{8,24},{9,... | collective-permute-start | bytes 1204232 | tf_op jit(solution)/shard_map/ppermute | solution.py:183
  86.7 28.5 %collective-permute-start.5 = (bf16[224,896]{1,0:T(8,128)(2,1)S(1)}, bf16[224,896]{1,0:T(8,128)(2,1)}, u32[]{:S(2)}, u32[]{:S(2)}) collective-permute-start(bf16[224,896]{1,0:T(8,128)(2,1)S(1)} %maximum_maximum_fusion), channel_id=1, source_target_pairs={{0,24},{1,25},{2,26},{3,27},{4,28},{5,29},{6,30},{7,31},{8,16},{9,... | collective-permute-start | bytes 1204232 | tf_op jit(solution)/shard_map/ppermute | solution.py:183
  114.6 23.7 %collective-permute-start.19 = (bf16[8,560,256]{2,1,0:T(8,128)(2,1)S(1)}, bf16[8,560,256]{2,1,0:T(8,128)(2,1)}, u32[]{:S(2)}, u32[]{:S(2)}) collective-permute-start(bf16[8,560,256]{2,1,0:T(8,128)(2,1)S(1)} %pad_maximum_fusion.2.refs_0_), channel_id=1, source_target_pairs={{0,1},{1,0},{2,3},{3,2},{4,5},{5,4},{6,7},{7,6},{8,9},{9,8},{10,11... | collective-permute-start | bytes 6881288 | tf_op jit(solution)/shard_map/ppermute | solution.py:199
  115.3 23.0 %collective-permute-start.20 = (bf16[8,560,256]{2,1,0:T(8,128)(2,1)}, bf16[8,560,256]{2,1,0:T(8,128)(2,1)}, u32[]{:S(2)}, u32[]{:S(2)}) collective-permute-start(bf16[8,560,256]{2,1,0:T(8,128)(2,1)} %collective-permute-done.15.refs_1_), channel_id=1, source_target_pairs={{0,1},{1,0},{2,3},{3,2},{4,5},{5,4},{6,7},{7,6},{8,9},{9,8},{10,11... | collective-permute-start | bytes 6881288 | tf_op jit(solution)/shard_map/ppermute | solution.py:199
  117.8 9.2 %collective-permute-start.17 = (bf16[512,256]{1,0:T(8,128)(2,1)S(1)}, bf16[512,256]{1,0:T(8,128)(2,1)S(1)}, u32[]{:S(2)}, u32[]{:S(2)}) collective-permute-start(bf16[512,256]{1,0:T(8,128)(2,1)S(1)} %get-tuple-element.200), channel_id=1, source_target_pairs={{0,2},{1,3},{2,0},{3,1},{4,6},{5,7},{6,4},{7,5},{8,10},{9,11},{10,... | collective-permute-start | bytes 786440 | tf_op jit(solution)/shard_map/ppermute | solution.py:59
  118.6 12.2 %collective-permute-start.18 = (bf16[512,256]{1,0:T(8,128)(2,1)S(1)}, bf16[512,256]{1,0:T(8,128)(2,1)S(1)}, u32[]{:S(2)}, u32[]{:S(2)}) collective-permute-start(bf16[512,256]{1,0:T(8,128)(2,1)S(1)} %get-tuple-element.199), channel_id=1, source_target_pairs={{0,3},{1,2},{2,1},{3,0},{4,7},{5,6},{6,5},{7,4},{8,11},{9,10},{10,... | collective-permute-start | bytes 786440 | tf_op jit(solution)/shard_map/ppermute | solution.py:59
  133.9 21.1 %collective-permute-start.21 = (bf16[4,224,896]{2,1,0:T(8,128)(2,1)}, bf16[4,224,896]{2,1,0:T(8,128)(2,1)}, u32[]{:S(2)}, u32[]{:S(2)}) collective-permute-start(bf16[4,224,896]{2,1,0:T(8,128)(2,1)} %pad_maximum_fusion.3), channel_id=1, source_target_pairs={{0,2},{1,5},{2,0},{3,7},{4,6},{5,1},{6,4},{7,3},{8,10},{9,13},{10,... | collective-permute-start | bytes 4816904 | tf_op jit(solution)/shard_map/ppermute | solution.py:187
  156.6 38.1 %collective-permute-start.22 = (bf16[8,224,896]{2,1,0:T(8,128)(2,1)S(1)}, bf16[8,224,896]{2,1,0:T(8,128)(2,1)}, u32[]{:S(2)}, u32[]{:S(2)}) collective-permute-start(bf16[8,224,896]{2,1,0:T(8,128)(2,1)S(1)} %constant_dynamic-update-slice_fusion.6.refs_0_), channel_id=1, source_target_pairs={{0,4},{1,3},{2,6},{3,1},{4,0},{5,7},{6,2},{7,5},{8,12},{9,11},{10,... | collective-permute-start | bytes 9633800 | tf_op jit(solution)/shard_map/ppermute | solution.py:193
  159.1 39.1 %collective-permute-start.23 = (bf16[8,224,896]{2,1,0:T(8,128)(2,1)S(1)}, bf16[8,224,896]{2,1,0:T(8,128)(2,1)}, u32[]{:S(2)}, u32[]{:S(2)}) collective-permute-start(bf16[8,224,896]{2,1,0:T(8,128)(2,1)S(1)} %constant_dynamic-update-slice_fusion.6.refs_0_), channel_id=1, source_target_pairs={{0,1},{1,0},{2,3},{3,2},{4,5},{5,4},{6,7},{7,6},{8,9},{9,8},{10,11... | collective-permute-start | bytes 9633800 | tf_op jit(solution)/shard_map/ppermute | solution.py:199
  254.7 12.3 %collective-permute-start.25 = (bf16[2,2,4,224,896]{4,3,2,1,0:T(8,128)(2,1)}, bf16[2,2,4,224,896]{4,3,2,1,0:T(8,128)(2,1)S(1)}, u32[]{:S(2)}, u32[]{:S(2)}) collective-permute-start(bf16[2,2,4,224,896]{4,3,2,1,0:T(8,128)(2,1)} %get-tuple-element.120), channel_id=1, source_target_pairs={{0,1},{1,0},{2,3},{3,2},{4,5},{5,4},{6,7},{7,6},{8,9},{9,8},{10,11... | collective-permute-start | bytes 19267592 | tf_op jit(solution)/shard_map/ppermute | solution.py:199
  270.6 47.0 %collective-permute-start.26 = (bf16[2,4,224,896]{3,2,1,0:T(8,128)(2,1)}, bf16[2,4,224,896]{3,2,1,0:T(8,128)(2,1)}, u32[]{:S(2)}, u32[]{:S(2)}) collective-permute-start(bf16[2,4,224,896]{3,2,1,0:T(8,128)(2,1)} %fusion.10), channel_id=1, source_target_pairs={{0,4},{1,3},{2,6},{3,1},{4,0},{5,7},{6,2},{7,5},{8,12},{9,11},{10,... | collective-permute-start | bytes 9633800 | tf_op jit(solution)/shard_map/ppermute | solution.py:193
  330.0 35.2 %collective-permute-start.30 = (bf16[2,2,4,560,256]{4,3,2,1,0:T(8,128)(2,1)}, bf16[2,2,4,560,256]{4,3,2,1,0:T(8,128)(2,1)}, u32[]{:S(2)}, u32[]{:S(2)}) collective-permute-start(bf16[2,2,4,560,256]{4,3,2,1,0:T(8,128)(2,1)} %get-tuple-element.138), channel_id=1, source_target_pairs={{0,1},{1,0},{2,3},{3,2},{4,5},{5,4},{6,7},{7,6},{8,9},{9,8},{10,11... | collective-permute-start | bytes 13762568 | tf_op jit(solution)/shard_map/ppermute | solution.py:199
  334.6 35.7 %collective-permute-start.31 = (bf16[4,224,896]{2,1,0:T(8,128)(2,1)}, bf16[4,224,896]{2,1,0:T(8,128)(2,1)}, u32[]{:S(2)}, u32[]{:S(2)}) collective-permute-start(bf16[4,224,896]{2,1,0:T(8,128)(2,1)} %fusion.13), channel_id=1, source_target_pairs={{0,2},{1,5},{2,0},{3,7},{4,6},{5,1},{6,4},{7,3},{8,10},{9,13},{10,... | collective-permute-start | bytes 4816904 | tf_op jit(solution)/shard_map/ppermute | solution.py:187
  340.0 17.4 %collective-permute-start.27 = (bf16[512,256]{1,0:T(8,128)(2,1)}, bf16[512,256]{1,0:T(8,128)(2,1)S(1)}, u32[]{:S(2)}, u32[]{:S(2)}) collective-permute-start(bf16[512,256]{1,0:T(8,128)(2,1)} %get-tuple-element.134), channel_id=1, source_target_pairs={{0,1},{1,0},{2,3},{3,2},{4,5},{5,4},{6,7},{7,6},{8,9},{9,8},{10,11... | collective-permute-start | bytes 786440 | tf_op jit(solution)/shard_map/ppermute | solution.py:59
  340.0 24.1 %collective-permute-start.28 = (bf16[512,256]{1,0:T(8,128)(2,1)}, bf16[512,256]{1,0:T(8,128)(2,1)S(1)}, u32[]{:S(2)}, u32[]{:S(2)}) collective-permute-start(bf16[512,256]{1,0:T(8,128)(2,1)} %get-tuple-element.135), channel_id=1, source_target_pairs={{0,2},{1,3},{2,0},{3,1},{4,6},{5,7},{6,4},{7,5},{8,10},{9,11},{10,... | collective-permute-start | bytes 786440 | tf_op jit(solution)/shard_map/ppermute | solution.py:59
  341.3 23.9 %collective-permute-start.29 = (bf16[512,256]{1,0:T(8,128)(2,1)}, bf16[512,256]{1,0:T(8,128)(2,1)S(1)}, u32[]{:S(2)}, u32[]{:S(2)}) collective-permute-start(bf16[512,256]{1,0:T(8,128)(2,1)} %get-tuple-element.136), channel_id=1, source_target_pairs={{0,3},{1,2},{2,1},{3,0},{4,7},{5,6},{6,5},{7,4},{8,11},{9,10},{10,... | collective-permute-start | bytes 786440 | tf_op jit(solution)/shard_map/ppermute | solution.py:59
  369.0 65.4 %collective-permute-start.32 = (bf16[2,4,560,256]{3,2,1,0:T(8,128)(2,1)}, bf16[2,4,560,256]{3,2,1,0:T(8,128)(2,1)}, u32[]{:S(2)}, u32[]{:S(2)}) collective-permute-start(bf16[2,4,560,256]{3,2,1,0:T(8,128)(2,1)} %fusion.14), channel_id=1, source_target_pairs={{0,4},{1,3},{2,6},{3,1},{4,0},{5,7},{6,2},{7,5},{8,12},{9,11},{10,... | collective-permute-start | bytes 6881288 | tf_op jit(solution)/shard_map/ppermute | solution.py:193
  375.1 57.9 %collective-permute-start.35 = (bf16[224,896]{1,0:T(8,128)(2,1)}, bf16[224,896]{1,0:T(8,128)(2,1)}, u32[]{:S(2)}, u32[]{:S(2)}) collective-permute-start(bf16[224,896]{1,0:T(8,128)(2,1)} %get-tuple-element.194), channel_id=1, source_target_pairs={{0,24},{1,25},{2,26},{3,27},{4,28},{5,29},{6,30},{7,31},{8,16},{9,... | collective-permute-start | bytes 1204232 | tf_op jit(solution)/shard_map/ppermute | solution.py:183
  377.5 55.4 %collective-permute-start.34 = (bf16[224,896]{1,0:T(8,128)(2,1)}, bf16[224,896]{1,0:T(8,128)(2,1)}, u32[]{:S(2)}, u32[]{:S(2)}) collective-permute-start(bf16[224,896]{1,0:T(8,128)(2,1)} %get-tuple-element.195), channel_id=1, source_target_pairs={{0,16},{1,17},{2,18},{3,19},{4,20},{5,21},{6,22},{7,23},{8,24},{9,... | collective-permute-start | bytes 1204232 | tf_op jit(solution)/shard_map/ppermute | solution.py:183
  383.9 49.1 %collective-permute-start.33 = (bf16[224,896]{1,0:T(8,128)(2,1)}, bf16[224,896]{1,0:T(8,128)(2,1)}, u32[]{:S(2)}, u32[]{:S(2)}) collective-permute-start(bf16[224,896]{1,0:T(8,128)(2,1)} %get-tuple-element.193), channel_id=1, source_target_pairs={{0,8},{1,9},{2,10},{3,11},{4,12},{5,13},{6,14},{7,15},{8,0},{9,1},... | collective-permute-start | bytes 1204232 | tf_op jit(solution)/shard_map/ppermute | solution.py:183
  454.9 25.9 %collective-permute-start.36 = (bf16[4,560,256]{2,1,0:T(8,128)(2,1)}, bf16[4,560,256]{2,1,0:T(8,128)(2,1)}, u32[]{:S(2)}, u32[]{:S(2)}) collective-permute-start(bf16[4,560,256]{2,1,0:T(8,128)(2,1)} %fusion.17), channel_id=1, source_target_pairs={{0,2},{1,5},{2,0},{3,7},{4,6},{5,1},{6,4},{7,3},{8,10},{9,13},{10,... | collective-permute-start | bytes 3440648 | tf_op jit(solution)/shard_map/ppermute | solution.py:187
  456.7 12.2 %collective-permute-start.43 = (f32[24,128]{1,0:T(8,128)S(1)}, f32[24,128]{1,0:T(8,128)S(1)}, u32[]{:S(2)}, u32[]{:S(2)}) collective-permute-start(f32[24,128]{1,0:T(8,128)S(1)} %fusion.73), channel_id=1, source_target_pairs={{0,16},{1,17},{2,18},{3,19},{4,20},{5,21},{6,22},{7,23},{8,24},{9,... | collective-permute-start | bytes 36872 | tf_op jit(solution)/shard_map/ppermute | solution.py:183
  467.4 10.5 %collective-permute-start.41 = (bf16[256,896]{1,0:T(8,128)(2,1)S(1)}, bf16[256,896]{1,0:T(8,128)(2,1)S(1)}, u32[]{:S(2)}, u32[]{:S(2)}) collective-permute-start(bf16[256,896]{1,0:T(8,128)(2,1)S(1)} %slice.259), channel_id=1, source_target_pairs={{1,0},{2,1},{3,2},{5,4},{6,5},{7,6},{9,8},{10,9},{11,10},{13,12},{... | collective-permute-start | bytes 1376264 | tf_op jit(solution)/shard_map/ppermute | solution.py:1054
  480.8 12.7 %collective-permute-start.46 = (f32[24,128]{1,0:T(8,128)S(1)}, f32[24,128]{1,0:T(8,128)S(1)}, u32[]{:S(2)}, u32[]{:S(2)}) collective-permute-start(f32[24,128]{1,0:T(8,128)S(1)} %add.219), channel_id=1, source_target_pairs={{0,1},{1,0},{2,3},{3,2},{4,5},{5,4},{6,7},{7,6},{8,9},{9,8},{10,11... | collective-permute-start | bytes 36872 | tf_op jit(solution)/shard_map/ppermute | solution.py:199
  482.5 33.6 %collective-permute-start.38 = (bf16[512,896]{1,0:T(8,128)(2,1)S(1)}, bf16[512,896]{1,0:T(8,128)(2,1)}, u32[]{:S(2)}, u32[]{:S(2)}) collective-permute-start(bf16[512,896]{1,0:T(8,128)(2,1)S(1)} %get-tuple-element.192), channel_id=1, source_target_pairs={{0,1},{1,0},{2,3},{3,2},{4,5},{5,4},{6,7},{7,6},{8,9},{9,8},{10,11... | collective-permute-start | bytes 2752520 | tf_op jit(solution)/shard_map/ppermute | solution.py:59
  487.0 11.9 %collective-permute-start.52 = (bf16[560,256]{1,0:T(8,128)(2,1)}, bf16[560,256]{1,0:T(8,128)(2,1)S(1)}, u32[]{:S(2)}, u32[]{:S(2)}) collective-permute-start(bf16[560,256]{1,0:T(8,128)(2,1)} %get-tuple-element.197), channel_id=1, source_target_pairs={{0,24},{1,25},{2,26},{3,27},{4,28},{5,29},{6,30},{7,31},{8,16},{9,... | collective-permute-start | bytes 860168 | tf_op jit(solution)/shard_map/ppermute | solution.py:183
  488.4 25.7 %collective-permute-start.51 = (bf16[560,256]{1,0:T(8,128)(2,1)}, bf16[560,256]{1,0:T(8,128)(2,1)}, u32[]{:S(2)}, u32[]{:S(2)}) collective-permute-start(bf16[560,256]{1,0:T(8,128)(2,1)} %get-tuple-element.198), channel_id=1, source_target_pairs={{0,16},{1,17},{2,18},{3,19},{4,20},{5,21},{6,22},{7,23},{8,24},{9,... | collective-permute-start | bytes 860168 | tf_op jit(solution)/shard_map/ppermute | solution.py:183
  488.6 25.5 %collective-permute-start.50 = (bf16[560,256]{1,0:T(8,128)(2,1)}, bf16[560,256]{1,0:T(8,128)(2,1)}, u32[]{:S(2)}, u32[]{:S(2)}) collective-permute-start(bf16[560,256]{1,0:T(8,128)(2,1)} %get-tuple-element.196), channel_id=1, source_target_pairs={{0,8},{1,9},{2,10},{3,11},{4,12},{5,13},{6,14},{7,15},{8,0},{9,1},... | collective-permute-start | bytes 860168 | tf_op jit(solution)/shard_map/ppermute | solution.py:183
  493.5 24.2 %collective-permute-start.39 = (bf16[4,112,768]{2,1,0:T(8,128)(2,1)}, bf16[4,112,768]{2,1,0:T(8,128)(2,1)}, u32[]{:S(2)}, u32[]{:S(2)}) collective-permute-start(bf16[4,112,768]{2,1,0:T(8,128)(2,1)} %get-tuple-element.153), channel_id=1, source_target_pairs={{0,4},{4,0},{8,12},{12,8},{16,20},{20,16},{24,28},{28,24},{1,5},{5... | collective-permute-start | bytes 2064392 | tf_op jit(solution)/shard_map/ppermute | solution.py:59
  498.8 36.0 %collective-permute-start.37 = (bf16[512,896]{1,0:T(8,128)(2,1)S(1)}, bf16[512,896]{1,0:T(8,128)(2,1)S(1)}, u32[]{:S(2)}, u32[]{:S(2)}) collective-permute-start(bf16[512,896]{1,0:T(8,128)(2,1)S(1)} %get-tuple-element.191), channel_id=1, source_target_pairs={{0,1},{1,0},{2,3},{3,2},{4,5},{5,4},{6,7},{7,6},{8,9},{9,8},{10,11... | collective-permute-start | bytes 2752520 | tf_op jit(solution)/shard_map/ppermute | solution.py:59
  517.7 21.5 %collective-permute-start.40 = (bf16[512,896]{1,0:T(8,128)(2,1)S(1)}, bf16[512,896]{1,0:T(8,128)(2,1)S(1)}, u32[]{:S(2)}, u32[]{:S(2)}) collective-permute-start(bf16[512,896]{1,0:T(8,128)(2,1)S(1)} %add_convert_fusion.2), channel_id=1, source_target_pairs={{0,2},{1,3},{2,0},{3,1},{4,6},{5,7},{6,4},{7,5},{8,10},{9,11},{10,... | collective-permute-start | bytes 2752520 | tf_op jit(solution)/shard_map/ppermute | solution.py:59
  519.3 9.2 %collective-permute-start.49 = (bf16[112,768]{1,0:T(8,128)(2,1)S(1)}, bf16[112,768]{1,0:T(8,128)(2,1)S(1)}, u32[]{:S(2)}, u32[]{:S(2)}) collective-permute-start(bf16[112,768]{1,0:T(8,128)(2,1)S(1)} %get-tuple-element.206), channel_id=1, source_target_pairs={{0,24},{1,25},{2,26},{3,27},{4,28},{5,29},{6,30},{7,31},{8,16},{9,... | collective-permute-start | bytes 516104 | tf_op jit(solution)/shard_map/ppermute | solution.py:183
  520.8 13.2 %collective-permute-start.48 = (bf16[112,768]{1,0:T(8,128)(2,1)S(1)}, bf16[112,768]{1,0:T(8,128)(2,1)S(1)}, u32[]{:S(2)}, u32[]{:S(2)}) collective-permute-start(bf16[112,768]{1,0:T(8,128)(2,1)S(1)} %get-tuple-element.207), channel_id=1, source_target_pairs={{0,16},{1,17},{2,18},{3,19},{4,20},{5,21},{6,22},{7,23},{8,24},{9,... | collective-permute-start | bytes 516104 | tf_op jit(solution)/shard_map/ppermute | solution.py:183
  520.8 13.2 %collective-permute-start.47 = (bf16[112,768]{1,0:T(8,128)(2,1)S(1)}, bf16[112,768]{1,0:T(8,128)(2,1)S(1)}, u32[]{:S(2)}, u32[]{:S(2)}) collective-permute-start(bf16[112,768]{1,0:T(8,128)(2,1)S(1)} %get-tuple-element.205), channel_id=1, source_target_pairs={{0,8},{1,9},{2,10},{3,11},{4,12},{5,13},{6,14},{7,15},{8,0},{9,1},... | collective-permute-start | bytes 516104 | tf_op jit(solution)/shard_map/ppermute | solution.py:183
  (58 other events, 695.3 us)

commit v4 on v3

--- a/solution.py
+++ b/solution.py
@@ -469,18 +469,74 @@
     return rounded(wide_sum(kept[0, 0], got[0, 0], got_b[0], got_a))
 
 
-def sum_over_z(line):
-    return wide_sum(line[0], *[over_z(line[k], k) for k in range(1, line.shape[0])])
-
-
-def butterfly(value):
-    k = 1
-    while k < lax.axis_size("dp") // 2:
-        value = value + over_z(value, k)
-        k *= 2
-    for step in (over_a, over_b, over_core):
-        value = value + step(value)
-    return value
+def all_over_z(line):
+    return [over_z(line[k], k) for k in range(1, line.shape[0])]
+
+
+def joint(values, *others):
+    out = lax.optimization_barrier(tuple(values) + others)
+    return list(out[: len(values)]), *out[len(values) :]
+
+
+def small_sum_kernel(dp, seq, in_ref, out_ref, slots, send_sems, recv_sems):
+    count = dp * seq
+    me = lax.axis_index("dp") * seq + lax.axis_index("seq")
+    barrier = pltpu.get_barrier_semaphore()
+
+    def peer(d):
+        other = lax.rem(me + d, count)
+        return lax.div(other, seq), lax.rem(other, seq)
+
+    def greet(d, carry):
+        pl.semaphore_signal(
+            barrier, inc=1, device_id=peer(d), device_id_type=pl.DeviceIdType.MESH
+        )
+        return carry
+
+    lax.fori_loop(1, count, greet, 0)
+    pl.semaphore_wait(barrier, count - 1)
+
+    def copy(d):
+        return pltpu.make_async_remote_copy(
+            src_ref=in_ref,
+            dst_ref=slots.at[d - 1],
+            send_sem=send_sems.at[d - 1],
+            recv_sem=recv_sems.at[d - 1],
+            device_id=peer(d),
+            device_id_type=pl.DeviceIdType.MESH,
+        )
+
+    def start(d, carry):
+        copy(d).start()
+        return carry
+
+    def wait(d, carry):
+        copy(d).wait()
+        return carry
+
+    lax.fori_loop(1, count, start, 0)
+    lax.fori_loop(1, count, wait, 0)
+    total = in_ref[...]
+    for d in range(count - 1):
+        total = total + slots[d]
+    out_ref[...] = total
+
+
+def small_sum(value):
+    dp, seq = lax.axis_size("dp"), lax.axis_size("seq")
+    others = dp * seq - 1
+    return pl.pallas_call(
+        functools.partial(small_sum_kernel, dp, seq),
+        in_specs=[vmem_spec()],
+        out_specs=vmem_spec(),
+        out_shape=jax.ShapeDtypeStruct(value.shape, value.dtype),
+        scratch_shapes=[
+            pltpu.VMEM((others,) + value.shape, value.dtype),
+            pltpu.SemaphoreType.DMA((others,)),
+            pltpu.SemaphoreType.DMA((others,)),
+        ],
+        compiler_params=pltpu.CompilerParams(collective_id=0, has_side_effects=True),
+    )(value)
 
 
 def triple_grad_kernel(place_ref, left, right, kept, sent):
@@ -985,7 +1041,6 @@
     gate_value = linear(third_normed, inner_full)
     activated, gelu_pull = jax.vjp(gelu_tanh, gate_value)
     hidden_act = rounded(activated)
-    outcome = after_cross + linear(hidden_act, outer_full)
 
     grad_feed = rounded(upstream)
     grad_hidden = input_grad(grad_feed, outer_full)
@@ -1026,7 +1081,6 @@
         sum_query = block_sum(second_normed, probe)
     norm_grad, gain_two = norm_back(after_self, norm_gains[1], input_grad(probe, query_full))
     grad_early = grad_late + norm_grad
-    states_round = rounded(input_grad(pair_round, recall_full))
 
     grad_self = rounded(grad_early)
     if fast:
@@ -1038,6 +1092,9 @@
     if fast:
         grad_attended = after(grad_attended, sent_a)
     grad_parts = exchanged(split_columns(grad_attended, span, pos))
+    if fast:
+        pair_round = after(pair_round, grad_attended)
+    states_round = rounded(input_grad(pair_round, recall_full))
     if fast:
         grad_parts = list(lax.optimization_barrier(tuple(grad_parts) + (states_round, last_got)))
         last_got, states_round = grad_parts.pop(), grad_parts.pop()
@@ -1045,54 +1102,84 @@
         last_b = rounded(wide_sum(last_kept[1], last_got[1]))
         grad_parts[0] = after(grad_parts[0], line, last_b)
         last_far = over_b(last_b)
-        feed_own = sum_over_z(line)
+        feed_own = [line[0]] + all_over_z(line)
+    grad_group = jnp.concatenate(grad_parts, axis=0)
+    def joined_states(whole_round, edge_round):
+        last = whole_round[segments * neigh_rows :].astype(F32) + edge_round.astype(F32)
+        return jnp.concatenate(
+            [whole_round[neigh_rows : segments * neigh_rows], rounded(last)], axis=0
+        )
+
+    returned = lax.ppermute(states_round[:neigh_rows], "seq", back_pairs)
+    triple_grad, bias_sums = self_bwd(pos, bias, qkv, mixed_group, grad_group, lse, rows)
+    if fast:
+        feed_own, triple_grad, last_far, returned = joint(feed_own, triple_grad, last_far, returned)
+        last_a = sum_second(last_kept, last_got, last_far)
+        last_near = over_a(last_a)
+        own_y, other_y = triple_pieces(place, first_normed, after(triple_grad, last_a))
+        other_y, last_near, triple_grad = lax.optimization_barrier((other_y, last_near, triple_grad))
+        got_y = swap(other_y, "dp", 1)
+    else:
+        grad_states = joined_states(states_round, returned)
+    partial = input_grad(triple_grad, triple_full)
+    gain_one = jnp.sum(partial * first_normed.astype(F32), axis=0) / norm_gains[0]
+    partial = rounded(partial)
+    if fast:
+        last_near = after(last_near, partial)
+        line = sum_third(last_kept, last_got, last_far, last_near)
+        last_own = [line[0]] + all_over_z(line)
+    partial = partial.reshape(span, rows, model)
+    blocks = {k: partial[k] for k in range(span)}
+    if fast:
+        near_zero, near_two = swap(partial[1], "seq", 1), swap(partial[3], "seq", 1)
+        leaves = rounded(wide_sum(partial[2], near_two))
+        last_own[1:-1], leaves, got_y, near_zero = joint(last_own[1:-1], leaves, got_y, near_zero)
+        arrived = swap(leaves, "seq", 2)
+        line = rounded(wide_sum(own_y, got_y))
+        own = [line[0]] + all_over_z(line)
+        feed_own, returned, hidden_act, _ = joint(feed_own, returned, hidden_act, own[1])
+        outcome = rounded(after_cross + linear(hidden_act, outer_full))
+        feed_own = wide_sum(*feed_own)
         part = feed_own.shape[0] // 2
         sum_inner = feed_own[:part]
         sum_outer = feed_own[part:].reshape(part, 4, model // 4)
         sum_outer = sum_outer.transpose(1, 0, 2).reshape(4 * part, -1)
-    grad_group = jnp.concatenate(grad_parts, axis=0)
-    returned = lax.ppermute(states_round[:neigh_rows], "seq", back_pairs)
-    last = states_round[segments * neigh_rows :].astype(F32) + returned.astype(F32)
-    grad_states = jnp.concatenate(
-        [states_round[neigh_rows : segments * neigh_rows], rounded(last)], axis=0
+        grad_states = joined_states(states_round, returned)
+    else:
+        outcome = rounded(after_cross + linear(hidden_act, outer_full))
+        bit = 1
+        while bit < span:
+            for k in sorted(blocks):
+                if not k & bit:
+                    got = swap(blocks[k | bit], "seq", bit)
+                    blocks[k] = blocks[k].astype(F32) + got.astype(F32)
+                    if bit * 2 < span and k:
+                        blocks[k] = rounded(blocks[k])
+            blocks = {k: v for k, v in blocks.items() if not k & bit}
+            bit *= 2
+    bias_local = jnp.sum(bias_sums, axis=(2, 3))
+    bias_all = lax.dynamic_update_slice_in_dim(
+        jnp.zeros((heads, NB), F32), bias_local, pos * group_heads, 0
     )
-    triple_grad, bias_sums = self_bwd(pos, bias, qkv, mixed_group, grad_group, lse, rows)
-    if fast:
-        triple_grad, last_far = lax.optimization_barrier((triple_grad, last_far, feed_own))[:2]
-        last_a = sum_second(last_kept, last_got, last_far)
-        last_near = over_a(last_a)
-        own_y, other_y = triple_pieces(place, first_normed, after(triple_grad, last_a))
-        got_y = swap(other_y, "dp", 1)
-        triple_grad = after(triple_grad, other_y)
-    partial = input_grad(triple_grad, triple_full)
-    gain_one = jnp.sum(partial * first_normed.astype(F32), axis=0) / norm_gains[0]
-    partial = rounded(partial)
-    if fast:
-        partial, last_near = lax.optimization_barrier((partial, last_near))
-        line = sum_third(last_kept, last_got, last_far, last_near)
-        own = sum_over_z(line)
-        part = own.shape[0] // 5
-        sum_key, sum_value, sum_query = (own[i * part : (i + 1) * part] for i in range(3))
-        sum_cross = turned_back(own[3 * part : 4 * part])
-        sum_output = turned_back(own[4 * part :])
-    partial = partial.reshape(span, rows, model)
-    blocks = {k: partial[k] for k in range(span)}
-    bit = 1
-    while bit < span:
-        for k in sorted(blocks):
-            if not k & bit:
-                leaves = blocks[k | bit]
-                if fast and bit == 2:
-                    leaves, got_y = lax.optimization_barrier((leaves, got_y))
-                got = swap(leaves, "seq", bit)
-                blocks[k] = blocks[k].astype(F32) + got.astype(F32)
-                if bit * 2 < span and k:
-                    blocks[k] = rounded(blocks[k])
-        blocks = {k: v for k, v in blocks.items() if not k & bit}
-        bit *= 2
-    if fast:
-        own = sum_over_z(rounded(wide_sum(own_y, got_y)))
-        own_self = [own[:, i * group_width : (i + 1) * group_width] for i in range(3)]
+    small = jnp.concatenate([gain_one, gain_two, gain_three, bias_all.reshape(-1)])
+    if fast:
+        size = small.shape[0]
+        small = jnp.pad(small, (0, -size % 1024)).reshape(-1, 128)
+        small = small_sum(after(small, own[1], outcome, grad_states, sum_inner, sum_outer))
+        rest, small = joint(own[1:] + last_own[-1:] + [arrived], small)
+        own[1:], last_own[-1], arrived = rest[:-2], rest[-2], rest[-1]
+        blocks[0] = wide_sum(partial[0], near_zero, arrived)
+        small = small.reshape(-1)[:size]
+    else:
+        small = lax.psum(small, BOTH)
+    if fast:
+        own_sum = wide_sum(*own)
+        own_self = [own_sum[:, i * group_width : (i + 1) * group_width] for i in range(3)]
+        last_own = wide_sum(*last_own)
+        part = last_own.shape[0] // 5
+        sum_key, sum_value, sum_query = (last_own[i * part : (i + 1) * part] for i in range(3))
+        sum_cross = turned_back(last_own[3 * part : 4 * part])
+        sum_output = turned_back(last_own[4 * part :])
     norm_grad, _ = norm_back(inputs, norm_gains[0], blocks[0])
     grad_inputs = grad_early + norm_grad
 
@@ -1104,21 +1191,10 @@
             wide = lax.dynamic_update_slice_in_dim(wide, columns, pos * group_width, 1)
             own_self.append(block_sum(first_normed, wide))
 
-    bias_local = jnp.sum(bias_sums, axis=(2, 3))
-    bias_all = lax.dynamic_update_slice_in_dim(
-        jnp.zeros((heads, NB), F32), bias_local, pos * group_heads, 0
-    )
-    small = jnp.concatenate([gain_one, gain_two, gain_three, bias_all.reshape(-1)])
-    if fast:
-        size = small.shape[0]
-        small = jnp.pad(small, (0, -size % 1024)).reshape(-1, 128)
-        small = butterfly(small).reshape(-1)[:size]
-    else:
-        small = lax.psum(small, BOTH)
     gains = small[: 3 * model].reshape(3, model)
     bias_total = small[3 * model :].reshape(heads, NB)
     return (
-        rounded(outcome).reshape(1, rows, model),
+        outcome.reshape(1, rows, model),
         rounded(grad_inputs).reshape(1, rows, model),
         grad_states.reshape(neighbours.shape),
         gains,

time: 547 us -> 545 us (level)
  waiting for transfers between devices: 99.5 us -> 79.4 us
  Pallas kernels: 202 us -> 213 us
  local copies, waits for them, and re-layouts: 29.5 us -> 37.6 us
    ppermute x17 -> x15, waiting for transfers between devices: 45.8 us -> 28.9 us  [over_z(): lax.ppermute(value, BOTH, device_pairs(lambda z, y, x, c: (z ^ k, y, x, c)))]
    pallas_call x0 -> x1, Pallas kernels: none -> 11.4 us  [small_sum(): pl.pallas_call(functools.partial(small_sum_kernel, dp, seq), in_specs=[vm...]
    ppermute x17 -> x15, starting transfers between devices: 43.3 us -> 39.6 us  [over_z(): lax.ppermute(value, BOTH, device_pairs(lambda z, y, x, c: (z ^ k, y, x, c)))]
    unnamed x112 -> x144, local copies, waits for them, and re-layouts: 13.2 us -> 15.8 us
    ppermute x5 -> x4, waiting for transfers between devices: 11.4 us -> 13.4 us  [over_a(): lax.ppermute(value, BOTH, device_pairs(lambda z, y, x, c: (z, y ^ c, x ^...]
  transfers between devices with their start and end apart: 53 -> 48, of which waited for: 21 -> 16; matrix products, arithmetic and copies ran while one was open for 21% -> 20% of each run, Pallas kernels for 29% -> 32%
where the time goes in v4:
time: 545 us; the launch traced here: 538 us
  Pallas kernels  213 us (39%)
  matrix products  87.1 us (16%)
  waiting for transfers between devices  79.4 us (15%)
  starting transfers between devices  72.7 us (13%)
  other arithmetic  45.9 us (8%)
  local copies, waits for them, and re-layouts  37.6 us (7%)
    dot_general x13, matrix products, dot(): lax.dot_general(a, b, (((ca,), (cb,)), ((), ())), preferred_element_type=...  87.1 us
    pallas_call x1, Pallas kernels, self_bwd(): pl.pallas_call(self_bwd_kernel, grid=(blocks,), in_specs=[smem_spec(), sm...  46.4 us
    pallas_call x5, Pallas kernels, group_grad(): pl.pallas_call(kernel, grid_spec=pltpu.PrefetchScalarGridSpec(num_scalar_...  40.7 us
    ppermute x15, starting transfers between devices, over_z(): lax.ppermute(value, BOTH, device_pairs(lambda z, y, x, c: (z ^ k, y, x, c)))  39.6 us
    ppermute x15, waiting for transfers between devices, over_z(): lax.ppermute(value, BOTH, device_pairs(lambda z, y, x, c: (z ^ k, y, x, c)))  28.9 us
    ppermute x17, waiting for transfers between devices, swap(): return lax.ppermute(value, axis, [(i, i ^ by) for i in range(peers)])  28 us
    convert_element_type x13, other arithmetic, rounded(): return v.astype(BF)  26.6 us
    pallas_call x1, Pallas kernels, self_fwd(): pl.pallas_call(self_fwd_kernel, grid=(blocks,), in_specs=[smem_spec(), sm...  25.6 us
  transfers between devices with their start and end apart: 48, of which 16 were waited for; matrix products, arithmetic and copies ran while one was open for 20% of the time, Pallas kernels for 32%

profile of v4, /device:TPU:0, one launch (start us, length us, event | category | flops | bytes accessed | tf_op | source)
XLA Modules:
  0.0 537.6 jit_solution(17785488877448160563)
XLA Ops:
  6.2 3.6 collective-permute-start.11
  14.7 10.3 %collective-permute-done.7.refs_2_ = bf16[512,896]{1,0:T(8,128)(2,1)S(1)} collective-permute-done((bf16[512,896]{1,0:T(8,128)(2,1)}, bf16[512,896]{1,0:T(8,128)(2,1)S(1)}, u32[]{:S(2)}, u32[]{:S(2)}) %collective-permute-start.7) | collective-permute-done | bytes 917536 | tf_op jit(solution)/shard_map/ppermute | solution.py:59
  25.0 3.9 collective-permute-start.2
  30.6 6.1 %collective-permute-done.2 = bf16[560,256]{1,0:T(8,128)(2,1)S(1)} collective-permute-done((bf16[560,256]{1,0:T(8,128)(2,1)S(1)}, bf16[560,256]{1,0:T(8,128)(2,1)S(1)}, u32[]{:S(2)}, u32[]{:S(2)}) %collective-permute-start.2) | collective-permute-done | bytes 286752 | tf_op jit(solution)/shard_map/ppermute | solution.py:183
  36.7 12.2 %collective-permute-start = (bf16[560,256]{1,0:T(8,128)(2,1)S(1)}, bf16[560,256]{1,0:T(8,128)(2,1)S(1)}, u32[]{:S(2)}, u32[]{:S(2)}) collective-permute-start(bf16[560,256]{1,0:T(8,128)(2,1)S(1)} %maximum_dynamic-update-slice_fusion), channel_id=1, source_target_pairs={{0,8},{1,9},{2,10},{3,11},{4,12},{5,13},{6,14},{7,15},{8,0},{9,1},... | collective-permute-start | bytes 860168 | tf_op jit(solution)/shard_map/ppermute | solution.py:183
  48.8 5.2 collective-permute-done.1
  54.1 6.0 %collective-permute-done = bf16[560,256]{1,0:T(8,128)(2,1)S(1)} collective-permute-done((bf16[560,256]{1,0:T(8,128)(2,1)S(1)}, bf16[560,256]{1,0:T(8,128)(2,1)S(1)}, u32[]{:S(2)}, u32[]{:S(2)}) %collective-permute-start) | collective-permute-done | bytes 286752 | tf_op jit(solution)/shard_map/ppermute | solution.py:183
  64.6 10.9 %shard_map.262 = (bf16[2048,896]{1,0:T(8,128)(2,1)}, bf16[2048,768]{1,0:T(8,128)(2,1)}, bf16[896,768]{1,0:T(8,128)(2,1)}) custom-call(s32[4]{0:T(128)} %pad_add_fusion.place_ref.refs_0_, bf16[4,112,768]{2,1,0:T(8,128)(2,1)} %copy-done.31, bf16[4,112,768]{2,1,0:T(8,128)(2,1)} %copy-done.38, f32[1,896]{1,0:T(1,128)} %get-tuple-element.273.gain_ref, ...), custom_call_target="tpu_custom_call" | custom-call | flops 56371444 | bytes 293601 | tf_op jit(solution)/shard_map/pallas_call | solution.py:111
  83.7 3.0 collective-permute-start.4
  88.8 25.6 %shard_map.263 = (bf16[2048,256]{1,0:T(8,128)(2,1)}, f32[8,8,256]{2,1,0:T(8,128)}) custom-call(s32[1]{0:T(128)} %bitcast.1.pos_ref.mine_ref, f32[4,6]{1,0:T(4,128)} %copy.47.bias_ref, bf16[2048,768]{1,0:T(8,128)(2,1)} %get-tuple-element.119.qkv_ref), custom_call_target="tpu_custom_call" | custom-call | flops 85899344 | bytes 83886 | tf_op jit(solution)/shard_map/pallas_call | solution.py:652
  122.8 4.0 collective-permute-done.17.refs_2_
  126.8 3.7 collective-permute-done.18.refs_3_
  138.1 8.1 %shard_map.265 = (bf16[896,2048]{1,0:T(8,128)(2,1)}, bf16[896,1024]{1,0:T(8,128)(2,1)}, bf16[896,1024]{1,0:T(8,128)(2,1)}, bf16[896,1024]{1,0:T(8,128)(2,1)}) custom-call(s32[4]{0:T(128)} %pad_add_fusion.place_ref.refs_0_, bf16[8,560,256]{2,1,0:T(8,128)(2,1)} %copy-done.5, bf16[8,560,256]{2,1,0:T(8,128)(2,1)} %collective-permute-done.15.refs_1_, ...), custom_call_target="tpu_custom_call" | custom-call | tf_op jit(solution)/shard_map/pallas_call | solution.py:261
  146.2 3.0 multiply_reduce_fusion.6
  149.5 5.3 collective-permute-done.21
  162.9 12.0 %convolution_convert_fusion.k_ref.v_ref = bf16[2304,2048]{1,0:T(8,128)(2,1)} fusion(bf16[2304,896]{1,0:T(8,128)(2,1)S(1)} %pad_maximum_fusion.refs_1_, bf16[896,2048]{1,0:T(8,128)(2,1)S(1)} %copy-done.60), kind=kOutput, calls=%fused_computation | convolution fusion | flops 8460435456 | bytes 17235968 | tf_op jit(solution)/shard_map/dot_general | solution.py:24
  174.9 13.2 %shard_map.266.refs_1_ = bf16[512,1024]{1,0:T(8,128)(2,1)} custom-call(bf16[512,1024]{1,0:T(8,128)(2,1)} %convolution_convert_fusion.4.q_ref, bf16[2304,2048]{1,0:T(8,128)(2,1)} %convolution_convert_fusion.k_ref.v_ref, bf16[2304,2048]{1,0:T(8,128)(2,1)} %convolution_convert_fusion.k_ref.v_ref), custom_call_target="tpu_custom_call" | custom-call | flops 48318384 | bytes 188743 | tf_op jit(solution)/shard_map/pallas_call | solution.py:844
  188.2 6.4 %collective-permute-done.22.refs_1_ = bf16[8,224,896]{2,1,0:T(8,128)(2,1)} collective-permute-done((bf16[8,224,896]{2,1,0:T(8,128)(2,1)S(1)}, bf16[8,224,896]{2,1,0:T(8,128)(2,1)}, u32[]{:S(2)}, u32[]{:S(2)}) %collective-permute-start.22) | collective-permute-done | bytes 3211296 | tf_op jit(solution)/shard_map/ppermute | solution.py:193
  194.6 3.2 multiply_reduce_fusion.5
  200.7 12.8 %shard_map.267 = (bf16[896,3584]{1,0:T(8,128)(2,1)}, bf16[3584,896]{1,0:T(8,128)(2,1)}) custom-call(s32[4]{0:T(128)} %pad_add_fusion.place_ref.refs_0_, bf16[8,224,896]{2,1,0:T(8,128)(2,1)} %copy-done.17, bf16[8,224,896]{2,1,0:T(8,128)(2,1)} %collective-permute-done.22.refs_1_, bf16[8,224,896]{2,1,0:T(8,128)(2,1)} %collective-permute-done.23.refs_2_, ...), custom_call_target="tpu_custom_call" | custom-call | tf_op jit(solution)/shard_map/pallas_call | solution.py:307
  213.5 9.9 %multiply_convert_fusion = (bf16[512,3584]{1,0:T(8,128)(2,1)}, f32[512,3584]{1,0:T(8,128)S(1)}) fusion(bf16[512,896]{1,0:T(8,128)(2,1)S(1)} %multiply_convert_fusion.1.refs_1_, bf16[896,3584]{1,0:T(8,128)(2,1)} %get-tuple-element.139), kind=kOutput, calls=%fused_computation.16 | convolution fusion | flops 3304849408 | bytes 18350080 | tf_op jit(solution)/shard_map/dot_general | solution.py:24
  223.4 10.2 %fusion.6.refs_2_.refs_3_ = bf16[512,3584]{1,0:T(8,128)(2,1)} fusion(f32[512,3584]{1,0:T(8,128)S(1)} %get-tuple-element.282, bf16[3584,896]{1,0:T(8,128)(2,1)S(1)} %copy-done.59, bf16[1,512,896]{2,1,0:T(8,128)(2,1)S(1)} %copy-done.8), kind=kOutput, calls=%fused_computation.9 | convolution fusion | flops 3325034496 | bytes 18350080 | tf_op jit(solution)/shard_map/dot_general | solution.py:24
  233.6 10.9 %shard_map.268 = (bf16[2,2,4,224,896]{4,3,2,1,0:T(8,128)(2,1)}, bf16[2,2,4,224,896]{4,3,2,1,0:T(8,128)(2,1)}) custom-call(s32[4]{0:T(128)} %pad_add_fusion.place_ref.refs_0_, bf16[512,3584]{1,0:T(8,128)(2,1)} %get-tuple-element.191.left, bf16[512,896]{1,0:T(8,128)(2,1)} %bitcast.151), custom_call_target="tpu_custom_call" | custom-call | flops 65766688 | bytes 220200 | tf_op jit(solution)/shard_map/pallas_call | solution.py:388
  244.5 9.8 %shard_map.269 = (bf16[2,2,4,224,896]{4,3,2,1,0:T(8,128)(2,1)}, bf16[2,2,4,224,896]{4,3,2,1,0:T(8,128)(2,1)}) custom-call(s32[4]{0:T(128)} %pad_add_fusion.place_ref.refs_0_, bf16[512,896]{1,0:T(8,128)(2,1)} %copy-done.28, bf16[512,3584]{1,0:T(8,128)(2,1)} %fusion.6.refs_2_.refs_3_, ...), custom_call_target="tpu_custom_call", output_to_operand_aliasing={{0}: (4, {}), {1}: (5, {})} | custom-call | flops 65766688 | bytes 220200 | tf_op jit(solution)/shard_map/pallas_call | solution.py:441
  254.5 8.6 %multiply_reduce_fusion.1 = (f32[896]{0:T(1024)S(1)}, f32[512]{0:T(512)S(1)}, f32[512,896]{1,0:T(8,128)S(1)}) fusion(f32[512,896]{1,0:T(8,128)S(1)} %get-tuple-element.279, f32[512]{0:T(512)S(1)} %fusion.31, f32[896]{0:T(1024)S(1)} %get-tuple-element.231, bf16[512,3584]{1,0:T(8,128)(2,1)S(1)} %copy-done.3, bf16[896,3584]{1,0:T(8,128)(2,1)} %get-tuple-element.139), kind=kOutput, calls=%fused_computation.49 | convolution fusion | flops 3291085312 | bytes 13773824 | tf_op jit(solution)/shard_map/dot_general | solution.py:24
  267.5 2.7 fusion.10
  271.3 5.8 %shard_map.271 = (bf16[2,2,4,560,256]{4,3,2,1,0:T(8,128)(2,1)}, bf16[2,2,4,560,256]{4,3,2,1,0:T(8,128)(2,1)}) custom-call(s32[4]{0:T(128)} %pad_add_fusion.place_ref.refs_0_, bf16[512,1024]{1,0:T(8,128)(2,1)} %shard_map.266.refs_1_, bf16[512,896]{1,0:T(8,128)(2,1)} %copy-done.27), custom_call_target="tpu_custom_call" | custom-call | flops 18790480 | bytes 76021 | tf_op jit(solution)/shard_map/pallas_call | solution.py:441
  277.0 21.0 %shard_map.270 = (bf16[512,1024]{1,0:T(8,128)(2,1)}, bf16[2304,2048]{1,0:T(8,128)(2,1)}) custom-call(bf16[512,1024]{1,0:T(8,128)(2,1)} %convolution_convert_fusion.4.q_ref, bf16[512,1024]{1,0:T(8,128)(2,1)} %convolution_convert_fusion.3.g_ref, bf16[2304,2048]{1,0:T(8,128)(2,1)} %convolution_convert_fusion.k_ref.v_ref, ...), custom_call_target="tpu_custom_call" | custom-call | flops 120795952 | bytes 377487 | tf_op jit(solution)/shard_map/pallas_call | solution.py:898
  298.0 4.8 shard_map.272
  302.8 14.4 %shard_map.273 = (bf16[2,2,4,560,256]{4,3,2,1,0:T(8,128)(2,1)}, bf16[2,2,4,560,256]{4,3,2,1,0:T(8,128)(2,1)}) custom-call(s32[4]{0:T(128)} %pad_add_fusion.place_ref.refs_0_, bf16[2304,896]{1,0:T(8,128)(2,1)} %copy-done.2, bf16[2304,2048]{1,0:T(8,128)(2,1)} %get-tuple-element.160.refs_2_.refs_3_, ...), custom_call_target="tpu_custom_call", output_to_operand_aliasing={{0}: (4, {}), {1}: (5, {})} | custom-call | flops 169114336 | bytes 344719 | tf_op jit(solution)/shard_map/pallas_call | solution.py:441
  317.3 4.0 multiply_reduce_fusion.2
  323.8 5.8 %shard_map.275 = (bf16[2,2,4,560,256]{4,3,2,1,0:T(8,128)(2,1)}, bf16[2,2,4,560,256]{4,3,2,1,0:T(8,128)(2,1)}) custom-call(s32[4]{0:T(128)} %pad_add_fusion.place_ref.refs_0_, bf16[512,1024]{1,0:T(8,128)(2,1)} %shard_map.264.refs_1_, bf16[512,896]{1,0:T(8,128)(2,1)} %get-tuple-element.233.refs_2_, ...), custom_call_target="tpu_custom_call", output_to_operand_aliasing={{0}: (3, {}), {1}: (4, {})} | custom-call | flops 18790480 | bytes 76021 | tf_op jit(solution)/shard_map/pallas_call | solution.py:441
  330.4 3.9 fusion.11
  341.4 14.5 %convolution_convert_fusion.1 = bf16[2304,896]{1,0:T(8,128)(2,1)S(1)} fusion(bf16[2304,2048]{1,0:T(8,128)(2,1)} %get-tuple-element.160.refs_2_.refs_3_, bf16[896,2048]{1,0:T(8,128)(2,1)} %get-tuple-element.128), kind=kOutput, calls=%fused_computation.18 | convolution fusion | flops 8457781248 | bytes 17235968 | tf_op jit(solution)/shard_map/dot_general | solution.py:24
  356.0 7.7 %collective-permute-done.29 = bf16[512,256]{1,0:T(8,128)(2,1)S(1)} collective-permute-done((bf16[512,256]{1,0:T(8,128)(2,1)}, bf16[512,256]{1,0:T(8,128)(2,1)S(1)}, u32[]{:S(2)}, u32[]{:S(2)}) %collective-permute-start.29) | collective-permute-done | bytes 262176 | tf_op jit(solution)/shard_map/ppermute | solution.py:59
  364.8 3.8 fusion.14
  372.5 3.7 fusion.13
  377.4 7.6 %collective-permute-start.32 = (bf16[224,896]{1,0:T(8,128)(2,1)}, bf16[224,896]{1,0:T(8,128)(2,1)S(1)}, u32[]{:S(2)}, u32[]{:S(2)}) collective-permute-start(bf16[224,896]{1,0:T(8,128)(2,1)} %get-tuple-element.241), channel_id=1, source_target_pairs={{0,8},{1,9},{2,10},{3,11},{4,12},{5,13},{6,14},{7,15},{8,0},{9,1},... | collective-permute-start | bytes 1204232 | tf_op jit(solution)/shard_map/ppermute | solution.py:183
  388.5 46.4 %shard_map.276 = (bf16[2048,768]{1,0:T(8,128)(2,1)}, f32[4,6,8,256]{3,2,1,0:T(8,128)}) custom-call(s32[1]{0:T(128)} %bitcast.1.pos_ref.mine_ref, f32[4,6]{1,0:T(4,128)} %copy.47.bias_ref, bf16[2048,768]{1,0:T(8,128)(2,1)} %get-tuple-element.119.qkv_ref, bf16[2048,256]{1,0:T(8,128)(2,1)} %get-tuple-element.123.o_ref, ...), custom_call_target="tpu_custom_call" | custom-call | flops 214748368 | bytes 167772 | tf_op jit(solution)/shard_map/pallas_call | solution.py:754
  438.1 3.3 collective-permute-start.37
  441.4 7.6 %shard_map.277 = (bf16[4,112,768]{2,1,0:T(8,128)(2,1)}, bf16[4,112,768]{2,1,0:T(8,128)(2,1)}) custom-call(s32[4]{0:T(128)} %pad_add_fusion.place_ref.refs_0_, bf16[2048,896]{1,0:T(8,128)(2,1)} %get-tuple-element.179.left, bf16[2048,768]{1,0:T(8,128)(2,1)} %get-tuple-element.186.right), custom_call_target="tpu_custom_call" | custom-call | flops 56371444 | bytes 136314 | tf_op jit(solution)/shard_map/pallas_call | solution.py:560
  449.0 6.3 %collective-permute-done.37 = bf16[4,560,256]{2,1,0:T(8,128)(2,1)} collective-permute-done((bf16[4,560,256]{2,1,0:T(8,128)(2,1)S(1)}, bf16[4,560,256]{2,1,0:T(8,128)(2,1)}, u32[]{:S(2)}, u32[]{:S(2)}) %collective-permute-start.37) | collective-permute-done | bytes 1146912 | tf_op jit(solution)/shard_map/ppermute | solution.py:187
  455.3 5.9 %multiply_reduce_fusion = (f32[896]{0:T(1024)S(1)}, bf16[2048,896]{1,0:T(8,128)(2,1)S(1)}) fusion(bf16[2048,896]{1,0:T(8,128)(2,1)S(1)} %copy-done.26, bf16[2048,768]{1,0:T(8,128)(2,1)} %get-tuple-element.186.right, bf16[896,768]{1,0:T(8,128)(2,1)} %get-tuple-element.187), kind=kOutput, calls=%fused_computation.15 | convolution fusion | flops 2825911296 | bytes 11865600 | tf_op jit(solution)/shard_map/dot_general | solution.py:24
  464.7 2.9 fusion.16
  473.9 9.7 %collective-permute-done.38 = bf16[560,256]{1,0:T(8,128)(2,1)S(1)} collective-permute-done((bf16[560,256]{1,0:T(8,128)(2,1)S(1)}, bf16[560,256]{1,0:T(8,128)(2,1)S(1)}, u32[]{:S(2)}, u32[]{:S(2)}) %collective-permute-start.38) | collective-permute-done | bytes 286752 | tf_op jit(solution)/shard_map/ppermute | solution.py:183
  495.6 8.9 %add_convert_fusion.2 = bf16[512,896]{1,0:T(8,128)(2,1)} fusion(f32[512,896]{1,0:T(8,128)S(1)} %get-tuple-element.279, bf16[512,3584]{1,0:T(8,128)(2,1)} %get-tuple-element.191.left, bf16[3584,896]{1,0:T(8,128)(2,1)} %get-tuple-element.138), kind=kOutput, calls=%fused_computation.51 | convolution fusion | flops 3289251840 | bytes 12845056 | tf_op jit(solution)/shard_map/dot_general | solution.py:24
  513.4 11.4 %shard_map.278 = f32[24,128]{1,0:T(8,128)} custom-call(f32[24,128]{1,0:T(8,128)} %fusion.29.in_ref), custom_call_target="tpu_custom_call" | custom-call | tf_op jit(solution)/shard_map/pallas_call | solution.py:528
  533.6 3.2 fusion.24
  (289 shorter events, 122.6 us)
Async XLA Ops:
  0.7 59.6 %collective-permute-start.6 = (bf16[512,896]{1,0:T(8,128)(2,1)}, bf16[512,896]{1,0:T(8,128)(2,1)S(1)}, u32[]{:S(2)}, u32[]{:S(2)}) collective-permute-start(bf16[512,896]{1,0:T(8,128)(2,1)} %bitcast.148), channel_id=1, source_target_pairs={{0,1},{1,0},{2,3},{3,2},{4,5},{5,4},{6,7},{7,6},{8,9},{9,8},{10,11... | collective-permute-start | bytes 2752520 | tf_op jit(solution)/shard_map/ppermute | solution.py:59
  1.2 23.7 %collective-permute-start.7 = (bf16[512,896]{1,0:T(8,128)(2,1)}, bf16[512,896]{1,0:T(8,128)(2,1)S(1)}, u32[]{:S(2)}, u32[]{:S(2)}) collective-permute-start(bf16[512,896]{1,0:T(8,128)(2,1)} %bitcast.149), channel_id=1, source_target_pairs={{0,2},{1,3},{2,0},{3,1},{4,6},{5,7},{6,4},{7,5},{8,10},{9,11},{10,... | collective-permute-start | bytes 2752520 | tf_op jit(solution)/shard_map/ppermute | solution.py:59
  6.2 18.7 %collective-permute-start.11 = (bf16[112,768]{1,0:T(8,128)(2,1)S(1)}, bf16[112,768]{1,0:T(8,128)(2,1)S(1)}, u32[]{:S(2)}, u32[]{:S(2)}) collective-permute-start(bf16[112,768]{1,0:T(8,128)(2,1)S(1)} %constant_dynamic-update-slice_fusion.3), channel_id=1, source_target_pairs={{0,24},{4,28},{8,16},{12,20},{16,8},{20,12},{24,0},{28,4},{1,25},{... | collective-permute-start | bytes 516104 | tf_op jit(solution)/shard_map/ppermute | solution.py:59
  9.8 19.0 %collective-permute-start.10 = (bf16[112,768]{1,0:T(8,128)(2,1)S(1)}, bf16[112,768]{1,0:T(8,128)(2,1)S(1)}, u32[]{:S(2)}, u32[]{:S(2)}) collective-permute-start(bf16[112,768]{1,0:T(8,128)(2,1)S(1)} %constant_dynamic-update-slice_fusion.3), channel_id=1, source_target_pairs={{0,16},{4,20},{8,24},{12,28},{16,0},{20,4},{24,8},{28,12},{1,17},{... | collective-permute-start | bytes 516104 | tf_op jit(solution)/shard_map/ppermute | solution.py:59
  9.9 19.0 %collective-permute-start.9 = (bf16[112,768]{1,0:T(8,128)(2,1)S(1)}, bf16[112,768]{1,0:T(8,128)(2,1)S(1)}, u32[]{:S(2)}, u32[]{:S(2)}) collective-permute-start(bf16[112,768]{1,0:T(8,128)(2,1)S(1)} %constant_dynamic-update-slice_fusion.3), channel_id=1, source_target_pairs={{0,8},{4,12},{8,0},{12,4},{16,24},{20,28},{24,16},{28,20},{1,9},{5... | collective-permute-start | bytes 516104 | tf_op jit(solution)/shard_map/ppermute | solution.py:59
  24.9 35.4 %collective-permute-start.8 = (bf16[512,896]{1,0:T(8,128)(2,1)S(1)}, bf16[512,896]{1,0:T(8,128)(2,1)S(1)}, u32[]{:S(2)}, u32[]{:S(2)}) collective-permute-start(bf16[512,896]{1,0:T(8,128)(2,1)S(1)} %collective-permute-done.7.refs_2_), channel_id=1, source_target_pairs={{0,1},{1,0},{2,3},{3,2},{4,5},{5,4},{6,7},{7,6},{8,9},{9,8},{10,11... | collective-permute-start | bytes 2752520 | tf_op jit(solution)/shard_map/ppermute | solution.py:59
  25.0 11.7 %collective-permute-start.2 = (bf16[560,256]{1,0:T(8,128)(2,1)S(1)}, bf16[560,256]{1,0:T(8,128)(2,1)S(1)}, u32[]{:S(2)}, u32[]{:S(2)}) collective-permute-start(bf16[560,256]{1,0:T(8,128)(2,1)S(1)} %maximum_dynamic-update-slice_fusion), channel_id=1, source_target_pairs={{0,24},{1,25},{2,26},{3,27},{4,28},{5,29},{6,30},{7,31},{8,16},{9,... | collective-permute-start | bytes 860168 | tf_op jit(solution)/shard_map/ppermute | solution.py:183
  29.0 31.3 %collective-permute-start.12 = (bf16[4,112,768]{2,1,0:T(8,128)(2,1)S(1)}, bf16[4,112,768]{2,1,0:T(8,128)(2,1)S(1)}, u32[]{:S(2)}, u32[]{:S(2)}) collective-permute-start(bf16[4,112,768]{2,1,0:T(8,128)(2,1)S(1)} %pad_maximum_fusion.6.near_ref), channel_id=1, source_target_pairs={{0,4},{4,0},{8,12},{12,8},{16,20},{20,16},{24,28},{28,24},{1,5},{5... | collective-permute-start | bytes 2064392 | tf_op jit(solution)/shard_map/ppermute | solution.py:59
  30.6 23.5 %collective-permute-start.1 = (bf16[560,256]{1,0:T(8,128)(2,1)S(1)}, bf16[560,256]{1,0:T(8,128)(2,1)S(1)}, u32[]{:S(2)}, u32[]{:S(2)}) collective-permute-start(bf16[560,256]{1,0:T(8,128)(2,1)S(1)} %maximum_dynamic-update-slice_fusion), channel_id=1, source_target_pairs={{0,16},{1,17},{2,18},{3,19},{4,20},{5,21},{6,22},{7,23},{8,24},{9,... | collective-permute-start | bytes 860168 | tf_op jit(solution)/shard_map/ppermute | solution.py:183
  36.7 23.4 %collective-permute-start = (bf16[560,256]{1,0:T(8,128)(2,1)S(1)}, bf16[560,256]{1,0:T(8,128)(2,1)S(1)}, u32[]{:S(2)}, u32[]{:S(2)}) collective-permute-start(bf16[560,256]{1,0:T(8,128)(2,1)S(1)} %maximum_dynamic-update-slice_fusion), channel_id=1, source_target_pairs={{0,8},{1,9},{2,10},{3,11},{4,12},{5,13},{6,14},{7,15},{8,0},{9,1},... | collective-permute-start | bytes 860168 | tf_op jit(solution)/shard_map/ppermute | solution.py:183
  61.3 16.0 %collective-permute-start.14 = (bf16[4,560,256]{2,1,0:T(8,128)(2,1)S(1)}, bf16[4,560,256]{2,1,0:T(8,128)(2,1)}, u32[]{:S(2)}, u32[]{:S(2)}) collective-permute-start(bf16[4,560,256]{2,1,0:T(8,128)(2,1)S(1)} %pad_maximum_fusion.4), channel_id=1, source_target_pairs={{0,2},{1,5},{2,0},{3,7},{4,6},{5,1},{6,4},{7,3},{8,10},{9,13},{10,... | collective-permute-start | bytes 3440648 | tf_op jit(solution)/shard_map/ppermute | solution.py:187
  78.7 36.4 %collective-permute-start.15 = (bf16[8,560,256]{2,1,0:T(8,128)(2,1)S(1)}, bf16[8,560,256]{2,1,0:T(8,128)(2,1)}, u32[]{:S(2)}, u32[]{:S(2)}) collective-permute-start(bf16[8,560,256]{2,1,0:T(8,128)(2,1)S(1)} %pad_maximum_fusion.2.refs_0_), channel_id=1, source_target_pairs={{0,4},{1,3},{2,6},{3,1},{4,0},{5,7},{6,2},{7,5},{8,12},{9,11},{10,... | collective-permute-start | bytes 6881288 | tf_op jit(solution)/shard_map/ppermute | solution.py:193
  81.4 33.7 %collective-permute-start.13 = (bf16[256,896]{1,0:T(8,128)(2,1)S(1)}, bf16[256,896]{1,0:T(8,128)(2,1)}, u32[]{:S(2)}, u32[]{:S(2)}) collective-permute-start(bf16[256,896]{1,0:T(8,128)(2,1)S(1)} %bitcast.157), channel_id=1, source_target_pairs={{0,1},{1,2},{2,3},{4,5},{5,6},{6,7},{8,9},{9,10},{10,11},{12,13},{... | collective-permute-start | bytes 1376264 | tf_op jit(solution)/shard_map/ppermute | solution.py:1004
  83.6 30.8 %collective-permute-start.3 = (bf16[224,896]{1,0:T(8,128)(2,1)S(1)}, bf16[224,896]{1,0:T(8,128)(2,1)}, u32[]{:S(2)}, u32[]{:S(2)}) collective-permute-start(bf16[224,896]{1,0:T(8,128)(2,1)S(1)} %maximum_maximum_fusion), channel_id=1, source_target_pairs={{0,8},{1,9},{2,10},{3,11},{4,12},{5,13},{6,14},{7,15},{8,0},{9,1},... | collective-permute-start | bytes 1204232 | tf_op jit(solution)/shard_map/ppermute | solution.py:183
  83.7 31.4 %collective-permute-start.4 = (bf16[224,896]{1,0:T(8,128)(2,1)S(1)}, bf16[224,896]{1,0:T(8,128)(2,1)}, u32[]{:S(2)}, u32[]{:S(2)}) collective-permute-start(bf16[224,896]{1,0:T(8,128)(2,1)S(1)} %maximum_maximum_fusion), channel_id=1, source_target_pairs={{0,16},{1,17},{2,18},{3,19},{4,20},{5,21},{6,22},{7,23},{8,24},{9,... | collective-permute-start | bytes 1204232 | tf_op jit(solution)/shard_map/ppermute | solution.py:183
  86.8 28.4 %collective-permute-start.5 = (bf16[224,896]{1,0:T(8,128)(2,1)S(1)}, bf16[224,896]{1,0:T(8,128)(2,1)}, u32[]{:S(2)}, u32[]{:S(2)}) collective-permute-start(bf16[224,896]{1,0:T(8,128)(2,1)S(1)} %maximum_maximum_fusion), channel_id=1, source_target_pairs={{0,24},{1,25},{2,26},{3,27},{4,28},{5,29},{6,30},{7,31},{8,16},{9,... | collective-permute-start | bytes 1204232 | tf_op jit(solution)/shard_map/ppermute | solution.py:183
  114.4 23.6 %collective-permute-start.19 = (bf16[8,560,256]{2,1,0:T(8,128)(2,1)S(1)}, bf16[8,560,256]{2,1,0:T(8,128)(2,1)}, u32[]{:S(2)}, u32[]{:S(2)}) collective-permute-start(bf16[8,560,256]{2,1,0:T(8,128)(2,1)S(1)} %pad_maximum_fusion.2.refs_0_), channel_id=1, source_target_pairs={{0,1},{1,0},{2,3},{3,2},{4,5},{5,4},{6,7},{7,6},{8,9},{9,8},{10,11... | collective-permute-start | bytes 6881288 | tf_op jit(solution)/shard_map/ppermute | solution.py:199
  115.1 22.9 %collective-permute-start.20 = (bf16[8,560,256]{2,1,0:T(8,128)(2,1)}, bf16[8,560,256]{2,1,0:T(8,128)(2,1)}, u32[]{:S(2)}, u32[]{:S(2)}) collective-permute-start(bf16[8,560,256]{2,1,0:T(8,128)(2,1)} %collective-permute-done.15.refs_1_), channel_id=1, source_target_pairs={{0,1},{1,0},{2,3},{3,2},{4,5},{5,4},{6,7},{7,6},{8,9},{9,8},{10,11... | collective-permute-start | bytes 6881288 | tf_op jit(solution)/shard_map/ppermute | solution.py:199
  117.2 5.6 %collective-permute-start.16 = (bf16[512,256]{1,0:T(8,128)(2,1)S(1)}, bf16[512,256]{1,0:T(8,128)(2,1)S(1)}, u32[]{:S(2)}, u32[]{:S(2)}) collective-permute-start(bf16[512,256]{1,0:T(8,128)(2,1)S(1)} %get-tuple-element.248), channel_id=1, source_target_pairs={{0,1},{1,0},{2,3},{3,2},{4,5},{5,4},{6,7},{7,6},{8,9},{9,8},{10,11... | collective-permute-start | bytes 786440 | tf_op jit(solution)/shard_map/ppermute | solution.py:59
  117.7 9.2 %collective-permute-start.17 = (bf16[512,256]{1,0:T(8,128)(2,1)S(1)}, bf16[512,256]{1,0:T(8,128)(2,1)S(1)}, u32[]{:S(2)}, u32[]{:S(2)}) collective-permute-start(bf16[512,256]{1,0:T(8,128)(2,1)S(1)} %get-tuple-element.247), channel_id=1, source_target_pairs={{0,2},{1,3},{2,0},{3,1},{4,6},{5,7},{6,4},{7,5},{8,10},{9,11},{10,... | collective-permute-start | bytes 786440 | tf_op jit(solution)/shard_map/ppermute | solution.py:59
  118.4 12.1 %collective-permute-start.18 = (bf16[512,256]{1,0:T(8,128)(2,1)S(1)}, bf16[512,256]{1,0:T(8,128)(2,1)S(1)}, u32[]{:S(2)}, u32[]{:S(2)}) collective-permute-start(bf16[512,256]{1,0:T(8,128)(2,1)S(1)} %get-tuple-element.246), channel_id=1, source_target_pairs={{0,3},{1,2},{2,1},{3,0},{4,7},{5,6},{6,5},{7,4},{8,11},{9,10},{10,... | collective-permute-start | bytes 786440 | tf_op jit(solution)/shard_map/ppermute | solution.py:59
  133.7 21.1 %collective-permute-start.21 = (bf16[4,224,896]{2,1,0:T(8,128)(2,1)}, bf16[4,224,896]{2,1,0:T(8,128)(2,1)}, u32[]{:S(2)}, u32[]{:S(2)}) collective-permute-start(bf16[4,224,896]{2,1,0:T(8,128)(2,1)} %pad_maximum_fusion.3), channel_id=1, source_target_pairs={{0,2},{1,5},{2,0},{3,7},{4,6},{5,1},{6,4},{7,3},{8,10},{9,13},{10,... | collective-permute-start | bytes 4816904 | tf_op jit(solution)/shard_map/ppermute | solution.py:187
  156.4 38.1 %collective-permute-start.22 = (bf16[8,224,896]{2,1,0:T(8,128)(2,1)S(1)}, bf16[8,224,896]{2,1,0:T(8,128)(2,1)}, u32[]{:S(2)}, u32[]{:S(2)}) collective-permute-start(bf16[8,224,896]{2,1,0:T(8,128)(2,1)S(1)} %constant_dynamic-update-slice_fusion.6.refs_0_), channel_id=1, source_target_pairs={{0,4},{1,3},{2,6},{3,1},{4,0},{5,7},{6,2},{7,5},{8,12},{9,11},{10,... | collective-permute-start | bytes 9633800 | tf_op jit(solution)/shard_map/ppermute | solution.py:193
  159.0 39.1 %collective-permute-start.23 = (bf16[8,224,896]{2,1,0:T(8,128)(2,1)S(1)}, bf16[8,224,896]{2,1,0:T(8,128)(2,1)}, u32[]{:S(2)}, u32[]{:S(2)}) collective-permute-start(bf16[8,224,896]{2,1,0:T(8,128)(2,1)S(1)} %constant_dynamic-update-slice_fusion.6.refs_0_), channel_id=1, source_target_pairs={{0,1},{1,0},{2,3},{3,2},{4,5},{5,4},{6,7},{7,6},{8,9},{9,8},{10,11... | collective-permute-start | bytes 9633800 | tf_op jit(solution)/shard_map/ppermute | solution.py:199
  194.6 6.1 %collective-permute-start.24 = (bf16[8,224,896]{2,1,0:T(8,128)(2,1)}, bf16[8,224,896]{2,1,0:T(8,128)(2,1)}, u32[]{:S(2)}, u32[]{:S(2)}) collective-permute-start(bf16[8,224,896]{2,1,0:T(8,128)(2,1)} %collective-permute-done.22.refs_1_), channel_id=1, source_target_pairs={{0,1},{1,0},{2,3},{3,2},{4,5},{5,4},{6,7},{7,6},{8,9},{9,8},{10,11... | collective-permute-start | bytes 9633800 | tf_op jit(solution)/shard_map/ppermute | solution.py:199
  254.4 12.3 %collective-permute-start.25 = (bf16[2,2,4,224,896]{4,3,2,1,0:T(8,128)(2,1)}, bf16[2,2,4,224,896]{4,3,2,1,0:T(8,128)(2,1)S(1)}, u32[]{:S(2)}, u32[]{:S(2)}) collective-permute-start(bf16[2,2,4,224,896]{4,3,2,1,0:T(8,128)(2,1)} %get-tuple-element.143), channel_id=1, source_target_pairs={{0,1},{1,0},{2,3},{3,2},{4,5},{5,4},{6,7},{7,6},{8,9},{9,8},{10,11... | collective-permute-start | bytes 19267592 | tf_op jit(solution)/shard_map/ppermute | solution.py:199
  270.2 47.0 %collective-permute-start.26 = (bf16[2,4,224,896]{3,2,1,0:T(8,128)(2,1)}, bf16[2,4,224,896]{3,2,1,0:T(8,128)(2,1)}, u32[]{:S(2)}, u32[]{:S(2)}) collective-permute-start(bf16[2,4,224,896]{3,2,1,0:T(8,128)(2,1)} %fusion.10), channel_id=1, source_target_pairs={{0,4},{1,3},{2,6},{3,1},{4,0},{5,7},{6,2},{7,5},{8,12},{9,11},{10,... | collective-permute-start | bytes 9633800 | tf_op jit(solution)/shard_map/ppermute | solution.py:193
  329.7 35.2 %collective-permute-start.31 = (bf16[2,2,4,560,256]{4,3,2,1,0:T(8,128)(2,1)}, bf16[2,2,4,560,256]{4,3,2,1,0:T(8,128)(2,1)}, u32[]{:S(2)}, u32[]{:S(2)}) collective-permute-start(bf16[2,2,4,560,256]{4,3,2,1,0:T(8,128)(2,1)} %get-tuple-element.162), channel_id=1, source_target_pairs={{0,1},{1,0},{2,3},{3,2},{4,5},{5,4},{6,7},{7,6},{8,9},{9,8},{10,11... | collective-permute-start | bytes 13762568 | tf_op jit(solution)/shard_map/ppermute | solution.py:199
  334.3 35.7 %collective-permute-start.27 = (bf16[4,224,896]{2,1,0:T(8,128)(2,1)}, bf16[4,224,896]{2,1,0:T(8,128)(2,1)S(1)}, u32[]{:S(2)}, u32[]{:S(2)}) collective-permute-start(bf16[4,224,896]{2,1,0:T(8,128)(2,1)} %fusion.11), channel_id=1, source_target_pairs={{0,2},{1,5},{2,0},{3,7},{4,6},{5,1},{6,4},{7,3},{8,10},{9,13},{10,... | collective-permute-start | bytes 4816904 | tf_op jit(solution)/shard_map/ppermute | solution.py:187
  339.6 16.4 %collective-permute-start.28 = (bf16[512,256]{1,0:T(8,128)(2,1)}, bf16[512,256]{1,0:T(8,128)(2,1)S(1)}, u32[]{:S(2)}, u32[]{:S(2)}) collective-permute-start(bf16[512,256]{1,0:T(8,128)(2,1)} %get-tuple-element.157), channel_id=1, source_target_pairs={{0,1},{1,0},{2,3},{3,2},{4,5},{5,4},{6,7},{7,6},{8,9},{9,8},{10,11... | collective-permute-start | bytes 786440 | tf_op jit(solution)/shard_map/ppermute | solution.py:59
  339.6 24.1 %collective-permute-start.29 = (bf16[512,256]{1,0:T(8,128)(2,1)}, bf16[512,256]{1,0:T(8,128)(2,1)S(1)}, u32[]{:S(2)}, u32[]{:S(2)}) collective-permute-start(bf16[512,256]{1,0:T(8,128)(2,1)} %get-tuple-element.158), channel_id=1, source_target_pairs={{0,2},{1,3},{2,0},{3,1},{4,6},{5,7},{6,4},{7,5},{8,10},{9,11},{10,... | collective-permute-start | bytes 786440 | tf_op jit(solution)/shard_map/ppermute | solution.py:59
  341.0 23.9 %collective-permute-start.30 = (bf16[512,256]{1,0:T(8,128)(2,1)}, bf16[512,256]{1,0:T(8,128)(2,1)S(1)}, u32[]{:S(2)}, u32[]{:S(2)}) collective-permute-start(bf16[512,256]{1,0:T(8,128)(2,1)} %get-tuple-element.159), channel_id=1, source_target_pairs={{0,3},{1,2},{2,1},{3,0},{4,7},{5,6},{6,5},{7,4},{8,11},{9,10},{10,... | collective-permute-start | bytes 786440 | tf_op jit(solution)/shard_map/ppermute | solution.py:59
  368.6 66.4 %collective-permute-start.35 = (bf16[2,4,560,256]{3,2,1,0:T(8,128)(2,1)}, bf16[2,4,560,256]{3,2,1,0:T(8,128)(2,1)}, u32[]{:S(2)}, u32[]{:S(2)}) collective-permute-start(bf16[2,4,560,256]{3,2,1,0:T(8,128)(2,1)} %fusion.14), channel_id=1, source_target_pairs={{0,4},{1,3},{2,6},{3,1},{4,0},{5,7},{6,2},{7,5},{8,12},{9,11},{10,... | collective-permute-start | bytes 6881288 | tf_op jit(solution)/shard_map/ppermute | solution.py:193
  371.3 63.7 %collective-permute-start.36 = (bf16[256,896]{1,0:T(8,128)(2,1)}, bf16[256,896]{1,0:T(8,128)(2,1)}, u32[]{:S(2)}, u32[]{:S(2)}) collective-permute-start(bf16[256,896]{1,0:T(8,128)(2,1)} %slice.250), channel_id=1, source_target_pairs={{1,0},{2,1},{3,2},{5,4},{6,5},{7,6},{9,8},{10,9},{11,10},{13,12},{... | collective-permute-start | bytes 1376264 | tf_op jit(solution)/shard_map/ppermute | solution.py:1113
  377.4 57.5 %collective-permute-start.32 = (bf16[224,896]{1,0:T(8,128)(2,1)}, bf16[224,896]{1,0:T(8,128)(2,1)S(1)}, u32[]{:S(2)}, u32[]{:S(2)}) collective-permute-start(bf16[224,896]{1,0:T(8,128)(2,1)} %get-tuple-element.241), channel_id=1, source_target_pairs={{0,8},{1,9},{2,10},{3,11},{4,12},{5,13},{6,14},{7,15},{8,0},{9,1},... | collective-permute-start | bytes 1204232 | tf_op jit(solution)/shard_map/ppermute | solution.py:183
  385.0 49.9 %collective-permute-start.33 = (bf16[224,896]{1,0:T(8,128)(2,1)}, bf16[224,896]{1,0:T(8,128)(2,1)S(1)}, u32[]{:S(2)}, u32[]{:S(2)}) collective-permute-start(bf16[224,896]{1,0:T(8,128)(2,1)} %get-tuple-element.240), channel_id=1, source_target_pairs={{0,16},{1,17},{2,18},{3,19},{4,20},{5,21},{6,22},{7,23},{8,24},{9,... | collective-permute-start | bytes 1204232 | tf_op jit(solution)/shard_map/ppermute | solution.py:183
  386.0 48.9 %collective-permute-start.34 = (bf16[224,896]{1,0:T(8,128)(2,1)}, bf16[224,896]{1,0:T(8,128)(2,1)S(1)}, u32[]{:S(2)}, u32[]{:S(2)}) collective-permute-start(bf16[224,896]{1,0:T(8,128)(2,1)} %get-tuple-element.239), channel_id=1, source_target_pairs={{0,24},{1,25},{2,26},{3,27},{4,28},{5,29},{6,30},{7,31},{8,16},{9,... | collective-permute-start | bytes 1204232 | tf_op jit(solution)/shard_map/ppermute | solution.py:183
  438.1 17.2 %collective-permute-start.37 = (bf16[4,560,256]{2,1,0:T(8,128)(2,1)S(1)}, bf16[4,560,256]{2,1,0:T(8,128)(2,1)}, u32[]{:S(2)}, u32[]{:S(2)}) collective-permute-start(bf16[4,560,256]{2,1,0:T(8,128)(2,1)S(1)} %fusion.17), channel_id=1, source_target_pairs={{0,2},{1,5},{2,0},{3,7},{4,6},{5,1},{6,4},{7,3},{8,10},{9,13},{10,... | collective-permute-start | bytes 3440648 | tf_op jit(solution)/shard_map/ppermute | solution.py:187
  462.4 8.9 %collective-permute-start.40 = (bf16[512,896]{1,0:T(8,128)(2,1)}, bf16[512,896]{1,0:T(8,128)(2,1)}, u32[]{:S(2)}, u32[]{:S(2)}) collective-permute-start(bf16[512,896]{1,0:T(8,128)(2,1)} %get-tuple-element.238), channel_id=1, source_target_pairs={{0,1},{1,0},{2,3},{3,2},{4,5},{5,4},{6,7},{7,6},{8,9},{9,8},{10,11... | collective-permute-start | bytes 2752520 | tf_op jit(solution)/shard_map/ppermute | solution.py:59
  463.7 21.7 %collective-permute-start.41 = (bf16[4,112,768]{2,1,0:T(8,128)(2,1)}, bf16[4,112,768]{2,1,0:T(8,128)(2,1)S(1)}, u32[]{:S(2)}, u32[]{:S(2)}) collective-permute-start(bf16[4,112,768]{2,1,0:T(8,128)(2,1)} %get-tuple-element.189), channel_id=1, source_target_pairs={{0,4},{4,0},{8,12},{12,8},{16,20},{20,16},{24,28},{28,24},{1,5},{5... | collective-permute-start | bytes 2064392 | tf_op jit(solution)/shard_map/ppermute | solution.py:59
  464.7 20.7 %collective-permute-start.42 = (bf16[512,896]{1,0:T(8,128)(2,1)S(1)}, bf16[512,896]{1,0:T(8,128)(2,1)S(1)}, u32[]{:S(2)}, u32[]{:S(2)}) collective-permute-start(bf16[512,896]{1,0:T(8,128)(2,1)S(1)} %get-tuple-element.237), channel_id=1, source_target_pairs={{0,1},{1,0},{2,3},{3,2},{4,5},{5,4},{6,7},{7,6},{8,9},{9,8},{10,11... | collective-permute-start | bytes 2752520 | tf_op jit(solution)/shard_map/ppermute | solution.py:59
  468.3 15.3 %collective-permute-start.38 = (bf16[560,256]{1,0:T(8,128)(2,1)S(1)}, bf16[560,256]{1,0:T(8,128)(2,1)S(1)}, u32[]{:S(2)}, u32[]{:S(2)}) collective-permute-start(bf16[560,256]{1,0:T(8,128)(2,1)S(1)} %get-tuple-element.245), channel_id=1, source_target_pairs={{0,8},{1,9},{2,10},{3,11},{4,12},{5,13},{6,14},{7,15},{8,0},{9,1},... | collective-permute-start | bytes 860168 | tf_op jit(solution)/shard_map/ppermute | solution.py:183
  469.4 16.1 %collective-permute-start.39 = (bf16[560,256]{1,0:T(8,128)(2,1)S(1)}, bf16[560,256]{1,0:T(8,128)(2,1)S(1)}, u32[]{:S(2)}, u32[]{:S(2)}) collective-permute-start(bf16[560,256]{1,0:T(8,128)(2,1)S(1)} %get-tuple-element.244), channel_id=1, source_target_pairs={{0,16},{1,17},{2,18},{3,19},{4,20},{5,21},{6,22},{7,23},{8,24},{9,... | collective-permute-start | bytes 860168 | tf_op jit(solution)/shard_map/ppermute | solution.py:183
  486.8 8.8 %collective-permute-start.43 = (bf16[112,768]{1,0:T(8,128)(2,1)S(1)}, bf16[112,768]{1,0:T(8,128)(2,1)S(1)}, u32[]{:S(2)}, u32[]{:S(2)}) collective-permute-start(bf16[112,768]{1,0:T(8,128)(2,1)S(1)} %get-tuple-element.254), channel_id=1, source_target_pairs={{0,8},{1,9},{2,10},{3,11},{4,12},{5,13},{6,14},{7,15},{8,0},{9,1},... | collective-permute-start | bytes 516104 | tf_op jit(solution)/shard_map/ppermute | solution.py:183
  487.3 37.5 %collective-permute-start.46 = (bf16[560,256]{1,0:T(8,128)(2,1)}, bf16[560,256]{1,0:T(8,128)(2,1)}, u32[]{:S(2)}, u32[]{:S(2)}) collective-permute-start(bf16[560,256]{1,0:T(8,128)(2,1)} %get-tuple-element.243), channel_id=1, source_target_pairs={{0,24},{1,25},{2,26},{3,27},{4,28},{5,29},{6,30},{7,31},{8,16},{9,... | collective-permute-start | bytes 860168 | tf_op jit(solution)/shard_map/ppermute | solution.py:183
  490.1 34.8 %collective-permute-start.44 = (bf16[112,768]{1,0:T(8,128)(2,1)}, bf16[112,768]{1,0:T(8,128)(2,1)}, u32[]{:S(2)}, u32[]{:S(2)}) collective-permute-start(bf16[112,768]{1,0:T(8,128)(2,1)} %get-tuple-element.253), channel_id=1, source_target_pairs={{0,16},{1,17},{2,18},{3,19},{4,20},{5,21},{6,22},{7,23},{8,24},{9,... | collective-permute-start | bytes 516104 | tf_op jit(solution)/shard_map/ppermute | solution.py:183
  491.1 33.8 %collective-permute-start.45 = (bf16[112,768]{1,0:T(8,128)(2,1)}, bf16[112,768]{1,0:T(8,128)(2,1)}, u32[]{:S(2)}, u32[]{:S(2)}) collective-permute-start(bf16[112,768]{1,0:T(8,128)(2,1)} %get-tuple-element.252), channel_id=1, source_target_pairs={{0,24},{1,25},{2,26},{3,27},{4,28},{5,29},{6,30},{7,31},{8,16},{9,... | collective-permute-start | bytes 516104 | tf_op jit(solution)/shard_map/ppermute | solution.py:183
  493.6 31.3 %collective-permute-start.47 = (bf16[512,896]{1,0:T(8,128)(2,1)}, bf16[512,896]{1,0:T(8,128)(2,1)}, u32[]{:S(2)}, u32[]{:S(2)}) collective-permute-start(bf16[512,896]{1,0:T(8,128)(2,1)} %add_convert_fusion.3), channel_id=1, source_target_pairs={{0,2},{1,3},{2,0},{3,1},{4,6},{5,7},{6,4},{7,5},{8,10},{9,11},{10,... | collective-permute-start | bytes 2752520 | tf_op jit(solution)/shard_map/ppermute | solution.py:59
  (69 other events, 766.1 us)

commit v5 on v4

--- a/solution.py
+++ b/solution.py
@@ -1117,7 +1117,15 @@
         last_a = sum_second(last_kept, last_got, last_far)
         last_near = over_a(last_a)
         own_y, other_y = triple_pieces(place, first_normed, after(triple_grad, last_a))
-        other_y, last_near, triple_grad = lax.optimization_barrier((other_y, last_near, triple_grad))
+        feed_own = wide_sum(*feed_own)
+        part = feed_own.shape[0] // 2
+        sum_inner = feed_own[:part]
+        sum_outer = feed_own[part:].reshape(part, 4, model // 4)
+        sum_outer = sum_outer.transpose(1, 0, 2).reshape(4 * part, -1)
+        fillers, other_y, last_near, triple_grad = joint(
+            [sum_inner, sum_outer], other_y, last_near, triple_grad
+        )
+        sum_inner, sum_outer = fillers
         got_y = swap(other_y, "dp", 1)
     else:
         grad_states = joined_states(states_round, returned)
@@ -1137,13 +1145,8 @@
         arrived = swap(leaves, "seq", 2)
         line = rounded(wide_sum(own_y, got_y))
         own = [line[0]] + all_over_z(line)
-        feed_own, returned, hidden_act, _ = joint(feed_own, returned, hidden_act, own[1])
+        returned, hidden_act = lax.optimization_barrier((returned, hidden_act, own[1]))[:2]
         outcome = rounded(after_cross + linear(hidden_act, outer_full))
-        feed_own = wide_sum(*feed_own)
-        part = feed_own.shape[0] // 2
-        sum_inner = feed_own[:part]
-        sum_outer = feed_own[part:].reshape(part, 4, model // 4)
-        sum_outer = sum_outer.transpose(1, 0, 2).reshape(4 * part, -1)
         grad_states = joined_states(states_round, returned)
     else:
         outcome = rounded(after_cross + linear(hidden_act, outer_full))
@@ -1165,7 +1168,7 @@
     if fast:
         size = small.shape[0]
         small = jnp.pad(small, (0, -size % 1024)).reshape(-1, 128)
-        small = small_sum(after(small, own[1], outcome, grad_states, sum_inner, sum_outer))
+        small = small_sum(after(small, own[1], outcome, grad_states))
         rest, small = joint(own[1:] + last_own[-1:] + [arrived], small)
         own[1:], last_own[-1], arrived = rest[:-2], rest[-2], rest[-1]
         blocks[0] = wide_sum(partial[0], near_zero, arrived)

time: 545 us -> 547 us (level)
  Pallas kernels: 213 us -> 221 us
    pallas_call x1, Pallas kernels: 11.4 us -> 19.1 us  [small_sum(): pl.pallas_call(functools.partial(small_sum_kernel, dp, seq), in_specs=[vm...]
    unnamed x144 -> x128, local copies, waits for them, and re-layouts: 15.8 us -> 15.6 us
  transfers between devices with their start and end apart: 48 -> 48, of which waited for: 16 -> 16; matrix products, arithmetic and copies ran while one was open for 20% -> 19% of each run, Pallas kernels for 32% -> 34%
where the time goes in v5:
time: 547 us; the launch traced here: 541 us
  Pallas kernels  221 us (40%)
  matrix products  87.3 us (16%)
  waiting for transfers between devices  77.7 us (14%)
  starting transfers between devices  72 us (13%)
  other arithmetic  47.2 us (9%)
  local copies, waits for them, and re-layouts  34.2 us (6%)
    dot_general x13, matrix products, dot(): lax.dot_general(a, b, (((ca,), (cb,)), ((), ())), preferred_element_type=...  87.3 us
    pallas_call x1, Pallas kernels, self_bwd(): pl.pallas_call(self_bwd_kernel, grid=(blocks,), in_specs=[smem_spec(), sm...  46.6 us
    pallas_call x5, Pallas kernels, group_grad(): pl.pallas_call(kernel, grid_spec=pltpu.PrefetchScalarGridSpec(num_scalar_...  40.6 us
    ppermute x15, starting transfers between devices, over_z(): lax.ppermute(value, BOTH, device_pairs(lambda z, y, x, c: (z ^ k, y, x, c)))  39 us
    ppermute x15, waiting for transfers between devices, over_z(): lax.ppermute(value, BOTH, device_pairs(lambda z, y, x, c: (z ^ k, y, x, c)))  29 us
    ppermute x17, waiting for transfers between devices, swap(): return lax.ppermute(value, axis, [(i, i ^ by) for i in range(peers)])  28.1 us
    convert_element_type x13, other arithmetic, rounded(): return v.astype(BF)  27.5 us
    pallas_call x1, Pallas kernels, self_fwd(): pl.pallas_call(self_fwd_kernel, grid=(blocks,), in_specs=[smem_spec(), sm...  26 us
  transfers between devices with their start and end apart: 48, of which 16 were waited for; matrix products, arithmetic and copies ran while one was open for 19% of the time, Pallas kernels for 34%

profile of v5, /device:TPU:0, one launch (start us, length us, event | category | flops | bytes accessed | tf_op | source)
XLA Modules:
  0.0 541.2 jit_solution(988316229287781399)
XLA Ops:
  6.2 3.6 collective-permute-start.11
  14.7 10.3 %collective-permute-done.7.refs_2_ = bf16[512,896]{1,0:T(8,128)(2,1)S(1)} collective-permute-done((bf16[512,896]{1,0:T(8,128)(2,1)}, bf16[512,896]{1,0:T(8,128)(2,1)S(1)}, u32[]{:S(2)}, u32[]{:S(2)}) %collective-permute-start.7) | collective-permute-done | bytes 917536 | tf_op jit(solution)/shard_map/ppermute | solution.py:59
  25.0 3.9 collective-permute-start.2
  30.6 6.1 %collective-permute-done.2 = bf16[560,256]{1,0:T(8,128)(2,1)S(1)} collective-permute-done((bf16[560,256]{1,0:T(8,128)(2,1)S(1)}, bf16[560,256]{1,0:T(8,128)(2,1)S(1)}, u32[]{:S(2)}, u32[]{:S(2)}) %collective-permute-start.2) | collective-permute-done | bytes 286752 | tf_op jit(solution)/shard_map/ppermute | solution.py:183
  36.7 12.2 %collective-permute-start = (bf16[560,256]{1,0:T(8,128)(2,1)S(1)}, bf16[560,256]{1,0:T(8,128)(2,1)S(1)}, u32[]{:S(2)}, u32[]{:S(2)}) collective-permute-start(bf16[560,256]{1,0:T(8,128)(2,1)S(1)} %maximum_dynamic-update-slice_fusion), channel_id=1, source_target_pairs={{0,8},{1,9},{2,10},{3,11},{4,12},{5,13},{6,14},{7,15},{8,0},{9,1},... | collective-permute-start | bytes 860168 | tf_op jit(solution)/shard_map/ppermute | solution.py:183
  48.8 5.2 collective-permute-done.1
  54.1 6.0 %collective-permute-done = bf16[560,256]{1,0:T(8,128)(2,1)S(1)} collective-permute-done((bf16[560,256]{1,0:T(8,128)(2,1)S(1)}, bf16[560,256]{1,0:T(8,128)(2,1)S(1)}, u32[]{:S(2)}, u32[]{:S(2)}) %collective-permute-start) | collective-permute-done | bytes 286752 | tf_op jit(solution)/shard_map/ppermute | solution.py:183
  64.6 10.8 %shard_map.262 = (bf16[2048,896]{1,0:T(8,128)(2,1)}, bf16[2048,768]{1,0:T(8,128)(2,1)}, bf16[896,768]{1,0:T(8,128)(2,1)}) custom-call(s32[4]{0:T(128)} %pad_add_fusion.place_ref.refs_0_, bf16[4,112,768]{2,1,0:T(8,128)(2,1)} %copy-done.29, bf16[4,112,768]{2,1,0:T(8,128)(2,1)} %copy-done.36, f32[1,896]{1,0:T(1,128)} %get-tuple-element.269.gain_ref, ...), custom_call_target="tpu_custom_call" | custom-call | flops 56371444 | bytes 293601 | tf_op jit(solution)/shard_map/pallas_call | solution.py:111
  83.7 3.0 collective-permute-start.4
  88.8 26.0 %shard_map.263 = (bf16[2048,256]{1,0:T(8,128)(2,1)}, f32[8,8,256]{2,1,0:T(8,128)}) custom-call(s32[1]{0:T(128)} %bitcast.1.pos_ref.mine_ref, f32[4,6]{1,0:T(4,128)} %copy.47.bias_ref, bf16[2048,768]{1,0:T(8,128)(2,1)} %get-tuple-element.117.qkv_ref), custom_call_target="tpu_custom_call" | custom-call | flops 85899344 | bytes 83886 | tf_op jit(solution)/shard_map/pallas_call | solution.py:652
  123.2 4.0 collective-permute-done.17.refs_2_
  127.2 3.7 collective-permute-done.18.refs_3_
  138.5 8.1 %shard_map.265 = (bf16[896,2048]{1,0:T(8,128)(2,1)}, bf16[896,1024]{1,0:T(8,128)(2,1)}, bf16[896,1024]{1,0:T(8,128)(2,1)}, bf16[896,1024]{1,0:T(8,128)(2,1)}) custom-call(s32[4]{0:T(128)} %pad_add_fusion.place_ref.refs_0_, bf16[8,560,256]{2,1,0:T(8,128)(2,1)} %copy-done.6, bf16[8,560,256]{2,1,0:T(8,128)(2,1)} %collective-permute-done.15.refs_1_, ...), custom_call_target="tpu_custom_call" | custom-call | tf_op jit(solution)/shard_map/pallas_call | solution.py:261
  146.6 3.0 multiply_reduce_fusion.6
  149.9 5.2 collective-permute-done.21
  163.2 12.0 %convolution_convert_fusion.k_ref.v_ref = bf16[2304,2048]{1,0:T(8,128)(2,1)} fusion(bf16[2304,896]{1,0:T(8,128)(2,1)S(1)} %pad_maximum_fusion.refs_1_, bf16[896,2048]{1,0:T(8,128)(2,1)S(1)} %copy-done.51), kind=kOutput, calls=%fused_computation | convolution fusion | flops 8460435456 | bytes 17235968 | tf_op jit(solution)/shard_map/dot_general | solution.py:24
  175.2 13.2 %shard_map.266.refs_1_ = bf16[512,1024]{1,0:T(8,128)(2,1)} custom-call(bf16[512,1024]{1,0:T(8,128)(2,1)} %convolution_convert_fusion.4.q_ref, bf16[2304,2048]{1,0:T(8,128)(2,1)} %convolution_convert_fusion.k_ref.v_ref, bf16[2304,2048]{1,0:T(8,128)(2,1)} %convolution_convert_fusion.k_ref.v_ref), custom_call_target="tpu_custom_call" | custom-call | flops 48318384 | bytes 188743 | tf_op jit(solution)/shard_map/pallas_call | solution.py:844
  188.4 6.5 %collective-permute-done.22.refs_1_ = bf16[8,224,896]{2,1,0:T(8,128)(2,1)} collective-permute-done((bf16[8,224,896]{2,1,0:T(8,128)(2,1)S(1)}, bf16[8,224,896]{2,1,0:T(8,128)(2,1)}, u32[]{:S(2)}, u32[]{:S(2)}) %collective-permute-start.22) | collective-permute-done | bytes 3211296 | tf_op jit(solution)/shard_map/ppermute | solution.py:193
  195.0 3.2 multiply_reduce_fusion.5
  201.1 12.5 %shard_map.267 = (bf16[896,3584]{1,0:T(8,128)(2,1)}, bf16[3584,896]{1,0:T(8,128)(2,1)}) custom-call(s32[4]{0:T(128)} %pad_add_fusion.place_ref.refs_0_, bf16[8,224,896]{2,1,0:T(8,128)(2,1)} %copy-done.18, bf16[8,224,896]{2,1,0:T(8,128)(2,1)} %collective-permute-done.22.refs_1_, bf16[8,224,896]{2,1,0:T(8,128)(2,1)} %collective-permute-done.23.refs_2_, ...), custom_call_target="tpu_custom_call" | custom-call | tf_op jit(solution)/shard_map/pallas_call | solution.py:307
  213.6 9.9 %multiply_convert_fusion = (bf16[512,3584]{1,0:T(8,128)(2,1)}, f32[512,3584]{1,0:T(8,128)S(1)}) fusion(bf16[512,896]{1,0:T(8,128)(2,1)S(1)} %multiply_convert_fusion.1.refs_1_, bf16[896,3584]{1,0:T(8,128)(2,1)} %get-tuple-element.137), kind=kOutput, calls=%fused_computation.16 | convolution fusion | flops 3304849408 | bytes 18350080 | tf_op jit(solution)/shard_map/dot_general | solution.py:24
  223.5 10.2 %fusion.6.refs_2_.refs_3_ = bf16[512,3584]{1,0:T(8,128)(2,1)} fusion(f32[512,3584]{1,0:T(8,128)S(1)} %get-tuple-element.278, bf16[3584,896]{1,0:T(8,128)(2,1)S(1)} %copy-done.50, bf16[1,512,896]{2,1,0:T(8,128)(2,1)S(1)} %copy-done.9), kind=kOutput, calls=%fused_computation.9 | convolution fusion | flops 3325034496 | bytes 18350080 | tf_op jit(solution)/shard_map/dot_general | solution.py:24
  233.7 11.0 %shard_map.268 = (bf16[2,2,4,224,896]{4,3,2,1,0:T(8,128)(2,1)}, bf16[2,2,4,224,896]{4,3,2,1,0:T(8,128)(2,1)}) custom-call(s32[4]{0:T(128)} %pad_add_fusion.place_ref.refs_0_, bf16[512,3584]{1,0:T(8,128)(2,1)} %get-tuple-element.189.left, bf16[512,896]{1,0:T(8,128)(2,1)} %bitcast.151), custom_call_target="tpu_custom_call" | custom-call | flops 65766688 | bytes 220200 | tf_op jit(solution)/shard_map/pallas_call | solution.py:388
  244.7 9.8 %shard_map.269 = (bf16[2,2,4,224,896]{4,3,2,1,0:T(8,128)(2,1)}, bf16[2,2,4,224,896]{4,3,2,1,0:T(8,128)(2,1)}) custom-call(s32[4]{0:T(128)} %pad_add_fusion.place_ref.refs_0_, bf16[512,896]{1,0:T(8,128)(2,1)} %copy-done.26, bf16[512,3584]{1,0:T(8,128)(2,1)} %fusion.6.refs_2_.refs_3_, ...), custom_call_target="tpu_custom_call", output_to_operand_aliasing={{0}: (4, {}), {1}: (5, {})} | custom-call | flops 65766688 | bytes 220200 | tf_op jit(solution)/shard_map/pallas_call | solution.py:441
  254.7 8.7 %multiply_reduce_fusion.1 = (f32[896]{0:T(1024)S(1)}, f32[512]{0:T(512)S(1)}, f32[512,896]{1,0:T(8,128)S(1)}) fusion(f32[512,896]{1,0:T(8,128)S(1)} %get-tuple-element.275, f32[512]{0:T(512)S(1)} %fusion.31, f32[896]{0:T(1024)S(1)} %get-tuple-element.227, bf16[512,3584]{1,0:T(8,128)(2,1)S(1)} %copy-done.3, bf16[896,3584]{1,0:T(8,128)(2,1)} %get-tuple-element.137), kind=kOutput, calls=%fused_computation.49 | convolution fusion | flops 3291085312 | bytes 13773824 | tf_op jit(solution)/shard_map/dot_general | solution.py:24
  271.4 5.8 %shard_map.271 = (bf16[2,2,4,560,256]{4,3,2,1,0:T(8,128)(2,1)}, bf16[2,2,4,560,256]{4,3,2,1,0:T(8,128)(2,1)}) custom-call(s32[4]{0:T(128)} %pad_add_fusion.place_ref.refs_0_, bf16[512,1024]{1,0:T(8,128)(2,1)} %shard_map.266.refs_1_, bf16[512,896]{1,0:T(8,128)(2,1)} %copy-done.25), custom_call_target="tpu_custom_call" | custom-call | flops 18790480 | bytes 76021 | tf_op jit(solution)/shard_map/pallas_call | solution.py:441
  277.2 21.0 %shard_map.270 = (bf16[512,1024]{1,0:T(8,128)(2,1)}, bf16[2304,2048]{1,0:T(8,128)(2,1)}) custom-call(bf16[512,1024]{1,0:T(8,128)(2,1)} %convolution_convert_fusion.4.q_ref, bf16[512,1024]{1,0:T(8,128)(2,1)} %convolution_convert_fusion.3.g_ref, bf16[2304,2048]{1,0:T(8,128)(2,1)} %convolution_convert_fusion.k_ref.v_ref, ...), custom_call_target="tpu_custom_call" | custom-call | flops 120795952 | bytes 377487 | tf_op jit(solution)/shard_map/pallas_call | solution.py:898
  298.2 4.8 shard_map.272
  302.9 14.5 %shard_map.273 = (bf16[2,2,4,560,256]{4,3,2,1,0:T(8,128)(2,1)}, bf16[2,2,4,560,256]{4,3,2,1,0:T(8,128)(2,1)}) custom-call(s32[4]{0:T(128)} %pad_add_fusion.place_ref.refs_0_, bf16[2304,896]{1,0:T(8,128)(2,1)} %copy-done.2, bf16[2304,2048]{1,0:T(8,128)(2,1)} %get-tuple-element.158.refs_2_.refs_3_, ...), custom_call_target="tpu_custom_call", output_to_operand_aliasing={{0}: (4, {}), {1}: (5, {})} | custom-call | flops 169114336 | bytes 344719 | tf_op jit(solution)/shard_map/pallas_call | solution.py:441
  317.4 4.0 multiply_reduce_fusion.2
  324.0 5.8 %shard_map.275 = (bf16[2,2,4,560,256]{4,3,2,1,0:T(8,128)(2,1)}, bf16[2,2,4,560,256]{4,3,2,1,0:T(8,128)(2,1)}) custom-call(s32[4]{0:T(128)} %pad_add_fusion.place_ref.refs_0_, bf16[512,1024]{1,0:T(8,128)(2,1)} %shard_map.264.refs_1_, bf16[512,896]{1,0:T(8,128)(2,1)} %get-tuple-element.229.refs_2_, ...), custom_call_target="tpu_custom_call", output_to_operand_aliasing={{0}: (3, {}), {1}: (4, {})} | custom-call | flops 18790480 | bytes 76021 | tf_op jit(solution)/shard_map/pallas_call | solution.py:441
  330.6 3.9 fusion.11
  341.7 14.5 %convolution_convert_fusion.1 = bf16[2304,896]{1,0:T(8,128)(2,1)S(1)} fusion(bf16[2304,2048]{1,0:T(8,128)(2,1)} %get-tuple-element.158.refs_2_.refs_3_, bf16[896,2048]{1,0:T(8,128)(2,1)} %get-tuple-element.126), kind=kOutput, calls=%fused_computation.18 | convolution fusion | flops 8457781248 | bytes 17235968 | tf_op jit(solution)/shard_map/dot_general | solution.py:24
  356.2 7.7 %collective-permute-done.29 = bf16[512,256]{1,0:T(8,128)(2,1)S(1)} collective-permute-done((bf16[512,256]{1,0:T(8,128)(2,1)}, bf16[512,256]{1,0:T(8,128)(2,1)S(1)}, u32[]{:S(2)}, u32[]{:S(2)}) %collective-permute-start.29) | collective-permute-done | bytes 262176 | tf_op jit(solution)/shard_map/ppermute | solution.py:59
  365.1 3.8 fusion.14
  372.8 3.7 fusion.13
  377.7 7.1 %collective-permute-start.32 = (bf16[224,896]{1,0:T(8,128)(2,1)}, bf16[224,896]{1,0:T(8,128)(2,1)S(1)}, u32[]{:S(2)}, u32[]{:S(2)}) collective-permute-start(bf16[224,896]{1,0:T(8,128)(2,1)} %get-tuple-element.237), channel_id=1, source_target_pairs={{0,8},{1,9},{2,10},{3,11},{4,12},{5,13},{6,14},{7,15},{8,0},{9,1},... | collective-permute-start | bytes 1204232 | tf_op jit(solution)/shard_map/ppermute | solution.py:183
  388.3 46.6 %shard_map.276 = (bf16[2048,768]{1,0:T(8,128)(2,1)}, f32[4,6,8,256]{3,2,1,0:T(8,128)}) custom-call(s32[1]{0:T(128)} %bitcast.1.pos_ref.mine_ref, f32[4,6]{1,0:T(4,128)} %copy.47.bias_ref, bf16[2048,768]{1,0:T(8,128)(2,1)} %get-tuple-element.117.qkv_ref, bf16[2048,256]{1,0:T(8,128)(2,1)} %get-tuple-element.121.o_ref, ...), custom_call_target="tpu_custom_call" | custom-call | flops 214748368 | bytes 167772 | tf_op jit(solution)/shard_map/pallas_call | solution.py:754
  434.9 3.2 fusion.17
  438.1 3.3 collective-permute-start.37
  443.6 7.4 %shard_map.277 = (bf16[4,112,768]{2,1,0:T(8,128)(2,1)}, bf16[4,112,768]{2,1,0:T(8,128)(2,1)}) custom-call(s32[4]{0:T(128)} %pad_add_fusion.place_ref.refs_0_, bf16[2048,896]{1,0:T(8,128)(2,1)} %get-tuple-element.173.left, bf16[2048,768]{1,0:T(8,128)(2,1)} %get-tuple-element.184.right), custom_call_target="tpu_custom_call" | custom-call | flops 56371444 | bytes 136314 | tf_op jit(solution)/shard_map/pallas_call | solution.py:560
  451.0 4.5 collective-permute-done.37
  455.5 6.1 %multiply_reduce_fusion = (f32[896]{0:T(1024)S(1)}, bf16[2048,896]{1,0:T(8,128)(2,1)S(1)}) fusion(bf16[2048,896]{1,0:T(8,128)(2,1)S(1)} %copy-done.24, bf16[2048,768]{1,0:T(8,128)(2,1)} %get-tuple-element.184.right, bf16[896,768]{1,0:T(8,128)(2,1)S(1)} %copy-done.55), kind=kOutput, calls=%fused_computation.15 | convolution fusion | flops 2825911296 | bytes 11865600 | tf_op jit(solution)/shard_map/dot_general | solution.py:24
  465.4 2.9 fusion.16
  474.6 9.7 %collective-permute-done.38 = bf16[560,256]{1,0:T(8,128)(2,1)S(1)} collective-permute-done((bf16[560,256]{1,0:T(8,128)(2,1)S(1)}, bf16[560,256]{1,0:T(8,128)(2,1)S(1)}, u32[]{:S(2)}, u32[]{:S(2)}) %collective-permute-start.38) | collective-permute-done | bytes 286752 | tf_op jit(solution)/shard_map/ppermute | solution.py:183
  496.7 9.0 %add_convert_fusion.2 = bf16[512,896]{1,0:T(8,128)(2,1)} fusion(f32[512,896]{1,0:T(8,128)S(1)} %get-tuple-element.275, bf16[512,3584]{1,0:T(8,128)(2,1)} %get-tuple-element.189.left, bf16[3584,896]{1,0:T(8,128)(2,1)} %get-tuple-element.136), kind=kOutput, calls=%fused_computation.51 | convolution fusion | flops 3289251840 | bytes 12845056 | tf_op jit(solution)/shard_map/dot_general | solution.py:24
  509.0 19.1 %shard_map.278 = f32[24,128]{1,0:T(8,128)} custom-call(f32[24,128]{1,0:T(8,128)} %fusion.29.in_ref), custom_call_target="tpu_custom_call" | custom-call | tf_op jit(solution)/shard_map/pallas_call | solution.py:528
  536.9 3.4 fusion.24
  (273 shorter events, 119.7 us)
Async XLA Ops:
  0.7 59.6 %collective-permute-start.6 = (bf16[512,896]{1,0:T(8,128)(2,1)}, bf16[512,896]{1,0:T(8,128)(2,1)S(1)}, u32[]{:S(2)}, u32[]{:S(2)}) collective-permute-start(bf16[512,896]{1,0:T(8,128)(2,1)} %bitcast.148), channel_id=1, source_target_pairs={{0,1},{1,0},{2,3},{3,2},{4,5},{5,4},{6,7},{7,6},{8,9},{9,8},{10,11... | collective-permute-start | bytes 2752520 | tf_op jit(solution)/shard_map/ppermute | solution.py:59
  1.2 23.7 %collective-permute-start.7 = (bf16[512,896]{1,0:T(8,128)(2,1)}, bf16[512,896]{1,0:T(8,128)(2,1)S(1)}, u32[]{:S(2)}, u32[]{:S(2)}) collective-permute-start(bf16[512,896]{1,0:T(8,128)(2,1)} %bitcast.149), channel_id=1, source_target_pairs={{0,2},{1,3},{2,0},{3,1},{4,6},{5,7},{6,4},{7,5},{8,10},{9,11},{10,... | collective-permute-start | bytes 2752520 | tf_op jit(solution)/shard_map/ppermute | solution.py:59
  6.2 18.7 %collective-permute-start.11 = (bf16[112,768]{1,0:T(8,128)(2,1)S(1)}, bf16[112,768]{1,0:T(8,128)(2,1)S(1)}, u32[]{:S(2)}, u32[]{:S(2)}) collective-permute-start(bf16[112,768]{1,0:T(8,128)(2,1)S(1)} %constant_dynamic-update-slice_fusion.3), channel_id=1, source_target_pairs={{0,24},{4,28},{8,16},{12,20},{16,8},{20,12},{24,0},{28,4},{1,25},{... | collective-permute-start | bytes 516104 | tf_op jit(solution)/shard_map/ppermute | solution.py:59
  9.8 19.0 %collective-permute-start.10 = (bf16[112,768]{1,0:T(8,128)(2,1)S(1)}, bf16[112,768]{1,0:T(8,128)(2,1)S(1)}, u32[]{:S(2)}, u32[]{:S(2)}) collective-permute-start(bf16[112,768]{1,0:T(8,128)(2,1)S(1)} %constant_dynamic-update-slice_fusion.3), channel_id=1, source_target_pairs={{0,16},{4,20},{8,24},{12,28},{16,0},{20,4},{24,8},{28,12},{1,17},{... | collective-permute-start | bytes 516104 | tf_op jit(solution)/shard_map/ppermute | solution.py:59
  9.9 19.0 %collective-permute-start.9 = (bf16[112,768]{1,0:T(8,128)(2,1)S(1)}, bf16[112,768]{1,0:T(8,128)(2,1)S(1)}, u32[]{:S(2)}, u32[]{:S(2)}) collective-permute-start(bf16[112,768]{1,0:T(8,128)(2,1)S(1)} %constant_dynamic-update-slice_fusion.3), channel_id=1, source_target_pairs={{0,8},{4,12},{8,0},{12,4},{16,24},{20,28},{24,16},{28,20},{1,9},{5... | collective-permute-start | bytes 516104 | tf_op jit(solution)/shard_map/ppermute | solution.py:59
  24.9 35.4 %collective-permute-start.8 = (bf16[512,896]{1,0:T(8,128)(2,1)S(1)}, bf16[512,896]{1,0:T(8,128)(2,1)S(1)}, u32[]{:S(2)}, u32[]{:S(2)}) collective-permute-start(bf16[512,896]{1,0:T(8,128)(2,1)S(1)} %collective-permute-done.7.refs_2_), channel_id=1, source_target_pairs={{0,1},{1,0},{2,3},{3,2},{4,5},{5,4},{6,7},{7,6},{8,9},{9,8},{10,11... | collective-permute-start | bytes 2752520 | tf_op jit(solution)/shard_map/ppermute | solution.py:59
  25.0 11.7 %collective-permute-start.2 = (bf16[560,256]{1,0:T(8,128)(2,1)S(1)}, bf16[560,256]{1,0:T(8,128)(2,1)S(1)}, u32[]{:S(2)}, u32[]{:S(2)}) collective-permute-start(bf16[560,256]{1,0:T(8,128)(2,1)S(1)} %maximum_dynamic-update-slice_fusion), channel_id=1, source_target_pairs={{0,24},{1,25},{2,26},{3,27},{4,28},{5,29},{6,30},{7,31},{8,16},{9,... | collective-permute-start | bytes 860168 | tf_op jit(solution)/shard_map/ppermute | solution.py:183
  29.0 31.3 %collective-permute-start.12 = (bf16[4,112,768]{2,1,0:T(8,128)(2,1)S(1)}, bf16[4,112,768]{2,1,0:T(8,128)(2,1)S(1)}, u32[]{:S(2)}, u32[]{:S(2)}) collective-permute-start(bf16[4,112,768]{2,1,0:T(8,128)(2,1)S(1)} %pad_maximum_fusion.6.near_ref), channel_id=1, source_target_pairs={{0,4},{4,0},{8,12},{12,8},{16,20},{20,16},{24,28},{28,24},{1,5},{5... | collective-permute-start | bytes 2064392 | tf_op jit(solution)/shard_map/ppermute | solution.py:59
  30.6 23.5 %collective-permute-start.1 = (bf16[560,256]{1,0:T(8,128)(2,1)S(1)}, bf16[560,256]{1,0:T(8,128)(2,1)S(1)}, u32[]{:S(2)}, u32[]{:S(2)}) collective-permute-start(bf16[560,256]{1,0:T(8,128)(2,1)S(1)} %maximum_dynamic-update-slice_fusion), channel_id=1, source_target_pairs={{0,16},{1,17},{2,18},{3,19},{4,20},{5,21},{6,22},{7,23},{8,24},{9,... | collective-permute-start | bytes 860168 | tf_op jit(solution)/shard_map/ppermute | solution.py:183
  36.7 23.4 %collective-permute-start = (bf16[560,256]{1,0:T(8,128)(2,1)S(1)}, bf16[560,256]{1,0:T(8,128)(2,1)S(1)}, u32[]{:S(2)}, u32[]{:S(2)}) collective-permute-start(bf16[560,256]{1,0:T(8,128)(2,1)S(1)} %maximum_dynamic-update-slice_fusion), channel_id=1, source_target_pairs={{0,8},{1,9},{2,10},{3,11},{4,12},{5,13},{6,14},{7,15},{8,0},{9,1},... | collective-permute-start | bytes 860168 | tf_op jit(solution)/shard_map/ppermute | solution.py:183
  61.3 16.0 %collective-permute-start.14 = (bf16[4,560,256]{2,1,0:T(8,128)(2,1)S(1)}, bf16[4,560,256]{2,1,0:T(8,128)(2,1)}, u32[]{:S(2)}, u32[]{:S(2)}) collective-permute-start(bf16[4,560,256]{2,1,0:T(8,128)(2,1)S(1)} %pad_maximum_fusion.4), channel_id=1, source_target_pairs={{0,2},{1,5},{2,0},{3,7},{4,6},{5,1},{6,4},{7,3},{8,10},{9,13},{10,... | collective-permute-start | bytes 3440648 | tf_op jit(solution)/shard_map/ppermute | solution.py:187
  78.7 36.8 %collective-permute-start.15 = (bf16[8,560,256]{2,1,0:T(8,128)(2,1)S(1)}, bf16[8,560,256]{2,1,0:T(8,128)(2,1)}, u32[]{:S(2)}, u32[]{:S(2)}) collective-permute-start(bf16[8,560,256]{2,1,0:T(8,128)(2,1)S(1)} %pad_maximum_fusion.2.refs_0_), channel_id=1, source_target_pairs={{0,4},{1,3},{2,6},{3,1},{4,0},{5,7},{6,2},{7,5},{8,12},{9,11},{10,... | collective-permute-start | bytes 6881288 | tf_op jit(solution)/shard_map/ppermute | solution.py:193
  81.4 34.1 %collective-permute-start.13 = (bf16[256,896]{1,0:T(8,128)(2,1)S(1)}, bf16[256,896]{1,0:T(8,128)(2,1)}, u32[]{:S(2)}, u32[]{:S(2)}) collective-permute-start(bf16[256,896]{1,0:T(8,128)(2,1)S(1)} %bitcast.157), channel_id=1, source_target_pairs={{0,1},{1,2},{2,3},{4,5},{5,6},{6,7},{8,9},{9,10},{10,11},{12,13},{... | collective-permute-start | bytes 1376264 | tf_op jit(solution)/shard_map/ppermute | solution.py:1004
  83.6 31.2 %collective-permute-start.3 = (bf16[224,896]{1,0:T(8,128)(2,1)S(1)}, bf16[224,896]{1,0:T(8,128)(2,1)}, u32[]{:S(2)}, u32[]{:S(2)}) collective-permute-start(bf16[224,896]{1,0:T(8,128)(2,1)S(1)} %maximum_maximum_fusion), channel_id=1, source_target_pairs={{0,8},{1,9},{2,10},{3,11},{4,12},{5,13},{6,14},{7,15},{8,0},{9,1},... | collective-permute-start | bytes 1204232 | tf_op jit(solution)/shard_map/ppermute | solution.py:183
  83.7 31.8 %collective-permute-start.4 = (bf16[224,896]{1,0:T(8,128)(2,1)S(1)}, bf16[224,896]{1,0:T(8,128)(2,1)}, u32[]{:S(2)}, u32[]{:S(2)}) collective-permute-start(bf16[224,896]{1,0:T(8,128)(2,1)S(1)} %maximum_maximum_fusion), channel_id=1, source_target_pairs={{0,16},{1,17},{2,18},{3,19},{4,20},{5,21},{6,22},{7,23},{8,24},{9,... | collective-permute-start | bytes 1204232 | tf_op jit(solution)/shard_map/ppermute | solution.py:183
  86.7 28.8 %collective-permute-start.5 = (bf16[224,896]{1,0:T(8,128)(2,1)S(1)}, bf16[224,896]{1,0:T(8,128)(2,1)}, u32[]{:S(2)}, u32[]{:S(2)}) collective-permute-start(bf16[224,896]{1,0:T(8,128)(2,1)S(1)} %maximum_maximum_fusion), channel_id=1, source_target_pairs={{0,24},{1,25},{2,26},{3,27},{4,28},{5,29},{6,30},{7,31},{8,16},{9,... | collective-permute-start | bytes 1204232 | tf_op jit(solution)/shard_map/ppermute | solution.py:183
  114.8 23.7 %collective-permute-start.19 = (bf16[8,560,256]{2,1,0:T(8,128)(2,1)S(1)}, bf16[8,560,256]{2,1,0:T(8,128)(2,1)}, u32[]{:S(2)}, u32[]{:S(2)}) collective-permute-start(bf16[8,560,256]{2,1,0:T(8,128)(2,1)S(1)} %pad_maximum_fusion.2.refs_0_), channel_id=1, source_target_pairs={{0,1},{1,0},{2,3},{3,2},{4,5},{5,4},{6,7},{7,6},{8,9},{9,8},{10,11... | collective-permute-start | bytes 6881288 | tf_op jit(solution)/shard_map/ppermute | solution.py:199
  115.5 23.0 %collective-permute-start.20 = (bf16[8,560,256]{2,1,0:T(8,128)(2,1)}, bf16[8,560,256]{2,1,0:T(8,128)(2,1)}, u32[]{:S(2)}, u32[]{:S(2)}) collective-permute-start(bf16[8,560,256]{2,1,0:T(8,128)(2,1)} %collective-permute-done.15.refs_1_), channel_id=1, source_target_pairs={{0,1},{1,0},{2,3},{3,2},{4,5},{5,4},{6,7},{7,6},{8,9},{9,8},{10,11... | collective-permute-start | bytes 6881288 | tf_op jit(solution)/shard_map/ppermute | solution.py:199
  117.5 5.6 %collective-permute-start.16 = (bf16[512,256]{1,0:T(8,128)(2,1)S(1)}, bf16[512,256]{1,0:T(8,128)(2,1)S(1)}, u32[]{:S(2)}, u32[]{:S(2)}) collective-permute-start(bf16[512,256]{1,0:T(8,128)(2,1)S(1)} %get-tuple-element.244), channel_id=1, source_target_pairs={{0,1},{1,0},{2,3},{3,2},{4,5},{5,4},{6,7},{7,6},{8,9},{9,8},{10,11... | collective-permute-start | bytes 786440 | tf_op jit(solution)/shard_map/ppermute | solution.py:59
  118.0 9.2 %collective-permute-start.17 = (bf16[512,256]{1,0:T(8,128)(2,1)S(1)}, bf16[512,256]{1,0:T(8,128)(2,1)S(1)}, u32[]{:S(2)}, u32[]{:S(2)}) collective-permute-start(bf16[512,256]{1,0:T(8,128)(2,1)S(1)} %get-tuple-element.243), channel_id=1, source_target_pairs={{0,2},{1,3},{2,0},{3,1},{4,6},{5,7},{6,4},{7,5},{8,10},{9,11},{10,... | collective-permute-start | bytes 786440 | tf_op jit(solution)/shard_map/ppermute | solution.py:59
  118.8 12.1 %collective-permute-start.18 = (bf16[512,256]{1,0:T(8,128)(2,1)S(1)}, bf16[512,256]{1,0:T(8,128)(2,1)S(1)}, u32[]{:S(2)}, u32[]{:S(2)}) collective-permute-start(bf16[512,256]{1,0:T(8,128)(2,1)S(1)} %get-tuple-element.242), channel_id=1, source_target_pairs={{0,3},{1,2},{2,1},{3,0},{4,7},{5,6},{6,5},{7,4},{8,11},{9,10},{10,... | collective-permute-start | bytes 786440 | tf_op jit(solution)/shard_map/ppermute | solution.py:59
  134.0 21.1 %collective-permute-start.21 = (bf16[4,224,896]{2,1,0:T(8,128)(2,1)}, bf16[4,224,896]{2,1,0:T(8,128)(2,1)}, u32[]{:S(2)}, u32[]{:S(2)}) collective-permute-start(bf16[4,224,896]{2,1,0:T(8,128)(2,1)} %pad_maximum_fusion.3), channel_id=1, source_target_pairs={{0,2},{1,5},{2,0},{3,7},{4,6},{5,1},{6,4},{7,3},{8,10},{9,13},{10,... | collective-permute-start | bytes 4816904 | tf_op jit(solution)/shard_map/ppermute | solution.py:187
  156.8 38.1 %collective-permute-start.22 = (bf16[8,224,896]{2,1,0:T(8,128)(2,1)S(1)}, bf16[8,224,896]{2,1,0:T(8,128)(2,1)}, u32[]{:S(2)}, u32[]{:S(2)}) collective-permute-start(bf16[8,224,896]{2,1,0:T(8,128)(2,1)S(1)} %constant_dynamic-update-slice_fusion.6.refs_0_), channel_id=1, source_target_pairs={{0,4},{1,3},{2,6},{3,1},{4,0},{5,7},{6,2},{7,5},{8,12},{9,11},{10,... | collective-permute-start | bytes 9633800 | tf_op jit(solution)/shard_map/ppermute | solution.py:193
  159.3 39.1 %collective-permute-start.23 = (bf16[8,224,896]{2,1,0:T(8,128)(2,1)S(1)}, bf16[8,224,896]{2,1,0:T(8,128)(2,1)}, u32[]{:S(2)}, u32[]{:S(2)}) collective-permute-start(bf16[8,224,896]{2,1,0:T(8,128)(2,1)S(1)} %constant_dynamic-update-slice_fusion.6.refs_0_), channel_id=1, source_target_pairs={{0,1},{1,0},{2,3},{3,2},{4,5},{5,4},{6,7},{7,6},{8,9},{9,8},{10,11... | collective-permute-start | bytes 9633800 | tf_op jit(solution)/shard_map/ppermute | solution.py:199
  195.0 6.1 %collective-permute-start.24 = (bf16[8,224,896]{2,1,0:T(8,128)(2,1)}, bf16[8,224,896]{2,1,0:T(8,128)(2,1)}, u32[]{:S(2)}, u32[]{:S(2)}) collective-permute-start(bf16[8,224,896]{2,1,0:T(8,128)(2,1)} %collective-permute-done.22.refs_1_), channel_id=1, source_target_pairs={{0,1},{1,0},{2,3},{3,2},{4,5},{5,4},{6,7},{7,6},{8,9},{9,8},{10,11... | collective-permute-start | bytes 9633800 | tf_op jit(solution)/shard_map/ppermute | solution.py:199
  254.5 12.3 %collective-permute-start.25 = (bf16[2,2,4,224,896]{4,3,2,1,0:T(8,128)(2,1)}, bf16[2,2,4,224,896]{4,3,2,1,0:T(8,128)(2,1)S(1)}, u32[]{:S(2)}, u32[]{:S(2)}) collective-permute-start(bf16[2,2,4,224,896]{4,3,2,1,0:T(8,128)(2,1)} %get-tuple-element.141), channel_id=1, source_target_pairs={{0,1},{1,0},{2,3},{3,2},{4,5},{5,4},{6,7},{7,6},{8,9},{9,8},{10,11... | collective-permute-start | bytes 19267592 | tf_op jit(solution)/shard_map/ppermute | solution.py:199
  270.5 46.9 %collective-permute-start.26 = (bf16[2,4,224,896]{3,2,1,0:T(8,128)(2,1)}, bf16[2,4,224,896]{3,2,1,0:T(8,128)(2,1)}, u32[]{:S(2)}, u32[]{:S(2)}) collective-permute-start(bf16[2,4,224,896]{3,2,1,0:T(8,128)(2,1)} %fusion.10), channel_id=1, source_target_pairs={{0,4},{1,3},{2,6},{3,1},{4,0},{5,7},{6,2},{7,5},{8,12},{9,11},{10,... | collective-permute-start | bytes 9633800 | tf_op jit(solution)/shard_map/ppermute | solution.py:193
  329.8 35.3 %collective-permute-start.31 = (bf16[2,2,4,560,256]{4,3,2,1,0:T(8,128)(2,1)}, bf16[2,2,4,560,256]{4,3,2,1,0:T(8,128)(2,1)}, u32[]{:S(2)}, u32[]{:S(2)}) collective-permute-start(bf16[2,2,4,560,256]{4,3,2,1,0:T(8,128)(2,1)} %get-tuple-element.160), channel_id=1, source_target_pairs={{0,1},{1,0},{2,3},{3,2},{4,5},{5,4},{6,7},{7,6},{8,9},{9,8},{10,11... | collective-permute-start | bytes 13762568 | tf_op jit(solution)/shard_map/ppermute | solution.py:199
  334.4 35.7 %collective-permute-start.27 = (bf16[4,224,896]{2,1,0:T(8,128)(2,1)}, bf16[4,224,896]{2,1,0:T(8,128)(2,1)S(1)}, u32[]{:S(2)}, u32[]{:S(2)}) collective-permute-start(bf16[4,224,896]{2,1,0:T(8,128)(2,1)} %fusion.11), channel_id=1, source_target_pairs={{0,2},{1,5},{2,0},{3,7},{4,6},{5,1},{6,4},{7,3},{8,10},{9,13},{10,... | collective-permute-start | bytes 4816904 | tf_op jit(solution)/shard_map/ppermute | solution.py:187
  339.8 16.4 %collective-permute-start.28 = (bf16[512,256]{1,0:T(8,128)(2,1)}, bf16[512,256]{1,0:T(8,128)(2,1)S(1)}, u32[]{:S(2)}, u32[]{:S(2)}) collective-permute-start(bf16[512,256]{1,0:T(8,128)(2,1)} %get-tuple-element.155), channel_id=1, source_target_pairs={{0,1},{1,0},{2,3},{3,2},{4,5},{5,4},{6,7},{7,6},{8,9},{9,8},{10,11... | collective-permute-start | bytes 786440 | tf_op jit(solution)/shard_map/ppermute | solution.py:59
  339.8 24.0 %collective-permute-start.29 = (bf16[512,256]{1,0:T(8,128)(2,1)}, bf16[512,256]{1,0:T(8,128)(2,1)S(1)}, u32[]{:S(2)}, u32[]{:S(2)}) collective-permute-start(bf16[512,256]{1,0:T(8,128)(2,1)} %get-tuple-element.156), channel_id=1, source_target_pairs={{0,2},{1,3},{2,0},{3,1},{4,6},{5,7},{6,4},{7,5},{8,10},{9,11},{10,... | collective-permute-start | bytes 786440 | tf_op jit(solution)/shard_map/ppermute | solution.py:59
  341.2 23.9 %collective-permute-start.30 = (bf16[512,256]{1,0:T(8,128)(2,1)}, bf16[512,256]{1,0:T(8,128)(2,1)S(1)}, u32[]{:S(2)}, u32[]{:S(2)}) collective-permute-start(bf16[512,256]{1,0:T(8,128)(2,1)} %get-tuple-element.157), channel_id=1, source_target_pairs={{0,3},{1,2},{2,1},{3,0},{4,7},{5,6},{6,5},{7,4},{8,11},{9,10},{10,... | collective-permute-start | bytes 786440 | tf_op jit(solution)/shard_map/ppermute | solution.py:59
  368.9 66.0 %collective-permute-start.35 = (bf16[2,4,560,256]{3,2,1,0:T(8,128)(2,1)}, bf16[2,4,560,256]{3,2,1,0:T(8,128)(2,1)}, u32[]{:S(2)}, u32[]{:S(2)}) collective-permute-start(bf16[2,4,560,256]{3,2,1,0:T(8,128)(2,1)} %fusion.14), channel_id=1, source_target_pairs={{0,4},{1,3},{2,6},{3,1},{4,0},{5,7},{6,2},{7,5},{8,12},{9,11},{10,... | collective-permute-start | bytes 6881288 | tf_op jit(solution)/shard_map/ppermute | solution.py:193
  371.5 63.4 %collective-permute-start.36 = (bf16[256,896]{1,0:T(8,128)(2,1)}, bf16[256,896]{1,0:T(8,128)(2,1)}, u32[]{:S(2)}, u32[]{:S(2)}) collective-permute-start(bf16[256,896]{1,0:T(8,128)(2,1)} %slice.250), channel_id=1, source_target_pairs={{1,0},{2,1},{3,2},{5,4},{6,5},{7,6},{9,8},{10,9},{11,10},{13,12},{... | collective-permute-start | bytes 1376264 | tf_op jit(solution)/shard_map/ppermute | solution.py:1113
  377.7 57.2 %collective-permute-start.32 = (bf16[224,896]{1,0:T(8,128)(2,1)}, bf16[224,896]{1,0:T(8,128)(2,1)S(1)}, u32[]{:S(2)}, u32[]{:S(2)}) collective-permute-start(bf16[224,896]{1,0:T(8,128)(2,1)} %get-tuple-element.237), channel_id=1, source_target_pairs={{0,8},{1,9},{2,10},{3,11},{4,12},{5,13},{6,14},{7,15},{8,0},{9,1},... | collective-permute-start | bytes 1204232 | tf_op jit(solution)/shard_map/ppermute | solution.py:183
  384.8 50.0 %collective-permute-start.33 = (bf16[224,896]{1,0:T(8,128)(2,1)}, bf16[224,896]{1,0:T(8,128)(2,1)S(1)}, u32[]{:S(2)}, u32[]{:S(2)}) collective-permute-start(bf16[224,896]{1,0:T(8,128)(2,1)} %get-tuple-element.236), channel_id=1, source_target_pairs={{0,16},{1,17},{2,18},{3,19},{4,20},{5,21},{6,22},{7,23},{8,24},{9,... | collective-permute-start | bytes 1204232 | tf_op jit(solution)/shard_map/ppermute | solution.py:183
  385.8 49.1 %collective-permute-start.34 = (bf16[224,896]{1,0:T(8,128)(2,1)}, bf16[224,896]{1,0:T(8,128)(2,1)S(1)}, u32[]{:S(2)}, u32[]{:S(2)}) collective-permute-start(bf16[224,896]{1,0:T(8,128)(2,1)} %get-tuple-element.235), channel_id=1, source_target_pairs={{0,24},{1,25},{2,26},{3,27},{4,28},{5,29},{6,30},{7,31},{8,16},{9,... | collective-permute-start | bytes 1204232 | tf_op jit(solution)/shard_map/ppermute | solution.py:183
  438.1 17.4 %collective-permute-start.37 = (bf16[4,560,256]{2,1,0:T(8,128)(2,1)}, bf16[4,560,256]{2,1,0:T(8,128)(2,1)}, u32[]{:S(2)}, u32[]{:S(2)}) collective-permute-start(bf16[4,560,256]{2,1,0:T(8,128)(2,1)} %fusion.17), channel_id=1, source_target_pairs={{0,2},{1,5},{2,0},{3,7},{4,6},{5,1},{6,4},{7,3},{8,10},{9,13},{10,... | collective-permute-start | bytes 3440648 | tf_op jit(solution)/shard_map/ppermute | solution.py:187
  463.2 8.8 %collective-permute-start.40 = (bf16[512,896]{1,0:T(8,128)(2,1)}, bf16[512,896]{1,0:T(8,128)(2,1)}, u32[]{:S(2)}, u32[]{:S(2)}) collective-permute-start(bf16[512,896]{1,0:T(8,128)(2,1)} %get-tuple-element.234), channel_id=1, source_target_pairs={{0,1},{1,0},{2,3},{3,2},{4,5},{5,4},{6,7},{7,6},{8,9},{9,8},{10,11... | collective-permute-start | bytes 2752520 | tf_op jit(solution)/shard_map/ppermute | solution.py:59
  464.4 21.7 %collective-permute-start.41 = (bf16[4,112,768]{2,1,0:T(8,128)(2,1)}, bf16[4,112,768]{2,1,0:T(8,128)(2,1)S(1)}, u32[]{:S(2)}, u32[]{:S(2)}) collective-permute-start(bf16[4,112,768]{2,1,0:T(8,128)(2,1)} %get-tuple-element.187), channel_id=1, source_target_pairs={{0,4},{4,0},{8,12},{12,8},{16,20},{20,16},{24,28},{28,24},{1,5},{5... | collective-permute-start | bytes 2064392 | tf_op jit(solution)/shard_map/ppermute | solution.py:59
  465.4 20.8 %collective-permute-start.42 = (bf16[512,896]{1,0:T(8,128)(2,1)}, bf16[512,896]{1,0:T(8,128)(2,1)}, u32[]{:S(2)}, u32[]{:S(2)}) collective-permute-start(bf16[512,896]{1,0:T(8,128)(2,1)} %get-tuple-element.233), channel_id=1, source_target_pairs={{0,1},{1,0},{2,3},{3,2},{4,5},{5,4},{6,7},{7,6},{8,9},{9,8},{10,11... | collective-permute-start | bytes 2752520 | tf_op jit(solution)/shard_map/ppermute | solution.py:59
  469.0 15.2 %collective-permute-start.38 = (bf16[560,256]{1,0:T(8,128)(2,1)S(1)}, bf16[560,256]{1,0:T(8,128)(2,1)S(1)}, u32[]{:S(2)}, u32[]{:S(2)}) collective-permute-start(bf16[560,256]{1,0:T(8,128)(2,1)S(1)} %get-tuple-element.241), channel_id=1, source_target_pairs={{0,8},{1,9},{2,10},{3,11},{4,12},{5,13},{6,14},{7,15},{8,0},{9,1},... | collective-permute-start | bytes 860168 | tf_op jit(solution)/shard_map/ppermute | solution.py:183
  470.1 16.1 %collective-permute-start.39 = (bf16[560,256]{1,0:T(8,128)(2,1)S(1)}, bf16[560,256]{1,0:T(8,128)(2,1)S(1)}, u32[]{:S(2)}, u32[]{:S(2)}) collective-permute-start(bf16[560,256]{1,0:T(8,128)(2,1)S(1)} %get-tuple-element.240), channel_id=1, source_target_pairs={{0,16},{1,17},{2,18},{3,19},{4,20},{5,21},{6,22},{7,23},{8,24},{9,... | collective-permute-start | bytes 860168 | tf_op jit(solution)/shard_map/ppermute | solution.py:183
  488.0 8.7 %collective-permute-start.43 = (bf16[112,768]{1,0:T(8,128)(2,1)}, bf16[112,768]{1,0:T(8,128)(2,1)S(1)}, u32[]{:S(2)}, u32[]{:S(2)}) collective-permute-start(bf16[112,768]{1,0:T(8,128)(2,1)} %get-tuple-element.250), channel_id=1, source_target_pairs={{0,8},{1,9},{2,10},{3,11},{4,12},{5,13},{6,14},{7,15},{8,0},{9,1},... | collective-permute-start | bytes 516104 | tf_op jit(solution)/shard_map/ppermute | solution.py:183
  488.5 39.7 %collective-permute-start.46 = (bf16[560,256]{1,0:T(8,128)(2,1)}, bf16[560,256]{1,0:T(8,128)(2,1)}, u32[]{:S(2)}, u32[]{:S(2)}) collective-permute-start(bf16[560,256]{1,0:T(8,128)(2,1)} %get-tuple-element.239), channel_id=1, source_target_pairs={{0,24},{1,25},{2,26},{3,27},{4,28},{5,29},{6,30},{7,31},{8,16},{9,... | collective-permute-start | bytes 860168 | tf_op jit(solution)/shard_map/ppermute | solution.py:183
  491.2 37.0 %collective-permute-start.44 = (bf16[112,768]{1,0:T(8,128)(2,1)}, bf16[112,768]{1,0:T(8,128)(2,1)}, u32[]{:S(2)}, u32[]{:S(2)}) collective-permute-start(bf16[112,768]{1,0:T(8,128)(2,1)} %get-tuple-element.249), channel_id=1, source_target_pairs={{0,16},{1,17},{2,18},{3,19},{4,20},{5,21},{6,22},{7,23},{8,24},{9,... | collective-permute-start | bytes 516104 | tf_op jit(solution)/shard_map/ppermute | solution.py:183
  492.3 35.9 %collective-permute-start.45 = (bf16[112,768]{1,0:T(8,128)(2,1)}, bf16[112,768]{1,0:T(8,128)(2,1)}, u32[]{:S(2)}, u32[]{:S(2)}) collective-permute-start(bf16[112,768]{1,0:T(8,128)(2,1)} %get-tuple-element.248), channel_id=1, source_target_pairs={{0,24},{1,25},{2,26},{3,27},{4,28},{5,29},{6,30},{7,31},{8,16},{9,... | collective-permute-start | bytes 516104 | tf_op jit(solution)/shard_map/ppermute | solution.py:183
  494.7 33.5 %collective-permute-start.47 = (bf16[512,896]{1,0:T(8,128)(2,1)}, bf16[512,896]{1,0:T(8,128)(2,1)}, u32[]{:S(2)}, u32[]{:S(2)}) collective-permute-start(bf16[512,896]{1,0:T(8,128)(2,1)} %add_convert_fusion.3), channel_id=1, source_target_pairs={{0,2},{1,3},{2,0},{3,1},{4,6},{5,7},{6,4},{7,5},{8,10},{9,11},{10,... | collective-permute-start | bytes 2752520 | tf_op jit(solution)/shard_map/ppermute | solution.py:59
  (61 other events, 732.2 us)
